TPU v7x, 128 devices: a whole 4x4x4 slice. The times are simulated.
128 devices in a mesh: seq: 32 (over z, y, core), head: 4 (over x).
Axes of the slice: x: 4, y: 4, z: 4, core: 2. Of those that a mesh axis runs over, the one named last changes fastest.
Arguments:
- queries: bfloat16 [16384, 4096], P('seq', 'head'), may hold values from -4 to 4
- key_vectors: bfloat16 [16384, 4096], P('seq', 'head'), may hold values from -6 to 6
- output_grad: bfloat16 [16384, 4096], P('seq', 'head'), may hold values from -6 to 6
- value_weight: bfloat16 [6144, 4096], P('seq', 'head'), may hold values from -0.078125 to 0.078125
- decay_rate: float32 [32], P('head'), may hold values from 1.2207031e-05 to 0.035
- doc_lengths: int32 [4], replicated, may hold values from 1 to 8192, 16384 in all
- owner_block: int32 [16384, 1], P('seq'), may hold values from 0 to 127; in each aligned block of 128 rows (0 to 127, 128 to 255, ...) at most 2 rows name the same one
- row_offset: int32 [16384], P('seq'), may hold values from 0 to 781
Outputs:
- row_grads: bfloat16 [128, 128, 2, 6144], P(('seq', 'head'))
Inputs may be any that keep to these rules, and one draw needn't show every extreme that they name: `doc_lengths`: the longest document has exactly 8192 positions. `owner_block`: in each aligned block of 128 positions no owner is named more than 2 times; some block names some owner exactly 2 times.
All inputs are finite; a program needn't handle non-finite values.
Results may differ from a plain program's by a relative error of at most 0.0071.
Values may be sent and summed in bfloat16 or wider, within the bound.
No kernel may reach another device: no remote copies, remote signals or barrier semaphores. Data moves between devices by JAX's collectives and lax.ppermute only.
A program may use at most 128 MiB of HBM per device.

v0:
```python
import jax
import jax.numpy as jnp
from jax import lax
from jax.experimental import pallas as pl
from jax.experimental.pallas import tpu as pltpu
from jax.sharding import PartitionSpec as P

BF16 = jnp.bfloat16
F32 = jnp.float32
CAPACITY = 2
ROWS_BLK = 128


def doc_of(positions, doc_ends):
    return jnp.sum((positions[:, None] >= doc_ends[None, :]).astype(jnp.int32), axis=1)


def intra_terms(query_blk, key_blk, grad_blk, decay_rates, doc_blk, pos_blk):
    head_dim = query_blk.shape[-1]
    scores = (
        jnp.einsum("she,the->hst", key_blk, query_blk, preferred_element_type=F32) / head_dim
    )
    distance = pos_blk[None, :] - pos_blk[:, None]
    allowed = (distance >= 0) & (doc_blk[:, None] == doc_blk[None, :])
    spans = jnp.maximum(distance, 0).astype(F32)
    decayed = jnp.where(allowed[None], jnp.exp(-decay_rates[:, None, None] * spans[None]), 0.0)
    weights = (decayed * scores).astype(BF16)
    return jnp.einsum("hst,thf->shf", weights, grad_blk, preferred_element_type=F32)


def state_terms(query_blk, grad_blk, decay_rates, doc_blk, pos_blk, doc_before, pos_before):
    spans = (pos_blk - pos_before).astype(F32)
    lead_decay = jnp.where(
        (doc_blk == doc_before)[:, None], jnp.exp(-decay_rates[None, :] * spans[:, None]), 0.0
    )
    scaled = (query_blk.astype(F32) * lead_decay[:, :, None]).astype(BF16)
    return jnp.einsum("the,thf->hef", scaled, grad_blk, preferred_element_type=F32)


def inter_terms(key_blk, carried, decay_rates, doc_blk, pos_blk):
    head_dim = key_blk.shape[-1]
    spans = (pos_blk[-1] - pos_blk).astype(F32)
    tail_decay = jnp.where(
        (doc_blk == doc_blk[-1])[:, None], jnp.exp(-decay_rates[None, :] * spans[:, None]), 0.0
    )
    product = jnp.einsum("she,hef->shf", key_blk, carried, preferred_element_type=F32) / head_dim
    return product * tail_decay[:, :, None]


def project_body(slot_ref, grads_ref, weight_ref, out_ref, pick_ref):
    slots, toks = pick_ref.shape

    @pl.when(pl.program_id(0) == 0)
    def _():
        rows = lax.broadcasted_iota(jnp.int32, (slots, toks), 0)
        pick_ref[...] = (rows == slot_ref[...]).astype(F32).astype(BF16)

    total = None
    for group in range(grads_ref.shape[0]):
        part = lax.dot_general(
            grads_ref[group],
            weight_ref[group],
            (((1,), (1,)), ((), ())),
            preferred_element_type=F32,
        )
        part = part.astype(BF16).astype(F32)
        total = part if total is None else total + part
    out_ref[...] = jnp.dot(
        pick_ref[...], total.astype(BF16), preferred_element_type=F32
    ).astype(BF16)


def project(slot_index, grads, weight, slots, tile):
    groups, toks, depth = grads.shape
    width = weight.shape[1]
    return pl.pallas_call(
        project_body,
        grid=(width // tile,),
        in_specs=[
            pl.BlockSpec((1, toks), lambda i: (0, 0)),
            pl.BlockSpec((groups, toks, depth), lambda i: (0, 0, 0)),
            pl.BlockSpec((groups, tile, depth), lambda i: (0, i, 0)),
        ],
        out_specs=pl.BlockSpec((slots, tile), lambda i: (0, i)),
        out_shape=jax.ShapeDtypeStruct((slots, width), BF16),
        scratch_shapes=[pltpu.VMEM((slots, toks), BF16)],
        compiler_params=pltpu.CompilerParams(
            dimension_semantics=("arbitrary",), vmem_limit_bytes=56 << 20
        ),
        name="project",
    )(slot_index[None, :], grads, weight)


def merge_body(column_ref, row_ref, rows_ref, out_ref):
    slots = column_ref.shape[0]
    width = rows_ref.shape[-1]
    same = (column_ref[...] == row_ref[...]) & (column_ref[...] >= 0)
    same = same.astype(F32).astype(BF16)
    rows = rows_ref[...].reshape(slots, width)
    total = jnp.dot(same, rows, preferred_element_type=F32).astype(BF16)
    out_ref[...] = total.reshape(out_ref.shape)


def merge(offsets, got, capacity):
    n_seq, n_head, per, width = got.shape
    slots = n_seq * per
    return pl.pallas_call(
        merge_body,
        grid=(n_head,),
        in_specs=[
            pl.BlockSpec((slots, 1), lambda i: (0, 0)),
            pl.BlockSpec((1, slots), lambda i: (0, 0)),
            pl.BlockSpec((n_seq, 1, per, width), lambda i: (0, i, 0, 0)),
        ],
        out_specs=pl.BlockSpec((1, slots // capacity, capacity, width), lambda i: (0, 0, 0, i)),
        out_shape=jax.ShapeDtypeStruct((1, slots // capacity, capacity, n_head * width), BF16),
        compiler_params=pltpu.CompilerParams(
            dimension_semantics=("arbitrary",), vmem_limit_bytes=56 << 20
        ),
        name="merge",
    )(offsets.reshape(slots, 1), offsets.reshape(1, slots), got)


def slots_of(owners, blocks, capacity):
    toks = owners.shape[0]
    width = toks // blocks
    grouped = owners.reshape(blocks, width)
    same_owner = grouped[:, :, None] == grouped[:, None, :]
    lower = jnp.arange(width, dtype=jnp.int32)
    earlier = lower[None, :] < lower[:, None]
    rank = jnp.sum((same_owner & earlier[None]).astype(jnp.int32), axis=2)
    block_ids = jnp.arange(blocks, dtype=jnp.int32)[:, None]
    return ((grouped * blocks + block_ids) * capacity + rank).reshape(toks)


def per_device(
    queries,
    key_vectors,
    output_grad,
    value_weight,
    decay_rate,
    doc_lengths,
    owner_block,
    row_offset,
):
    n_seq = lax.axis_size("seq")
    n_head = lax.axis_size("head")
    devices_all = n_seq * n_head
    tok_rows = queries.shape[0]
    head_local = decay_rate.shape[0]
    head_dim = queries.shape[1] // head_local
    seq_rank = lax.axis_index("seq")
    head_rank = lax.axis_index("head")

    plane = n_seq // n_head
    swap = [
        ((a * plane + p) * n_head + b, (b * plane + p) * n_head + a)
        for a in range(n_head)
        for p in range(plane)
        for b in range(n_head)
    ]
    swapped = lax.ppermute(value_weight, ("seq", "head"), swap)
    weight = lax.all_gather(swapped, "seq", axis=0, tiled=True)
    weight = weight.reshape(n_head, -1, value_weight.shape[1])

    first_row = seq_rank * tok_rows
    positions = first_row + jnp.arange(tok_rows, dtype=jnp.int32)
    doc_ends = jnp.cumsum(doc_lengths)
    doc_index = doc_of(positions, doc_ends)
    pos_before = first_row - 1
    doc_before = doc_of(jnp.maximum(pos_before, 0)[None], doc_ends)[0]
    query_blk = queries.reshape(tok_rows, head_local, head_dim)
    key_blk = key_vectors.reshape(tok_rows, head_local, head_dim)
    grad_blk = output_grad.reshape(tok_rows, head_local, head_dim)

    blocks = tok_rows // ROWS_BLK
    per = blocks * CAPACITY
    slot_index = slots_of(owner_block[:, 0], blocks, CAPACITY)
    my_slots = (
        (jnp.arange(n_seq, dtype=jnp.int32)[:, None] * n_head + head_rank) * per
        + jnp.arange(per, dtype=jnp.int32)[None, :]
    )
    hit = my_slots[:, :, None] == slot_index[None, None, :]
    named = jnp.sum(jnp.where(hit, row_offset[None, None, :] + 1, 0), axis=2)
    high, low = (named // 32).astype(BF16), (named % 32).astype(BF16)

    local_state = state_terms(
        query_blk, grad_blk, decay_rate, doc_index, positions, doc_before, pos_before
    )
    share = head_local * head_dim * head_dim // n_seq // head_dim
    note = jnp.concatenate([high, low], axis=1)
    note = jnp.pad(note, ((0, 0), (0, head_dim - 2 * per)))[:, None, :]
    note = jnp.pad(note, ((0, 0), (0, 7), (0, 0)))
    sent = jnp.concatenate(
        [local_state.astype(BF16).reshape(n_seq, share, head_dim), note], axis=1
    )
    state_in = lax.all_to_all(sent, "seq", split_axis=0, concat_axis=0, tiled=True)
    offsets = (
        state_in[:, share, :per].astype(jnp.int32) * 32
        + state_in[:, share, per : 2 * per].astype(jnp.int32)
        - 1
    )
    ranks = jnp.arange(n_seq, dtype=jnp.int32)
    doc_last = doc_of((ranks + 1) * tok_rows - 1, doc_ends)
    doc_prior = doc_of(jnp.maximum(ranks * tok_rows - 1, 0), doc_ends)
    my_rate = decay_rate[seq_rank // (n_seq // head_local)]
    ahead = ranks[None, :] - ranks[:, None] - 1
    reach = (ahead >= 0) & (doc_last[:, None] == doc_prior[None, :])
    chain = jnp.where(
        reach, jnp.exp(-my_rate * (jnp.maximum(ahead, 0) * tok_rows).astype(F32)), 0.0
    )
    carried_all = jnp.einsum(
        "bc,cxy->bxy",
        chain,
        state_in[:, :share].astype(F32),
        precision=lax.Precision.HIGHEST,
        preferred_element_type=F32,
    ).astype(BF16)
    carried = lax.all_to_all(carried_all, "seq", split_axis=0, concat_axis=0, tiled=True)
    carried = carried.reshape(head_local, head_dim, head_dim)

    intra_part = intra_terms(query_blk, key_blk, grad_blk, decay_rate, doc_index, positions)
    inter_part = inter_terms(key_blk, carried, decay_rate, doc_index, positions)
    value_grad = (intra_part + inter_part).astype(BF16).reshape(tok_rows, head_local * head_dim)
    grads = lax.all_gather(value_grad, "head", axis=0)

    send = project(slot_index, grads, weight, devices_all * per, 256)
    send = send.reshape(devices_all, per, -1)
    got = lax.all_to_all(send, ("seq", "head"), split_axis=0, concat_axis=0, tiled=True)
    got = got.reshape(n_seq, n_head, per, -1)
    return merge(offsets, got, CAPACITY)


def solution(mesh):
    return jax.shard_map(
        per_device,
        mesh=mesh,
        in_specs=(
            P("seq", "head"),
            P("seq", "head"),
            P("seq", "head"),
            P("seq", "head"),
            P("head"),
            P(),
            P("seq", None),
            P("seq"),
        ),
        out_specs=P(("seq", "head"), None, None, None),
        check_vma=False,
    )
```

profile of v0, /device:TPU:1, one launch (start us, length us, event | category | flops | bytes accessed | tf_op | source)
XLA Modules:
  0.0 253.0 jit_solution(9152786524429787858)
XLA Ops:
  6.5 0.0 copy-start
  6.6 0.9 reduce-window.4
  7.5 0.7 neg.13
  8.2 0.6 slice.19
  8.7 0.7 fusion.50
  9.4 0.1 convert_reduce_fusion.1
  9.5 0.6 slice.18
  10.1 0.7 broadcast_multiply_fusion
  10.8 0.6 subtract_convert_fusion
  11.4 0.1 iota_add_fusion
  11.5 1.0 convert_reduce_fusion
  12.5 0.7 bitcast_add_fusion.1
  13.2 0.7 select_reduce_fusion
  13.9 0.1 fusion.39
  14.0 0.0 copy-start.5
  14.0 1.5 copy.62
  15.5 1.5 copy.63
  17.0 0.0 copy-start.1
  17.0 1.3 broadcast_compare_fusion
  18.3 0.1 select_multiply_fusion
  18.4 0.4 convolution_convert_fusion
  18.8 0.8 fusion.16
  19.6 9.6 %all-to-all-start = ((bf16[32,40,128]{2,1,0:T(8,128)(2,1)}), bf16[32,40,128]{2,1,0:T(8,128)(2,1)S(1)}, u32[]{:S(2)}, u32[]{:S(2)}) async-start(bf16[32,40,128]{2,1,0:T(8,128)(2,1)} %fusion.16), calls=%async_computation | async-start | bytes 655360 | tf_op jit(solution)/shard_map/all_to_all | solution.py:197
  29.2 1.0 fusion.11
  30.3 0.0 copy-done.5
  30.3 0.7 dynamic_slice.3
  31.6 0.1 convert_reduce_fusion.3
  31.7 1.2 fusion.6
  32.9 5.8 %all-to-all-done = bf16[32,40,128]{2,1,0:T(8,128)(2,1)S(1)} async-done(((bf16[32,40,128]{2,1,0:T(8,128)(2,1)}), bf16[32,40,128]{2,1,0:T(8,128)(2,1)S(1)}, u32[]{:S(2)}, u32[]{:S(2)}) %all-to-all-start) | async-done | bytes 327712 | tf_op jit(solution)/shard_map/all_to_all | solution.py:197
  38.8 0.4 convolution_convert_fusion.1
  39.2 0.8 copy.54
  40.0 0.0 copy-done.1
  40.0 3.8 %all-to-all-start.1 = ((bf16[32,32,128]{2,1,0:T(8,128)(2,1)}), bf16[32,32,128]{2,1,0:T(8,128)(2,1)S(1)}, u32[]{:S(2)}, u32[]{:S(2)}) async-start(bf16[32,32,128]{2,1,0:T(8,128)(2,1)} %copy.54), calls=%async_computation.1 | async-start | bytes 524288 | tf_op jit(solution)/shard_map/all_to_all | solution.py:219
  43.8 0.0 all-gather.3.cloned.1.call-start
  43.9 0.0 copy-done
  43.9 6.5 %fusion = f32[8,512,128]{1,2,0:T(8,128)} fusion(bf16[512,8,128]{0,2,1:T(8,128)(2,1)} %bitcast.70, f32[512,512]{1,0:T(8,128)} %fusion.6, f32[8]{0:T(128)S(1)} %neg.13, pred[512,512]{1,0:T(8,128)(4,1)} %fusion.11, bf16[512,8,128]{0,2,1:T(8,128)(2,1)S(1)} %bitcast.68, bf16[512,1024]{1,0:T(8,128)(2,1)S(1)} %copy-done), kind=kOutput, calls=%fused_computation.1 | convolution fusion | flops 1084227584 | bytes 6553632 | tf_op jit(solution)/shard_map/hst,thf->shf/dot_general | solution.py:28
  50.4 0.0 copy-start.4
  50.4 0.0 copy-start.3
  50.4 2.5 all-to-all-done.1
  52.8 2.1 fusion.5
  55.0 1.3 copy.57
  56.3 0.0 all-gather.3.cloned.1.call-update
  56.3 0.0 all-gather.5.cloned.1.call-start
  56.3 0.0 copy-done.4
  56.4 0.7 collective-permute-start
  57.0 0.0 collective-permute-done
  57.1 0.0 copy-start.2
  57.1 0.7 copy-done.2
  57.8 0.0 all-gather.5.cloned.1.call-update
  57.8 0.0 copy-done.3
  57.9 0.6 fusion.48.slot_ref
  58.5 55.2 %all-gather.3.cloned.1.call-done.grads_ref = bf16[4,512,1024]{2,1,0:T(8,128)(2,1)} async-done(((bf16[1,512,1024]{2,1,0:T(8,128)(2,1)}), bf16[4,512,1024]{2,1,0:T(8,128)(2,1)}) %all-gather.3.cloned.1.call-update) | async-done | bytes 4194320 | tf_op jit(solution)/shard_map/all_gather | solution.py:225
  113.6 63.9 %all-gather.5.cloned.1.call-done = bf16[6144,1024]{1,0:T(8,128)(2,1)} async-done(((bf16[192,1024]{1,0:T(8,128)(2,1)}), bf16[6144,1024]{1,0:T(8,128)(2,1)}) %all-gather.5.cloned.1.call-update) | async-done | bytes 12582928 | tf_op jit(solution)/shard_map/all_gather | solution.py:163
  177.5 14.2 %project.1 = bf16[1024,1536]{1,0:T(8,128)(2,1)} custom-call(s32[1,512]{1,0:T(1,128)} %fusion.48.slot_ref, bf16[4,512,1024]{2,1,0:T(8,128)(2,1)} %all-gather.3.cloned.1.call-done.grads_ref, bf16[4,1536,1024]{2,1,0:T(8,128)(2,1)} %bitcast.64), custom_call_target="tpu_custom_call" | custom-call | tf_op jit(solution)/shard_map/project/pallas_call | solution.py:76
  191.7 7.7 %all-to-all-start.2 = ((bf16[128,8,1536]{2,1,0:T(8,128)(2,1)}), bf16[128,8,1536]{2,1,0:T(8,128)(2,1)}, u32[]{:S(2)}, u32[]{:S(2)}) async-start(bf16[128,8,1536]{2,1,0:T(8,128)(2,1)} %bitcast.63), calls=%async_computation.2 | async-start | bytes 6291456 | tf_op jit(solution)/shard_map/all_to_all | solution.py:229
  199.4 0.5 broadcast.385
  199.9 0.7 fusion.57
  200.6 0.7 sub.98.row_ref
  201.2 0.7 sub.111.column_ref
  202.0 39.2 %all-to-all-done.2 = bf16[128,8,1536]{2,1,0:T(8,128)(2,1)} async-done(((bf16[128,8,1536]{2,1,0:T(8,128)(2,1)}), bf16[128,8,1536]{2,1,0:T(8,128)(2,1)}, u32[]{:S(2)}, u32[]{:S(2)}) %all-to-all-start.2) | async-done | bytes 3145760 | tf_op jit(solution)/shard_map/all_to_all | solution.py:229
  241.2 5.0 %merge.1 = bf16[1,128,2,6144]{3,2,1,0:T(2,128)(2,1)} custom-call(s32[256,1]{1,0:T(8,128)} %sub.111.column_ref, s32[1,256]{1,0:T(1,128)} %sub.98.row_ref, bf16[32,4,8,1536]{3,2,1,0:T(8,128)(2,1)} %bitcast.21.rows_ref), custom_call_target="tpu_custom_call" | custom-call | tf_op jit(solution)/shard_map/merge/pallas_call | solution.py:107
  (8 shorter events, 0.1 us)
Async XLA Ops:
  6.5 37.3 %copy-start = (bf16[512,1024]{1,0:T(8,128)(2,1)S(1)}, bf16[512,1024]{1,0:T(8,128)(2,1)}, u32[]{:S(2)}) copy-start(bf16[512,1024]{1,0:T(8,128)(2,1)} %param.9) | copy-start | bytes 3145732
  14.0 16.2 %copy-start.5 = (f32[8]{0:T(128)S(1)}, f32[8]{0:T(128)}, u32[]{:S(2)}) copy-start(f32[8]{0:T(128)} %param.12) | copy-start | bytes 100
  17.0 23.0 %copy-start.1 = (bf16[512,1024]{0,1:T(8,128)(2,1)}, bf16[512,1024]{0,1:T(8,128)(2,1)S(1)}, u32[]{:S(2)}) copy-start(bf16[512,1024]{0,1:T(8,128)(2,1)S(1)} %copy.63) | copy-start | bytes 3145732
  19.6 19.2 %all-to-all-start = ((bf16[32,40,128]{2,1,0:T(8,128)(2,1)}), bf16[32,40,128]{2,1,0:T(8,128)(2,1)S(1)}, u32[]{:S(2)}, u32[]{:S(2)}) async-start(bf16[32,40,128]{2,1,0:T(8,128)(2,1)} %fusion.16), calls=%async_computation | async-start | bytes 655360 | tf_op jit(solution)/shard_map/all_to_all | solution.py:197
  40.0 12.8 %all-to-all-start.1 = ((bf16[32,32,128]{2,1,0:T(8,128)(2,1)}), bf16[32,32,128]{2,1,0:T(8,128)(2,1)S(1)}, u32[]{:S(2)}, u32[]{:S(2)}) async-start(bf16[32,32,128]{2,1,0:T(8,128)(2,1)} %copy.54), calls=%async_computation.1 | async-start | bytes 524288 | tf_op jit(solution)/shard_map/all_to_all | solution.py:219
  43.8 69.8 %all-gather.3.cloned.1.call-start = ((), (), s32[]{:S(2)}) async-start(), calls=%async_computation.3 | async-start | bytes 5242880 | tf_op jit(solution)/shard_map/all_gather | solution.py:225
  50.4 6.0 %copy-start.4 = (bf16[192,1024]{1,0:T(8,128)(2,1)S(1)}, bf16[192,1024]{1,0:T(8,128)(2,1)}, u32[]{:S(2)}) copy-start(bf16[192,1024]{1,0:T(8,128)(2,1)} %param.11) | copy-start | bytes 1179652
  50.4 7.5 %copy-start.3 = (s32[512,1]{0,1:T(1,128)S(1)}, s32[512,1]{0,1:T(1,128)}, u32[]{:S(2)}) copy-start(s32[512,1]{0,1:T(1,128)} %param.14) | copy-start | bytes 6148
  56.3 121.2 %all-gather.5.cloned.1.call-start = ((), (), s32[]{:S(2)}) async-start(), calls=%async_computation.4 | async-start | bytes 12976128 | tf_op jit(solution)/shard_map/all_gather | solution.py:163
  56.4 0.7 collective-permute-start
  57.1 0.8 copy-start.2
  191.7 49.5 %all-to-all-start.2 = ((bf16[128,8,1536]{2,1,0:T(8,128)(2,1)}), bf16[128,8,1536]{2,1,0:T(8,128)(2,1)}, u32[]{:S(2)}, u32[]{:S(2)}) async-start(bf16[128,8,1536]{2,1,0:T(8,128)(2,1)} %bitcast.63), calls=%async_computation.2 | async-start | bytes 6291456 | tf_op jit(solution)/shard_map/all_to_all | solution.py:229
Sparse Core Ops, SparseCore 0:
  56.4 57.1 all-gather.2
  115.9 61.5 all-gather.4
where the time goes:
time: 254 us; the launch traced here: 253 us
  waiting for transfers between devices  167 us (66%)
  starting transfers between devices  21.9 us (9%)
  Pallas kernels  19.1 us (8%)
  between operations  14.3 us (6%)
  other arithmetic  12 us (5%)
  local copies, waits for them, and re-layouts  9.6 us (4%)
  matrix products  9.43 us (4%)
    all_gather x1, waiting for transfers between devices, per_device(): weight = lax.all_gather(swapped, 'seq', axis=0, tiled=True)  63.9 us
    all_gather x1, waiting for transfers between devices, per_device(): grads = lax.all_gather(value_grad, 'head', axis=0)  55.2 us
    all_to_all x1, waiting for transfers between devices, per_device(): lax.all_to_all(send, ('seq', 'head'), split_axis=0, concat_axis=0, tiled=...  39.2 us
    pallas_call x1, Pallas kernels, project(): pl.pallas_call(project_body, grid=(width // tile,), in_specs=[pl.BlockSpe...  14.2 us
    all_to_all x1, starting transfers between devices, per_device(): lax.all_to_all(sent, 'seq', split_axis=0, concat_axis=0, tiled=True)  9.61 us
    all_to_all x1, starting transfers between devices, per_device(): lax.all_to_all(send, ('seq', 'head'), split_axis=0, concat_axis=0, tiled=...  7.71 us
    dot_general x1, matrix products, intra_terms(): jnp.einsum('hst,thf->shf', weights, grad_blk, preferred_element_type=F32)  6.47 us
    all_to_all x1, waiting for transfers between devices, per_device(): lax.all_to_all(sent, 'seq', split_axis=0, concat_axis=0, tiled=True)  5.85 us
  transfers between devices with their start and end apart: 6, of which 5 were waited for; matrix products, arithmetic and copies ran while one was open for 5% of the time, Pallas kernels for 0%

commit v1 on v0

v1 whole, which is shorter than its diff:
```python
import jax
import jax.numpy as jnp
from jax import lax
from jax.experimental import pallas as pl
from jax.experimental.pallas import tpu as pltpu
from jax.sharding import PartitionSpec as P

BF16 = jnp.bfloat16
F32 = jnp.float32
CAPACITY = 2
ROWS_BLK = 128


def doc_of(positions, doc_ends):
    return jnp.sum((positions[:, None] >= doc_ends[None, :]).astype(jnp.int32), axis=1)


BIG = 1 << 30


def doc_limit(positions, lengths_ref):
    end = lengths_ref[0]
    limit = jnp.where(positions < end, end, BIG)
    for doc in range(1, lengths_ref.shape[0]):
        end = end + lengths_ref[doc]
        limit = jnp.minimum(limit, jnp.where(positions < end, end, BIG))
    return limit


def local_state_body(rate_ref, lengths_ref, query_ref, grad_ref, out_ref):
    toks = query_ref.shape[0]
    rate = rate_ref[pl.program_id(0)]
    first = lax.axis_index("seq") * toks
    limit = doc_limit(jnp.maximum(first - 1, 0), lengths_ref)
    step = lax.broadcasted_iota(jnp.int32, (toks, 1), 0)
    lead = jnp.where(first + step < limit, jnp.exp(-rate * (step + 1).astype(F32)), 0.0)
    scaled = (query_ref[...].astype(F32) * lead).astype(BF16)
    out_ref[0] = lax.dot_general(
        scaled, grad_ref[...], (((0,), (0,)), ((), ())), preferred_element_type=F32
    ).astype(out_ref.dtype)


def local_states(rates, lengths, queries, grads):
    heads = rates.shape[0]
    toks, dim = queries.shape[0], queries.shape[1] // heads
    blk = pl.BlockSpec((toks, dim), lambda h: (0, h))
    return pl.pallas_call(
        local_state_body,
        grid=(heads,),
        in_specs=[
            pl.BlockSpec(memory_space=pltpu.SMEM),
            pl.BlockSpec(memory_space=pltpu.SMEM),
            blk,
            blk,
        ],
        out_specs=pl.BlockSpec((1, dim, dim), lambda h: (h, 0, 0)),
        out_shape=jax.ShapeDtypeStruct((heads, dim, dim), BF16),
        compiler_params=pltpu.CompilerParams(dimension_semantics=("arbitrary",)),
        name="local_states",
    )(rates, lengths, queries, grads)


def within_body(rate_ref, lengths_ref, query_ref, key_ref, grad_ref, out_ref):
    toks, dim = query_ref.shape
    rate = rate_ref[pl.program_id(0)]
    first = lax.axis_index("seq") * toks
    half = toks // 2
    for lo in (0, half):
        src = lax.broadcasted_iota(jnp.int32, (half, 1), 0) + lo
        dst = lax.broadcasted_iota(jnp.int32, (1, toks - lo), 1) + lo
        limit = doc_limit(src + first, lengths_ref) - first
        rise = jnp.exp(rate * src.astype(F32)) * (1.0 / dim)
        fall = jnp.exp(-rate * dst.astype(F32))
        scores = lax.dot_general(
            key_ref[lo : lo + half, :],
            query_ref[lo:, :],
            (((1,), (1,)), ((), ())),
            preferred_element_type=F32,
        )
        seen = (dst >= src) & (dst < limit)
        weights = jnp.where(seen, scores * rise * fall, 0.0).astype(BF16)
        out_ref[lo : lo + half, :] = jnp.dot(
            weights, grad_ref[lo:, :], preferred_element_type=F32
        )


def within(rates, lengths, queries, keys, grads):
    heads = rates.shape[0]
    toks, dim = queries.shape[0], queries.shape[1] // heads
    blk = pl.BlockSpec((toks, dim), lambda h: (0, h))
    return pl.pallas_call(
        within_body,
        grid=(heads,),
        in_specs=[
            pl.BlockSpec(memory_space=pltpu.SMEM),
            pl.BlockSpec(memory_space=pltpu.SMEM),
            blk,
            blk,
            blk,
        ],
        out_specs=blk,
        out_shape=jax.ShapeDtypeStruct((toks, heads * dim), F32),
        compiler_params=pltpu.CompilerParams(dimension_semantics=("arbitrary",)),
        name="within",
    )(rates, lengths, queries, keys, grads)


def across_body(start, rate_ref, lengths_ref, key_ref, state_ref, intra_ref, out_ref):
    toks, dim = key_ref.shape
    rate = rate_ref[pl.program_id(0) + start]
    first = lax.axis_index("seq") * toks
    src = lax.broadcasted_iota(jnp.int32, (toks, 1), 0)
    limit = doc_limit(src + first, lengths_ref) - first
    tail = jnp.where(
        toks - 1 < limit, jnp.exp(-rate * (toks - 1 - src).astype(F32)) * (1.0 / dim), 0.0
    )
    product = jnp.dot(key_ref[...], state_ref[0], preferred_element_type=F32)
    out_ref[...] = (intra_ref[...] + product * tail).astype(BF16)


def across(rates, lengths, keys, states, intra, start, count):
    dim = states.shape[-1]
    toks = keys.shape[0]
    blk = pl.BlockSpec((toks, dim), lambda h: (0, h + start))
    return pl.pallas_call(
        lambda *refs: across_body(start, *refs),
        grid=(count,),
        in_specs=[
            pl.BlockSpec(memory_space=pltpu.SMEM),
            pl.BlockSpec(memory_space=pltpu.SMEM),
            blk,
            pl.BlockSpec((1, dim, dim), lambda h: (h + start, 0, 0)),
            blk,
        ],
        out_specs=pl.BlockSpec((toks, dim), lambda h: (0, h)),
        out_shape=jax.ShapeDtypeStruct((toks, count * dim), BF16),
        compiler_params=pltpu.CompilerParams(dimension_semantics=("arbitrary",)),
        name="across",
    )(rates, lengths, keys, states, intra)


def times(rows, weight):
    return lax.dot_general(rows, weight, (((1,), (1,)), ((), ())), preferred_element_type=F32)


def near_body(which_ref, a0, a1, b0, b1, c0, c1, wa, wb, wc, out_ref):
    half = a0.shape[1]
    total = None
    for lo, hi, weight in ((a0, a1, wa), (b0, b1, wb), (c0, c1, wc)):
        part = times(lo[...], weight[0, :, :half]) + times(hi[...], weight[0, :, half:])
        part = part.astype(BF16).astype(F32)
        total = part if total is None else total + part
    out_ref[...] = total


def project_near(which, pieces, weight, tile):
    toks, half = pieces[0].shape
    width, depth = weight.shape[1:]
    whole = pl.BlockSpec((toks, half), lambda i, w: (0, 0))
    return pl.pallas_call(
        near_body,
        grid_spec=pltpu.PrefetchScalarGridSpec(
            num_scalar_prefetch=1,
            grid=(width // tile,),
            in_specs=[whole] * 6
            + [
                pl.BlockSpec((1, tile, depth), lambda i, w, k=k: (w[k], i, 0))
                for k in range(3)
            ],
            out_specs=pl.BlockSpec((toks, tile), lambda i, w: (0, i)),
        ),
        out_shape=jax.ShapeDtypeStruct((toks, width), F32),
        compiler_params=pltpu.CompilerParams(
            dimension_semantics=("arbitrary",), vmem_limit_bytes=50 << 20
        ),
        name="project_near",
    )(which, *pieces, weight, weight, weight)


def far_body(which_ref, slot_ref, lo, hi, weight, near_ref, out_ref, pick_ref):
    slots, toks = pick_ref.shape
    half = lo.shape[1]

    @pl.when(pl.program_id(0) == 0)
    def _():
        rows = lax.broadcasted_iota(jnp.int32, (slots, toks), 0)
        pick_ref[...] = (rows == slot_ref[...]).astype(F32).astype(BF16)

    part = times(lo[...], weight[0, :, :half]) + times(hi[...], weight[0, :, half:])
    total = near_ref[...] + part.astype(BF16).astype(F32)
    out_ref[...] = jnp.dot(
        pick_ref[...], total.astype(BF16), preferred_element_type=F32
    ).astype(BF16)


def project_far(which, slot_index, lo, hi, weight, near, slots, tile):
    toks, half = lo.shape
    width, depth = weight.shape[1:]
    whole = pl.BlockSpec((toks, half), lambda i, w: (0, 0))
    return pl.pallas_call(
        far_body,
        grid_spec=pltpu.PrefetchScalarGridSpec(
            num_scalar_prefetch=1,
            grid=(width // tile,),
            in_specs=[
                pl.BlockSpec((1, toks), lambda i, w: (0, 0)),
                whole,
                whole,
                pl.BlockSpec((1, tile, depth), lambda i, w: (w[3], i, 0)),
                pl.BlockSpec((toks, tile), lambda i, w: (0, i)),
            ],
            out_specs=pl.BlockSpec((slots, tile), lambda i, w: (0, i)),
            scratch_shapes=[pltpu.VMEM((slots, toks), BF16)],
        ),
        out_shape=jax.ShapeDtypeStruct((slots, width), BF16),
        compiler_params=pltpu.CompilerParams(
            dimension_semantics=("arbitrary",), vmem_limit_bytes=50 << 20
        ),
        name="project_far",
    )(which, slot_index[None, :], lo, hi, weight, near)


def merge_body(column_ref, row_ref, rows_ref, out_ref):
    slots = column_ref.shape[0]
    width = rows_ref.shape[-1]
    same = (column_ref[...] == row_ref[...]) & (column_ref[...] >= 0)
    same = same.astype(F32).astype(BF16)
    rows = rows_ref[...].reshape(slots, width)
    total = jnp.dot(same, rows, preferred_element_type=F32).astype(BF16)
    out_ref[...] = total.reshape(out_ref.shape)


def merge(offsets, got, capacity):
    n_seq, n_head, per, width = got.shape
    slots = n_seq * per
    return pl.pallas_call(
        merge_body,
        grid=(n_head,),
        in_specs=[
            pl.BlockSpec((slots, 1), lambda i: (0, 0)),
            pl.BlockSpec((1, slots), lambda i: (0, 0)),
            pl.BlockSpec((n_seq, 1, per, width), lambda i: (0, i, 0, 0)),
        ],
        out_specs=pl.BlockSpec((1, slots // capacity, capacity, width), lambda i: (0, 0, 0, i)),
        out_shape=jax.ShapeDtypeStruct((1, slots // capacity, capacity, n_head * width), BF16),
        compiler_params=pltpu.CompilerParams(
            dimension_semantics=("arbitrary",), vmem_limit_bytes=56 << 20
        ),
        name="merge",
    )(offsets.reshape(slots, 1), offsets.reshape(1, slots), got)


def slots_of(owners, blocks, capacity):
    toks = owners.shape[0]
    width = toks // blocks
    grouped = owners.reshape(blocks, width)
    same_owner = grouped[:, :, None] == grouped[:, None, :]
    lower = jnp.arange(width, dtype=jnp.int32)
    earlier = lower[None, :] < lower[:, None]
    rank = jnp.sum((same_owner & earlier[None]).astype(jnp.int32), axis=2)
    block_ids = jnp.arange(blocks, dtype=jnp.int32)[:, None]
    return ((grouped * blocks + block_ids) * capacity + rank).reshape(toks)


def per_device(
    queries,
    key_vectors,
    output_grad,
    value_weight,
    decay_rate,
    doc_lengths,
    owner_block,
    row_offset,
):
    n_seq = lax.axis_size("seq")
    n_head = lax.axis_size("head")
    devices_all = n_seq * n_head
    tok_rows = queries.shape[0]
    head_local = decay_rate.shape[0]
    head_dim = queries.shape[1] // head_local
    seq_rank = lax.axis_index("seq")
    head_rank = lax.axis_index("head")

    plane = n_seq // n_head
    swap = [
        ((a * plane + p) * n_head + b, (b * plane + p) * n_head + a)
        for a in range(n_head)
        for p in range(plane)
        for b in range(n_head)
    ]
    swapped = lax.ppermute(value_weight, ("seq", "head"), swap)
    weight = lax.all_gather(swapped, "seq", axis=0, tiled=True)
    weight = weight.reshape(n_head, -1, value_weight.shape[1])

    blocks = tok_rows // ROWS_BLK
    per = blocks * CAPACITY
    slot_index = slots_of(owner_block[:, 0], blocks, CAPACITY)
    my_slots = (
        (jnp.arange(n_seq, dtype=jnp.int32)[:, None] * n_head + head_rank) * per
        + jnp.arange(per, dtype=jnp.int32)[None, :]
    )
    hit = my_slots[:, :, None] == slot_index[None, None, :]
    named = jnp.sum(jnp.where(hit, row_offset[None, None, :] + 1, 0), axis=2)
    note = jnp.concatenate([(named // 32).astype(BF16), (named % 32).astype(BF16)], axis=1)
    note = jnp.pad(note[:, None, :], ((0, 0), (0, 7), (0, head_dim - 2 * per)))

    state = local_states(decay_rate, doc_lengths, queries, output_grad)
    share = head_local * head_dim // n_seq
    state_in = lax.all_to_all(
        state.reshape(n_seq, share, head_dim), "seq", split_axis=0, concat_axis=0, tiled=True
    )
    intra = within(decay_rate, doc_lengths, queries, key_vectors, output_grad)

    doc_ends = jnp.cumsum(doc_lengths)
    ranks = jnp.arange(n_seq, dtype=jnp.int32)
    doc_last = doc_of((ranks + 1) * tok_rows - 1, doc_ends)
    doc_prior = doc_of(jnp.maximum(ranks * tok_rows - 1, 0), doc_ends)
    my_rate = decay_rate[seq_rank // (n_seq // head_local)]
    ahead = ranks[None, :] - ranks[:, None] - 1
    reach = (ahead >= 0) & (doc_last[:, None] == doc_prior[None, :])
    chain = jnp.where(
        reach, jnp.exp(-my_rate * (jnp.maximum(ahead, 0) * tok_rows).astype(F32)), 0.0
    )
    carried_all = jnp.einsum(
        "bc,cxy->bxy",
        chain,
        state_in.astype(F32),
        precision=lax.Precision.HIGHEST,
        preferred_element_type=F32,
    ).astype(BF16)
    carried = lax.all_to_all(
        jnp.concatenate([carried_all, note], axis=1),
        "seq",
        split_axis=0,
        concat_axis=0,
        tiled=True,
    )
    offsets = (
        carried[:, share, :per].astype(jnp.int32) * 32
        + carried[:, share, per : 2 * per].astype(jnp.int32)
        - 1
    )
    carried = carried[:, :share].reshape(head_local, head_dim, head_dim)

    half = head_local // 2
    own = [
        across(decay_rate, doc_lengths, key_vectors, carried, intra, start, half)
        for start in (0, half)
    ]
    up = [(i, (i + 1) % n_head) for i in range(n_head)]
    down = [(i, (i - 1) % n_head) for i in range(n_head)]
    left_lo = lax.ppermute(own[0], "head", up)
    right_hi = lax.ppermute(own[1], "head", down)
    left_hi = lax.ppermute(own[1], "head", up)
    right_lo = lax.ppermute(own[0], "head", down)
    far_lo = lax.ppermute(left_lo, "head", up)
    far_hi = lax.ppermute(right_hi, "head", down)
    which = (head_rank + jnp.array([0, n_head - 1, 1, 2], jnp.int32)) % n_head

    near = project_near(
        which, (own[0], own[1], left_lo, left_hi, right_lo, right_hi), weight, 256
    )
    send = project_far(which, slot_index, far_lo, far_hi, weight, near, devices_all * per, 256)
    send = send.reshape(devices_all, per, -1)
    got = lax.all_to_all(send, ("seq", "head"), split_axis=0, concat_axis=0, tiled=True)
    got = got.reshape(n_seq, n_head, per, -1)
    return merge(offsets, got, CAPACITY)


def solution(mesh):
    return jax.shard_map(
        per_device,
        mesh=mesh,
        in_specs=(
            P("seq", "head"),
            P("seq", "head"),
            P("seq", "head"),
            P("seq", "head"),
            P("head"),
            P(),
            P("seq", None),
            P("seq"),
        ),
        out_specs=P(("seq", "head"), None, None, None),
        check_vma=False,
    )
```

time: 254 us -> 198 us (0.78)
  waiting for transfers between devices: 167 us -> 67.5 us
  starting transfers between devices: 21.9 us -> 54.9 us
  Pallas kernels: 19.1 us -> 49.6 us
  other arithmetic: 12 us -> 2.24 us
  matrix products: 9.43 us -> 0.42 us
    all_gather x1, waiting for transfers between devices: 63.9 us -> 0.01 us  [per_device(): weight = lax.all_gather(swapped, 'seq', axis=0, tiled=True)]
    all_gather x1 -> x0, waiting for transfers between devices: 55.2 us -> none  [per_device(): grads = lax.all_gather(value_grad, 'head', axis=0)]
    pallas_call x1 -> x6, Pallas kernels: 14.2 us -> 44.6 us  [the longest x1 11.1 us: project_far(): pl.pallas_call(far_body, grid_spec=pltpu.PrefetchScalarGridSpec(num_scala...]
    all_to_all x2, starting transfers between devices: 13.4 us -> 36.5 us  [the longest x1 32.6 us: per_device(): lax.all_to_all(state.reshape(n_seq, share, head_dim), 'seq', split_axis=0...]
    ppermute x0 -> x6, waiting for transfers between devices: none -> 18 us  [the longest x1 7.78 us: per_device(): right_lo = lax.ppermute(own[0], 'head', down)]
    dot_general x4 -> x1, matrix products: 9.43 us -> 0.42 us  [per_device(): jnp.einsum('bc,cxy->bxy', chain, state_in.astype(F32), precision=lax.Prec...]
    ppermute x0 -> x6, starting transfers between devices: none -> 7.56 us  [the longest x1 3.31 us: per_device(): far_hi = lax.ppermute(right_hi, 'head', down)]
    reshape x2 -> x0, local copies, waits for them, and re-layouts: 3 us -> none  [the longest x1 1.5 us: per_device(): query_blk = queries.reshape(tok_rows, head_local, head_dim)]
  transfers between devices with their start and end apart: 6 -> 11, of which waited for: 5 -> 6; matrix products, arithmetic and copies ran while one was open for 5% -> 3% of each run, Pallas kernels for 0% -> 17%
where the time goes in v1:
time: 198 us; the launch traced here: 196 us
  waiting for transfers between devices  67.5 us (34%)
  starting transfers between devices  54.9 us (28%)
  Pallas kernels  49.6 us (25%)
  between operations  14.2 us (7%)
  local copies, waits for them, and re-layouts  7.58 us (4%)
  other arithmetic  2.24 us (1%)
    all_to_all x1, waiting for transfers between devices, per_device(): lax.all_to_all(send, ('seq', 'head'), split_axis=0, concat_axis=0, tiled=...  39.3 us
    all_to_all x1, starting transfers between devices, per_device(): lax.all_to_all(state.reshape(n_seq, share, head_dim), 'seq', split_axis=0...  32.6 us
    pallas_call x1, Pallas kernels, project_far(): pl.pallas_call(far_body, grid_spec=pltpu.PrefetchScalarGridSpec(num_scala...  11.1 us
    pallas_call x1, Pallas kernels, project_near(): pl.pallas_call(near_body, grid_spec=pltpu.PrefetchScalarGridSpec(num_scal...  10.2 us
    all_to_all x1, starting transfers between devices, per_device(): lax.all_to_all(send, ('seq', 'head'), split_axis=0, concat_axis=0, tiled=...  9.03 us
    pallas_call x1, Pallas kernels, within(): pl.pallas_call(within_body, grid=(heads,), in_specs=[pl.BlockSpec(memory_...  8.58 us
    pallas_call x2, Pallas kernels, across(): pl.pallas_call(lambda *refs: across_body(start, *refs), grid=(count,), in...  8.26 us
    all_to_all x1, waiting for transfers between devices, per_device(): lax.all_to_all(state.reshape(n_seq, share, head_dim), 'seq', split_axis=0...  7.94 us
  transfers between devices with their start and end apart: 11, of which 6 were waited for; matrix products, arithmetic and copies ran while one was open for 3% of the time, Pallas kernels for 17%

profile of v1, /device:TPU:1, one launch (start us, length us, event | category | flops | bytes accessed | tf_op | source)
XLA Modules:
  0.0 196.5 jit_solution(9545801478284988622)
XLA Ops:
  6.5 0.0 copy-start.6
  6.5 0.0 copy-start.5
  6.5 0.0 copy-start.4
  6.5 0.0 copy-start.7
  6.5 0.0 all-gather.2.cloned.1.call-start
  6.6 1.8 collective-permute-start.4
  8.4 0.0 collective-permute-done.4
  8.4 0.0 copy-start.3
  8.4 0.7 copy-done.3
  9.1 0.0 all-gather.2.cloned.1.call-update
  9.1 6.5 %local_states.1 = bf16[8,128,128]{2,1,0:T(8,128)(2,1)} custom-call(f32[8]{0:T(128)} %refs_0_.3, s32[4]{0:T(128)} %refs_1_.3, bf16[512,1024]{1,0:T(8,128)(2,1)} %query_ref.3, bf16[512,1024]{1,0:T(8,128)(2,1)} %grad_ref.3), custom_call_target="tpu_custom_call" | custom-call | tf_op jit(solution)/shard_map/local_states/pallas_call | solution.py:47
  15.6 32.6 %all-to-all-start = ((bf16[32,32,128]{2,1,0:T(8,128)(2,1)}), bf16[32,32,128]{2,1,0:T(8,128)(2,1)S(1)}, u32[]{:S(2)}, u32[]{:S(2)}) async-start(bf16[32,32,128]{2,1,0:T(8,128)(2,1)} %bitcast.40), calls=%async_computation | async-start | bytes 524288 | tf_op jit(solution)/shard_map/all_to_all | solution.py:309
  48.3 0.0 copy-done.4
  48.4 0.2 convert_reduce_fusion
  48.6 0.0 copy-done.7
  48.6 0.1 iota_add_fusion
  48.7 0.7 select_reduce_fusion
  49.5 0.0 copy-done.5
  49.5 0.6 dynamic_slice.3
  50.7 0.0 copy-done.6
  50.7 0.2 reduce-window.8
  50.9 0.1 maximum_bitcast_fusion
  51.0 0.1 convert_reduce_fusion.2
  51.1 7.9 %all-to-all-done = bf16[32,32,128]{2,1,0:T(8,128)(2,1)S(1)} async-done(((bf16[32,32,128]{2,1,0:T(8,128)(2,1)}), bf16[32,32,128]{2,1,0:T(8,128)(2,1)S(1)}, u32[]{:S(2)}, u32[]{:S(2)}) %all-to-all-start) | async-done | bytes 262176 | tf_op jit(solution)/shard_map/all_to_all | solution.py:309
  59.0 0.4 convolution_convert_fusion
  59.5 0.9 copy.19
  60.4 3.8 %all-to-all-start.1 = ((bf16[32,40,128]{2,1,0:T(8,128)(2,1)}), bf16[32,40,128]{2,1,0:T(8,128)(2,1)S(1)}, u32[]{:S(2)}, u32[]{:S(2)}) async-start(bf16[32,40,128]{2,1,0:T(8,128)(2,1)} %copy.19), calls=%async_computation.1 | async-start | bytes 655360 | tf_op jit(solution)/shard_map/all_to_all | solution.py:331
  64.2 8.6 %within.1.refs_4_ = f32[512,1024]{1,0:T(8,128)} custom-call(f32[8]{0:T(128)} %refs_0_.3, s32[4]{0:T(128)} %refs_1_.3, bf16[512,1024]{1,0:T(8,128)(2,1)} %query_ref.3, bf16[512,1024]{1,0:T(8,128)(2,1)} %refs_2_.3, bf16[512,1024]{1,0:T(8,128)(2,1)} %grad_ref.3), custom_call_target="tpu_custom_call" | custom-call | tf_op jit(solution)/shard_map/within/pallas_call | solution.py:91
  72.8 2.2 %all-to-all-done.1 = bf16[32,40,128]{2,1,0:T(8,128)(2,1)S(1)} async-done(((bf16[32,40,128]{2,1,0:T(8,128)(2,1)}), bf16[32,40,128]{2,1,0:T(8,128)(2,1)S(1)}, u32[]{:S(2)}, u32[]{:S(2)}) %all-to-all-start.1) | async-done | bytes 327712 | tf_op jit(solution)/shard_map/all_to_all | solution.py:331
  75.0 0.7 slice.14
  75.7 0.0 copy-start.8
  75.7 4.1 %across.2.a0 = bf16[512,512]{1,0:T(8,128)(2,1)} custom-call(f32[8]{0:T(128)} %refs_0_.3, s32[4]{0:T(128)} %refs_1_.3, bf16[512,1024]{1,0:T(8,128)(2,1)} %refs_2_.3, bf16[8,128,128]{2,1,0:T(8,128)(2,1)} %bitcast.38, f32[512,1024]{1,0:T(8,128)} %within.1.refs_4_), custom_call_target="tpu_custom_call" | custom-call | tf_op jit(solution)/shard_map/across/pallas_call | solution.py:125
  79.8 0.0 copy-start
  79.8 0.0 collective-permute-start
  79.8 4.2 %across.3.a1 = bf16[512,512]{1,0:T(8,128)(2,1)} custom-call(f32[8]{0:T(128)} %refs_0_.3, s32[4]{0:T(128)} %refs_1_.3, bf16[512,1024]{1,0:T(8,128)(2,1)} %refs_2_.3, bf16[8,128,128]{2,1,0:T(8,128)(2,1)} %bitcast.39, f32[512,1024]{1,0:T(8,128)} %within.1.refs_4_), custom_call_target="tpu_custom_call" | custom-call | tf_op jit(solution)/shard_map/across/pallas_call | solution.py:125
  84.0 2.8 %collective-permute-start.2 = (bf16[512,512]{1,0:T(8,128)(2,1)}, bf16[512,512]{1,0:T(8,128)(2,1)S(1)}, u32[]{:S(2)}, u32[]{:S(2)}) collective-permute-start(bf16[512,512]{1,0:T(8,128)(2,1)} %across.3.a1), channel_id=1, source_target_pairs={{0,3},{1,0},{2,1},{3,2},{4,7},{5,4},{6,5},{7,6},{8,11},{9,8},{10,9... | collective-permute-start | bytes 1572872 | tf_op jit(solution)/shard_map/ppermute | solution.py:353
  86.8 0.0 copy-done
  86.8 0.0 collective-permute-start.6
  86.8 1.4 collective-permute-start.5
  88.3 6.7 %collective-permute-done.b0 = bf16[512,512]{1,0:T(8,128)(2,1)S(1)} collective-permute-done((bf16[512,512]{1,0:T(8,128)(2,1)}, bf16[512,512]{1,0:T(8,128)(2,1)S(1)}, u32[]{:S(2)}, u32[]{:S(2)}) %collective-permute-start) | collective-permute-done | bytes 524320 | tf_op jit(solution)/shard_map/ppermute | solution.py:352
  95.0 0.0 collective-permute-start.1
  95.0 3.5 %collective-permute-done.2.c1 = bf16[512,512]{1,0:T(8,128)(2,1)S(1)} collective-permute-done((bf16[512,512]{1,0:T(8,128)(2,1)}, bf16[512,512]{1,0:T(8,128)(2,1)S(1)}, u32[]{:S(2)}, u32[]{:S(2)}) %collective-permute-start.2) | collective-permute-done | bytes 524320 | tf_op jit(solution)/shard_map/ppermute | solution.py:353
  98.5 3.3 %collective-permute-start.3 = (bf16[512,512]{1,0:T(8,128)(2,1)S(1)}, bf16[512,512]{1,0:T(8,128)(2,1)}, u32[]{:S(2)}, u32[]{:S(2)}) collective-permute-start(bf16[512,512]{1,0:T(8,128)(2,1)S(1)} %collective-permute-done.2.c1), channel_id=1, source_target_pairs={{0,3},{1,0},{2,1},{3,2},{4,7},{5,4},{6,5},{7,6},{8,11},{9,8},{10,9... | collective-permute-start | bytes 1572872 | tf_op jit(solution)/shard_map/ppermute | solution.py:357
  101.8 0.0 copy-done.8
  101.8 7.8 %collective-permute-done.6.c0 = bf16[512,512]{1,0:T(8,128)(2,1)S(1)} collective-permute-done((bf16[512,512]{1,0:T(8,128)(2,1)S(1)}, bf16[512,512]{1,0:T(8,128)(2,1)S(1)}, u32[]{:S(2)}, u32[]{:S(2)}) %collective-permute-start.6) | collective-permute-done | bytes 524320 | tf_op jit(solution)/shard_map/ppermute | solution.py:355
  109.6 0.0 collective-permute-done.5.b1
  109.6 0.0 all-gather.2.cloned.1.call-done
  109.6 0.0 copy-start.1
  109.6 1.0 copy-done.1
  110.6 10.2 %project_near.1.near_ref = f32[512,1536]{1,0:T(8,128)} custom-call(s32[4]{0:T(128)S(1)} %and_select_fusion.which_ref, bf16[512,512]{1,0:T(8,128)(2,1)S(1)} %copy-done, bf16[512,512]{1,0:T(8,128)(2,1)S(1)} %copy-done.1, bf16[512,512]{1,0:T(8,128)(2,1)S(1)} %collective-permute-done.b0, bf16[512,512]{1,0:T(8,128)(2,1)S(1)} %collective-permute-done.5.b1, ...), custom_call_target="tpu_custom_call" | custom-call | tf_op jit(solution)/shard_map/project_near/pallas_call | solution.py:160
  120.8 0.0 collective-permute-done.1.lo
  120.8 0.0 collective-permute-done.3.hi
  120.8 11.1 %project_far.1 = bf16[1024,1536]{1,0:T(8,128)(2,1)} custom-call(s32[4]{0:T(128)S(1)} %and_select_fusion.which_ref, s32[1,512]{1,0:T(1,128)S(1)} %fusion.29.slot_ref, bf16[512,512]{1,0:T(8,128)(2,1)S(1)} %collective-permute-done.1.lo, bf16[512,512]{1,0:T(8,128)(2,1)} %collective-permute-done.3.hi, bf16[4,1536,1024]{2,1,0:T(8,128)(2,1)} %bitcast.35, ...), custom_call_target="tpu_custom_call" | custom-call | tf_op jit(solution)/shard_map/project_far/pallas_call | solution.py:200
  131.9 9.0 %all-to-all-start.2 = ((bf16[128,8,1536]{2,1,0:T(8,128)(2,1)}), bf16[128,8,1536]{2,1,0:T(8,128)(2,1)S(1)}, u32[]{:S(2)}, u32[]{:S(2)}) async-start(bf16[128,8,1536]{2,1,0:T(8,128)(2,1)} %bitcast.36), calls=%async_computation.2 | async-start | bytes 6291456 | tf_op jit(solution)/shard_map/all_to_all | solution.py:365
  141.0 0.5 broadcast.204
  141.5 0.8 fusion.36
  142.3 0.7 sub.59.row_ref
  143.0 0.7 sub.60.column_ref
  143.7 39.3 %all-to-all-done.2 = bf16[128,8,1536]{2,1,0:T(8,128)(2,1)S(1)} async-done(((bf16[128,8,1536]{2,1,0:T(8,128)(2,1)}), bf16[128,8,1536]{2,1,0:T(8,128)(2,1)S(1)}, u32[]{:S(2)}, u32[]{:S(2)}) %all-to-all-start.2) | async-done | bytes 3145760 | tf_op jit(solution)/shard_map/all_to_all | solution.py:365
  183.0 0.0 copy-start.2
  183.0 1.6 copy-done.2
  184.7 4.9 %merge.1 = bf16[1,128,2,6144]{3,2,1,0:T(2,128)(2,1)} custom-call(s32[256,1]{1,0:T(8,128)} %sub.60.column_ref, s32[1,256]{1,0:T(1,128)} %sub.59.row_ref, bf16[32,4,8,1536]{3,2,1,0:T(8,128)(2,1)} %bitcast.37), custom_call_target="tpu_custom_call" | custom-call | tf_op jit(solution)/shard_map/merge/pallas_call | solution.py:236
  (10 shorter events, 0.1 us)
Async XLA Ops:
  6.5 44.2 %copy-start.6 = (s32[4]{0:T(128)S(1)}, s32[4]{0:T(128)}, u32[]{:S(2)}) copy-start(s32[4]{0:T(128)} %refs_1_.3) | copy-start | bytes 52
  6.5 42.9 %copy-start.5 = (f32[8]{0:T(128)S(1)}, f32[8]{0:T(128)}, u32[]{:S(2)}) copy-start(f32[8]{0:T(128)} %refs_0_.3) | copy-start | bytes 100
  6.5 41.8 %copy-start.4 = (s32[512,1]{0,1:T(1,128)S(1)}, s32[512,1]{0,1:T(1,128)}, u32[]{:S(2)}) copy-start(s32[512,1]{0,1:T(1,128)} %param.15) | copy-start | bytes 6148
  6.5 42.1 %copy-start.7 = (s32[512]{0:T(512)S(1)}, s32[512]{0:T(512)}, u32[]{:S(2)}) copy-start(s32[512]{0:T(512)} %param.16) | copy-start | bytes 6148
  6.5 103.0 %all-gather.2.cloned.1.call-start = ((), (), s32[]{:S(2)}) async-start(), calls=%async_computation.3 | async-start | bytes 12976128 | tf_op jit(solution)/shard_map/all_gather | solution.py:292
  6.6 1.8 collective-permute-start.4
  8.4 0.7 copy-start.3
  15.6 43.4 %all-to-all-start = ((bf16[32,32,128]{2,1,0:T(8,128)(2,1)}), bf16[32,32,128]{2,1,0:T(8,128)(2,1)S(1)}, u32[]{:S(2)}, u32[]{:S(2)}) async-start(bf16[32,32,128]{2,1,0:T(8,128)(2,1)} %bitcast.40), calls=%async_computation | async-start | bytes 524288 | tf_op jit(solution)/shard_map/all_to_all | solution.py:309
  60.4 14.6 %all-to-all-start.1 = ((bf16[32,40,128]{2,1,0:T(8,128)(2,1)}), bf16[32,40,128]{2,1,0:T(8,128)(2,1)S(1)}, u32[]{:S(2)}, u32[]{:S(2)}) async-start(bf16[32,40,128]{2,1,0:T(8,128)(2,1)} %copy.19), calls=%async_computation.1 | async-start | bytes 655360 | tf_op jit(solution)/shard_map/all_to_all | solution.py:331
  75.7 26.0 %copy-start.8 = (s32[4]{0:T(128)S(1)}, s32[4]{0:T(128)}, u32[]{:S(2)}) copy-start(s32[4]{0:T(128)} %constant.92.clone) | copy-start | bytes 52
  79.8 7.0 %copy-start = (bf16[512,512]{1,0:T(8,128)(2,1)S(1)}, bf16[512,512]{1,0:T(8,128)(2,1)}, u32[]{:S(2)}) copy-start(bf16[512,512]{1,0:T(8,128)(2,1)} %across.2.a0) | copy-start | bytes 1572868
  79.8 15.1 %collective-permute-start = (bf16[512,512]{1,0:T(8,128)(2,1)}, bf16[512,512]{1,0:T(8,128)(2,1)S(1)}, u32[]{:S(2)}, u32[]{:S(2)}) collective-permute-start(bf16[512,512]{1,0:T(8,128)(2,1)} %across.2.a0), channel_id=1, source_target_pairs={{0,1},{1,2},{2,3},{3,0},{4,5},{5,6},{6,7},{7,4},{8,9},{9,10},{10,1... | collective-permute-start | bytes 1572872 | tf_op jit(solution)/shard_map/ppermute | solution.py:352
  84.0 14.5 %collective-permute-start.2 = (bf16[512,512]{1,0:T(8,128)(2,1)}, bf16[512,512]{1,0:T(8,128)(2,1)S(1)}, u32[]{:S(2)}, u32[]{:S(2)}) collective-permute-start(bf16[512,512]{1,0:T(8,128)(2,1)} %across.3.a1), channel_id=1, source_target_pairs={{0,3},{1,0},{2,1},{3,2},{4,7},{5,4},{6,5},{7,6},{8,11},{9,8},{10,9... | collective-permute-start | bytes 1572872 | tf_op jit(solution)/shard_map/ppermute | solution.py:353
  86.8 22.8 %collective-permute-start.6 = (bf16[512,512]{1,0:T(8,128)(2,1)S(1)}, bf16[512,512]{1,0:T(8,128)(2,1)S(1)}, u32[]{:S(2)}, u32[]{:S(2)}) collective-permute-start(bf16[512,512]{1,0:T(8,128)(2,1)S(1)} %copy-done), channel_id=1, source_target_pairs={{0,3},{1,0},{2,1},{3,2},{4,7},{5,4},{6,5},{7,6},{8,11},{9,8},{10,9... | collective-permute-start | bytes 1572872 | tf_op jit(solution)/shard_map/ppermute | solution.py:355
  86.8 22.8 %collective-permute-start.5 = (bf16[512,512]{1,0:T(8,128)(2,1)}, bf16[512,512]{1,0:T(8,128)(2,1)S(1)}, u32[]{:S(2)}, u32[]{:S(2)}) collective-permute-start(bf16[512,512]{1,0:T(8,128)(2,1)} %across.3.a1), channel_id=1, source_target_pairs={{0,1},{1,2},{2,3},{3,0},{4,5},{5,6},{6,7},{7,4},{8,9},{9,10},{10,1... | collective-permute-start | bytes 1572872 | tf_op jit(solution)/shard_map/ppermute | solution.py:354
  95.0 25.9 %collective-permute-start.1 = (bf16[512,512]{1,0:T(8,128)(2,1)S(1)}, bf16[512,512]{1,0:T(8,128)(2,1)S(1)}, u32[]{:S(2)}, u32[]{:S(2)}) collective-permute-start(bf16[512,512]{1,0:T(8,128)(2,1)S(1)} %collective-permute-done.b0), channel_id=1, source_target_pairs={{0,1},{1,2},{2,3},{3,0},{4,5},{5,6},{6,7},{7,4},{8,9},{9,10},{10,1... | collective-permute-start | bytes 1572872 | tf_op jit(solution)/shard_map/ppermute | solution.py:356
  98.5 22.4 %collective-permute-start.3 = (bf16[512,512]{1,0:T(8,128)(2,1)S(1)}, bf16[512,512]{1,0:T(8,128)(2,1)}, u32[]{:S(2)}, u32[]{:S(2)}) collective-permute-start(bf16[512,512]{1,0:T(8,128)(2,1)S(1)} %collective-permute-done.2.c1), channel_id=1, source_target_pairs={{0,3},{1,0},{2,1},{3,2},{4,7},{5,4},{6,5},{7,6},{8,11},{9,8},{10,9... | collective-permute-start | bytes 1572872 | tf_op jit(solution)/shard_map/ppermute | solution.py:357
  109.6 1.0 copy-start.1
  131.9 51.1 %all-to-all-start.2 = ((bf16[128,8,1536]{2,1,0:T(8,128)(2,1)}), bf16[128,8,1536]{2,1,0:T(8,128)(2,1)S(1)}, u32[]{:S(2)}, u32[]{:S(2)}) async-start(bf16[128,8,1536]{2,1,0:T(8,128)(2,1)} %bitcast.36), calls=%async_computation.2 | async-start | bytes 6291456 | tf_op jit(solution)/shard_map/all_to_all | solution.py:365
  183.0 1.6 copy-start.2
Sparse Core Ops, SparseCore 0:
  9.6 90.2 all-gather.1

commit v2 on v1

v2 whole, which is shorter than its diff:
```python
import functools

import jax
import jax.numpy as jnp
from jax import lax
from jax.experimental import pallas as pl
from jax.experimental.pallas import tpu as pltpu
from jax.sharding import PartitionSpec as P

BF16 = jnp.bfloat16
F32 = jnp.float32
CAPACITY = 2
ROWS_BLK = 128
BIG = 1 << 30
CORES = 2


def doc_of(positions, doc_ends):
    return jnp.sum((positions[:, None] >= doc_ends[None, :]).astype(jnp.int32), axis=1)


def doc_limit(positions, lengths_ref):
    end = lengths_ref[0]
    limit = jnp.where(positions < end, end, BIG)
    for doc in range(1, lengths_ref.shape[0]):
        end = end + lengths_ref[doc]
        limit = jnp.minimum(limit, jnp.where(positions < end, end, BIG))
    return limit


def params(mib=48):
    return pltpu.CompilerParams(
        dimension_semantics=("arbitrary",), vmem_limit_bytes=mib << 20
    )


SCALARS = pl.BlockSpec(memory_space=pltpu.SMEM)


def local_state_body(rate_ref, lengths_ref, query_ref, grad_ref, out_ref):
    count, dim = out_ref.shape[:2]
    toks = query_ref.shape[0]
    first = lax.axis_index("seq") * toks
    limit = doc_limit(jnp.maximum(first - 1, 0), lengths_ref)
    step = lax.broadcasted_iota(jnp.int32, (toks, dim), 0)
    inside = first + step < limit
    span = (step + 1).astype(F32)
    for h in range(count):
        rate = rate_ref[pl.program_id(0) * count + h]
        cols = slice(h * dim, (h + 1) * dim)
        lead = jnp.where(inside, jnp.exp(-rate * span), 0.0)
        scaled = (query_ref[:, cols].astype(F32) * lead).astype(BF16)
        out_ref[h] = lax.dot_general(
            scaled, grad_ref[:, cols], (((0,), (0,)), ((), ())), preferred_element_type=F32
        ).astype(out_ref.dtype)


def local_states(rates, lengths, queries, grads, count):
    heads = rates.shape[0]
    toks, dim = queries.shape[0], queries.shape[1] // heads
    blk = pl.BlockSpec((toks, count * dim), lambda h: (0, h))
    return pl.pallas_call(
        local_state_body,
        grid=(heads // count,),
        in_specs=[SCALARS, SCALARS, blk, blk],
        out_specs=pl.BlockSpec((count, dim, dim), lambda h: (h, 0, 0)),
        out_shape=jax.ShapeDtypeStruct((heads, dim, dim), BF16),
        compiler_params=params(),
        name="local_states",
    )(rates, lengths, queries, grads)


def within_body(count, rate_ref, lengths_ref, query_ref, key_ref, grad_ref, out_ref):
    toks = query_ref.shape[0]
    dim = query_ref.shape[1] // count
    first = lax.axis_index("seq") * toks
    half = toks // 2
    for lo in (0, half):
        src = lax.broadcasted_iota(jnp.int32, (half, 1), 0) + lo
        dst = lax.broadcasted_iota(jnp.int32, (1, toks - lo), 1) + lo
        limit = doc_limit(src + first, lengths_ref) - first
        seen = (dst >= src) & (dst < limit)
        for h in range(count):
            rate = rate_ref[pl.program_id(0) * count + h]
            cols = slice(h * dim, (h + 1) * dim)
            rise = jnp.exp(rate * src.astype(F32)) * (1.0 / dim)
            fall = jnp.exp(-rate * dst.astype(F32))
            scores = lax.dot_general(
                key_ref[lo : lo + half, cols],
                query_ref[lo:, cols],
                (((1,), (1,)), ((), ())),
                preferred_element_type=F32,
            )
            weights = jnp.where(seen, scores * rise * fall, 0.0).astype(BF16)
            out_ref[lo : lo + half, cols] = jnp.dot(
                weights, grad_ref[lo:, cols], preferred_element_type=F32
            )


def within(rates, lengths, queries, keys, grads, count):
    heads = rates.shape[0]
    toks, dim = queries.shape[0], queries.shape[1] // heads
    blk = pl.BlockSpec((toks, count * dim), lambda h: (0, h))
    return pl.pallas_call(
        functools.partial(within_body, count),
        grid=(heads // count,),
        in_specs=[SCALARS, SCALARS, blk, blk, blk],
        out_specs=blk,
        out_shape=jax.ShapeDtypeStruct((toks, heads * dim), F32),
        compiler_params=params(),
        name="within",
    )(rates, lengths, queries, keys, grads)


def across_body(start, rate_ref, lengths_ref, key_ref, state_ref, intra_ref, out_ref):
    count, dim = state_ref.shape[:2]
    toks = key_ref.shape[0]
    first = lax.axis_index("seq") * toks
    src = lax.broadcasted_iota(jnp.int32, (toks, dim), 0)
    last = first + toks - 1
    inside = last < doc_limit(src + first, lengths_ref)
    span = (toks - 1 - src).astype(F32)
    for h in range(count):
        rate = rate_ref[start + h]
        cols = slice(h * dim, (h + 1) * dim)
        tail = jnp.where(inside, jnp.exp(-rate * span) * (1.0 / dim), 0.0)
        product = jnp.dot(key_ref[:, cols], state_ref[h], preferred_element_type=F32)
        out_ref[:, cols] = (intra_ref[:, cols] + product * tail).astype(BF16)


def across(rates, lengths, keys, states, intra, part, count):
    dim = states.shape[-1]
    toks = keys.shape[0]
    blk = pl.BlockSpec((toks, count * dim), lambda i: (0, part))
    return pl.pallas_call(
        functools.partial(across_body, part * count),
        grid=(1,),
        in_specs=[
            SCALARS,
            SCALARS,
            blk,
            pl.BlockSpec((count, dim, dim), lambda i: (part, 0, 0)),
            blk,
        ],
        out_specs=pl.BlockSpec((toks, count * dim), lambda i: (0, 0)),
        out_shape=jax.ShapeDtypeStruct((toks, count * dim), BF16),
        compiler_params=params(),
        name="across",
    )(rates, lengths, keys, states, intra)


def times(lo, hi, weight):
    half = lo.shape[1]
    dims = (((1,), (1,)), ((), ()))
    part = lax.dot_general(lo[...], weight[0, :, :half], dims, preferred_element_type=F32)
    part += lax.dot_general(hi[...], weight[0, :, half:], dims, preferred_element_type=F32)
    return part.astype(BF16).astype(F32)


def near_body(place, a0, a1, b0, b1, c0, c1, wa, wb, wc, out_ref):
    total = times(a0, a1, wa) + times(b0, b1, wb)
    out_ref[...] = total + times(c0, c1, wc)


def project_near(place, pieces, weight, tile):
    toks, half = pieces[0].shape
    width, depth = weight.shape[1:]
    whole = pl.BlockSpec((toks, half), lambda i, p: (0, 0))
    return pl.pallas_call(
        near_body,
        grid_spec=pltpu.PrefetchScalarGridSpec(
            num_scalar_prefetch=1,
            grid=(width // tile,),
            in_specs=[whole] * 6
            + [
                pl.BlockSpec((1, tile, depth), lambda i, p, k=k: (p[k], i, 0))
                for k in range(3)
            ],
            out_specs=pl.BlockSpec((toks, tile), lambda i, p: (0, i)),
        ),
        out_shape=jax.ShapeDtypeStruct((toks, width), F32),
        compiler_params=params(),
        name="project_near",
    )(place, *pieces, weight, weight, weight)


def far_body(tiles, place, pick, lo, hi, mine, other, near_mine, near_other, out_ref):
    def fill(weight, near):
        total = near[...] + times(lo, hi, weight)
        out_ref[...] = jnp.dot(
            pick[...], total.astype(BF16), preferred_element_type=F32
        ).astype(BF16)

    first = pl.program_id(0) < tiles
    pl.when(first)(lambda: fill(mine, near_mine))
    pl.when(jnp.logical_not(first))(lambda: fill(other, near_other))


def project_far(place, pick, lo, hi, mine, other, near_mine, near_other, tile):
    toks, half = lo.shape
    slots = pick.shape[0]
    width, depth = mine.shape[1:]
    tiles = width // tile
    whole = pl.BlockSpec((toks, half), lambda i, p: (0, 0))

    def early(i):
        return jnp.minimum(i, tiles - 1)

    def late(i):
        return jnp.maximum(i - tiles, 0)

    def target(i, p):
        turn = jnp.where(i < tiles, p[4], CORES - 1 - p[4])
        return (0, turn * tiles + jnp.where(i < tiles, i, i - tiles))

    return pl.pallas_call(
        functools.partial(far_body, tiles),
        grid_spec=pltpu.PrefetchScalarGridSpec(
            num_scalar_prefetch=1,
            grid=(CORES * tiles,),
            in_specs=[
                pl.BlockSpec((slots, toks), lambda i, p: (0, 0)),
                whole,
                whole,
                pl.BlockSpec((1, tile, depth), lambda i, p: (p[3], early(i), 0)),
                pl.BlockSpec((1, tile, depth), lambda i, p: (p[3], late(i), 0)),
                pl.BlockSpec((toks, tile), lambda i, p: (0, early(i))),
                pl.BlockSpec((toks, tile), lambda i, p: (0, late(i))),
            ],
            out_specs=pl.BlockSpec((slots, tile), target),
        ),
        out_shape=jax.ShapeDtypeStruct((slots, CORES * width), BF16),
        compiler_params=params(),
        name="project_far",
    )(place, pick, lo, hi, mine, other, near_mine, near_other)


def merge_body(column_ref, row_ref, rows_ref, out_ref):
    slots = column_ref.shape[0]
    width = rows_ref.shape[-1]
    same = (column_ref[...] == row_ref[...]) & (column_ref[...] >= 0)
    same = same.astype(F32).astype(BF16)
    rows = rows_ref[...].reshape(slots, width)
    total = jnp.dot(same, rows, preferred_element_type=F32).astype(BF16)
    out_ref[...] = total.reshape(out_ref.shape)


def merge(offsets, got, tile):
    n_seq, n_head, per, width = got.shape
    slots = n_seq * per
    tiles = width // tile
    return pl.pallas_call(
        merge_body,
        grid=(n_head * tiles,),
        in_specs=[
            pl.BlockSpec((slots, 1), lambda i: (0, 0)),
            pl.BlockSpec((1, slots), lambda i: (0, 0)),
            pl.BlockSpec((n_seq, 1, per, tile), lambda i: (0, i // tiles, 0, i % tiles)),
        ],
        out_specs=pl.BlockSpec((1, slots // CAPACITY, CAPACITY, tile), lambda i: (0, 0, 0, i)),
        out_shape=jax.ShapeDtypeStruct((1, slots // CAPACITY, CAPACITY, n_head * width), BF16),
        compiler_params=params(),
        name="merge",
    )(offsets.reshape(slots, 1), offsets.reshape(1, slots), got)


def slots_of(owners, blocks, capacity):
    toks = owners.shape[0]
    width = toks // blocks
    grouped = owners.reshape(blocks, width)
    same_owner = grouped[:, :, None] == grouped[:, None, :]
    lower = jnp.arange(width, dtype=jnp.int32)
    earlier = lower[None, :] < lower[:, None]
    rank = jnp.sum((same_owner & earlier[None]).astype(jnp.int32), axis=2)
    block_ids = jnp.arange(blocks, dtype=jnp.int32)[:, None]
    return ((grouped * blocks + block_ids) * capacity + rank).reshape(toks)


def weight_route(n_seq, n_head):
    rows = n_seq // n_head // CORES
    pairs = []
    for z in range(n_head):
        for y in range(rows):
            for core in range(CORES):
                for x in range(n_head):
                    spot = y * CORES + core
                    to_core, to_y = spot // rows, spot % rows
                    source = ((z * rows + y) * CORES + core) * n_head + x
                    target = ((x * rows + to_y) * CORES + to_core) * n_head + z
                    pairs.append((source, target))
    return pairs


def per_device(
    queries,
    key_vectors,
    output_grad,
    value_weight,
    decay_rate,
    doc_lengths,
    owner_block,
    row_offset,
):
    n_seq = lax.axis_size("seq")
    n_head = lax.axis_size("head")
    devices_all = n_seq * n_head
    tok_rows = queries.shape[0]
    head_local = decay_rate.shape[0]
    head_dim = queries.shape[1] // head_local
    seq_rank = lax.axis_index("seq")
    head_rank = lax.axis_index("head")

    swapped = lax.ppermute(value_weight, ("seq", "head"), weight_route(n_seq, n_head))
    state = local_states(decay_rate, doc_lengths, queries, output_grad, head_local // 2)

    blocks = tok_rows // ROWS_BLK
    per = blocks * CAPACITY
    slot_index = slots_of(owner_block[:, 0], blocks, CAPACITY)
    my_slots = (
        (jnp.arange(n_seq, dtype=jnp.int32)[:, None] * n_head + head_rank) * per
        + jnp.arange(per, dtype=jnp.int32)[None, :]
    )
    hit = my_slots[:, :, None] == slot_index[None, None, :]
    named = jnp.sum(jnp.where(hit, row_offset[None, None, :] + 1, 0), axis=2)
    note = jnp.concatenate([(named // 32).astype(BF16), (named % 32).astype(BF16)], axis=1)
    note = jnp.pad(note[:, None, :], ((0, 0), (0, 7), (0, head_dim - 2 * per)))
    all_slots = jnp.arange(devices_all * per, dtype=jnp.int32)
    pick = (all_slots[:, None] == slot_index[None, :]).astype(BF16)

    share = head_local * head_dim // n_seq
    state_in = lax.all_to_all(
        state.reshape(n_seq, share, head_dim), "seq", split_axis=0, concat_axis=0, tiled=True
    )
    intra = within(
        decay_rate, doc_lengths, queries, key_vectors, output_grad, head_local // 2
    )

    doc_ends = jnp.cumsum(doc_lengths)
    ranks = jnp.arange(n_seq, dtype=jnp.int32)
    doc_last = doc_of((ranks + 1) * tok_rows - 1, doc_ends)
    doc_prior = doc_of(jnp.maximum(ranks * tok_rows - 1, 0), doc_ends)
    my_rate = decay_rate[seq_rank // (n_seq // head_local)]
    ahead = ranks[None, :] - ranks[:, None] - 1
    reach = (ahead >= 0) & (doc_last[:, None] == doc_prior[None, :])
    chain = jnp.where(
        reach, jnp.exp(-my_rate * (jnp.maximum(ahead, 0) * tok_rows).astype(F32)), 0.0
    )
    carried_all = jnp.einsum(
        "bc,cxy->bxy",
        chain,
        state_in.astype(F32),
        precision=lax.Precision.HIGHEST,
        preferred_element_type=F32,
    ).astype(BF16)
    carried_all = jnp.concatenate([carried_all, note], axis=1)
    swapped, _ = lax.optimization_barrier((swapped, carried_all))
    groups = [list(range(core, n_seq, CORES)) for core in range(CORES)]
    mine = lax.all_gather(swapped, "seq", axis=0, tiled=True, axis_index_groups=groups)
    mine = mine.reshape(n_head, -1, value_weight.shape[1])

    carried = lax.all_to_all(
        carried_all,
        "seq",
        split_axis=0,
        concat_axis=0,
        tiled=True,
    )
    offsets = (
        carried[:, share, :per].astype(jnp.int32) * 32
        + carried[:, share, per : 2 * per].astype(jnp.int32)
        - 1
    )
    carried = carried[:, :share].reshape(head_local, head_dim, head_dim)

    own = [
        across(decay_rate, doc_lengths, key_vectors, carried, intra, part, head_local // 2)
        for part in range(2)
    ]
    up = [(i, (i + 1) % n_head) for i in range(n_head)]
    down = [(i, (i - 1) % n_head) for i in range(n_head)]
    left_lo = lax.ppermute(own[0], "head", up)
    right_hi = lax.ppermute(own[1], "head", down)
    left_hi = lax.ppermute(own[1], "head", up)
    right_lo = lax.ppermute(own[0], "head", down)
    far_lo = lax.ppermute(left_lo, "head", up)
    far_hi = lax.ppermute(right_hi, "head", down)
    mine, *_ = lax.optimization_barrier((mine, left_lo, right_hi, left_hi, right_lo))
    other = lax.ppermute(mine, "seq", [(i, i ^ 1) for i in range(n_seq)])
    ring = (head_rank + jnp.array([0, n_head - 1, 1, 2], jnp.int32)) % n_head
    place = jnp.concatenate([ring, (seq_rank % CORES)[None]])

    pieces = (own[0], own[1], left_lo, left_hi, right_lo, right_hi)
    near_mine = project_near(place, pieces, mine, 256)
    near_other = project_near(place, pieces, other, 256)
    send = project_far(place, pick, far_lo, far_hi, mine, other, near_mine, near_other, 256)
    send = send.reshape(devices_all, per, -1)
    got = lax.all_to_all(send, ("seq", "head"), split_axis=0, concat_axis=0, tiled=True)
    return merge(offsets, got.reshape(n_seq, n_head, per, -1), 768)


def solution(mesh):
    return jax.shard_map(
        per_device,
        mesh=mesh,
        in_specs=(
            P("seq", "head"),
            P("seq", "head"),
            P("seq", "head"),
            P("seq", "head"),
            P("head"),
            P(),
            P("seq", None),
            P("seq"),
        ),
        out_specs=P(("seq", "head"), None, None, None),
        check_vma=False,
    )
```

time: 198 us -> 205 us (1.035)
  waiting for transfers between devices: 67.5 us -> 97.8 us
  starting transfers between devices: 54.9 us -> 37.6 us
  Pallas kernels: 49.6 us -> 35.1 us
  local copies, waits for them, and re-layouts: 7.58 us -> 12.9 us
  other arithmetic: 2.24 us -> 5.54 us
    all_to_all x1, starting transfers between devices: 32.6 us -> 9.61 us  [per_device(): lax.all_to_all(state.reshape(n_seq, share, head_dim), 'seq', split_axis=0...]
    ppermute x1 -> x2, waiting for transfers between devices: 0.01 us -> 18.1 us  [the longest x1 18.1 us: per_device(): lax.ppermute(value_weight, ('seq', 'head'), weight_route(n_seq, n_head))]
    pallas_call x6, Pallas kernels: 39.4 us -> 24.3 us  [the longest x1 11 us: project_far(): pl.pallas_call(functools.partial(far_body, tiles), grid_spec=pltpu.Prefet...]
    all_gather x1, waiting for transfers between devices: 0.01 us -> 13.2 us  [per_device(): lax.all_gather(swapped, 'seq', axis=0, tiled=True, axis_index_groups=groups)]
    ppermute x1, waiting for transfers between devices: 0.01 us -> 11.2 us  [per_device(): left_hi = lax.ppermute(own[1], 'head', up)]
    all_to_all x1, waiting for transfers between devices: 7.94 us -> 0.01 us  [per_device(): lax.all_to_all(state.reshape(n_seq, share, head_dim), 'seq', split_axis=0...]
    unnamed x18 -> x30, local copies, waits for them, and re-layouts: 3.43 us -> 9.93 us
    all_to_all x1, starting transfers between devices: 3.82 us -> 9.86 us  [per_device(): lax.all_to_all(carried_all, 'seq', split_axis=0, concat_axis=0, tiled=True)]
  transfers between devices with their start and end apart: 11 -> 12, of which waited for: 6 -> 7; matrix products, arithmetic and copies ran while one was open for 3% -> 4% of each run, Pallas kernels for 17% -> 8%
where the time goes in v2:
time: 205 us; the launch traced here: 204 us
  waiting for transfers between devices  97.8 us (48%)
  starting transfers between devices  37.6 us (18%)
  Pallas kernels  35.1 us (17%)
  between operations  14.4 us (7%)
  local copies, waits for them, and re-layouts  12.9 us (6%)
  other arithmetic  5.54 us (3%)
    all_to_all x1, waiting for transfers between devices, per_device(): lax.all_to_all(send, ('seq', 'head'), split_axis=0, concat_axis=0, tiled=...  40.5 us
    ppermute x1, waiting for transfers between devices, per_device(): lax.ppermute(value_weight, ('seq', 'head'), weight_route(n_seq, n_head))  18.1 us
    all_gather x1, waiting for transfers between devices, per_device(): lax.all_gather(swapped, 'seq', axis=0, tiled=True, axis_index_groups=groups)  13.2 us
    ppermute x1, waiting for transfers between devices, per_device(): left_hi = lax.ppermute(own[1], 'head', up)  11.2 us
    pallas_call x1, Pallas kernels, project_far(): pl.pallas_call(functools.partial(far_body, tiles), grid_spec=pltpu.Prefet...  11 us
    pallas_call x2, Pallas kernels, project_near(): pl.pallas_call(near_body, grid_spec=pltpu.PrefetchScalarGridSpec(num_scal...  10.9 us
    unnamed x30, local copies, waits for them, and re-layouts  9.93 us
    all_to_all x1, starting transfers between devices, per_device(): lax.all_to_all(carried_all, 'seq', split_axis=0, concat_axis=0, tiled=True)  9.86 us
  transfers between devices with their start and end apart: 12, of which 7 were waited for; matrix products, arithmetic and copies ran while one was open for 4% of the time, Pallas kernels for 8%

profile of v2, /device:TPU:1, one launch (start us, length us, event | category | flops | bytes accessed | tf_op | source)
XLA Modules:
  0.0 203.7 jit_solution(18301124357720317513)
XLA Ops:
  6.5 1.2 copy-done.5
  7.8 1.2 copy-done.7
  9.0 0.7 copy-done.9
  9.6 0.7 copy-done.11
  10.3 2.4 %local_states.1 = bf16[8,128,128]{2,1,0:T(8,128)(2,1)} custom-call(f32[8]{0:T(128)S(1)} %copy-done.9, s32[4]{0:T(128)S(1)} %copy-done.11, bf16[512,1024]{1,0:T(8,128)(2,1)S(1)} %copy-done.5, bf16[512,1024]{1,0:T(8,128)(2,1)S(1)} %copy-done.7), custom_call_target="tpu_custom_call" | custom-call | tf_op jit(solution)/shard_map/local_states/pallas_call | solution.py:62
  12.7 9.6 %all-to-all-start = ((bf16[32,32,128]{2,1,0:T(8,128)(2,1)}), bf16[32,32,128]{2,1,0:T(8,128)(2,1)S(1)}, u32[]{:S(2)}, u32[]{:S(2)}) async-start(bf16[32,32,128]{2,1,0:T(8,128)(2,1)} %bitcast.4), calls=%async_computation | async-start | bytes 524288 | tf_op jit(solution)/shard_map/all_to_all | solution.py:331
  22.3 0.0 all-gather.2.cloned.1.call-start
  22.4 3.5 %collective-permute-start.4 = (bf16[192,1024]{1,0:T(8,128)(2,1)}, bf16[192,1024]{1,0:T(8,128)(2,1)S(1)}, u32[]{:S(2)}, u32[]{:S(2)}) collective-permute-start(bf16[192,1024]{1,0:T(8,128)(2,1)} %param.12), channel_id=1, source_target_pairs={{0,0},{1,32},{2,64},{3,96},{4,8},{5,40},{6,72},{7,104},{8,16},{9,4... | collective-permute-start | bytes 1179656 | tf_op jit(solution)/shard_map/ppermute | solution.py:313
  26.0 0.7 broadcast_multiply_fusion
  26.6 0.1 iota_add_fusion
  26.7 1.0 convert_reduce_fusion
  27.7 0.7 bitcast_add_fusion
  28.4 0.7 select_reduce_fusion
  29.1 0.8 reduce-window.8
  30.0 0.1 convert_reduce_fusion.2
  30.1 0.1 maximum_bitcast_fusion
  30.1 1.3 dynamic_slice.3
  32.1 0.0 all-to-all-done
  32.2 0.4 convolution_convert_fusion
  32.6 18.1 %collective-permute-done.4 = bf16[192,1024]{1,0:T(8,128)(2,1)S(1)} collective-permute-done((bf16[192,1024]{1,0:T(8,128)(2,1)}, bf16[192,1024]{1,0:T(8,128)(2,1)S(1)}, u32[]{:S(2)}, u32[]{:S(2)}) %collective-permute-start.4) | collective-permute-done | bytes 393248 | tf_op jit(solution)/shard_map/ppermute | solution.py:313
  50.7 0.8 copy-done.13
  51.5 0.0 all-gather.2.cloned.1.call-update
  51.5 0.9 copy.19
  52.3 9.9 %all-to-all-start.1 = ((bf16[32,40,128]{2,1,0:T(8,128)(2,1)}), bf16[32,40,128]{2,1,0:T(8,128)(2,1)S(1)}, u32[]{:S(2)}, u32[]{:S(2)}) async-start(bf16[32,40,128]{2,1,0:T(8,128)(2,1)} %copy.19), calls=%async_computation.1 | async-start | bytes 655360 | tf_op jit(solution)/shard_map/all_to_all | solution.py:361
  62.2 0.0 copy-done
  62.2 0.0 copy-done.10
  62.2 0.0 copy-start.6
  62.3 1.3 copy-done.6
  63.5 1.2 copy-done.8
  64.8 3.7 %within.1.intra_ref = f32[512,1024]{1,0:T(8,128)S(1)} custom-call(f32[8]{0:T(128)S(1)} %copy-done.10, s32[4]{0:T(128)S(1)} %copy-done.12, bf16[512,1024]{1,0:T(8,128)(2,1)S(1)} %copy-done.6, bf16[512,1024]{1,0:T(8,128)(2,1)S(1)} %copy-done, bf16[512,1024]{1,0:T(8,128)(2,1)S(1)} %copy-done.8), custom_call_target="tpu_custom_call" | custom-call | tf_op jit(solution)/shard_map/within/pallas_call | solution.py:104
  68.5 4.8 %all-to-all-done.1 = bf16[32,40,128]{2,1,0:T(8,128)(2,1)S(1)} async-done(((bf16[32,40,128]{2,1,0:T(8,128)(2,1)}), bf16[32,40,128]{2,1,0:T(8,128)(2,1)S(1)}, u32[]{:S(2)}, u32[]{:S(2)}) %all-to-all-start.1) | async-done | bytes 327712 | tf_op jit(solution)/shard_map/all_to_all | solution.py:361
  73.4 0.0 copy-start.14
  73.4 1.1 across.3.a1
  74.5 1.1 across.2.a0
  75.6 0.1 collective-permute-start.6
  75.7 1.5 collective-permute-start
  77.1 0.8 copy-done.3
  77.9 0.0 collective-permute-start.5
  77.9 2.7 %collective-permute-start.2 = (bf16[512,512]{1,0:T(8,128)(2,1)S(1)}, bf16[512,512]{1,0:T(8,128)(2,1)S(1)}, u32[]{:S(2)}, u32[]{:S(2)}) collective-permute-start(bf16[512,512]{1,0:T(8,128)(2,1)S(1)} %across.3.a1), channel_id=1, source_target_pairs={{0,3},{1,0},{2,1},{3,2},{4,7},{5,4},{6,5},{7,6},{8,11},{9,8},{10,9... | collective-permute-start | bytes 1572872 | tf_op jit(solution)/shard_map/ppermute | solution.py:382
  80.6 8.8 %collective-permute-done.6.c0 = bf16[512,512]{1,0:T(8,128)(2,1)S(1)} collective-permute-done((bf16[512,512]{1,0:T(8,128)(2,1)S(1)}, bf16[512,512]{1,0:T(8,128)(2,1)S(1)}, u32[]{:S(2)}, u32[]{:S(2)}) %collective-permute-start.6) | collective-permute-done | bytes 524320 | tf_op jit(solution)/shard_map/ppermute | solution.py:384
  89.4 1.2 collective-permute-done.b0
  90.6 11.2 %collective-permute-done.5.b1 = bf16[512,512]{1,0:T(8,128)(2,1)S(1)} collective-permute-done((bf16[512,512]{1,0:T(8,128)(2,1)S(1)}, bf16[512,512]{1,0:T(8,128)(2,1)S(1)}, u32[]{:S(2)}, u32[]{:S(2)}) %collective-permute-start.5) | collective-permute-done | bytes 524320 | tf_op jit(solution)/shard_map/ppermute | solution.py:383
  101.8 0.0 collective-permute-done.2.c1
  101.8 13.2 %all-gather.2.cloned.1.call-done = bf16[3072,1024]{1,0:T(8,128)(2,1)} async-done(((bf16[192,1024]{1,0:T(8,128)(2,1)}), bf16[3072,1024]{1,0:T(8,128)(2,1)}) %all-gather.2.cloned.1.call-update) | async-done | bytes 6291472 | tf_op jit(solution)/shard_map/all_gather | solution.py:358
  115.0 0.7 collective-permute-start.7
  115.7 1.2 collective-permute-start.1
  116.9 1.5 collective-permute-start.3
  118.4 0.1 pad_add_fusion.place
  118.4 0.4 fusion.pick
  118.9 1.0 copy-done.2
  119.9 1.0 copy-done.4
  120.9 5.4 %project_near.2.near_mine = f32[512,768]{1,0:T(8,128)S(1)} custom-call(s32[5]{0:T(128)S(1)} %pad_add_fusion.place, bf16[512,512]{1,0:T(8,128)(2,1)S(1)} %copy-done.4, bf16[512,512]{1,0:T(8,128)(2,1)S(1)} %copy-done.2, bf16[512,512]{1,0:T(8,128)(2,1)S(1)} %collective-permute-done.b0, bf16[512,512]{1,0:T(8,128)(2,1)S(1)} %collective-permute-done.5.b1, ...), custom_call_target="tpu_custom_call" | custom-call | tf_op jit(solution)/shard_map/project_near/pallas_call | solution.py:169
  126.4 0.0 collective-permute-done.7.wa.wb.wc.other
  126.4 5.4 %project_near.3.near_other = f32[512,768]{1,0:T(8,128)S(1)} custom-call(s32[5]{0:T(128)S(1)} %pad_add_fusion.place, bf16[512,512]{1,0:T(8,128)(2,1)S(1)} %copy-done.4, bf16[512,512]{1,0:T(8,128)(2,1)S(1)} %copy-done.2, bf16[512,512]{1,0:T(8,128)(2,1)S(1)} %collective-permute-done.b0, bf16[512,512]{1,0:T(8,128)(2,1)S(1)} %collective-permute-done.5.b1, ...), custom_call_target="tpu_custom_call" | custom-call | tf_op jit(solution)/shard_map/project_near/pallas_call | solution.py:169
  131.8 0.0 collective-permute-done.1.lo
  131.8 0.0 collective-permute-done.3.hi
  131.8 11.0 %project_far.1 = bf16[1024,1536]{1,0:T(8,128)(2,1)} custom-call(s32[5]{0:T(128)S(1)} %pad_add_fusion.place, bf16[1024,512]{1,0:T(8,128)(2,1)S(1)} %fusion.pick, bf16[512,512]{1,0:T(8,128)(2,1)S(1)} %collective-permute-done.1.lo, bf16[512,512]{1,0:T(8,128)(2,1)S(1)} %collective-permute-done.3.hi, bf16[4,768,1024]{2,1,0:T(8,128)(2,1)} %bitcast.33, ...), custom_call_target="tpu_custom_call" | custom-call | tf_op jit(solution)/shard_map/project_far/pallas_call | solution.py:216
  142.9 7.0 %all-to-all-start.2 = ((bf16[128,8,1536]{2,1,0:T(8,128)(2,1)}), bf16[128,8,1536]{2,1,0:T(8,128)(2,1)S(1)}, u32[]{:S(2)}, u32[]{:S(2)}) async-start(bf16[128,8,1536]{2,1,0:T(8,128)(2,1)} %bitcast.34), calls=%async_computation.2 | async-start | bytes 6291456 | tf_op jit(solution)/shard_map/all_to_all | solution.py:397
  149.9 0.6 broadcast.197
  150.5 0.8 fusion.35
  151.3 0.1 sub.59.row_ref
  151.4 0.1 sub.60.column_ref
  151.5 40.5 %all-to-all-done.2 = bf16[128,8,1536]{2,1,0:T(8,128)(2,1)S(1)} async-done(((bf16[128,8,1536]{2,1,0:T(8,128)(2,1)}), bf16[128,8,1536]{2,1,0:T(8,128)(2,1)S(1)}, u32[]{:S(2)}, u32[]{:S(2)}) %all-to-all-start.2) | async-done | bytes 3145760 | tf_op jit(solution)/shard_map/all_to_all | solution.py:397
  191.9 4.9 %merge.1 = bf16[1,128,2,6144]{3,2,1,0:T(2,128)(2,1)} custom-call(s32[256,1]{1,0:T(8,128)S(1)} %sub.60.column_ref, s32[1,256]{1,0:T(1,128)S(1)} %sub.59.row_ref, bf16[32,4,8,1536]{3,2,1,0:T(8,128)(2,1)S(1)} %bitcast.25), custom_call_target="tpu_custom_call" | custom-call | tf_op jit(solution)/shard_map/merge/pallas_call | solution.py:252
  (23 shorter events, 0.1 us)
Async XLA Ops:
  6.5 1.2 copy-start.5
  7.8 1.2 copy-start.7
  9.0 0.7 copy-start.9
  9.6 0.7 copy-start.11
  10.3 51.9 %copy-start = (bf16[512,1024]{1,0:T(8,128)(2,1)S(1)}, bf16[512,1024]{1,0:T(8,128)(2,1)}, u32[]{:S(2)}) copy-start(bf16[512,1024]{1,0:T(8,128)(2,1)} %key_ref.5) | copy-start | bytes 3145732
  10.3 51.9 %copy-start.10 = (f32[8]{0:T(128)S(1)}, f32[8]{0:T(128)}, u32[]{:S(2)}) copy-start(f32[8]{0:T(128)} %rate_ref.7) | copy-start | bytes 100
  10.3 51.9 %copy-start.12 = (s32[4]{0:T(128)S(1)}, s32[4]{0:T(128)}, u32[]{:S(2)}) copy-start(s32[4]{0:T(128)} %lengths_ref.7) | copy-start | bytes 52
  12.7 19.4 %all-to-all-start = ((bf16[32,32,128]{2,1,0:T(8,128)(2,1)}), bf16[32,32,128]{2,1,0:T(8,128)(2,1)S(1)}, u32[]{:S(2)}, u32[]{:S(2)}) async-start(bf16[32,32,128]{2,1,0:T(8,128)(2,1)} %bitcast.4), calls=%async_computation | async-start | bytes 524288 | tf_op jit(solution)/shard_map/all_to_all | solution.py:331
  22.3 92.7 %all-gather.2.cloned.1.call-start = ((), (), s32[]{:S(2)}) async-start(), calls=%async_computation.3 | async-start | bytes 6684672 | tf_op jit(solution)/shard_map/all_gather | solution.py:358
  22.4 28.3 %collective-permute-start.4 = (bf16[192,1024]{1,0:T(8,128)(2,1)}, bf16[192,1024]{1,0:T(8,128)(2,1)S(1)}, u32[]{:S(2)}, u32[]{:S(2)}) collective-permute-start(bf16[192,1024]{1,0:T(8,128)(2,1)} %param.12), channel_id=1, source_target_pairs={{0,0},{1,32},{2,64},{3,96},{4,8},{5,40},{6,72},{7,104},{8,16},{9,4... | collective-permute-start | bytes 1179656 | tf_op jit(solution)/shard_map/ppermute | solution.py:313
  50.7 0.8 copy-start.13
  52.3 21.0 %all-to-all-start.1 = ((bf16[32,40,128]{2,1,0:T(8,128)(2,1)}), bf16[32,40,128]{2,1,0:T(8,128)(2,1)S(1)}, u32[]{:S(2)}, u32[]{:S(2)}) async-start(bf16[32,40,128]{2,1,0:T(8,128)(2,1)} %copy.19), calls=%async_computation.1 | async-start | bytes 655360 | tf_op jit(solution)/shard_map/all_to_all | solution.py:361
  62.2 1.3 copy-start.6
  63.5 1.3 copy-start.8
  73.4 45.0 %copy-start.14 = (s32[4]{0:T(128)S(1)}, s32[4]{0:T(128)}, u32[]{:S(2)}) copy-start(s32[4]{0:T(128)} %constant.102.clone) | copy-start | bytes 52
  74.5 3.4 %copy-start.1 = (bf16[512,512]{1,0:T(8,128)(2,1)}, bf16[512,512]{1,0:T(8,128)(2,1)S(1)}, u32[]{:S(2)}) copy-start(bf16[512,512]{1,0:T(8,128)(2,1)S(1)} %across.3.a1) | copy-start | bytes 1572868
  75.6 13.8 %collective-permute-start.6 = (bf16[512,512]{1,0:T(8,128)(2,1)S(1)}, bf16[512,512]{1,0:T(8,128)(2,1)S(1)}, u32[]{:S(2)}, u32[]{:S(2)}) collective-permute-start(bf16[512,512]{1,0:T(8,128)(2,1)S(1)} %across.2.a0), channel_id=1, source_target_pairs={{0,3},{1,0},{2,1},{3,2},{4,7},{5,4},{6,5},{7,6},{8,11},{9,8},{10,9... | collective-permute-start | bytes 1572872 | tf_op jit(solution)/shard_map/ppermute | solution.py:384
  75.7 14.9 %collective-permute-start = (bf16[512,512]{1,0:T(8,128)(2,1)S(1)}, bf16[512,512]{1,0:T(8,128)(2,1)S(1)}, u32[]{:S(2)}, u32[]{:S(2)}) collective-permute-start(bf16[512,512]{1,0:T(8,128)(2,1)S(1)} %across.2.a0), channel_id=1, source_target_pairs={{0,1},{1,2},{2,3},{3,0},{4,5},{5,6},{6,7},{7,4},{8,9},{9,10},{10,1... | collective-permute-start | bytes 1572872 | tf_op jit(solution)/shard_map/ppermute | solution.py:381
  77.1 0.8 copy-start.3
  77.9 23.9 %collective-permute-start.5 = (bf16[512,512]{1,0:T(8,128)(2,1)S(1)}, bf16[512,512]{1,0:T(8,128)(2,1)S(1)}, u32[]{:S(2)}, u32[]{:S(2)}) collective-permute-start(bf16[512,512]{1,0:T(8,128)(2,1)S(1)} %across.3.a1), channel_id=1, source_target_pairs={{0,1},{1,2},{2,3},{3,0},{4,5},{5,6},{6,7},{7,4},{8,9},{9,10},{10,1... | collective-permute-start | bytes 1572872 | tf_op jit(solution)/shard_map/ppermute | solution.py:383
  77.9 23.9 %collective-permute-start.2 = (bf16[512,512]{1,0:T(8,128)(2,1)S(1)}, bf16[512,512]{1,0:T(8,128)(2,1)S(1)}, u32[]{:S(2)}, u32[]{:S(2)}) collective-permute-start(bf16[512,512]{1,0:T(8,128)(2,1)S(1)} %across.3.a1), channel_id=1, source_target_pairs={{0,3},{1,0},{2,1},{3,2},{4,7},{5,4},{6,5},{7,6},{8,11},{9,8},{10,9... | collective-permute-start | bytes 1572872 | tf_op jit(solution)/shard_map/ppermute | solution.py:382
  115.0 11.4 %collective-permute-start.7 = (bf16[4,768,1024]{2,1,0:T(8,128)(2,1)}, bf16[4,768,1024]{2,1,0:T(8,128)(2,1)}, u32[]{:S(2)}, u32[]{:S(2)}) collective-permute-start(bf16[4,768,1024]{2,1,0:T(8,128)(2,1)} %bitcast.29), channel_id=1, source_target_pairs={{0,4},{4,0},{8,12},{12,8},{16,20},{20,16},{24,28},{28,24},{32,36},... | collective-permute-start | bytes 18874376 | tf_op jit(solution)/shard_map/ppermute | solution.py:388
  115.7 16.2 %collective-permute-start.1 = (bf16[512,512]{1,0:T(8,128)(2,1)S(1)}, bf16[512,512]{1,0:T(8,128)(2,1)S(1)}, u32[]{:S(2)}, u32[]{:S(2)}) collective-permute-start(bf16[512,512]{1,0:T(8,128)(2,1)S(1)} %collective-permute-done.b0), channel_id=1, source_target_pairs={{0,1},{1,2},{2,3},{3,0},{4,5},{5,6},{6,7},{7,4},{8,9},{9,10},{10,1... | collective-permute-start | bytes 1572872 | tf_op jit(solution)/shard_map/ppermute | solution.py:385
  116.9 15.0 %collective-permute-start.3 = (bf16[512,512]{1,0:T(8,128)(2,1)S(1)}, bf16[512,512]{1,0:T(8,128)(2,1)S(1)}, u32[]{:S(2)}, u32[]{:S(2)}) collective-permute-start(bf16[512,512]{1,0:T(8,128)(2,1)S(1)} %collective-permute-done.2.c1), channel_id=1, source_target_pairs={{0,3},{1,0},{2,1},{3,2},{4,7},{5,4},{6,5},{7,6},{8,11},{9,8},{10,9... | collective-permute-start | bytes 1572872 | tf_op jit(solution)/shard_map/ppermute | solution.py:386
  118.9 1.0 copy-start.2
  119.9 1.0 copy-start.4
  142.9 49.0 %all-to-all-start.2 = ((bf16[128,8,1536]{2,1,0:T(8,128)(2,1)}), bf16[128,8,1536]{2,1,0:T(8,128)(2,1)S(1)}, u32[]{:S(2)}, u32[]{:S(2)}) async-start(bf16[128,8,1536]{2,1,0:T(8,128)(2,1)} %bitcast.34), calls=%async_computation.2 | async-start | bytes 6291456 | tf_op jit(solution)/shard_map/all_to_all | solution.py:397
Sparse Core Ops, SparseCore 0:
  51.6 63.3 all-gather.1

commit v3 on v2

--- a/solution.py
+++ b/solution.py
@@ -12,7 +12,6 @@
 CAPACITY = 2
 ROWS_BLK = 128
 BIG = 1 << 30
-CORES = 2
 
 
 def doc_of(positions, doc_ends):
@@ -149,90 +148,80 @@
     )(rates, lengths, keys, states, intra)
 
 
-def times(lo, hi, weight):
-    half = lo.shape[1]
-    dims = (((1,), (1,)), ((), ()))
-    part = lax.dot_general(lo[...], weight[0, :, :half], dims, preferred_element_type=F32)
-    part += lax.dot_general(hi[...], weight[0, :, half:], dims, preferred_element_type=F32)
-    return part.astype(BF16).astype(F32)
-
-
-def near_body(place, a0, a1, b0, b1, c0, c1, wa, wb, wc, out_ref):
-    total = times(a0, a1, wa) + times(b0, b1, wb)
-    out_ref[...] = total + times(c0, c1, wc)
-
-
-def project_near(place, pieces, weight, tile):
+def times(rows, weight):
+    return lax.dot_general(
+        rows[...], weight[0], (((1,), (1,)), ((), ())), preferred_element_type=F32
+    )
+
+
+def near_body(count, place, *refs):
+    out_ref = refs[-1]
+    total = None
+    for rows, weight in zip(refs[:count], refs[count : 2 * count]):
+        part = times(rows, weight)
+        total = part if total is None else total + part
+    for held in refs[2 * count : -1]:
+        total = total + held[...]
+    out_ref[...] = total
+
+
+def project_near(place, pieces, weight, held, tile):
+    count = len(pieces)
     toks, half = pieces[0].shape
     width, depth = weight.shape[1:]
     whole = pl.BlockSpec((toks, half), lambda i, p: (0, 0))
-    return pl.pallas_call(
-        near_body,
+    part = pl.BlockSpec((toks, tile), lambda i, p: (0, i))
+    return pl.pallas_call(
+        functools.partial(near_body, count),
         grid_spec=pltpu.PrefetchScalarGridSpec(
             num_scalar_prefetch=1,
             grid=(width // tile,),
-            in_specs=[whole] * 6
+            in_specs=[whole] * count
             + [
                 pl.BlockSpec((1, tile, depth), lambda i, p, k=k: (p[k], i, 0))
-                for k in range(3)
-            ],
-            out_specs=pl.BlockSpec((toks, tile), lambda i, p: (0, i)),
+                for k in range(count)
+            ]
+            + [part] * len(held),
+            out_specs=part,
         ),
         out_shape=jax.ShapeDtypeStruct((toks, width), F32),
         compiler_params=params(),
         name="project_near",
-    )(place, *pieces, weight, weight, weight)
-
-
-def far_body(tiles, place, pick, lo, hi, mine, other, near_mine, near_other, out_ref):
-    def fill(weight, near):
-        total = near[...] + times(lo, hi, weight)
-        out_ref[...] = jnp.dot(
-            pick[...], total.astype(BF16), preferred_element_type=F32
-        ).astype(BF16)
-
-    first = pl.program_id(0) < tiles
-    pl.when(first)(lambda: fill(mine, near_mine))
-    pl.when(jnp.logical_not(first))(lambda: fill(other, near_other))
-
-
-def project_far(place, pick, lo, hi, mine, other, near_mine, near_other, tile):
+    )(place, *pieces, *[weight] * count, *held)
+
+
+def far_body(place, pick, lo, hi, weight_lo, weight_hi, near, out_ref):
+    total = near[...] + times(lo, weight_lo) + times(hi, weight_hi)
+    out_ref[...] = jnp.dot(
+        pick[...], total.astype(BF16), preferred_element_type=F32
+    ).astype(BF16)
+
+
+def project_far(place, pick, lo, hi, weight_lo, weight_hi, near, tile):
     toks, half = lo.shape
     slots = pick.shape[0]
-    width, depth = mine.shape[1:]
-    tiles = width // tile
+    width, depth = weight_lo.shape[1:]
     whole = pl.BlockSpec((toks, half), lambda i, p: (0, 0))
-
-    def early(i):
-        return jnp.minimum(i, tiles - 1)
-
-    def late(i):
-        return jnp.maximum(i - tiles, 0)
-
-    def target(i, p):
-        turn = jnp.where(i < tiles, p[4], CORES - 1 - p[4])
-        return (0, turn * tiles + jnp.where(i < tiles, i, i - tiles))
-
-    return pl.pallas_call(
-        functools.partial(far_body, tiles),
+    part = pl.BlockSpec((1, tile, depth), lambda i, p: (p[3], i, 0))
+    return pl.pallas_call(
+        far_body,
         grid_spec=pltpu.PrefetchScalarGridSpec(
             num_scalar_prefetch=1,
-            grid=(CORES * tiles,),
+            grid=(width // tile,),
             in_specs=[
                 pl.BlockSpec((slots, toks), lambda i, p: (0, 0)),
                 whole,
                 whole,
-                pl.BlockSpec((1, tile, depth), lambda i, p: (p[3], early(i), 0)),
-                pl.BlockSpec((1, tile, depth), lambda i, p: (p[3], late(i), 0)),
-                pl.BlockSpec((toks, tile), lambda i, p: (0, early(i))),
-                pl.BlockSpec((toks, tile), lambda i, p: (0, late(i))),
+                part,
+                part,
+                pl.BlockSpec((toks, tile), lambda i, p: (0, i)),
             ],
-            out_specs=pl.BlockSpec((slots, tile), target),
+            out_specs=pl.BlockSpec((slots, tile), lambda i, p: (0, i)),
         ),
-        out_shape=jax.ShapeDtypeStruct((slots, CORES * width), BF16),
+        out_shape=jax.ShapeDtypeStruct((slots, width), BF16),
         compiler_params=params(),
         name="project_far",
-    )(place, pick, lo, hi, mine, other, near_mine, near_other)
+    )(place, pick, lo, hi, weight_lo, weight_hi, near)
 
 
 def merge_body(column_ref, row_ref, rows_ref, out_ref):
@@ -277,18 +266,13 @@
 
 
 def weight_route(n_seq, n_head):
-    rows = n_seq // n_head // CORES
-    pairs = []
-    for z in range(n_head):
-        for y in range(rows):
-            for core in range(CORES):
-                for x in range(n_head):
-                    spot = y * CORES + core
-                    to_core, to_y = spot // rows, spot % rows
-                    source = ((z * rows + y) * CORES + core) * n_head + x
-                    target = ((x * rows + to_y) * CORES + to_core) * n_head + z
-                    pairs.append((source, target))
-    return pairs
+    plane = n_seq // n_head
+    return [
+        ((a * plane + p) * n_head + b, (b * plane + p) * n_head + a)
+        for a in range(n_head)
+        for p in range(plane)
+        for b in range(n_head)
+    ]
 
 
 def per_device(
@@ -310,8 +294,13 @@
     seq_rank = lax.axis_index("seq")
     head_rank = lax.axis_index("head")
 
-    swapped = lax.ppermute(value_weight, ("seq", "head"), weight_route(n_seq, n_head))
     state = local_states(decay_rate, doc_lengths, queries, output_grad, head_local // 2)
+    route = weight_route(n_seq, n_head)
+    middle = value_weight.shape[1] // 2
+    swap_lo = lax.ppermute(value_weight[:, :middle], ("seq", "head"), route)
+    state, swap_lo = lax.optimization_barrier((state, swap_lo))
+    weight_lo = lax.all_gather(swap_lo, "seq", axis=0, tiled=True)
+    weight_lo = weight_lo.reshape(n_head, -1, middle)
 
     blocks = tok_rows // ROWS_BLK
     per = blocks * CAPACITY
@@ -331,6 +320,8 @@
     state_in = lax.all_to_all(
         state.reshape(n_seq, share, head_dim), "seq", split_axis=0, concat_axis=0, tiled=True
     )
+    tail, _ = lax.optimization_barrier((value_weight[:, middle:], state_in))
+    swap_hi = lax.ppermute(tail, ("seq", "head"), route)
     intra = within(
         decay_rate, doc_lengths, queries, key_vectors, output_grad, head_local // 2
     )
@@ -353,11 +344,6 @@
         preferred_element_type=F32,
     ).astype(BF16)
     carried_all = jnp.concatenate([carried_all, note], axis=1)
-    swapped, _ = lax.optimization_barrier((swapped, carried_all))
-    groups = [list(range(core, n_seq, CORES)) for core in range(CORES)]
-    mine = lax.all_gather(swapped, "seq", axis=0, tiled=True, axis_index_groups=groups)
-    mine = mine.reshape(n_head, -1, value_weight.shape[1])
-
     carried = lax.all_to_all(
         carried_all,
         "seq",
@@ -365,6 +351,9 @@
         concat_axis=0,
         tiled=True,
     )
+    swap_hi, carried, intra = lax.optimization_barrier((swap_hi, carried, intra))
+    weight_hi = lax.all_gather(swap_hi, "seq", axis=0, tiled=True)
+    weight_hi = weight_hi.reshape(n_head, -1, middle)
     offsets = (
         carried[:, share, :per].astype(jnp.int32) * 32
         + carried[:, share, per : 2 * per].astype(jnp.int32)
@@ -384,15 +373,11 @@
     right_lo = lax.ppermute(own[0], "head", down)
     far_lo = lax.ppermute(left_lo, "head", up)
     far_hi = lax.ppermute(right_hi, "head", down)
-    mine, *_ = lax.optimization_barrier((mine, left_lo, right_hi, left_hi, right_lo))
-    other = lax.ppermute(mine, "seq", [(i, i ^ 1) for i in range(n_seq)])
-    ring = (head_rank + jnp.array([0, n_head - 1, 1, 2], jnp.int32)) % n_head
-    place = jnp.concatenate([ring, (seq_rank % CORES)[None]])
-
-    pieces = (own[0], own[1], left_lo, left_hi, right_lo, right_hi)
-    near_mine = project_near(place, pieces, mine, 256)
-    near_other = project_near(place, pieces, other, 256)
-    send = project_far(place, pick, far_lo, far_hi, mine, other, near_mine, near_other, 256)
+    place = (head_rank + jnp.array([0, n_head - 1, 1, 2], jnp.int32)) % n_head
+
+    near = project_near(place, (own[0], left_lo, right_lo), weight_lo, (), 256)
+    near = project_near(place, (own[1], left_hi, right_hi), weight_hi, (near,), 256)
+    send = project_far(place, pick, far_lo, far_hi, weight_lo, weight_hi, near, 256)
     send = send.reshape(devices_all, per, -1)
     got = lax.all_to_all(send, ("seq", "head"), split_axis=0, concat_axis=0, tiled=True)
     return merge(offsets, got.reshape(n_seq, n_head, per, -1), 768)

time: 205 us -> 214 us (1.044)
  waiting for transfers between devices: 97.8 us -> 88.8 us
  starting transfers between devices: 37.6 us -> 46.5 us
  local copies, waits for them, and re-layouts: 12.9 us -> 20 us
  Pallas kernels: 35.1 us -> 38.2 us
    ppermute x2, waiting for transfers between devices: 18.1 us -> 0.01 us  [the longest x1 0.01 us: per_device(): swap_lo = lax.ppermute(value_weight[:, :middle], ('seq', 'head'), route)]
    all_gather x1 -> x2, waiting for transfers between devices: 13.2 us -> 26.3 us  [the longest x1 26.3 us: per_device(): weight_hi = lax.all_gather(swap_hi, 'seq', axis=0, tiled=True)]
    ppermute x1, waiting for transfers between devices: 11.2 us -> 0.01 us  [per_device(): left_hi = lax.ppermute(own[1], 'head', up)]
    all_to_all x1, starting transfers between devices: 9.61 us -> 18.8 us  [per_device(): lax.all_to_all(state.reshape(n_seq, share, head_dim), 'seq', split_axis=0...]
    all_to_all x1, waiting for transfers between devices: 0.01 us -> 8.36 us  [per_device(): lax.all_to_all(state.reshape(n_seq, share, head_dim), 'seq', split_axis=0...]
    ppermute x1, waiting for transfers between devices: 0.01 us -> 6.3 us  [per_device(): right_hi = lax.ppermute(own[1], 'head', down)]
    all_to_all x1, starting transfers between devices: 9.86 us -> 3.9 us  [per_device(): lax.all_to_all(carried_all, 'seq', split_axis=0, concat_axis=0, tiled=True)]
    unnamed x30 -> x36, local copies, waits for them, and re-layouts: 9.93 us -> 15.9 us
  transfers between devices with their start and end apart: 12 -> 13, of which waited for: 7 -> 7; matrix products, arithmetic and copies ran while one was open for 4% -> 4% of each run, Pallas kernels for 8% -> 11%
where the time goes in v3:
time: 214 us; the launch traced here: 213 us
  waiting for transfers between devices  88.8 us (41%)
  starting transfers between devices  46.5 us (22%)
  Pallas kernels  38.2 us (18%)
  local copies, waits for them, and re-layouts  20 us (9%)
  between operations  14.3 us (7%)
  other arithmetic  4.82 us (2%)
    all_to_all x1, waiting for transfers between devices, per_device(): lax.all_to_all(send, ('seq', 'head'), split_axis=0, concat_axis=0, tiled=...  40.5 us
    all_gather x1, waiting for transfers between devices, per_device(): weight_hi = lax.all_gather(swap_hi, 'seq', axis=0, tiled=True)  26.3 us
    all_to_all x1, starting transfers between devices, per_device(): lax.all_to_all(state.reshape(n_seq, share, head_dim), 'seq', split_axis=0...  18.8 us
    unnamed x36, local copies, waits for them, and re-layouts  15.9 us
    pallas_call x2, Pallas kernels, project_near(): pl.pallas_call(functools.partial(near_body, count), grid_spec=pltpu.Prefe...  14.3 us
    pallas_call x1, Pallas kernels, project_far(): pl.pallas_call(far_body, grid_spec=pltpu.PrefetchScalarGridSpec(num_scala...  9.86 us
    all_to_all x1, waiting for transfers between devices, per_device(): lax.all_to_all(state.reshape(n_seq, share, head_dim), 'seq', split_axis=0...  8.36 us
    ppermute x1, starting transfers between devices, per_device(): right_hi = lax.ppermute(own[1], 'head', down)  7.23 us
  transfers between devices with their start and end apart: 13, of which 7 were waited for; matrix products, arithmetic and copies ran while one was open for 4% of the time, Pallas kernels for 11%

profile of v3, /device:TPU:1, one launch (start us, length us, event | category | flops | bytes accessed | tf_op | source)
XLA Modules:
  0.0 213.1 jit_solution(11933664491844471338)
XLA Ops:
  6.5 1.8 fusion.33
  8.4 0.7 collective-permute-start
  9.0 0.0 copy-start.4
  9.0 1.2 copy-done.4
  10.3 1.2 copy-done.6
  11.5 0.7 copy-done.12
  12.1 0.7 copy-done.14
  12.8 2.4 %local_states.1 = bf16[8,128,128]{2,1,0:T(8,128)(2,1)} custom-call(f32[8]{0:T(128)S(1)} %copy-done.12, s32[4]{0:T(128)S(1)} %copy-done.14, bf16[512,1024]{1,0:T(8,128)(2,1)S(1)} %copy-done.4, bf16[512,1024]{1,0:T(8,128)(2,1)S(1)} %copy-done.6), custom_call_target="tpu_custom_call" | custom-call | tf_op jit(solution)/shard_map/local_states/pallas_call | solution.py:61
  15.2 0.0 collective-permute-done
  15.2 0.7 copy-done.16
  15.9 0.0 all-gather.3.cloned.1.call-update
  15.9 1.0 convert_reduce_fusion
  16.9 0.7 broadcast_multiply_fusion
  17.6 0.7 broadcast_add_fusion
  18.3 0.1 iota_add_fusion
  18.4 0.7 select_reduce_fusion
  19.1 18.8 %all-to-all-start = ((bf16[32,32,128]{2,1,0:T(8,128)(2,1)}), bf16[32,32,128]{2,1,0:T(8,128)(2,1)S(1)}, u32[]{:S(2)}, u32[]{:S(2)}) async-start(bf16[32,32,128]{2,1,0:T(8,128)(2,1)} %bitcast), calls=%async_computation | async-start | bytes 524288 | tf_op jit(solution)/shard_map/all_to_all | solution.py:320
  38.0 0.7 dynamic_slice.3
  39.3 0.2 reduce-window.8
  39.5 0.1 maximum_bitcast_fusion
  39.6 0.1 convert_reduce_fusion.2
  39.7 8.4 %all-to-all-done = bf16[32,32,128]{2,1,0:T(8,128)(2,1)S(1)} async-done(((bf16[32,32,128]{2,1,0:T(8,128)(2,1)}), bf16[32,32,128]{2,1,0:T(8,128)(2,1)S(1)}, u32[]{:S(2)}, u32[]{:S(2)}) %all-to-all-start) | async-done | bytes 262176 | tf_op jit(solution)/shard_map/all_to_all | solution.py:320
  48.0 0.4 convolution_convert_fusion
  48.5 0.9 copy.19
  49.3 3.9 %all-to-all-start.1 = ((bf16[32,40,128]{2,1,0:T(8,128)(2,1)}), bf16[32,40,128]{2,1,0:T(8,128)(2,1)S(1)}, u32[]{:S(2)}, u32[]{:S(2)}) async-start(bf16[32,40,128]{2,1,0:T(8,128)(2,1)} %copy.19), calls=%async_computation.1 | async-start | bytes 655360 | tf_op jit(solution)/shard_map/all_to_all | solution.py:347
  53.3 0.0 all-gather.5.cloned.1.call-start
  53.3 3.0 %collective-permute-start.1 = (bf16[192,512]{1,0:T(8,128)(2,1)}, bf16[192,512]{1,0:T(8,128)(2,1)}, u32[]{:S(2)}, u32[]{:S(2)}) collective-permute-start(bf16[192,512]{1,0:T(8,128)(2,1)} %get-tuple-element.12), channel_id=1, source_target_pairs={{0,0},{1,32},{2,64},{3,96},{4,4},{5,36},{6,68},{7,100},{8,8},{9,40... | collective-permute-start | bytes 589832 | tf_op jit(solution)/shard_map/ppermute | solution.py:324
  56.3 1.2 copy-done.5
  57.5 1.5 copy-done.7
  59.1 3.7 %within.1.intra_ref = f32[512,1024]{1,0:T(8,128)S(1)} custom-call(f32[8]{0:T(128)S(1)} %copy-done.13, s32[4]{0:T(128)S(1)} %copy-done.15, bf16[512,1024]{1,0:T(8,128)(2,1)S(1)} %copy-done.5, bf16[512,1024]{1,0:T(8,128)(2,1)S(1)} %copy-done.3, bf16[512,1024]{1,0:T(8,128)(2,1)S(1)} %copy-done.7), custom_call_target="tpu_custom_call" | custom-call | tf_op jit(solution)/shard_map/within/pallas_call | solution.py:103
  62.8 0.1 all-to-all-done.1
  62.9 0.0 all-gather.5.cloned.1.call-update
  63.0 0.0 copy-start.17
  63.0 2.0 across.3.refs_0_
  64.9 7.2 %collective-permute-start.4 = (bf16[512,512]{1,0:T(8,128)(2,1)}, bf16[512,512]{1,0:T(8,128)(2,1)}, u32[]{:S(2)}, u32[]{:S(2)}) collective-permute-start(bf16[512,512]{1,0:T(8,128)(2,1)} %across.3.refs_0_), channel_id=1, source_target_pairs={{0,3},{1,0},{2,1},{3,2},{4,7},{5,4},{6,5},{7,6},{8,11},{9,8},{10,9... | collective-permute-start | bytes 1572872 | tf_op jit(solution)/shard_map/ppermute | solution.py:371
  72.2 1.1 across.2.refs_0_
  73.3 0.1 collective-permute-start.2
  73.4 2.7 %collective-permute-start.7 = (bf16[512,512]{1,0:T(8,128)(2,1)S(1)}, bf16[512,512]{1,0:T(8,128)(2,1)S(1)}, u32[]{:S(2)}, u32[]{:S(2)}) collective-permute-start(bf16[512,512]{1,0:T(8,128)(2,1)S(1)} %across.2.refs_0_), channel_id=1, source_target_pairs={{0,3},{1,0},{2,1},{3,2},{4,7},{5,4},{6,5},{7,6},{8,11},{9,8},{10,9... | collective-permute-start | bytes 1572872 | tf_op jit(solution)/shard_map/ppermute | solution.py:373
  76.0 0.8 copy-done.8
  76.8 6.3 %collective-permute-done.4.refs_2_ = bf16[512,512]{1,0:T(8,128)(2,1)} collective-permute-done((bf16[512,512]{1,0:T(8,128)(2,1)}, bf16[512,512]{1,0:T(8,128)(2,1)}, u32[]{:S(2)}, u32[]{:S(2)}) %collective-permute-start.4) | collective-permute-done | bytes 524320 | tf_op jit(solution)/shard_map/ppermute | solution.py:371
  83.1 3.4 %collective-permute-start.5 = (bf16[512,512]{1,0:T(8,128)(2,1)}, bf16[512,512]{1,0:T(8,128)(2,1)S(1)}, u32[]{:S(2)}, u32[]{:S(2)}) collective-permute-start(bf16[512,512]{1,0:T(8,128)(2,1)} %collective-permute-done.4.refs_2_), channel_id=1, source_target_pairs={{0,3},{1,0},{2,1},{3,2},{4,7},{5,4},{6,5},{7,6},{8,11},{9,8},{10,9... | collective-permute-start | bytes 1572872 | tf_op jit(solution)/shard_map/ppermute | solution.py:375
  86.5 0.5 collective-permute-done.2.refs_1_
  87.1 0.4 fusion.pick
  87.5 6.8 %collective-permute-done.7.refs_2_ = bf16[512,512]{1,0:T(8,128)(2,1)S(1)} collective-permute-done((bf16[512,512]{1,0:T(8,128)(2,1)S(1)}, bf16[512,512]{1,0:T(8,128)(2,1)S(1)}, u32[]{:S(2)}, u32[]{:S(2)}) %collective-permute-start.7) | collective-permute-done | bytes 524320 | tf_op jit(solution)/shard_map/ppermute | solution.py:373
  94.2 0.8 copy-done.10
  95.1 1.0 copy-done.9
  96.1 1.0 copy-done.11
  97.1 6.6 %project_near.2.refs_6_ = f32[512,1536]{1,0:T(8,128)S(1)} custom-call(s32[4]{0:T(128)S(1)} %and_select_fusion.place, bf16[512,512]{1,0:T(8,128)(2,1)S(1)} %copy-done.9, bf16[512,512]{1,0:T(8,128)(2,1)S(1)} %collective-permute-done.2.refs_1_, bf16[512,512]{1,0:T(8,128)(2,1)S(1)} %copy-done.11, bf16[4,1536,512]{2,1,0:T(8,128)(2,1)} %bitcast.30, ...), custom_call_target="tpu_custom_call" | custom-call | tf_op jit(solution)/shard_map/project_near/pallas_call | solution.py:174
  103.8 0.0 copy-start
  103.8 1.7 copy-done
  105.4 26.3 %all-gather.5.cloned.1.call-done = bf16[6144,512]{1,0:T(8,128)(2,1)} async-done(((bf16[192,512]{1,0:T(8,128)(2,1)}), bf16[6144,512]{1,0:T(8,128)(2,1)}) %all-gather.5.cloned.1.call-update) | async-done | bytes 6291472 | tf_op jit(solution)/shard_map/all_gather | solution.py:355
  131.7 7.7 %project_near.3.near = f32[512,1536]{1,0:T(8,128)S(1)} custom-call(s32[4]{0:T(128)S(1)} %and_select_fusion.place, bf16[512,512]{1,0:T(8,128)(2,1)} %across.3.refs_0_, bf16[512,512]{1,0:T(8,128)(2,1)S(1)} %collective-permute-done.6.refs_1_, bf16[512,512]{1,0:T(8,128)(2,1)} %collective-permute-done.4.refs_2_, bf16[4,1536,512]{2,1,0:T(8,128)(2,1)} %bitcast.34, ...), custom_call_target="tpu_custom_call" | custom-call | tf_op jit(solution)/shard_map/project_near/pallas_call | solution.py:174
  139.4 0.0 copy-start.2
  139.4 1.7 copy-done.2
  141.1 9.9 %project_far.1 = bf16[1024,1536]{1,0:T(8,128)(2,1)S(1)} custom-call(s32[4]{0:T(128)S(1)} %and_select_fusion.place, bf16[1024,512]{1,0:T(8,128)(2,1)S(1)} %fusion.pick, bf16[512,512]{1,0:T(8,128)(2,1)S(1)} %collective-permute-done.3.lo, bf16[512,512]{1,0:T(8,128)(2,1)S(1)} %collective-permute-done.5.hi, bf16[4,1536,512]{2,1,0:T(8,128)(2,1)} %bitcast.33, ...), custom_call_target="tpu_custom_call" | custom-call | tf_op jit(solution)/shard_map/project_far/pallas_call | solution.py:206
  150.9 0.0 copy-start.1
  150.9 1.7 copy-done.1
  152.6 6.7 %all-to-all-start.2 = ((bf16[128,8,1536]{2,1,0:T(8,128)(2,1)}), bf16[128,8,1536]{2,1,0:T(8,128)(2,1)S(1)}, u32[]{:S(2)}, u32[]{:S(2)}) async-start(bf16[128,8,1536]{2,1,0:T(8,128)(2,1)} %bitcast.26), calls=%async_computation.2 | async-start | bytes 6291456 | tf_op jit(solution)/shard_map/all_to_all | solution.py:382
  159.3 0.6 broadcast.196
  159.9 0.8 fusion.32
  160.7 0.1 sub.60.column_ref
  160.8 0.1 sub.59.row_ref
  160.9 40.5 %all-to-all-done.2 = bf16[128,8,1536]{2,1,0:T(8,128)(2,1)S(1)} async-done(((bf16[128,8,1536]{2,1,0:T(8,128)(2,1)}), bf16[128,8,1536]{2,1,0:T(8,128)(2,1)S(1)}, u32[]{:S(2)}, u32[]{:S(2)}) %all-to-all-start.2) | async-done | bytes 3145760 | tf_op jit(solution)/shard_map/all_to_all | solution.py:382
  201.4 4.9 %merge.1 = bf16[1,128,2,6144]{3,2,1,0:T(2,128)(2,1)} custom-call(s32[256,1]{1,0:T(8,128)S(1)} %sub.60.column_ref, s32[1,256]{1,0:T(1,128)S(1)} %sub.59.row_ref, bf16[32,4,8,1536]{3,2,1,0:T(8,128)(2,1)S(1)} %bitcast.25), custom_call_target="tpu_custom_call" | custom-call | tf_op jit(solution)/shard_map/merge/pallas_call | solution.py:241
  (33 shorter events, 0.2 us)
Async XLA Ops:
  6.5 49.8 %copy-start.3 = (bf16[512,1024]{1,0:T(8,128)(2,1)S(1)}, bf16[512,1024]{1,0:T(8,128)(2,1)}, u32[]{:S(2)}) copy-start(bf16[512,1024]{1,0:T(8,128)(2,1)} %key_ref.5) | copy-start | bytes 3145732
  6.5 88.5 %all-gather.3.cloned.1.call-start = ((), (), s32[]{:S(2)}) async-start(), calls=%async_computation.3 | async-start | bytes 6488064 | tf_op jit(solution)/shard_map/all_gather | solution.py:302
  8.4 6.8 %collective-permute-start = (bf16[192,512]{1,0:T(8,128)(2,1)S(1)}, bf16[192,512]{1,0:T(8,128)(2,1)S(1)}, u32[]{:S(2)}, u32[]{:S(2)}) collective-permute-start(bf16[192,512]{1,0:T(8,128)(2,1)S(1)} %get-tuple-element.21), channel_id=1, source_target_pairs={{0,0},{1,32},{2,64},{3,96},{4,4},{5,36},{6,68},{7,100},{8,8},{9,40... | collective-permute-start | bytes 589832 | tf_op jit(solution)/shard_map/ppermute | solution.py:300
  9.0 1.2 copy-start.4
  10.3 1.2 copy-start.6
  11.5 0.7 copy-start.12
  12.1 0.7 copy-start.14
  12.8 25.2 %copy-start.13 = (f32[8]{0:T(128)S(1)}, f32[8]{0:T(128)}, u32[]{:S(2)}) copy-start(f32[8]{0:T(128)} %rate_ref.7) | copy-start | bytes 100
  12.8 26.5 %copy-start.15 = (s32[4]{0:T(128)S(1)}, s32[4]{0:T(128)}, u32[]{:S(2)}) copy-start(s32[4]{0:T(128)} %lengths_ref.7) | copy-start | bytes 52
  15.2 0.7 copy-start.16
  19.1 28.9 %all-to-all-start = ((bf16[32,32,128]{2,1,0:T(8,128)(2,1)}), bf16[32,32,128]{2,1,0:T(8,128)(2,1)S(1)}, u32[]{:S(2)}, u32[]{:S(2)}) async-start(bf16[32,32,128]{2,1,0:T(8,128)(2,1)} %bitcast), calls=%async_computation | async-start | bytes 524288 | tf_op jit(solution)/shard_map/all_to_all | solution.py:320
  49.3 13.6 %all-to-all-start.1 = ((bf16[32,40,128]{2,1,0:T(8,128)(2,1)}), bf16[32,40,128]{2,1,0:T(8,128)(2,1)S(1)}, u32[]{:S(2)}, u32[]{:S(2)}) async-start(bf16[32,40,128]{2,1,0:T(8,128)(2,1)} %copy.19), calls=%async_computation.1 | async-start | bytes 655360 | tf_op jit(solution)/shard_map/all_to_all | solution.py:347
  53.3 78.5 %all-gather.5.cloned.1.call-start = ((), (), s32[]{:S(2)}) async-start(), calls=%async_computation.4 | async-start | bytes 6488064 | tf_op jit(solution)/shard_map/all_gather | solution.py:355
  53.3 9.5 %collective-permute-start.1 = (bf16[192,512]{1,0:T(8,128)(2,1)}, bf16[192,512]{1,0:T(8,128)(2,1)}, u32[]{:S(2)}, u32[]{:S(2)}) collective-permute-start(bf16[192,512]{1,0:T(8,128)(2,1)} %get-tuple-element.12), channel_id=1, source_target_pairs={{0,0},{1,32},{2,64},{3,96},{4,4},{5,36},{6,68},{7,100},{8,8},{9,40... | collective-permute-start | bytes 589832 | tf_op jit(solution)/shard_map/ppermute | solution.py:324
  56.3 1.2 copy-start.5
  57.5 1.5 copy-start.7
  63.0 24.1 %copy-start.17 = (s32[4]{0:T(128)S(1)}, s32[4]{0:T(128)}, u32[]{:S(2)}) copy-start(s32[4]{0:T(128)} %constant.92.clone) | copy-start | bytes 52
  64.9 18.2 %collective-permute-start.4 = (bf16[512,512]{1,0:T(8,128)(2,1)}, bf16[512,512]{1,0:T(8,128)(2,1)}, u32[]{:S(2)}, u32[]{:S(2)}) collective-permute-start(bf16[512,512]{1,0:T(8,128)(2,1)} %across.3.refs_0_), channel_id=1, source_target_pairs={{0,3},{1,0},{2,1},{3,2},{4,7},{5,4},{6,5},{7,6},{8,11},{9,8},{10,9... | collective-permute-start | bytes 1572872 | tf_op jit(solution)/shard_map/ppermute | solution.py:371
  73.3 13.8 %collective-permute-start.2 = (bf16[512,512]{1,0:T(8,128)(2,1)S(1)}, bf16[512,512]{1,0:T(8,128)(2,1)S(1)}, u32[]{:S(2)}, u32[]{:S(2)}) collective-permute-start(bf16[512,512]{1,0:T(8,128)(2,1)S(1)} %across.2.refs_0_), channel_id=1, source_target_pairs={{0,1},{1,2},{2,3},{3,0},{4,5},{5,6},{6,7},{7,4},{8,9},{9,10},{10,1... | collective-permute-start | bytes 1572872 | tf_op jit(solution)/shard_map/ppermute | solution.py:370
  73.4 20.9 %collective-permute-start.7 = (bf16[512,512]{1,0:T(8,128)(2,1)S(1)}, bf16[512,512]{1,0:T(8,128)(2,1)S(1)}, u32[]{:S(2)}, u32[]{:S(2)}) collective-permute-start(bf16[512,512]{1,0:T(8,128)(2,1)S(1)} %across.2.refs_0_), channel_id=1, source_target_pairs={{0,3},{1,0},{2,1},{3,2},{4,7},{5,4},{6,5},{7,6},{8,11},{9,8},{10,9... | collective-permute-start | bytes 1572872 | tf_op jit(solution)/shard_map/ppermute | solution.py:373
  76.0 0.8 copy-start.8
  76.8 28.6 %collective-permute-start.6 = (bf16[512,512]{1,0:T(8,128)(2,1)}, bf16[512,512]{1,0:T(8,128)(2,1)S(1)}, u32[]{:S(2)}, u32[]{:S(2)}) collective-permute-start(bf16[512,512]{1,0:T(8,128)(2,1)} %across.3.refs_0_), channel_id=1, source_target_pairs={{0,1},{1,2},{2,3},{3,0},{4,5},{5,6},{6,7},{7,4},{8,9},{9,10},{10,1... | collective-permute-start | bytes 1572872 | tf_op jit(solution)/shard_map/ppermute | solution.py:372
  83.1 57.9 %collective-permute-start.5 = (bf16[512,512]{1,0:T(8,128)(2,1)}, bf16[512,512]{1,0:T(8,128)(2,1)S(1)}, u32[]{:S(2)}, u32[]{:S(2)}) collective-permute-start(bf16[512,512]{1,0:T(8,128)(2,1)} %collective-permute-done.4.refs_2_), channel_id=1, source_target_pairs={{0,3},{1,0},{2,1},{3,2},{4,7},{5,4},{6,5},{7,6},{8,11},{9,8},{10,9... | collective-permute-start | bytes 1572872 | tf_op jit(solution)/shard_map/ppermute | solution.py:375
  87.0 54.0 %collective-permute-start.3 = (bf16[512,512]{1,0:T(8,128)(2,1)S(1)}, bf16[512,512]{1,0:T(8,128)(2,1)S(1)}, u32[]{:S(2)}, u32[]{:S(2)}) collective-permute-start(bf16[512,512]{1,0:T(8,128)(2,1)S(1)} %collective-permute-done.2.refs_1_), channel_id=1, source_target_pairs={{0,1},{1,2},{2,3},{3,0},{4,5},{5,6},{6,7},{7,4},{8,9},{9,10},{10,1... | collective-permute-start | bytes 1572872 | tf_op jit(solution)/shard_map/ppermute | solution.py:374
  94.2 0.8 copy-start.10
  95.0 1.0 copy-start.9
  96.1 1.0 copy-start.11
  103.8 1.7 copy-start
  139.4 1.7 copy-start.2
  150.9 1.7 copy-start.1
  152.6 48.8 %all-to-all-start.2 = ((bf16[128,8,1536]{2,1,0:T(8,128)(2,1)}), bf16[128,8,1536]{2,1,0:T(8,128)(2,1)S(1)}, u32[]{:S(2)}, u32[]{:S(2)}) async-start(bf16[128,8,1536]{2,1,0:T(8,128)(2,1)} %bitcast.26), calls=%async_computation.2 | async-start | bytes 6291456 | tf_op jit(solution)/shard_map/all_to_all | solution.py:382
Sparse Core Ops, SparseCore 0:
  16.0 67.0 all-gather.2
  85.3 46.3 all-gather.4

commit v4 on v3

v4 whole, which is shorter than its diff:
```python
import functools

import jax
import jax.numpy as jnp
from jax import lax
from jax.experimental import pallas as pl
from jax.experimental.pallas import tpu as pltpu
from jax.sharding import Mesh, PartitionSpec as P

BF16 = jnp.bfloat16
F32 = jnp.float32
CAPACITY = 2
ROWS_BLK = 128
BIG = 1 << 30
SEQ = ("z", "y", "core")
ALL = ("z", "y", "core", "head")
TURNS = (0, 3, 1, 2)


def doc_of(positions, doc_ends):
    return jnp.sum((positions[:, None] >= doc_ends[None, :]).astype(jnp.int32), axis=1)


def doc_limit(positions, lengths_ref):
    end = lengths_ref[0]
    limit = jnp.where(positions < end, end, BIG)
    for doc in range(1, lengths_ref.shape[0]):
        end = end + lengths_ref[doc]
        limit = jnp.minimum(limit, jnp.where(positions < end, end, BIG))
    return limit


def params(mib=48):
    return pltpu.CompilerParams(
        dimension_semantics=("arbitrary",), vmem_limit_bytes=mib << 20
    )


SCALARS = pl.BlockSpec(memory_space=pltpu.SMEM)


def local_state_body(rate_ref, lengths_ref, query_ref, grad_ref, out_ref):
    count, dim = out_ref.shape[:2]
    toks = query_ref.shape[0]
    first = lax.axis_index(SEQ) * toks
    limit = doc_limit(jnp.maximum(first - 1, 0), lengths_ref)
    step = lax.broadcasted_iota(jnp.int32, (toks, dim), 0)
    inside = first + step < limit
    span = (step + 1).astype(F32)
    for h in range(count):
        rate = rate_ref[pl.program_id(0) * count + h]
        cols = slice(h * dim, (h + 1) * dim)
        lead = jnp.where(inside, jnp.exp(-rate * span), 0.0)
        scaled = (query_ref[:, cols].astype(F32) * lead).astype(BF16)
        out_ref[h] = lax.dot_general(
            scaled, grad_ref[:, cols], (((0,), (0,)), ((), ())), preferred_element_type=F32
        ).astype(out_ref.dtype)


def local_states(rates, lengths, queries, grads, count):
    heads = rates.shape[0]
    toks, dim = queries.shape[0], queries.shape[1] // heads
    blk = pl.BlockSpec((toks, count * dim), lambda h: (0, h))
    return pl.pallas_call(
        local_state_body,
        grid=(heads // count,),
        in_specs=[SCALARS, SCALARS, blk, blk],
        out_specs=pl.BlockSpec((count, dim, dim), lambda h: (h, 0, 0)),
        out_shape=jax.ShapeDtypeStruct((heads, dim, dim), BF16),
        compiler_params=params(),
        name="local_states",
    )(rates, lengths, queries, grads)


def within_body(count, rate_ref, lengths_ref, query_ref, key_ref, grad_ref, out_ref):
    toks = query_ref.shape[0]
    dim = query_ref.shape[1] // count
    first = lax.axis_index(SEQ) * toks
    half = toks // 2
    for lo in (0, half):
        src = lax.broadcasted_iota(jnp.int32, (half, 1), 0) + lo
        dst = lax.broadcasted_iota(jnp.int32, (1, toks - lo), 1) + lo
        limit = doc_limit(src + first, lengths_ref) - first
        seen = (dst >= src) & (dst < limit)
        for h in range(count):
            rate = rate_ref[pl.program_id(0) * count + h]
            cols = slice(h * dim, (h + 1) * dim)
            rise = jnp.exp(rate * src.astype(F32)) * (1.0 / dim)
            fall = jnp.exp(-rate * dst.astype(F32))
            scores = lax.dot_general(
                key_ref[lo : lo + half, cols],
                query_ref[lo:, cols],
                (((1,), (1,)), ((), ())),
                preferred_element_type=F32,
            )
            weights = jnp.where(seen, scores * rise * fall, 0.0).astype(BF16)
            out_ref[lo : lo + half, cols] = jnp.dot(
                weights, grad_ref[lo:, cols], preferred_element_type=F32
            )


def within(rates, lengths, queries, keys, grads, count):
    heads = rates.shape[0]
    toks, dim = queries.shape[0], queries.shape[1] // heads
    blk = pl.BlockSpec((toks, count * dim), lambda h: (0, h))
    return pl.pallas_call(
        functools.partial(within_body, count),
        grid=(heads // count,),
        in_specs=[SCALARS, SCALARS, blk, blk, blk],
        out_specs=blk,
        out_shape=jax.ShapeDtypeStruct((toks, heads * dim), F32),
        compiler_params=params(),
        name="within",
    )(rates, lengths, queries, keys, grads)


def across_body(rate_ref, lengths_ref, key_ref, state_ref, intra_ref, *outs):
    heads, dim = state_ref.shape[:2]
    toks = key_ref.shape[0]
    rows = toks // len(outs)
    first = lax.axis_index(SEQ) * toks
    last = first + toks - 1
    here = lax.axis_index("head")
    for turn, out_ref in enumerate(outs):
        start = pl.multiple_of(lax.rem(here + TURNS[turn], len(outs)) * rows, rows)
        src = lax.broadcasted_iota(jnp.int32, (rows, dim), 0) + start
        inside = last < doc_limit(src + first, lengths_ref)
        span = (toks - 1 - src).astype(F32)
        for h in range(heads):
            cols = slice(h * dim, (h + 1) * dim)
            tail = jnp.where(inside, jnp.exp(-rate_ref[h] * span) * (1.0 / dim), 0.0)
            product = jnp.dot(
                key_ref[pl.ds(start, rows), cols], state_ref[h], preferred_element_type=F32
            )
            out_ref[:, cols] = (intra_ref[pl.ds(start, rows), cols] + product * tail).astype(
                BF16
            )


def across(rates, lengths, keys, states, intra):
    heads, dim = states.shape[:2]
    toks, width = keys.shape
    rows = toks // len(TURNS)
    return pl.pallas_call(
        across_body,
        grid=(1,),
        in_specs=[
            SCALARS,
            SCALARS,
            pl.BlockSpec((toks, width), lambda i: (0, 0)),
            pl.BlockSpec((heads, dim, dim), lambda i: (0, 0, 0)),
            pl.BlockSpec((toks, width), lambda i: (0, 0)),
        ],
        out_specs=[pl.BlockSpec((rows, width), lambda i: (0, 0))] * len(TURNS),
        out_shape=[jax.ShapeDtypeStruct((rows, width), BF16)] * len(TURNS),
        compiler_params=params(),
        name="across",
    )(rates, lengths, keys, states, intra)


def times(rows, weight):
    rows = jnp.concatenate([part[...] for part in rows], axis=0)
    return lax.dot_general(
        rows, weight[0], (((1,), (1,)), ((), ())), preferred_element_type=F32
    )


def near_body(count, place, *refs):
    out_ref = refs[-1]
    each = len(TURNS)
    total = None
    for k in range(count):
        part = times(refs[k * each : (k + 1) * each], refs[count * each + k])
        total = part if total is None else total + part
    for held in refs[count * (each + 1) : -1]:
        total = total + held[...]
    out_ref[...] = total


def project_near(place, pieces, turns, weight, held, tile):
    count = len(pieces)
    rows, depth = pieces[0][0].shape
    toks = rows * len(TURNS)
    width = weight.shape[1]
    whole = pl.BlockSpec((rows, depth), lambda i, p: (0, 0))
    part = pl.BlockSpec((toks, tile), lambda i, p: (0, i))
    return pl.pallas_call(
        functools.partial(near_body, count),
        grid_spec=pltpu.PrefetchScalarGridSpec(
            num_scalar_prefetch=1,
            grid=(width // tile,),
            in_specs=[whole] * (count * len(TURNS))
            + [pl.BlockSpec((1, tile, depth), lambda i, p, k=k: (p[k], i, 0)) for k in turns]
            + [part] * len(held),
            out_specs=part,
        ),
        out_shape=jax.ShapeDtypeStruct((toks, width), F32),
        compiler_params=params(),
        name="project_near",
    )(place, *[q for piece in pieces for q in piece], *[weight] * count, *held)


def far_body(place, pick, *refs):
    weight, near, out_ref = refs[-3:]
    total = near[...] + times(refs[:-3], weight)
    out_ref[...] = jnp.dot(
        pick[...], total.astype(BF16), preferred_element_type=F32
    ).astype(BF16)


def project_far(place, pick, piece, turn, weight, near, tile):
    rows, depth = piece[0].shape
    slots, toks = pick.shape
    width = weight.shape[1]
    whole = pl.BlockSpec((rows, depth), lambda i, p: (0, 0))
    return pl.pallas_call(
        far_body,
        grid_spec=pltpu.PrefetchScalarGridSpec(
            num_scalar_prefetch=1,
            grid=(width // tile,),
            in_specs=[pl.BlockSpec((slots, toks), lambda i, p: (0, 0))]
            + [whole] * len(piece)
            + [
                pl.BlockSpec((1, tile, depth), lambda i, p: (p[turn], i, 0)),
                pl.BlockSpec((toks, tile), lambda i, p: (0, i)),
            ],
            out_specs=pl.BlockSpec((slots, tile), lambda i, p: (0, i)),
        ),
        out_shape=jax.ShapeDtypeStruct((slots, width), BF16),
        compiler_params=params(),
        name="project_far",
    )(place, pick, *piece, weight, near)


def merge_body(column_ref, row_ref, rows_ref, out_ref, same_ref):
    slots = column_ref.shape[0]
    count, width = rows_ref.shape[0], rows_ref.shape[-1]

    @pl.when(pl.program_id(0) == 0)
    def _():
        same = (column_ref[...] == row_ref[...]) & (column_ref[...] >= 0)
        same_ref[...] = same.astype(F32).astype(BF16)

    for j in range(count):
        rows = rows_ref[j].reshape(slots, width)
        total = jnp.dot(same_ref[...], rows, preferred_element_type=F32).astype(BF16)
        out_ref[0, :, :, j * width : (j + 1) * width] = total.reshape(out_ref.shape[1:3] + (width,))


def merge(column, row, got, count):
    parts, n_from, per, width = got.shape
    slots = n_from * per
    return pl.pallas_call(
        merge_body,
        grid=(parts // count,),
        in_specs=[
            pl.BlockSpec((slots, 1), lambda i: (0, 0)),
            pl.BlockSpec((1, slots), lambda i: (0, 0)),
            pl.BlockSpec((count, n_from, per, width), lambda i: (i, 0, 0, 0)),
        ],
        out_specs=pl.BlockSpec(
            (1, slots // CAPACITY, CAPACITY, count * width), lambda i: (0, 0, 0, i)
        ),
        out_shape=jax.ShapeDtypeStruct((1, slots // CAPACITY, CAPACITY, parts * width), BF16),
        scratch_shapes=[pltpu.VMEM((slots, slots), BF16)],
        compiler_params=params(),
        name="merge",
    )(column, row, got)


def slots_of(owners, block_ids):
    blocks, width = owners.shape
    same_owner = owners[:, :, None] == owners[:, None, :]
    lower = jnp.arange(width, dtype=jnp.int32)
    earlier = lower[None, :] < lower[:, None]
    rank = jnp.sum((same_owner & earlier[None]).astype(jnp.int32), axis=2)
    return ((owners * blocks + block_ids[:, None]) * CAPACITY + rank).reshape(blocks * width)


def shift(size, step):
    return [(i, (i + step) % size) for i in range(size)]


def per_device(
    queries,
    key_vectors,
    output_grad,
    value_weight,
    decay_rate,
    doc_lengths,
    owner_block,
    row_offset,
):
    n_z = lax.axis_size("z")
    n_seq = lax.axis_size(SEQ)
    n_head = lax.axis_size("head")
    devices_all = n_seq * n_head
    tok_rows = queries.shape[0]
    head_local = decay_rate.shape[0]
    head_dim = queries.shape[1] // head_local
    seq_rank = lax.axis_index(SEQ)
    head_rank = lax.axis_index("head")
    z_rank = lax.axis_index("z")
    plane = n_seq // n_z
    turns = jnp.array(TURNS, jnp.int32)

    weight = lax.all_gather(value_weight, ("head", "y", "core"), axis=0, tiled=True)
    weight = weight.reshape(n_head, -1, value_weight.shape[1])

    state = local_states(decay_rate, doc_lengths, queries, output_grad, head_local // 2)
    blocks = tok_rows // ROWS_BLK
    per = blocks * CAPACITY
    owners = owner_block[:, 0].reshape(blocks, ROWS_BLK)
    slot_index = slots_of(owners, jnp.arange(blocks, dtype=jnp.int32))
    my_slots = (
        (jnp.arange(n_seq, dtype=jnp.int32)[:, None] * n_head + head_rank) * per
        + jnp.arange(per, dtype=jnp.int32)[None, :]
    )
    hit = my_slots[:, :, None] == slot_index[None, None, :]
    named = jnp.sum(jnp.where(hit, row_offset[None, None, :] + 1, 0), axis=2)
    note = jnp.concatenate([(named // 32).astype(BF16), (named % 32).astype(BF16)], axis=1)
    note = jnp.pad(note[:, None, :], ((0, 0), (0, 0), (0, head_dim - 2 * per)))
    names = lax.dynamic_slice_in_dim(owners, head_rank, 1, 0).astype(BF16)
    names = jnp.broadcast_to(names[None], (n_seq, 1, ROWS_BLK))
    note = jnp.pad(jnp.concatenate([note, names], axis=1), ((0, 0), (0, 6), (0, 0)))

    share = head_local * head_dim // n_seq
    state_in = lax.all_to_all(
        state.reshape(n_seq, share, head_dim), SEQ, split_axis=0, concat_axis=0, tiled=True
    )
    intra = within(
        decay_rate, doc_lengths, queries, key_vectors, output_grad, head_local // 2
    )

    doc_ends = jnp.cumsum(doc_lengths)
    ranks = jnp.arange(n_seq, dtype=jnp.int32)
    doc_last = doc_of((ranks + 1) * tok_rows - 1, doc_ends)
    doc_prior = doc_of(jnp.maximum(ranks * tok_rows - 1, 0), doc_ends)
    my_rate = decay_rate[seq_rank // (n_seq // head_local)]
    ahead = ranks[None, :] - ranks[:, None] - 1
    reach = (ahead >= 0) & (doc_last[:, None] == doc_prior[None, :])
    chain = jnp.where(
        reach, jnp.exp(-my_rate * (jnp.maximum(ahead, 0) * tok_rows).astype(F32)), 0.0
    )
    carried_all = jnp.einsum(
        "bc,cxy->bxy",
        chain,
        state_in.astype(F32),
        precision=lax.Precision.HIGHEST,
        preferred_element_type=F32,
    ).astype(BF16)
    carried = lax.all_to_all(
        jnp.concatenate([carried_all, note], axis=1),
        SEQ,
        split_axis=0,
        concat_axis=0,
        tiled=True,
    )
    offsets = (
        carried[:, share, :per].astype(jnp.int32) * 32
        + carried[:, share, per : 2 * per].astype(jnp.int32)
        - 1
    )
    column = offsets.reshape(-1, 1)
    row = offsets.reshape(n_z, plane, blocks, CAPACITY).transpose(1, 2, 0, 3).reshape(1, -1)
    near_z = (z_rank + turns) % n_z
    theirs = carried[:, share + 1].reshape(n_z, plane, ROWS_BLK)
    theirs = lax.dynamic_slice_in_dim(theirs, seq_rank % plane, 1, 1)[:, 0]
    theirs = theirs[near_z].astype(jnp.int32)
    their_slots = slots_of(theirs, near_z)
    all_slots = jnp.arange(devices_all * per, dtype=jnp.int32)
    pick = (all_slots[:, None] == their_slots[None, :]).astype(BF16)
    carried = carried[:, :share].reshape(head_local, head_dim, head_dim)

    own = across(decay_rate, doc_lengths, key_vectors, carried, intra)
    mine = [own[0]]
    for turn in range(1, len(TURNS)):
        mine.append(lax.ppermute(own[turn], "head", shift(n_head, TURNS[turn])))
    place = (head_rank - turns) % n_head

    pieces = []
    for turn, rows in enumerate(mine):
        below = lax.ppermute(rows, "z", shift(n_z, 1))
        above = lax.ppermute(rows, "z", shift(n_z, -1))
        if turn % 2 == 0:
            across_z = lax.ppermute(below, "z", shift(n_z, 1))
        else:
            across_z = lax.ppermute(above, "z", shift(n_z, -1))
        pieces.append((rows, below, above, across_z))

    near = project_near(place, pieces[:2], (0, 1), weight, (), 256)
    near = project_near(place, pieces[2:3], (2,), weight, (near,), 256)
    send = project_far(place, pick, pieces[3], 3, weight, near, 512)
    send = send.reshape(devices_all, per, -1)
    got = lax.all_to_all(send, ALL, split_axis=0, concat_axis=0, tiled=True)
    got = got.reshape(n_z, plane * n_head, per, -1)
    return merge(column, row, got, 2)


def solution(mesh):
    planes = mesh.shape["head"]
    devices = mesh.devices.reshape(planes, -1, 2, planes)
    return jax.shard_map(
        per_device,
        mesh=Mesh(devices, ALL),
        in_specs=(
            P(SEQ, "head"),
            P(SEQ, "head"),
            P(SEQ, "head"),
            P(SEQ, "head"),
            P("head"),
            P(),
            P(SEQ, None),
            P(SEQ),
        ),
        out_specs=P(ALL, None, None, None),
        check_vma=False,
    )
```

time: 214 us -> 189 us (0.88)
  starting transfers between devices: 46.5 us -> 37.3 us
  Pallas kernels: 38.2 us -> 30.8 us
  waiting for transfers between devices: 88.8 us -> 82.2 us
  other arithmetic: 4.82 us -> 2.24 us
    all_gather x2 -> x1, waiting for transfers between devices: 26.3 us -> 0.01 us  [per_device(): lax.all_gather(value_weight, ('head', 'y', 'core'), axis=0, tiled=True)]
    ppermute x8 -> x15, waiting for transfers between devices: 13.6 us -> 29.7 us  [the longest x3 21.6 us: per_device(): mine.append(lax.ppermute(own[turn], 'head', shift(n_head, TURNS[turn])))]
    all_to_all x3, starting transfers between devices: 29.4 us -> 22.5 us  [the longest x1 9.61 us: per_device(): lax.all_to_all(state.reshape(n_seq, share, head_dim), SEQ, split_axis=0,...]
    pallas_call x3 -> x2, Pallas kernels: 7.95 us -> 3.92 us  [the longest x1 2.48 us: merge(): pl.pallas_call(merge_body, grid=(parts // count,), in_specs=[pl.BlockSpec...]
    pallas_call x1, Pallas kernels: 9.86 us -> 6.64 us  [project_far(): pl.pallas_call(far_body, grid_spec=pltpu.PrefetchScalarGridSpec(num_scala...]
    all_to_all x3, waiting for transfers between devices: 48.9 us -> 51.8 us  [the longest x1 40.3 us: per_device(): got = lax.all_to_all(send, ALL, split_axis=0, concat_axis=0, tiled=True)]
    ppermute x8 -> x15, starting transfers between devices: 17.1 us -> 14.8 us  [the longest x3 4.44 us: per_device(): mine.append(lax.ppermute(own[turn], 'head', shift(n_head, TURNS[turn])))]
    unnamed x36 -> x48, local copies, waits for them, and re-layouts: 15.9 us -> 16 us
  transfers between devices with their start and end apart: 13 -> 19, of which waited for: 7 -> 7; matrix products, arithmetic and copies ran while one was open for 4% -> 4% of each run, Pallas kernels for 11% -> 12%
where the time goes in v4:
time: 189 us; the launch traced here: 188 us
  waiting for transfers between devices  82.2 us (43%)
  starting transfers between devices  37.3 us (20%)
  Pallas kernels  30.8 us (16%)
  local copies, waits for them, and re-layouts  20.6 us (11%)
  between operations  14.5 us (8%)
  other arithmetic  2.24 us (1%)
    all_to_all x1, waiting for transfers between devices, per_device(): got = lax.all_to_all(send, ALL, split_axis=0, concat_axis=0, tiled=True)  40.3 us
    ppermute x3, waiting for transfers between devices, per_device(): mine.append(lax.ppermute(own[turn], 'head', shift(n_head, TURNS[turn])))  21.6 us
    unnamed x48, local copies, waits for them, and re-layouts  16 us
    pallas_call x2, Pallas kernels, project_near(): pl.pallas_call(functools.partial(near_body, count), grid_spec=pltpu.Prefe...  14.1 us
    all_to_all x1, starting transfers between devices, per_device(): lax.all_to_all(state.reshape(n_seq, share, head_dim), SEQ, split_axis=0,...  9.61 us
    all_to_all x1, starting transfers between devices, per_device(): got = lax.all_to_all(send, ALL, split_axis=0, concat_axis=0, tiled=True)  9.13 us
    all_to_all x1, waiting for transfers between devices, per_device(): lax.all_to_all(state.reshape(n_seq, share, head_dim), SEQ, split_axis=0,...  8.19 us
    ppermute x2, waiting for transfers between devices, per_device(): across_z = lax.ppermute(above, 'z', shift(n_z, -1))  8.11 us
  transfers between devices with their start and end apart: 19, of which 7 were waited for; matrix products, arithmetic and copies ran while one was open for 4% of the time, Pallas kernels for 12%

profile of v4, /device:TPU:1, one launch (start us, length us, event | category | flops | bytes accessed | tf_op | source)
XLA Modules:
  0.0 188.0 jit_solution(5470244458604683326)
XLA Ops:
  6.6 0.7 all-gather.2.cloned.1.call-update
  7.3 1.2 copy-done.3
  8.5 1.2 copy-done.5
  9.7 0.7 copy-done.13
  10.4 0.7 copy-done.15
  11.0 2.4 %local_states.1 = bf16[8,128,128]{2,1,0:T(8,128)(2,1)} custom-call(f32[8]{0:T(128)S(1)} %copy-done.13, s32[4]{0:T(128)S(1)} %copy-done.15, bf16[512,1024]{1,0:T(8,128)(2,1)S(1)} %copy-done.3, bf16[512,1024]{1,0:T(8,128)(2,1)S(1)} %copy-done.5), custom_call_target="tpu_custom_call" | custom-call | tf_op jit(solution)/shard_map/local_states/pallas_call | solution.py:64
  13.4 9.6 %all-to-all-start = ((bf16[32,32,128]{2,1,0:T(8,128)(2,1)}), bf16[32,32,128]{2,1,0:T(8,128)(2,1)S(1)}, u32[]{:S(2)}, u32[]{:S(2)}) async-start(bf16[32,32,128]{2,1,0:T(8,128)(2,1)} %bitcast.4), calls=%async_computation | async-start | bytes 524288 | tf_op jit(solution)/shard_map/all_to_all | solution.py:328
  23.1 0.2 convert_reduce_fusion.1
  23.5 0.7 select_reduce_fusion
  24.2 0.1 maximum_bitcast_fusion
  24.3 0.7 dynamic_slice.9
  25.7 0.2 reduce-window.8
  25.9 0.1 convert_reduce_fusion.3
  26.0 8.2 %all-to-all-done = bf16[32,32,128]{2,1,0:T(8,128)(2,1)S(1)} async-done(((bf16[32,32,128]{2,1,0:T(8,128)(2,1)}), bf16[32,32,128]{2,1,0:T(8,128)(2,1)S(1)}, u32[]{:S(2)}, u32[]{:S(2)}) %all-to-all-start) | async-done | bytes 262176 | tf_op jit(solution)/shard_map/all_to_all | solution.py:328
  34.1 0.4 convolution_convert_fusion
  34.6 0.9 copy.38
  35.5 3.7 %all-to-all-start.1 = ((bf16[32,40,128]{2,1,0:T(8,128)(2,1)}), bf16[32,40,128]{2,1,0:T(8,128)(2,1)S(1)}, u32[]{:S(2)}, u32[]{:S(2)}) async-start(bf16[32,40,128]{2,1,0:T(8,128)(2,1)} %copy.38), calls=%async_computation.1 | async-start | bytes 655360 | tf_op jit(solution)/shard_map/all_to_all | solution.py:352
  39.2 1.2 copy-done.6
  40.5 1.2 copy-done.7
  41.7 3.7 %within.1.intra_ref = f32[512,1024]{1,0:T(8,128)S(1)} custom-call(f32[8]{0:T(128)S(1)} %copy-done.14, s32[4]{0:T(128)S(1)} %copy-done.16, bf16[512,1024]{1,0:T(8,128)(2,1)S(1)} %copy-done.4, bf16[512,1024]{1,0:T(8,128)(2,1)S(1)} %copy-done.7, bf16[512,1024]{1,0:T(8,128)(2,1)S(1)} %copy-done.6), custom_call_target="tpu_custom_call" | custom-call | tf_op jit(solution)/shard_map/within/pallas_call | solution.py:106
  45.4 3.3 %all-to-all-done.1 = bf16[32,40,128]{2,1,0:T(8,128)(2,1)S(1)} async-done(((bf16[32,40,128]{2,1,0:T(8,128)(2,1)}), bf16[32,40,128]{2,1,0:T(8,128)(2,1)S(1)}, u32[]{:S(2)}, u32[]{:S(2)}) %all-to-all-start.1) | async-done | bytes 327712 | tf_op jit(solution)/shard_map/all_to_all | solution.py:352
  48.8 1.3 copy-done.8
  50.1 1.4 across.1
  51.6 0.5 collective-permute-start.8
  52.0 2.3 %collective-permute-start.9 = (bf16[128,1024]{1,0:T(8,128)(2,1)S(1)}, bf16[128,1024]{1,0:T(8,128)(2,1)S(1)}, u32[]{:S(2)}, u32[]{:S(2)}) collective-permute-start(bf16[128,1024]{1,0:T(8,128)(2,1)S(1)} %get-tuple-element.11.refs_0_), channel_id=1, source_target_pairs={{0,96},{32,0},{64,32},{96,64},{1,97},{33,1},{65,33},{97,65},{2,98}... | collective-permute-start | bytes 786440 | tf_op jit(solution)/shard_map/ppermute | solution.py:384
  54.3 2.7 %collective-permute-start.11 = (bf16[128,1024]{1,0:T(8,128)(2,1)S(1)}, bf16[128,1024]{1,0:T(8,128)(2,1)S(1)}, u32[]{:S(2)}, u32[]{:S(2)}) collective-permute-start(bf16[128,1024]{1,0:T(8,128)(2,1)S(1)} %get-tuple-element.12), channel_id=1, source_target_pairs={{0,3},{1,0},{2,1},{3,2},{4,7},{5,4},{6,5},{7,6},{8,11},{9,8},{10,9... | collective-permute-start | bytes 786440 | tf_op jit(solution)/shard_map/ppermute | solution.py:378
  57.0 1.7 collective-permute-start
  58.8 9.3 %collective-permute-done.11.refs_4_ = bf16[128,1024]{1,0:T(8,128)(2,1)S(1)} collective-permute-done((bf16[128,1024]{1,0:T(8,128)(2,1)S(1)}, bf16[128,1024]{1,0:T(8,128)(2,1)S(1)}, u32[]{:S(2)}, u32[]{:S(2)}) %collective-permute-start.11) | collective-permute-done | bytes 262176 | tf_op jit(solution)/shard_map/ppermute | solution.py:378
  68.1 0.1 collective-permute-start.13
  68.2 1.4 collective-permute-start.12
  69.5 0.1 collective-permute-start.10
  69.6 2.4 %collective-permute-done.4.refs_0_ = bf16[128,1024]{1,0:T(8,128)(2,1)S(1)} collective-permute-done((bf16[128,1024]{1,0:T(8,128)(2,1)S(1)}, bf16[128,1024]{1,0:T(8,128)(2,1)S(1)}, u32[]{:S(2)}, u32[]{:S(2)}) %collective-permute-start.4) | collective-permute-done | bytes 262176 | tf_op jit(solution)/shard_map/ppermute | solution.py:378
  72.0 9.9 %collective-permute-done.refs_0_ = bf16[128,1024]{1,0:T(8,128)(2,1)S(1)} collective-permute-done((bf16[128,1024]{1,0:T(8,128)(2,1)S(1)}, bf16[128,1024]{1,0:T(8,128)(2,1)S(1)}, u32[]{:S(2)}, u32[]{:S(2)}) %collective-permute-start) | collective-permute-done | bytes 262176 | tf_op jit(solution)/shard_map/ppermute | solution.py:378
  81.9 0.1 collective-permute-start.2
  82.0 0.9 slice.20
  82.9 0.6 gather_fusion
  83.5 0.2 convert_reduce_fusion
  83.7 0.6 collective-permute-start.6
  84.4 0.7 copy-done.9
  85.1 0.9 collective-permute-start.1
  86.0 1.8 collective-permute-start.14
  87.8 2.6 %collective-permute-start.3 = (bf16[128,1024]{1,0:T(8,128)(2,1)S(1)}, bf16[128,1024]{1,0:T(8,128)(2,1)}, u32[]{:S(2)}, u32[]{:S(2)}) collective-permute-start(bf16[128,1024]{1,0:T(8,128)(2,1)S(1)} %collective-permute-done.2.refs_2_), channel_id=1, source_target_pairs={{0,96},{32,0},{64,32},{96,64},{1,97},{33,1},{65,33},{97,65},{2,98}... | collective-permute-start | bytes 786440 | tf_op jit(solution)/shard_map/ppermute | solution.py:388
  90.5 0.4 fusion.pick
  90.9 8.1 %collective-permute-done.14.refs_7_ = bf16[128,1024]{1,0:T(8,128)(2,1)S(1)} collective-permute-done((bf16[128,1024]{1,0:T(8,128)(2,1)S(1)}, bf16[128,1024]{1,0:T(8,128)(2,1)S(1)}, u32[]{:S(2)}, u32[]{:S(2)}) %collective-permute-start.14) | collective-permute-done | bytes 262176 | tf_op jit(solution)/shard_map/ppermute | solution.py:388
  99.1 0.7 copy-done.11
  99.8 0.9 copy-done.10
  100.7 0.9 copy-done.12
  101.7 7.5 %project_near.2.refs_5_ = f32[512,1536]{1,0:T(8,128)S(1)} custom-call(s32[4]{0:T(128)S(1)} %and_select_fusion.1.place, bf16[128,1024]{1,0:T(8,128)(2,1)S(1)} %get-tuple-element.11.refs_0_, bf16[128,1024]{1,0:T(8,128)(2,1)S(1)} %collective-permute-done.8.refs_1_, bf16[128,1024]{1,0:T(8,128)(2,1)S(1)} %collective-permute-done.9.refs_2_, ...), custom_call_target="tpu_custom_call" | custom-call | tf_op jit(solution)/shard_map/project_near/pallas_call | solution.py:187
  109.2 1.7 copy-done
  110.8 6.7 %project_near.3.refs_5_ = f32[512,1536]{1,0:T(8,128)S(1)} custom-call(s32[4]{0:T(128)S(1)} %and_select_fusion.1.place, bf16[128,1024]{1,0:T(8,128)(2,1)S(1)} %collective-permute-done.4.refs_0_, bf16[128,1024]{1,0:T(8,128)(2,1)} %collective-permute-done.5.refs_1_, bf16[128,1024]{1,0:T(8,128)(2,1)} %collective-permute-done.6.refs_2_, ...), custom_call_target="tpu_custom_call" | custom-call | tf_op jit(solution)/shard_map/project_near/pallas_call | solution.py:187
  117.5 1.7 copy-done.2
  119.2 6.6 %project_far.1 = bf16[1024,1536]{1,0:T(8,128)(2,1)S(1)} custom-call(s32[4]{0:T(128)S(1)} %and_select_fusion.1.place, bf16[1024,512]{1,0:T(8,128)(2,1)S(1)} %fusion.pick, bf16[128,1024]{1,0:T(8,128)(2,1)S(1)} %collective-permute-done.refs_0_, bf16[128,1024]{1,0:T(8,128)(2,1)} %collective-permute-done.1.refs_1_, ...), custom_call_target="tpu_custom_call" | custom-call | tf_op jit(solution)/shard_map/project_far/pallas_call | solution.py:216
  125.8 1.7 copy-done.1
  127.5 9.1 %all-to-all-start.2 = ((bf16[128,8,1536]{2,1,0:T(8,128)(2,1)}), bf16[128,8,1536]{2,1,0:T(8,128)(2,1)S(1)}, u32[]{:S(2)}, u32[]{:S(2)}) async-start(bf16[128,8,1536]{2,1,0:T(8,128)(2,1)} %bitcast.39), calls=%async_computation.2 | async-start | bytes 6291456 | tf_op jit(solution)/shard_map/all_to_all | solution.py:395
  136.6 1.0 fusion.35
  137.6 0.1 copy.47
  137.7 0.1 copy.48
  137.8 0.1 copy.41
  137.9 0.1 sub.65
  137.9 0.1 sub.68.column_ref
  138.1 0.2 copy.42
  138.2 0.1 reshape.207.row_ref
  138.4 40.3 %all-to-all-done.2 = bf16[128,8,1536]{2,1,0:T(8,128)(2,1)S(1)} async-done(((bf16[128,8,1536]{2,1,0:T(8,128)(2,1)}), bf16[128,8,1536]{2,1,0:T(8,128)(2,1)S(1)}, u32[]{:S(2)}, u32[]{:S(2)}) %all-to-all-start.2) | async-done | bytes 3145760 | tf_op jit(solution)/shard_map/all_to_all | solution.py:395
  178.7 2.5 %merge.1 = bf16[1,128,2,6144]{3,2,1,0:T(2,128)(2,1)} custom-call(s32[256,1]{1,0:T(8,128)S(1)} %sub.68.column_ref, s32[1,256]{1,0:T(1,128)S(1)} %reshape.207.row_ref, bf16[4,32,8,1536]{3,2,1,0:T(8,128)(2,1)S(1)} %bitcast.38), custom_call_target="tpu_custom_call" | custom-call | tf_op jit(solution)/shard_map/merge/pallas_call | solution.py:253
  (67 shorter events, 0.5 us)
Async XLA Ops:
  6.5 17.8 %copy-start.14 = (f32[8]{0:T(128)S(1)}, f32[8]{0:T(128)}, u32[]{:S(2)}) copy-start(f32[8]{0:T(128)} %rate_ref.5) | copy-start | bytes 100
  6.5 19.1 %copy-start.16 = (s32[4]{0:T(128)S(1)}, s32[4]{0:T(128)}, u32[]{:S(2)}) copy-start(s32[4]{0:T(128)} %lengths_ref.5) | copy-start | bytes 52
  6.5 16.6 %copy-start.18 = (s32[512,1]{0,1:T(1,128)S(1)}, s32[512,1]{0,1:T(1,128)}, u32[]{:S(2)}) copy-start(s32[512,1]{0,1:T(1,128)} %param.15) | copy-start | bytes 6148
  6.5 16.8 %copy-start.19 = (s32[512]{0:T(512)S(1)}, s32[512]{0:T(512)}, u32[]{:S(2)}) copy-start(s32[512]{0:T(512)} %param.16) | copy-start | bytes 6148
  6.5 93.2 %all-gather.2.cloned.1.call-start = ((), (), s32[]{:S(2)}) async-start(), calls=%async_computation.3 | async-start | bytes 12976128 | tf_op jit(solution)/shard_map/all_gather | solution.py:307
  7.3 1.2 copy-start.3
  8.5 1.2 copy-start.5
  9.7 0.7 copy-start.13
  10.4 0.7 copy-start.15
  11.0 28.2 %copy-start.4 = (bf16[512,1024]{1,0:T(8,128)(2,1)S(1)}, bf16[512,1024]{1,0:T(8,128)(2,1)}, u32[]{:S(2)}) copy-start(bf16[512,1024]{1,0:T(8,128)(2,1)} %query_ref.3) | copy-start | bytes 3145732
  13.4 20.7 %all-to-all-start = ((bf16[32,32,128]{2,1,0:T(8,128)(2,1)}), bf16[32,32,128]{2,1,0:T(8,128)(2,1)S(1)}, u32[]{:S(2)}, u32[]{:S(2)}) async-start(bf16[32,32,128]{2,1,0:T(8,128)(2,1)} %bitcast.4), calls=%async_computation | async-start | bytes 524288 | tf_op jit(solution)/shard_map/all_to_all | solution.py:328
  35.5 13.3 %all-to-all-start.1 = ((bf16[32,40,128]{2,1,0:T(8,128)(2,1)}), bf16[32,40,128]{2,1,0:T(8,128)(2,1)S(1)}, u32[]{:S(2)}, u32[]{:S(2)}) async-start(bf16[32,40,128]{2,1,0:T(8,128)(2,1)} %copy.38), calls=%async_computation.1 | async-start | bytes 655360 | tf_op jit(solution)/shard_map/all_to_all | solution.py:352
  39.2 1.2 copy-start.6
  40.4 1.2 copy-start.7
  45.4 13.3 %copy-start.21 = (s32[4]{0:T(128)S(1)}, s32[4]{0:T(128)}, u32[]{:S(2)}) copy-start(s32[4]{0:T(128)} %constant.122) | copy-start | bytes 52
  45.4 13.3 %copy-start.20 = (s32[4]{0:T(128)S(1)}, s32[4]{0:T(128)}, u32[]{:S(2)}) copy-start(s32[4]{0:T(128)} %constant.117.clone) | copy-start | bytes 52
  48.7 8.3 %copy-start.17 = (bf16[32,40,128]{2,1,0:T(8,128)(2,1)}, bf16[32,40,128]{2,1,0:T(8,128)(2,1)S(1)}, u32[]{:S(2)}) copy-start(bf16[32,40,128]{2,1,0:T(8,128)(2,1)S(1)} %all-to-all-done.1) | copy-start | bytes 983044
  48.8 1.3 copy-start.8
  51.6 16.6 %collective-permute-start.8 = (bf16[128,1024]{1,0:T(8,128)(2,1)S(1)}, bf16[128,1024]{1,0:T(8,128)(2,1)S(1)}, u32[]{:S(2)}, u32[]{:S(2)}) collective-permute-start(bf16[128,1024]{1,0:T(8,128)(2,1)S(1)} %get-tuple-element.11.refs_0_), channel_id=1, source_target_pairs={{0,32},{32,64},{64,96},{96,0},{1,33},{33,65},{65,97},{97,1},{2,34}... | collective-permute-start | bytes 786440 | tf_op jit(solution)/shard_map/ppermute | solution.py:383
  52.0 17.5 %collective-permute-start.9 = (bf16[128,1024]{1,0:T(8,128)(2,1)S(1)}, bf16[128,1024]{1,0:T(8,128)(2,1)S(1)}, u32[]{:S(2)}, u32[]{:S(2)}) collective-permute-start(bf16[128,1024]{1,0:T(8,128)(2,1)S(1)} %get-tuple-element.11.refs_0_), channel_id=1, source_target_pairs={{0,96},{32,0},{64,32},{96,64},{1,97},{33,1},{65,33},{97,65},{2,98}... | collective-permute-start | bytes 786440 | tf_op jit(solution)/shard_map/ppermute | solution.py:384
  54.3 13.8 %collective-permute-start.11 = (bf16[128,1024]{1,0:T(8,128)(2,1)S(1)}, bf16[128,1024]{1,0:T(8,128)(2,1)S(1)}, u32[]{:S(2)}, u32[]{:S(2)}) collective-permute-start(bf16[128,1024]{1,0:T(8,128)(2,1)S(1)} %get-tuple-element.12), channel_id=1, source_target_pairs={{0,3},{1,0},{2,1},{3,2},{4,7},{5,4},{6,5},{7,6},{8,11},{9,8},{10,9... | collective-permute-start | bytes 786440 | tf_op jit(solution)/shard_map/ppermute | solution.py:378
  57.0 15.0 %collective-permute-start.4 = (bf16[128,1024]{1,0:T(8,128)(2,1)S(1)}, bf16[128,1024]{1,0:T(8,128)(2,1)S(1)}, u32[]{:S(2)}, u32[]{:S(2)}) collective-permute-start(bf16[128,1024]{1,0:T(8,128)(2,1)S(1)} %get-tuple-element.10), channel_id=1, source_target_pairs={{0,1},{1,2},{2,3},{3,0},{4,5},{5,6},{6,7},{7,4},{8,9},{9,10},{10,1... | collective-permute-start | bytes 786440 | tf_op jit(solution)/shard_map/ppermute | solution.py:378
  57.0 24.9 %collective-permute-start = (bf16[128,1024]{1,0:T(8,128)(2,1)S(1)}, bf16[128,1024]{1,0:T(8,128)(2,1)S(1)}, u32[]{:S(2)}, u32[]{:S(2)}) collective-permute-start(bf16[128,1024]{1,0:T(8,128)(2,1)S(1)} %get-tuple-element.9), channel_id=1, source_target_pairs={{0,2},{1,3},{2,0},{3,1},{4,6},{5,7},{6,4},{7,5},{8,10},{9,11},{10,... | collective-permute-start | bytes 786440 | tf_op jit(solution)/shard_map/ppermute | solution.py:378
  68.1 15.6 %collective-permute-start.13 = (bf16[128,1024]{1,0:T(8,128)(2,1)S(1)}, bf16[128,1024]{1,0:T(8,128)(2,1)S(1)}, u32[]{:S(2)}, u32[]{:S(2)}) collective-permute-start(bf16[128,1024]{1,0:T(8,128)(2,1)S(1)} %collective-permute-done.11.refs_4_), channel_id=1, source_target_pairs={{0,96},{32,0},{64,32},{96,64},{1,97},{33,1},{65,33},{97,65},{2,98}... | collective-permute-start | bytes 786440 | tf_op jit(solution)/shard_map/ppermute | solution.py:384
  68.2 17.8 %collective-permute-start.12 = (bf16[128,1024]{1,0:T(8,128)(2,1)S(1)}, bf16[128,1024]{1,0:T(8,128)(2,1)S(1)}, u32[]{:S(2)}, u32[]{:S(2)}) collective-permute-start(bf16[128,1024]{1,0:T(8,128)(2,1)S(1)} %collective-permute-done.11.refs_4_), channel_id=1, source_target_pairs={{0,32},{32,64},{64,96},{96,0},{1,33},{33,65},{65,97},{97,1},{2,34}... | collective-permute-start | bytes 786440 | tf_op jit(solution)/shard_map/ppermute | solution.py:383
  69.5 14.8 %collective-permute-start.10 = (bf16[128,1024]{1,0:T(8,128)(2,1)S(1)}, bf16[128,1024]{1,0:T(8,128)(2,1)S(1)}, u32[]{:S(2)}, u32[]{:S(2)}) collective-permute-start(bf16[128,1024]{1,0:T(8,128)(2,1)S(1)} %collective-permute-done.8.refs_1_), channel_id=1, source_target_pairs={{0,32},{32,64},{64,96},{96,0},{1,33},{33,65},{65,97},{97,1},{2,34}... | collective-permute-start | bytes 786440 | tf_op jit(solution)/shard_map/ppermute | solution.py:386
  72.0 15.7 %collective-permute-start.5 = (bf16[128,1024]{1,0:T(8,128)(2,1)S(1)}, bf16[128,1024]{1,0:T(8,128)(2,1)}, u32[]{:S(2)}, u32[]{:S(2)}) collective-permute-start(bf16[128,1024]{1,0:T(8,128)(2,1)S(1)} %collective-permute-done.4.refs_0_), channel_id=1, source_target_pairs={{0,32},{32,64},{64,96},{96,0},{1,33},{33,65},{65,97},{97,1},{2,34}... | collective-permute-start | bytes 786440 | tf_op jit(solution)/shard_map/ppermute | solution.py:383
  81.9 5.9 %collective-permute-start.2 = (bf16[128,1024]{1,0:T(8,128)(2,1)S(1)}, bf16[128,1024]{1,0:T(8,128)(2,1)S(1)}, u32[]{:S(2)}, u32[]{:S(2)}) collective-permute-start(bf16[128,1024]{1,0:T(8,128)(2,1)S(1)} %collective-permute-done.refs_0_), channel_id=1, source_target_pairs={{0,96},{32,0},{64,32},{96,64},{1,97},{33,1},{65,33},{97,65},{2,98}... | collective-permute-start | bytes 786440 | tf_op jit(solution)/shard_map/ppermute | solution.py:384
  83.7 27.1 %collective-permute-start.6 = (bf16[128,1024]{1,0:T(8,128)(2,1)S(1)}, bf16[128,1024]{1,0:T(8,128)(2,1)}, u32[]{:S(2)}, u32[]{:S(2)}) collective-permute-start(bf16[128,1024]{1,0:T(8,128)(2,1)S(1)} %collective-permute-done.4.refs_0_), channel_id=1, source_target_pairs={{0,96},{32,0},{64,32},{96,64},{1,97},{33,1},{65,33},{97,65},{2,98}... | collective-permute-start | bytes 786440 | tf_op jit(solution)/shard_map/ppermute | solution.py:384
  84.4 0.7 copy-start.9
  85.1 34.1 %collective-permute-start.1 = (bf16[128,1024]{1,0:T(8,128)(2,1)S(1)}, bf16[128,1024]{1,0:T(8,128)(2,1)}, u32[]{:S(2)}, u32[]{:S(2)}) collective-permute-start(bf16[128,1024]{1,0:T(8,128)(2,1)S(1)} %collective-permute-done.refs_0_), channel_id=1, source_target_pairs={{0,32},{32,64},{64,96},{96,0},{1,33},{33,65},{65,97},{97,1},{2,34}... | collective-permute-start | bytes 786440 | tf_op jit(solution)/shard_map/ppermute | solution.py:383
  86.0 13.1 %collective-permute-start.14 = (bf16[128,1024]{1,0:T(8,128)(2,1)S(1)}, bf16[128,1024]{1,0:T(8,128)(2,1)S(1)}, u32[]{:S(2)}, u32[]{:S(2)}) collective-permute-start(bf16[128,1024]{1,0:T(8,128)(2,1)S(1)} %collective-permute-done.13.refs_6_), channel_id=1, source_target_pairs={{0,96},{32,0},{64,32},{96,64},{1,97},{33,1},{65,33},{97,65},{2,98}... | collective-permute-start | bytes 786440 | tf_op jit(solution)/shard_map/ppermute | solution.py:388
  87.8 23.1 %collective-permute-start.7 = (bf16[128,1024]{1,0:T(8,128)(2,1)}, bf16[128,1024]{1,0:T(8,128)(2,1)}, u32[]{:S(2)}, u32[]{:S(2)}) collective-permute-start(bf16[128,1024]{1,0:T(8,128)(2,1)} %collective-permute-done.5.refs_1_), channel_id=1, source_target_pairs={{0,32},{32,64},{64,96},{96,0},{1,33},{33,65},{65,97},{97,1},{2,34}... | collective-permute-start | bytes 786440 | tf_op jit(solution)/shard_map/ppermute | solution.py:386
  87.8 31.3 %collective-permute-start.3 = (bf16[128,1024]{1,0:T(8,128)(2,1)S(1)}, bf16[128,1024]{1,0:T(8,128)(2,1)}, u32[]{:S(2)}, u32[]{:S(2)}) collective-permute-start(bf16[128,1024]{1,0:T(8,128)(2,1)S(1)} %collective-permute-done.2.refs_2_), channel_id=1, source_target_pairs={{0,96},{32,0},{64,32},{96,64},{1,97},{33,1},{65,33},{97,65},{2,98}... | collective-permute-start | bytes 786440 | tf_op jit(solution)/shard_map/ppermute | solution.py:388
  99.1 0.7 copy-start.11
  99.8 1.0 copy-start.10
  100.7 0.9 copy-start.12
  109.1 1.7 copy-start
  117.5 1.7 copy-start.2
  125.8 1.7 copy-start.1
  127.5 51.2 %all-to-all-start.2 = ((bf16[128,8,1536]{2,1,0:T(8,128)(2,1)}), bf16[128,8,1536]{2,1,0:T(8,128)(2,1)S(1)}, u32[]{:S(2)}, u32[]{:S(2)}) async-start(bf16[128,8,1536]{2,1,0:T(8,128)(2,1)} %bitcast.39), calls=%async_computation.2 | async-start | bytes 6291456 | tf_op jit(solution)/shard_map/all_to_all | solution.py:395
Sparse Core Ops, SparseCore 0:
  9.6 79.3 all-gather.1

commit v5 on v4

--- a/solution.py
+++ b/solution.py
@@ -165,71 +165,40 @@
     )
 
 
-def near_body(count, place, *refs):
+def project_body(turns, place, pick, *refs):
     out_ref = refs[-1]
-    each = len(TURNS)
     total = None
-    for k in range(count):
-        part = times(refs[k * each : (k + 1) * each], refs[count * each + k])
+    for k in range(turns):
+        part = times(refs[k * turns : (k + 1) * turns], refs[turns * turns + k])
         total = part if total is None else total + part
-    for held in refs[count * (each + 1) : -1]:
-        total = total + held[...]
-    out_ref[...] = total
-
-
-def project_near(place, pieces, turns, weight, held, tile):
-    count = len(pieces)
-    rows, depth = pieces[0][0].shape
-    toks = rows * len(TURNS)
-    width = weight.shape[1]
-    whole = pl.BlockSpec((rows, depth), lambda i, p: (0, 0))
-    part = pl.BlockSpec((toks, tile), lambda i, p: (0, i))
-    return pl.pallas_call(
-        functools.partial(near_body, count),
-        grid_spec=pltpu.PrefetchScalarGridSpec(
-            num_scalar_prefetch=1,
-            grid=(width // tile,),
-            in_specs=[whole] * (count * len(TURNS))
-            + [pl.BlockSpec((1, tile, depth), lambda i, p, k=k: (p[k], i, 0)) for k in turns]
-            + [part] * len(held),
-            out_specs=part,
-        ),
-        out_shape=jax.ShapeDtypeStruct((toks, width), F32),
-        compiler_params=params(),
-        name="project_near",
-    )(place, *[q for piece in pieces for q in piece], *[weight] * count, *held)
-
-
-def far_body(place, pick, *refs):
-    weight, near, out_ref = refs[-3:]
-    total = near[...] + times(refs[:-3], weight)
     out_ref[...] = jnp.dot(
         pick[...], total.astype(BF16), preferred_element_type=F32
     ).astype(BF16)
 
 
-def project_far(place, pick, piece, turn, weight, near, tile):
-    rows, depth = piece[0].shape
+def project(place, pick, pieces, weight, tile):
+    turns = len(pieces)
+    rows, depth = pieces[0][0].shape
     slots, toks = pick.shape
     width = weight.shape[1]
     whole = pl.BlockSpec((rows, depth), lambda i, p: (0, 0))
     return pl.pallas_call(
-        far_body,
+        functools.partial(project_body, turns),
         grid_spec=pltpu.PrefetchScalarGridSpec(
             num_scalar_prefetch=1,
             grid=(width // tile,),
             in_specs=[pl.BlockSpec((slots, toks), lambda i, p: (0, 0))]
-            + [whole] * len(piece)
+            + [whole] * (turns * turns)
             + [
-                pl.BlockSpec((1, tile, depth), lambda i, p: (p[turn], i, 0)),
-                pl.BlockSpec((toks, tile), lambda i, p: (0, i)),
+                pl.BlockSpec((1, tile, depth), lambda i, p, k=k: (p[k], i, 0))
+                for k in range(turns)
             ],
             out_specs=pl.BlockSpec((slots, tile), lambda i, p: (0, i)),
         ),
-        out_shape=jax.ShapeDtypeStruct((slots, width), BF16),
-        compiler_params=params(),
-        name="project_far",
-    )(place, pick, *piece, weight, near)
+        out_shape=pltpu.HBM((slots, width), BF16),
+        compiler_params=params(),
+        name="project",
+    )(place, pick, *[q for piece in pieces for q in piece], *[weight] * turns)
 
 
 def merge_body(column_ref, row_ref, rows_ref, out_ref, same_ref):
@@ -307,6 +276,10 @@
     weight = lax.all_gather(value_weight, ("head", "y", "core"), axis=0, tiled=True)
     weight = weight.reshape(n_head, -1, value_weight.shape[1])
 
+    queries, key_vectors, output_grad = (
+        pltpu.with_memory_space_constraint(array, pltpu.HBM)
+        for array in (queries, key_vectors, output_grad)
+    )
     state = local_states(decay_rate, doc_lengths, queries, output_grad, head_local // 2)
     blocks = tok_rows // ROWS_BLK
     per = blocks * CAPACITY
@@ -332,6 +305,7 @@
         decay_rate, doc_lengths, queries, key_vectors, output_grad, head_local // 2
     )
 
+    state_in, intra = lax.optimization_barrier((state_in, intra))
     doc_ends = jnp.cumsum(doc_lengths)
     ranks = jnp.arange(n_seq, dtype=jnp.int32)
     doc_last = doc_of((ranks + 1) * tok_rows - 1, doc_ends)
@@ -386,11 +360,10 @@
             across_z = lax.ppermute(below, "z", shift(n_z, 1))
         else:
             across_z = lax.ppermute(above, "z", shift(n_z, -1))
-        pieces.append((rows, below, above, across_z))
-
-    near = project_near(place, pieces[:2], (0, 1), weight, (), 256)
-    near = project_near(place, pieces[2:3], (2,), weight, (near,), 256)
-    send = project_far(place, pick, pieces[3], 3, weight, near, 512)
+        group = (rows, below, above, across_z)
+        pieces.append([pltpu.with_memory_space_constraint(q, pltpu.HBM) for q in group])
+
+    send = project(place, pick, pieces, weight, 512)
     send = send.reshape(devices_all, per, -1)
     got = lax.all_to_all(send, ALL, split_axis=0, concat_axis=0, tiled=True)
     got = got.reshape(n_z, plane * n_head, per, -1)

time: 189 us -> 177 us (0.937)
  local copies, waits for them, and re-layouts: 20.6 us -> 5.17 us
  blocking collectives: 0 us -> 15 us
  waiting for transfers between devices: 82.2 us -> 76.4 us
  Pallas kernels: 30.8 us -> 26.6 us
    all_to_all x0 -> x1, blocking collectives: none -> 15 us  [per_device(): lax.all_to_all(jnp.concatenate([carried_all, note], axis=1), SEQ, split_a...]
    unnamed x48, local copies, waits for them, and re-layouts: 16 us -> 2.24 us
    ppermute x2, waiting for transfers between devices: 0.01 us -> 10.8 us  [per_device(): across_z = lax.ppermute(below, 'z', shift(n_z, 1))]
    ppermute x2, waiting for transfers between devices: 8.11 us -> 0.01 us  [per_device(): across_z = lax.ppermute(above, 'z', shift(n_z, -1))]
    all_to_all x1, waiting for transfers between devices: 8.19 us -> 1.8 us  [per_device(): lax.all_to_all(state.reshape(n_seq, share, head_dim), SEQ, split_axis=0,...]
    pallas_call x3 -> x1, Pallas kernels: 20.8 us -> 14.4 us  [project(): pl.pallas_call(functools.partial(project_body, turns), grid_spec=pltpu.Pr...]
    ppermute x4, starting transfers between devices: 3.11 us -> 7.67 us  [per_device(): above = lax.ppermute(rows, 'z', shift(n_z, -1))]
    all_to_all x1 -> x0, starting transfers between devices: 3.74 us -> none  [per_device(): lax.all_to_all(jnp.concatenate([carried_all, note], axis=1), SEQ, split_a...]
  transfers between devices with their start and end apart: 19 -> 18, of which waited for: 7 -> 9; matrix products, arithmetic and copies ran while one was open for 4% -> 3% of each run, Pallas kernels for 12% -> 6%
where the time goes in v5:
time: 177 us; the launch traced here: 176 us
  waiting for transfers between devices  76.4 us (43%)
  starting transfers between devices  36 us (20%)
  Pallas kernels  26.6 us (15%)
  blocking collectives  15 us (8%)
  between operations  14.5 us (8%)
  local copies, waits for them, and re-layouts  5.17 us (3%)
  other arithmetic  2.24 us (1%)
    all_to_all x1, waiting for transfers between devices, per_device(): got = lax.all_to_all(send, ALL, split_axis=0, concat_axis=0, tiled=True)  40.3 us
    ppermute x3, waiting for transfers between devices, per_device(): mine.append(lax.ppermute(own[turn], 'head', shift(n_head, TURNS[turn])))  20.4 us
    all_to_all x1, blocking collectives, per_device(): lax.all_to_all(jnp.concatenate([carried_all, note], axis=1), SEQ, split_a...  15 us
    pallas_call x1, Pallas kernels, project(): pl.pallas_call(functools.partial(project_body, turns), grid_spec=pltpu.Pr...  14.4 us
    ppermute x2, waiting for transfers between devices, per_device(): across_z = lax.ppermute(below, 'z', shift(n_z, 1))  10.8 us
    all_to_all x1, starting transfers between devices, per_device(): lax.all_to_all(state.reshape(n_seq, share, head_dim), SEQ, split_axis=0,...  9.62 us
    ppermute x4, starting transfers between devices, per_device(): above = lax.ppermute(rows, 'z', shift(n_z, -1))  7.67 us
    ppermute x2, starting transfers between devices, per_device(): across_z = lax.ppermute(above, 'z', shift(n_z, -1))  7.03 us
  transfers between devices with their start and end apart: 18, of which 9 were waited for; matrix products, arithmetic and copies ran while one was open for 3% of the time, Pallas kernels for 6%

profile of v5, /device:TPU:1, one launch (start us, length us, event | category | flops | bytes accessed | tf_op | source)
XLA Modules:
  0.0 176.3 jit_solution(1260073297175698474)
XLA Ops:
  6.5 0.0 all-gather.2.cloned.1.call-start
  6.6 0.7 all-gather.2.cloned.1.call-update
  7.3 0.6 copy-done.1
  7.9 0.7 copy-done.3
  8.6 3.0 %local_states.1 = bf16[8,128,128]{2,1,0:T(8,128)(2,1)} custom-call(f32[8]{0:T(128)S(1)} %copy-done.1, s32[4]{0:T(128)S(1)} %copy-done.3, bf16[512,1024]{1,0:T(8,128)(2,1)} %query_ref.3, bf16[512,1024]{1,0:T(8,128)(2,1)} %grad_ref.3), custom_call_target="tpu_custom_call" | custom-call | tf_op jit(solution)/shard_map/local_states/pallas_call | solution.py:64
  11.6 9.6 %all-to-all-start = ((bf16[32,32,128]{2,1,0:T(8,128)(2,1)}), bf16[32,32,128]{2,1,0:T(8,128)(2,1)S(1)}, u32[]{:S(2)}, u32[]{:S(2)}) async-start(bf16[32,32,128]{2,1,0:T(8,128)(2,1)} %bitcast.4), calls=%async_computation | async-start | bytes 524288 | tf_op jit(solution)/shard_map/all_to_all | solution.py:301
  21.3 0.2 convert_reduce_fusion.1
  21.5 0.1 iota_add_fusion
  21.6 0.7 select_reduce_fusion
  22.3 0.1 maximum_bitcast_fusion
  22.5 0.6 dynamic_slice.9
  23.7 0.2 reduce-window.8
  23.9 4.5 %within.1.intra_ref = f32[512,1024]{1,0:T(8,128)S(1)} custom-call(f32[8]{0:T(128)S(1)} %copy-done.2, s32[4]{0:T(128)S(1)} %copy-done.4, bf16[512,1024]{1,0:T(8,128)(2,1)} %query_ref.3, bf16[512,1024]{1,0:T(8,128)(2,1)} %key_ref.3, bf16[512,1024]{1,0:T(8,128)(2,1)} %grad_ref.3), custom_call_target="tpu_custom_call" | custom-call | tf_op jit(solution)/shard_map/within/pallas_call | solution.py:106
  28.4 0.1 convert_reduce_fusion.3
  28.4 1.8 %all-to-all-done = bf16[32,32,128]{2,1,0:T(8,128)(2,1)S(1)} async-done(((bf16[32,32,128]{2,1,0:T(8,128)(2,1)}), bf16[32,32,128]{2,1,0:T(8,128)(2,1)S(1)}, u32[]{:S(2)}, u32[]{:S(2)}) %all-to-all-start) | async-done | bytes 262176 | tf_op jit(solution)/shard_map/all_to_all | solution.py:301
  30.2 0.4 convolution_convert_fusion
  30.7 0.1 copy.38
  30.8 15.0 %all_to_all.15 = bf16[32,40,128]{2,1,0:T(8,128)(2,1)S(1)} all-to-all(bf16[32,40,128]{2,1,0:T(8,128)(2,1)S(1)} %copy.38), channel_id=1, replica_groups=mesh['z'=4,'y'=4,'core'=2,'head'=4] {'z','y','core'}, dimensions={0} | all-to-all | bytes 655360 | tf_op jit(solution)/shard_map/all_to_all | solution.py:326
  45.9 2.3 %across.1 = (bf16[128,1024]{1,0:T(8,128)(2,1)S(1)}, bf16[128,1024]{1,0:T(8,128)(2,1)S(1)}, bf16[128,1024]{1,0:T(8,128)(2,1)S(1)}, bf16[128,1024]{1,0:T(8,128)(2,1)S(1)}) custom-call(f32[8]{0:T(128)S(1)} %copy-done.2, s32[4]{0:T(128)S(1)} %copy-done.4, bf16[512,1024]{1,0:T(8,128)(2,1)} %key_ref.3, bf16[8,128,128]{2,1,0:T(8,128)(2,1)S(1)} %bitcast.39, ...), custom_call_target="tpu_custom_call" | custom-call | tf_op jit(solution)/shard_map/across/pallas_call | solution.py:144
  48.2 0.9 collective-permute-start.1
  49.2 0.6 collective-permute-start
  49.8 2.6 %collective-permute-start.3 = (bf16[128,1024]{1,0:T(8,128)(2,1)S(1)}, bf16[128,1024]{1,0:T(8,128)(2,1)S(1)}, u32[]{:S(2)}, u32[]{:S(2)}) collective-permute-start(bf16[128,1024]{1,0:T(8,128)(2,1)S(1)} %get-tuple-element.14), channel_id=1, source_target_pairs={{0,3},{1,0},{2,1},{3,2},{4,7},{5,4},{6,5},{7,6},{8,11},{9,8},{10,9... | collective-permute-start | bytes 786440 | tf_op jit(solution)/shard_map/ppermute | solution.py:352
  52.4 0.0 collective-permute-start.7
  52.4 1.7 collective-permute-start.11
  54.2 9.2 %collective-permute-done.3.refs_4_ = bf16[128,1024]{1,0:T(8,128)(2,1)S(1)} collective-permute-done((bf16[128,1024]{1,0:T(8,128)(2,1)S(1)}, bf16[128,1024]{1,0:T(8,128)(2,1)S(1)}, u32[]{:S(2)}, u32[]{:S(2)}) %collective-permute-start.3) | collective-permute-done | bytes 262176 | tf_op jit(solution)/shard_map/ppermute | solution.py:352
  63.4 2.1 %collective-permute-start.5 = (bf16[128,1024]{1,0:T(8,128)(2,1)S(1)}, bf16[128,1024]{1,0:T(8,128)(2,1)S(1)}, u32[]{:S(2)}, u32[]{:S(2)}) collective-permute-start(bf16[128,1024]{1,0:T(8,128)(2,1)S(1)} %collective-permute-done.3.refs_4_), channel_id=1, source_target_pairs={{0,96},{32,0},{64,32},{96,64},{1,97},{33,1},{65,33},{97,65},{2,98}... | collective-permute-start | bytes 786440 | tf_op jit(solution)/shard_map/ppermute | solution.py:358
  65.5 1.9 %collective-permute-done.7.refs_8_ = bf16[128,1024]{1,0:T(8,128)(2,1)S(1)} collective-permute-done((bf16[128,1024]{1,0:T(8,128)(2,1)S(1)}, bf16[128,1024]{1,0:T(8,128)(2,1)S(1)}, u32[]{:S(2)}, u32[]{:S(2)}) %collective-permute-start.7) | collective-permute-done | bytes 262176 | tf_op jit(solution)/shard_map/ppermute | solution.py:352
  67.4 0.6 collective-permute-start.4
  68.0 9.3 %collective-permute-done.11.refs_12_ = bf16[128,1024]{1,0:T(8,128)(2,1)S(1)} collective-permute-done((bf16[128,1024]{1,0:T(8,128)(2,1)S(1)}, bf16[128,1024]{1,0:T(8,128)(2,1)S(1)}, u32[]{:S(2)}, u32[]{:S(2)}) %collective-permute-start.11) | collective-permute-done | bytes 262176 | tf_op jit(solution)/shard_map/ppermute | solution.py:352
  77.3 2.0 %collective-permute-start.9 = (bf16[128,1024]{1,0:T(8,128)(2,1)S(1)}, bf16[128,1024]{1,0:T(8,128)(2,1)S(1)}, u32[]{:S(2)}, u32[]{:S(2)}) collective-permute-start(bf16[128,1024]{1,0:T(8,128)(2,1)S(1)} %collective-permute-done.7.refs_8_), channel_id=1, source_target_pairs={{0,96},{32,0},{64,32},{96,64},{1,97},{33,1},{65,33},{97,65},{2,98}... | collective-permute-start | bytes 786440 | tf_op jit(solution)/shard_map/ppermute | solution.py:358
  79.3 0.0 collective-permute-done.1.refs_2_
  79.3 0.0 collective-permute-start.8
  79.3 0.0 collective-permute-done.refs_1_
  79.3 2.7 %collective-permute-start.13 = (bf16[128,1024]{1,0:T(8,128)(2,1)S(1)}, bf16[128,1024]{1,0:T(8,128)(2,1)}, u32[]{:S(2)}, u32[]{:S(2)}) collective-permute-start(bf16[128,1024]{1,0:T(8,128)(2,1)S(1)} %collective-permute-done.11.refs_12_), channel_id=1, source_target_pairs={{0,96},{32,0},{64,32},{96,64},{1,97},{33,1},{65,33},{97,65},{2,98}... | collective-permute-start | bytes 786440 | tf_op jit(solution)/shard_map/ppermute | solution.py:358
  82.1 0.6 gather_fusion
  82.6 0.2 convert_reduce_fusion
  82.9 0.0 collective-permute-done.5.refs_6_
  82.9 0.1 collective-permute-start.12
  83.0 0.0 collective-permute-done.4.refs_5_
  83.0 0.1 collective-permute-start.2
  83.1 0.2 collective-permute-done.9.refs_10_
  83.3 3.5 %collective-permute-start.6 = (bf16[128,1024]{1,0:T(8,128)(2,1)S(1)}, bf16[128,1024]{1,0:T(8,128)(2,1)S(1)}, u32[]{:S(2)}, u32[]{:S(2)}) collective-permute-start(bf16[128,1024]{1,0:T(8,128)(2,1)S(1)} %collective-permute-done.5.refs_6_), channel_id=1, source_target_pairs={{0,96},{32,0},{64,32},{96,64},{1,97},{33,1},{65,33},{97,65},{2,98}... | collective-permute-start | bytes 786440 | tf_op jit(solution)/shard_map/ppermute | solution.py:362
  86.8 0.0 collective-permute-done.8.refs_9_
  86.8 0.0 collective-permute-start.10
  86.8 2.1 %collective-permute-done.13.refs_14_ = bf16[128,1024]{1,0:T(8,128)(2,1)} collective-permute-done((bf16[128,1024]{1,0:T(8,128)(2,1)S(1)}, bf16[128,1024]{1,0:T(8,128)(2,1)}, u32[]{:S(2)}, u32[]{:S(2)}) %collective-permute-start.13) | collective-permute-done | bytes 262176 | tf_op jit(solution)/shard_map/ppermute | solution.py:358
  88.9 3.5 %collective-permute-start.14 = (bf16[128,1024]{1,0:T(8,128)(2,1)}, bf16[128,1024]{1,0:T(8,128)(2,1)}, u32[]{:S(2)}, u32[]{:S(2)}) collective-permute-start(bf16[128,1024]{1,0:T(8,128)(2,1)} %collective-permute-done.13.refs_14_), channel_id=1, source_target_pairs={{0,96},{32,0},{64,32},{96,64},{1,97},{33,1},{65,33},{97,65},{2,98}... | collective-permute-start | bytes 786440 | tf_op jit(solution)/shard_map/ppermute | solution.py:362
  92.4 0.1 add_bitcast_fusion
  92.5 0.4 fusion.pick
  92.9 5.2 %collective-permute-done.2.refs_3_ = bf16[128,1024]{1,0:T(8,128)(2,1)S(1)} collective-permute-done((bf16[128,1024]{1,0:T(8,128)(2,1)S(1)}, bf16[128,1024]{1,0:T(8,128)(2,1)S(1)}, u32[]{:S(2)}, u32[]{:S(2)}) %collective-permute-start.2) | collective-permute-done | bytes 262176 | tf_op jit(solution)/shard_map/ppermute | solution.py:360
  98.2 5.6 %collective-permute-done.10.refs_11_ = bf16[128,1024]{1,0:T(8,128)(2,1)S(1)} collective-permute-done((bf16[128,1024]{1,0:T(8,128)(2,1)}, bf16[128,1024]{1,0:T(8,128)(2,1)S(1)}, u32[]{:S(2)}, u32[]{:S(2)}) %collective-permute-start.10) | collective-permute-done | bytes 262176 | tf_op jit(solution)/shard_map/ppermute | solution.py:360
  103.8 0.7 copy-done.17
  104.5 0.0 collective-permute-done.14.refs_15_
  104.5 14.4 %project.1 = bf16[1024,1536]{1,0:T(8,128)(2,1)} custom-call(s32[4]{0:T(128)S(1)} %and_select_fusion.1.place, bf16[1024,512]{1,0:T(8,128)(2,1)S(1)} %fusion.pick, bf16[128,1024]{1,0:T(8,128)(2,1)} %copy-done, bf16[128,1024]{1,0:T(8,128)(2,1)} %copy-done.7, bf16[128,1024]{1,0:T(8,128)(2,1)} %copy-done.6, bf16[128,1024]{1,0:T(8,128)(2,1)} %copy-done.15, ...), custom_call_target="tpu_custom_call" | custom-call | tf_op jit(solution)/shard_map/project/pallas_call | solution.py:185
  118.9 5.9 %all-to-all-start.2 = ((bf16[128,8,1536]{2,1,0:T(8,128)(2,1)}), bf16[128,8,1536]{2,1,0:T(8,128)(2,1)S(1)}, u32[]{:S(2)}, u32[]{:S(2)}) async-start(bf16[128,8,1536]{2,1,0:T(8,128)(2,1)} %bitcast.45), calls=%async_computation.2 | async-start | bytes 6291456 | tf_op jit(solution)/shard_map/all_to_all | solution.py:368
  124.8 1.0 fusion.35
  125.8 0.1 copy.47
  125.9 0.1 copy.48
  126.0 0.1 sub.65
  126.1 0.1 copy.41
  126.2 0.2 copy.42
  126.3 0.2 reshape.207.row_ref
  126.5 0.1 sub.68.column_ref
  126.6 40.3 %all-to-all-done.2 = bf16[128,8,1536]{2,1,0:T(8,128)(2,1)S(1)} async-done(((bf16[128,8,1536]{2,1,0:T(8,128)(2,1)}), bf16[128,8,1536]{2,1,0:T(8,128)(2,1)S(1)}, u32[]{:S(2)}, u32[]{:S(2)}) %all-to-all-start.2) | async-done | bytes 3145760 | tf_op jit(solution)/shard_map/all_to_all | solution.py:368
  166.9 2.5 %merge.1 = bf16[1,128,2,6144]{3,2,1,0:T(2,128)(2,1)} custom-call(s32[256,1]{1,0:T(8,128)S(1)} %sub.68.column_ref, s32[1,256]{1,0:T(1,128)S(1)} %reshape.207.row_ref, bf16[4,32,8,1536]{3,2,1,0:T(8,128)(2,1)S(1)} %bitcast.38), custom_call_target="tpu_custom_call" | custom-call | tf_op jit(solution)/shard_map/merge/pallas_call | solution.py:222
  (64 shorter events, 0.3 us)
Async XLA Ops:
  6.5 17.1 %copy-start.4 = (s32[4]{0:T(128)S(1)}, s32[4]{0:T(128)}, u32[]{:S(2)}) copy-start(s32[4]{0:T(128)} %lengths_ref.5) | copy-start | bytes 52
  6.5 15.9 %copy-start.2 = (f32[8]{0:T(128)S(1)}, f32[8]{0:T(128)}, u32[]{:S(2)}) copy-start(f32[8]{0:T(128)} %rate_ref.5) | copy-start | bytes 100
  6.5 14.7 %copy-start.18 = (s32[512,1]{0,1:T(1,128)S(1)}, s32[512,1]{0,1:T(1,128)}, u32[]{:S(2)}) copy-start(s32[512,1]{0,1:T(1,128)} %param.15) | copy-start | bytes 6148
  6.5 15.0 %copy-start.19 = (s32[512]{0:T(512)S(1)}, s32[512]{0:T(512)}, u32[]{:S(2)}) copy-start(s32[512]{0:T(512)} %param.16) | copy-start | bytes 6148
  6.5 97.9 %all-gather.2.cloned.1.call-start = ((), (), s32[]{:S(2)}) async-start(), calls=%async_computation.3 | async-start | bytes 12976128 | tf_op jit(solution)/shard_map/all_gather | solution.py:276
  7.3 0.7 copy-start.1
  7.9 0.7 copy-start.3
  11.6 18.7 %all-to-all-start = ((bf16[32,32,128]{2,1,0:T(8,128)(2,1)}), bf16[32,32,128]{2,1,0:T(8,128)(2,1)S(1)}, u32[]{:S(2)}, u32[]{:S(2)}) async-start(bf16[32,32,128]{2,1,0:T(8,128)(2,1)} %bitcast.4), calls=%async_computation | async-start | bytes 524288 | tf_op jit(solution)/shard_map/all_to_all | solution.py:301
  30.2 23.9 %copy-start.21 = (s32[4]{0:T(128)S(1)}, s32[4]{0:T(128)}, u32[]{:S(2)}) copy-start(s32[4]{0:T(128)} %constant.122) | copy-start | bytes 52
  30.2 23.9 %copy-start.20 = (s32[4]{0:T(128)S(1)}, s32[4]{0:T(128)}, u32[]{:S(2)}) copy-start(s32[4]{0:T(128)} %constant.117.clone) | copy-start | bytes 52
  45.9 73.1 %copy-start.5 = (bf16[32,40,128]{2,1,0:T(8,128)(2,1)}, bf16[32,40,128]{2,1,0:T(8,128)(2,1)S(1)}, u32[]{:S(2)}) copy-start(bf16[32,40,128]{2,1,0:T(8,128)(2,1)S(1)} %all_to_all.15) | copy-start | bytes 983044
  48.2 56.3 %copy-start = (bf16[128,1024]{1,0:T(8,128)(2,1)}, bf16[128,1024]{1,0:T(8,128)(2,1)S(1)}, u32[]{:S(2)}) copy-start(bf16[128,1024]{1,0:T(8,128)(2,1)S(1)} %get-tuple-element.13.refs_0_) | copy-start | bytes 786436
  48.2 31.1 %collective-permute-start.1 = (bf16[128,1024]{1,0:T(8,128)(2,1)S(1)}, bf16[128,1024]{1,0:T(8,128)(2,1)S(1)}, u32[]{:S(2)}, u32[]{:S(2)}) collective-permute-start(bf16[128,1024]{1,0:T(8,128)(2,1)S(1)} %get-tuple-element.13.refs_0_), channel_id=1, source_target_pairs={{0,96},{32,0},{64,32},{96,64},{1,97},{33,1},{65,33},{97,65},{2,98}... | collective-permute-start | bytes 786440 | tf_op jit(solution)/shard_map/ppermute | solution.py:358
  49.2 30.2 %collective-permute-start = (bf16[128,1024]{1,0:T(8,128)(2,1)S(1)}, bf16[128,1024]{1,0:T(8,128)(2,1)S(1)}, u32[]{:S(2)}, u32[]{:S(2)}) collective-permute-start(bf16[128,1024]{1,0:T(8,128)(2,1)S(1)} %get-tuple-element.13.refs_0_), channel_id=1, source_target_pairs={{0,32},{32,64},{64,96},{96,0},{1,33},{33,65},{65,97},{97,1},{2,34}... | collective-permute-start | bytes 786440 | tf_op jit(solution)/shard_map/ppermute | solution.py:357
  49.8 13.7 %collective-permute-start.3 = (bf16[128,1024]{1,0:T(8,128)(2,1)S(1)}, bf16[128,1024]{1,0:T(8,128)(2,1)S(1)}, u32[]{:S(2)}, u32[]{:S(2)}) collective-permute-start(bf16[128,1024]{1,0:T(8,128)(2,1)S(1)} %get-tuple-element.14), channel_id=1, source_target_pairs={{0,3},{1,0},{2,1},{3,2},{4,7},{5,4},{6,5},{7,6},{8,11},{9,8},{10,9... | collective-permute-start | bytes 786440 | tf_op jit(solution)/shard_map/ppermute | solution.py:352
  52.4 15.0 %collective-permute-start.7 = (bf16[128,1024]{1,0:T(8,128)(2,1)S(1)}, bf16[128,1024]{1,0:T(8,128)(2,1)S(1)}, u32[]{:S(2)}, u32[]{:S(2)}) collective-permute-start(bf16[128,1024]{1,0:T(8,128)(2,1)S(1)} %get-tuple-element.15), channel_id=1, source_target_pairs={{0,1},{1,2},{2,3},{3,0},{4,5},{5,6},{6,7},{7,4},{8,9},{9,10},{10,1... | collective-permute-start | bytes 786440 | tf_op jit(solution)/shard_map/ppermute | solution.py:352
  52.4 24.9 %collective-permute-start.11 = (bf16[128,1024]{1,0:T(8,128)(2,1)S(1)}, bf16[128,1024]{1,0:T(8,128)(2,1)S(1)}, u32[]{:S(2)}, u32[]{:S(2)}) collective-permute-start(bf16[128,1024]{1,0:T(8,128)(2,1)S(1)} %get-tuple-element.16), channel_id=1, source_target_pairs={{0,2},{1,3},{2,0},{3,1},{4,6},{5,7},{6,4},{7,5},{8,10},{9,11},{10,... | collective-permute-start | bytes 786440 | tf_op jit(solution)/shard_map/ppermute | solution.py:352
  63.4 41.1 %copy-start.8 = (bf16[128,1024]{1,0:T(8,128)(2,1)}, bf16[128,1024]{1,0:T(8,128)(2,1)S(1)}, u32[]{:S(2)}) copy-start(bf16[128,1024]{1,0:T(8,128)(2,1)S(1)} %collective-permute-done.3.refs_4_) | copy-start | bytes 786436
  63.4 19.4 %collective-permute-start.5 = (bf16[128,1024]{1,0:T(8,128)(2,1)S(1)}, bf16[128,1024]{1,0:T(8,128)(2,1)S(1)}, u32[]{:S(2)}, u32[]{:S(2)}) collective-permute-start(bf16[128,1024]{1,0:T(8,128)(2,1)S(1)} %collective-permute-done.3.refs_4_), channel_id=1, source_target_pairs={{0,96},{32,0},{64,32},{96,64},{1,97},{33,1},{65,33},{97,65},{2,98}... | collective-permute-start | bytes 786440 | tf_op jit(solution)/shard_map/ppermute | solution.py:358
  67.4 37.1 %copy-start.9 = (bf16[128,1024]{1,0:T(8,128)(2,1)}, bf16[128,1024]{1,0:T(8,128)(2,1)S(1)}, u32[]{:S(2)}) copy-start(bf16[128,1024]{1,0:T(8,128)(2,1)S(1)} %collective-permute-done.7.refs_8_) | copy-start | bytes 786436
  67.4 15.6 %collective-permute-start.4 = (bf16[128,1024]{1,0:T(8,128)(2,1)S(1)}, bf16[128,1024]{1,0:T(8,128)(2,1)S(1)}, u32[]{:S(2)}, u32[]{:S(2)}) collective-permute-start(bf16[128,1024]{1,0:T(8,128)(2,1)S(1)} %collective-permute-done.3.refs_4_), channel_id=1, source_target_pairs={{0,32},{32,64},{64,96},{96,0},{1,33},{33,65},{65,97},{97,1},{2,34}... | collective-permute-start | bytes 786440 | tf_op jit(solution)/shard_map/ppermute | solution.py:357
  77.3 27.2 %copy-start.10 = (bf16[128,1024]{1,0:T(8,128)(2,1)}, bf16[128,1024]{1,0:T(8,128)(2,1)S(1)}, u32[]{:S(2)}) copy-start(bf16[128,1024]{1,0:T(8,128)(2,1)S(1)} %collective-permute-done.11.refs_12_) | copy-start | bytes 786436
  77.3 6.0 %collective-permute-start.9 = (bf16[128,1024]{1,0:T(8,128)(2,1)S(1)}, bf16[128,1024]{1,0:T(8,128)(2,1)S(1)}, u32[]{:S(2)}, u32[]{:S(2)}) collective-permute-start(bf16[128,1024]{1,0:T(8,128)(2,1)S(1)} %collective-permute-done.7.refs_8_), channel_id=1, source_target_pairs={{0,96},{32,0},{64,32},{96,64},{1,97},{33,1},{65,33},{97,65},{2,98}... | collective-permute-start | bytes 786440 | tf_op jit(solution)/shard_map/ppermute | solution.py:358
  79.3 25.2 %copy-start.6 = (bf16[128,1024]{1,0:T(8,128)(2,1)}, bf16[128,1024]{1,0:T(8,128)(2,1)S(1)}, u32[]{:S(2)}) copy-start(bf16[128,1024]{1,0:T(8,128)(2,1)S(1)} %collective-permute-done.1.refs_2_) | copy-start | bytes 786436
  79.3 7.5 %collective-permute-start.8 = (bf16[128,1024]{1,0:T(8,128)(2,1)S(1)}, bf16[128,1024]{1,0:T(8,128)(2,1)}, u32[]{:S(2)}, u32[]{:S(2)}) collective-permute-start(bf16[128,1024]{1,0:T(8,128)(2,1)S(1)} %collective-permute-done.7.refs_8_), channel_id=1, source_target_pairs={{0,32},{32,64},{64,96},{96,0},{1,33},{33,65},{65,97},{97,1},{2,34}... | collective-permute-start | bytes 786440 | tf_op jit(solution)/shard_map/ppermute | solution.py:357
  79.3 25.2 %copy-start.7 = (bf16[128,1024]{1,0:T(8,128)(2,1)}, bf16[128,1024]{1,0:T(8,128)(2,1)S(1)}, u32[]{:S(2)}) copy-start(bf16[128,1024]{1,0:T(8,128)(2,1)S(1)} %collective-permute-done.refs_1_) | copy-start | bytes 786436
  79.3 9.5 %collective-permute-start.13 = (bf16[128,1024]{1,0:T(8,128)(2,1)S(1)}, bf16[128,1024]{1,0:T(8,128)(2,1)}, u32[]{:S(2)}, u32[]{:S(2)}) collective-permute-start(bf16[128,1024]{1,0:T(8,128)(2,1)S(1)} %collective-permute-done.11.refs_12_), channel_id=1, source_target_pairs={{0,96},{32,0},{64,32},{96,64},{1,97},{33,1},{65,33},{97,65},{2,98}... | collective-permute-start | bytes 786440 | tf_op jit(solution)/shard_map/ppermute | solution.py:358
  82.9 21.6 %copy-start.11 = (bf16[128,1024]{1,0:T(8,128)(2,1)}, bf16[128,1024]{1,0:T(8,128)(2,1)S(1)}, u32[]{:S(2)}) copy-start(bf16[128,1024]{1,0:T(8,128)(2,1)S(1)} %collective-permute-done.5.refs_6_) | copy-start | bytes 786436
  82.9 10.0 %collective-permute-start.12 = (bf16[128,1024]{1,0:T(8,128)(2,1)S(1)}, bf16[128,1024]{1,0:T(8,128)(2,1)S(1)}, u32[]{:S(2)}, u32[]{:S(2)}) collective-permute-start(bf16[128,1024]{1,0:T(8,128)(2,1)S(1)} %collective-permute-done.11.refs_12_), channel_id=1, source_target_pairs={{0,32},{32,64},{64,96},{96,0},{1,33},{33,65},{65,97},{97,1},{2,34}... | collective-permute-start | bytes 786440 | tf_op jit(solution)/shard_map/ppermute | solution.py:357
  83.0 21.5 %copy-start.12 = (bf16[128,1024]{1,0:T(8,128)(2,1)}, bf16[128,1024]{1,0:T(8,128)(2,1)S(1)}, u32[]{:S(2)}) copy-start(bf16[128,1024]{1,0:T(8,128)(2,1)S(1)} %collective-permute-done.4.refs_5_) | copy-start | bytes 786436
  83.0 15.2 %collective-permute-start.2 = (bf16[128,1024]{1,0:T(8,128)(2,1)S(1)}, bf16[128,1024]{1,0:T(8,128)(2,1)S(1)}, u32[]{:S(2)}, u32[]{:S(2)}) collective-permute-start(bf16[128,1024]{1,0:T(8,128)(2,1)S(1)} %collective-permute-done.refs_1_), channel_id=1, source_target_pairs={{0,32},{32,64},{64,96},{96,0},{1,33},{33,65},{65,97},{97,1},{2,34}... | collective-permute-start | bytes 786440 | tf_op jit(solution)/shard_map/ppermute | solution.py:360
  83.3 9.1 %copy-start.13 = (bf16[128,1024]{1,0:T(8,128)(2,1)}, bf16[128,1024]{1,0:T(8,128)(2,1)S(1)}, u32[]{:S(2)}) copy-start(bf16[128,1024]{1,0:T(8,128)(2,1)S(1)} %collective-permute-done.9.refs_10_) | copy-start | bytes 786436
  83.3 14.9 %collective-permute-start.6 = (bf16[128,1024]{1,0:T(8,128)(2,1)S(1)}, bf16[128,1024]{1,0:T(8,128)(2,1)S(1)}, u32[]{:S(2)}, u32[]{:S(2)}) collective-permute-start(bf16[128,1024]{1,0:T(8,128)(2,1)S(1)} %collective-permute-done.5.refs_6_), channel_id=1, source_target_pairs={{0,96},{32,0},{64,32},{96,64},{1,97},{33,1},{65,33},{97,65},{2,98}... | collective-permute-start | bytes 786440 | tf_op jit(solution)/shard_map/ppermute | solution.py:362
  86.8 17.0 %collective-permute-start.10 = (bf16[128,1024]{1,0:T(8,128)(2,1)}, bf16[128,1024]{1,0:T(8,128)(2,1)S(1)}, u32[]{:S(2)}, u32[]{:S(2)}) collective-permute-start(bf16[128,1024]{1,0:T(8,128)(2,1)} %collective-permute-done.8.refs_9_), channel_id=1, source_target_pairs={{0,32},{32,64},{64,96},{96,0},{1,33},{33,65},{65,97},{97,1},{2,34}... | collective-permute-start | bytes 786440 | tf_op jit(solution)/shard_map/ppermute | solution.py:360
  88.9 15.6 %collective-permute-start.14 = (bf16[128,1024]{1,0:T(8,128)(2,1)}, bf16[128,1024]{1,0:T(8,128)(2,1)}, u32[]{:S(2)}, u32[]{:S(2)}) collective-permute-start(bf16[128,1024]{1,0:T(8,128)(2,1)} %collective-permute-done.13.refs_14_), channel_id=1, source_target_pairs={{0,96},{32,0},{64,32},{96,64},{1,97},{33,1},{65,33},{97,65},{2,98}... | collective-permute-start | bytes 786440 | tf_op jit(solution)/shard_map/ppermute | solution.py:362
  92.9 5.3 %copy-start.14 = (bf16[128,1024]{1,0:T(8,128)(2,1)}, bf16[128,1024]{1,0:T(8,128)(2,1)S(1)}, u32[]{:S(2)}) copy-start(bf16[128,1024]{1,0:T(8,128)(2,1)S(1)} %collective-permute-done.12.refs_13_) | copy-start | bytes 786436
  98.2 5.6 %copy-start.15 = (bf16[128,1024]{1,0:T(8,128)(2,1)}, bf16[128,1024]{1,0:T(8,128)(2,1)S(1)}, u32[]{:S(2)}) copy-start(bf16[128,1024]{1,0:T(8,128)(2,1)S(1)} %collective-permute-done.2.refs_3_) | copy-start | bytes 786436
  98.2 5.6 %copy-start.16 = (bf16[128,1024]{1,0:T(8,128)(2,1)}, bf16[128,1024]{1,0:T(8,128)(2,1)S(1)}, u32[]{:S(2)}) copy-start(bf16[128,1024]{1,0:T(8,128)(2,1)S(1)} %collective-permute-done.6.refs_7_) | copy-start | bytes 786436
  103.8 0.7 copy-start.17
  118.9 48.0 %all-to-all-start.2 = ((bf16[128,8,1536]{2,1,0:T(8,128)(2,1)}), bf16[128,8,1536]{2,1,0:T(8,128)(2,1)S(1)}, u32[]{:S(2)}, u32[]{:S(2)}) async-start(bf16[128,8,1536]{2,1,0:T(8,128)(2,1)} %bitcast.45), calls=%async_computation.2 | async-start | bytes 6291456 | tf_op jit(solution)/shard_map/all_to_all | solution.py:368
Sparse Core Ops, SparseCore 0:
  9.6 77.5 all-gather.1

commit v6 on v4

--- a/solution.py
+++ b/solution.py
@@ -15,6 +15,7 @@
 SEQ = ("z", "y", "core")
 ALL = ("z", "y", "core", "head")
 TURNS = (0, 3, 1, 2)
+ZTURNS = (1, 3, 2)
 
 
 def doc_of(positions, doc_ends):
@@ -194,7 +195,7 @@
             + [part] * len(held),
             out_specs=part,
         ),
-        out_shape=jax.ShapeDtypeStruct((toks, width), F32),
+        out_shape=pltpu.HBM((toks, width), F32),
         compiler_params=params(),
         name="project_near",
     )(place, *[q for piece in pieces for q in piece], *[weight] * count, *held)
@@ -226,7 +227,7 @@
             ],
             out_specs=pl.BlockSpec((slots, tile), lambda i, p: (0, i)),
         ),
-        out_shape=jax.ShapeDtypeStruct((slots, width), BF16),
+        out_shape=pltpu.HBM((slots, width), BF16),
         compiler_params=params(),
         name="project_far",
     )(place, pick, *piece, weight, near)
@@ -307,6 +308,10 @@
     weight = lax.all_gather(value_weight, ("head", "y", "core"), axis=0, tiled=True)
     weight = weight.reshape(n_head, -1, value_weight.shape[1])
 
+    queries, key_vectors, output_grad = (
+        pltpu.with_memory_space_constraint(array, pltpu.HBM)
+        for array in (queries, key_vectors, output_grad)
+    )
     state = local_states(decay_rate, doc_lengths, queries, output_grad, head_local // 2)
     blocks = tok_rows // ROWS_BLK
     per = blocks * CAPACITY
@@ -332,6 +337,7 @@
         decay_rate, doc_lengths, queries, key_vectors, output_grad, head_local // 2
     )
 
+    state_in, intra = lax.optimization_barrier((state_in, intra))
     doc_ends = jnp.cumsum(doc_lengths)
     ranks = jnp.arange(n_seq, dtype=jnp.int32)
     doc_last = doc_of((ranks + 1) * tok_rows - 1, doc_ends)
@@ -363,7 +369,7 @@
     )
     column = offsets.reshape(-1, 1)
     row = offsets.reshape(n_z, plane, blocks, CAPACITY).transpose(1, 2, 0, 3).reshape(1, -1)
-    near_z = (z_rank + turns) % n_z
+    near_z = (z_rank - jnp.array((0,) + ZTURNS, jnp.int32)) % n_z
     theirs = carried[:, share + 1].reshape(n_z, plane, ROWS_BLK)
     theirs = lax.dynamic_slice_in_dim(theirs, seq_rank % plane, 1, 1)[:, 0]
     theirs = theirs[near_z].astype(jnp.int32)
@@ -378,18 +384,24 @@
         mine.append(lax.ppermute(own[turn], "head", shift(n_head, TURNS[turn])))
     place = (head_rank - turns) % n_head
 
-    pieces = []
-    for turn, rows in enumerate(mine):
+    def spread(rows, flip):
         below = lax.ppermute(rows, "z", shift(n_z, 1))
         above = lax.ppermute(rows, "z", shift(n_z, -1))
-        if turn % 2 == 0:
-            across_z = lax.ppermute(below, "z", shift(n_z, 1))
-        else:
-            across_z = lax.ppermute(above, "z", shift(n_z, -1))
-        pieces.append((rows, below, above, across_z))
-
-    near = project_near(place, pieces[:2], (0, 1), weight, (), 256)
-    near = project_near(place, pieces[2:3], (2,), weight, (near,), 256)
+        relay = lax.ppermute(above if flip else below, "z", shift(n_z, -1 if flip else 1))
+        return rows, below, above, relay
+
+    groups = [spread(mine[0], False)]
+    mine[1], *_ = lax.optimization_barrier((mine[1],) + groups[0][1:3])
+    groups.append(spread(mine[1], True))
+    mine[2], mine[3], _ = lax.optimization_barrier((mine[2], mine[3], groups[0][3]))
+    groups.append(spread(mine[2], False))
+    groups.append(spread(mine[3], True))
+    pieces = [
+        [pltpu.with_memory_space_constraint(q, pltpu.HBM) for q in group] for group in groups
+    ]
+
+    near = project_near(place, pieces[:2], (0, 1), weight, (), 512)
+    near = project_near(place, pieces[2:3], (2,), weight, (near,), 512)
     send = project_far(place, pick, pieces[3], 3, weight, near, 512)
     send = send.reshape(devices_all, per, -1)
     got = lax.all_to_all(send, ALL, split_axis=0, concat_axis=0, tiled=True)

time: 189 us -> 185 us (0.979)
  blocking collectives: 0 us -> 15 us
  local copies, waits for them, and re-layouts: 20.6 us -> 8.25 us
  waiting for transfers between devices: 82.2 us -> 72.4 us
  Pallas kernels: 30.8 us -> 34 us
    all_to_all x0 -> x1, blocking collectives: none -> 15 us  [per_device(): lax.all_to_all(jnp.concatenate([carried_all, note], axis=1), SEQ, split_a...]
    unnamed x48 -> x44, local copies, waits for them, and re-layouts: 16 us -> 5.3 us
    all_to_all x1, waiting for transfers between devices: 8.19 us -> 1.79 us  [per_device(): lax.all_to_all(state.reshape(n_seq, share, head_dim), SEQ, split_axis=0,...]
    all_to_all x1 -> x0, starting transfers between devices: 3.74 us -> none  [per_device(): lax.all_to_all(jnp.concatenate([carried_all, note], axis=1), SEQ, split_a...]
    all_to_all x1 -> x0, waiting for transfers between devices: 3.31 us -> none  [per_device(): lax.all_to_all(jnp.concatenate([carried_all, note], axis=1), SEQ, split_a...]
    ppermute x12, starting transfers between devices: 10.3 us -> 12.5 us  [the longest x4 4.98 us: spread(): above = lax.ppermute(rows, 'z', shift(n_z, -1))]
    all_to_all x1, starting transfers between devices: 9.13 us -> 11.2 us  [per_device(): got = lax.all_to_all(send, ALL, split_axis=0, concat_axis=0, tiled=True)]
  transfers between devices with their start and end apart: 19 -> 18, of which waited for: 7 -> 8; matrix products, arithmetic and copies ran while one was open for 4% -> 3% of each run, Pallas kernels for 12% -> 13%
where the time goes in v6:
time: 185 us
  waiting for transfers between devices  72.4 us (39%)
  starting transfers between devices  37.8 us (20%)
  Pallas kernels  34 us (18%)
  blocking collectives  15 us (8%)
  between operations  14.4 us (8%)
  local copies, waits for them, and re-layouts  8.25 us (4%)
  other arithmetic  2.24 us (1%)
    all_to_all x1, waiting for transfers between devices, per_device(): got = lax.all_to_all(send, ALL, split_axis=0, concat_axis=0, tiled=True)  40.3 us
    ppermute x3, waiting for transfers between devices, per_device(): mine.append(lax.ppermute(own[turn], 'head', shift(n_head, TURNS[turn])))  19.9 us
    all_to_all x1, blocking collectives, per_device(): lax.all_to_all(jnp.concatenate([carried_all, note], axis=1), SEQ, split_a...  15 us
    pallas_call x2, Pallas kernels, project_near(): pl.pallas_call(functools.partial(near_body, count), grid_spec=pltpu.Prefe...  14.4 us
    all_to_all x1, starting transfers between devices, per_device(): got = lax.all_to_all(send, ALL, split_axis=0, concat_axis=0, tiled=True)  11.2 us
    all_to_all x1, starting transfers between devices, per_device(): lax.all_to_all(state.reshape(n_seq, share, head_dim), SEQ, split_axis=0,...  9.62 us
    ppermute x4, waiting for transfers between devices, spread(): lax.ppermute(above if flip else below, 'z', shift(n_z, -1 if flip else 1))  7.4 us
    pallas_call x1, Pallas kernels, project_far(): pl.pallas_call(far_body, grid_spec=pltpu.PrefetchScalarGridSpec(num_scala...  7.39 us
  transfers between devices with their start and end apart: 18, of which 8 were waited for; matrix products, arithmetic and copies ran while one was open for 3% of the time, Pallas kernels for 13%

profile of v6, /device:TPU:1, one launch (start us, length us, event | category | flops | bytes accessed | tf_op | source)
XLA Modules:
  0.0 184.5 jit_solution(2444554810963960752)
XLA Ops:
  6.5 0.0 all-gather.2.cloned.1.call-start
  6.6 0.7 all-gather.2.cloned.1.call-update
  7.3 0.6 copy-done.3
  7.9 0.7 copy-done.5
  8.6 3.0 %local_states.1 = bf16[8,128,128]{2,1,0:T(8,128)(2,1)} custom-call(f32[8]{0:T(128)S(1)} %copy-done.3, s32[4]{0:T(128)S(1)} %copy-done.5, bf16[512,1024]{1,0:T(8,128)(2,1)} %query_ref.3, bf16[512,1024]{1,0:T(8,128)(2,1)} %grad_ref.3), custom_call_target="tpu_custom_call" | custom-call | tf_op jit(solution)/shard_map/local_states/pallas_call | solution.py:65
  11.6 9.6 %all-to-all-start = ((bf16[32,32,128]{2,1,0:T(8,128)(2,1)}), bf16[32,32,128]{2,1,0:T(8,128)(2,1)S(1)}, u32[]{:S(2)}, u32[]{:S(2)}) async-start(bf16[32,32,128]{2,1,0:T(8,128)(2,1)} %bitcast.4), calls=%async_computation | async-start | bytes 524288 | tf_op jit(solution)/shard_map/all_to_all | solution.py:333
  21.3 0.2 convert_reduce_fusion.1
  21.5 0.1 iota_add_fusion
  21.6 0.7 select_reduce_fusion
  22.3 0.1 maximum_bitcast_fusion
  22.5 0.6 dynamic_slice.9
  23.7 0.2 reduce-window.8
  23.9 4.5 %within.1.intra_ref = f32[512,1024]{1,0:T(8,128)S(1)} custom-call(f32[8]{0:T(128)S(1)} %copy-done.4, s32[4]{0:T(128)S(1)} %copy-done.6, bf16[512,1024]{1,0:T(8,128)(2,1)} %query_ref.3, bf16[512,1024]{1,0:T(8,128)(2,1)} %key_ref.3, bf16[512,1024]{1,0:T(8,128)(2,1)} %grad_ref.3), custom_call_target="tpu_custom_call" | custom-call | tf_op jit(solution)/shard_map/within/pallas_call | solution.py:107
  28.4 0.1 convert_reduce_fusion.3
  28.5 1.8 all-to-all-done
  30.2 0.4 convolution_convert_fusion
  30.7 0.1 copy.39
  30.8 15.0 %all_to_all.15 = bf16[32,40,128]{2,1,0:T(8,128)(2,1)S(1)} all-to-all(bf16[32,40,128]{2,1,0:T(8,128)(2,1)S(1)} %copy.39), channel_id=1, replica_groups=mesh['z'=4,'y'=4,'core'=2,'head'=4] {'z','y','core'}, dimensions={0} | all-to-all | bytes 655360 | tf_op jit(solution)/shard_map/all_to_all | solution.py:358
  45.9 2.3 %across.1 = (bf16[128,1024]{1,0:T(8,128)(2,1)S(1)}, bf16[128,1024]{1,0:T(8,128)(2,1)S(1)}, bf16[128,1024]{1,0:T(8,128)(2,1)S(1)}, bf16[128,1024]{1,0:T(8,128)(2,1)S(1)}) custom-call(f32[8]{0:T(128)S(1)} %copy-done.4, s32[4]{0:T(128)S(1)} %copy-done.6, bf16[512,1024]{1,0:T(8,128)(2,1)} %key_ref.3, bf16[8,128,128]{2,1,0:T(8,128)(2,1)S(1)} %bitcast.39, ...), custom_call_target="tpu_custom_call" | custom-call | tf_op jit(solution)/shard_map/across/pallas_call | solution.py:145
  48.2 0.6 collective-permute-start.2
  48.9 2.1 %collective-permute-start.10 = (bf16[128,1024]{1,0:T(8,128)(2,1)S(1)}, bf16[128,1024]{1,0:T(8,128)(2,1)S(1)}, u32[]{:S(2)}, u32[]{:S(2)}) collective-permute-start(bf16[128,1024]{1,0:T(8,128)(2,1)S(1)} %get-tuple-element.18.refs_0_), channel_id=1, source_target_pairs={{0,96},{32,0},{64,32},{96,64},{1,97},{33,1},{65,33},{97,65},{2,98}... | collective-permute-start | bytes 786440 | tf_op jit(solution)/shard_map/ppermute | solution.py:389
  51.0 2.6 %collective-permute-start.11 = (bf16[128,1024]{1,0:T(8,128)(2,1)S(1)}, bf16[128,1024]{1,0:T(8,128)(2,1)S(1)}, u32[]{:S(2)}, u32[]{:S(2)}) collective-permute-start(bf16[128,1024]{1,0:T(8,128)(2,1)S(1)} %get-tuple-element.21), channel_id=1, source_target_pairs={{0,3},{1,0},{2,1},{3,2},{4,7},{5,4},{6,5},{7,6},{8,11},{9,8},{10,9... | collective-permute-start | bytes 786440 | tf_op jit(solution)/shard_map/ppermute | solution.py:384
  53.6 1.7 collective-permute-start.1
  55.4 1.7 collective-permute-done.2.refs_1_
  57.1 0.0 collective-permute-start.3
  57.2 7.5 %collective-permute-done.11.refs_4_ = bf16[128,1024]{1,0:T(8,128)(2,1)S(1)} collective-permute-done((bf16[128,1024]{1,0:T(8,128)(2,1)S(1)}, bf16[128,1024]{1,0:T(8,128)(2,1)S(1)}, u32[]{:S(2)}, u32[]{:S(2)}) %collective-permute-start.11) | collective-permute-done | bytes 262176 | tf_op jit(solution)/shard_map/ppermute | solution.py:384
  64.6 0.1 collective-permute-start.13
  64.7 1.4 collective-permute-start.12
  66.1 2.5 %collective-permute-done.refs_0_ = bf16[128,1024]{1,0:T(8,128)(2,1)S(1)} collective-permute-done((bf16[128,1024]{1,0:T(8,128)(2,1)S(1)}, bf16[128,1024]{1,0:T(8,128)(2,1)S(1)}, u32[]{:S(2)}, u32[]{:S(2)}) %collective-permute-start) | collective-permute-done | bytes 262176 | tf_op jit(solution)/shard_map/ppermute | solution.py:384
  68.6 9.9 %collective-permute-done.1.refs_0_ = bf16[128,1024]{1,0:T(8,128)(2,1)S(1)} collective-permute-done((bf16[128,1024]{1,0:T(8,128)(2,1)S(1)}, bf16[128,1024]{1,0:T(8,128)(2,1)S(1)}, u32[]{:S(2)}, u32[]{:S(2)}) %collective-permute-start.1) | collective-permute-done | bytes 262176 | tf_op jit(solution)/shard_map/ppermute | solution.py:384
  78.5 0.0 collective-permute-done.3.refs_3_
  78.5 0.1 collective-permute-start.7
  78.6 2.7 %collective-permute-start.5 = (bf16[128,1024]{1,0:T(8,128)(2,1)S(1)}, bf16[128,1024]{1,0:T(8,128)(2,1)S(1)}, u32[]{:S(2)}, u32[]{:S(2)}) collective-permute-start(bf16[128,1024]{1,0:T(8,128)(2,1)S(1)} %collective-permute-done.1.refs_0_), channel_id=1, source_target_pairs={{0,96},{32,0},{64,32},{96,64},{1,97},{33,1},{65,33},{97,65},{2,98}... | collective-permute-start | bytes 786440 | tf_op jit(solution)/shard_map/ppermute | solution.py:389
  81.3 0.6 gather_fusion
  81.9 0.2 convert_reduce_fusion
  82.1 0.1 collective-permute-start.8
  82.2 0.0 collective-permute-done.13.refs_6_
  82.2 1.4 collective-permute-start.4
  83.7 1.3 collective-permute-start.14
  85.0 0.7 collective-permute-done.7.refs_1_
  85.7 0.0 collective-permute-start.9
  85.7 0.0 collective-permute-done.5.refs_2_
  85.7 2.7 %collective-permute-start.6 = (bf16[128,1024]{1,0:T(8,128)(2,1)S(1)}, bf16[128,1024]{1,0:T(8,128)(2,1)}, u32[]{:S(2)}, u32[]{:S(2)}) collective-permute-start(bf16[128,1024]{1,0:T(8,128)(2,1)S(1)} %collective-permute-done.5.refs_2_), channel_id=1, source_target_pairs={{0,96},{32,0},{64,32},{96,64},{1,97},{33,1},{65,33},{97,65},{2,98}... | collective-permute-start | bytes 786440 | tf_op jit(solution)/shard_map/ppermute | solution.py:390
  88.4 0.1 add_bitcast_fusion
  88.5 0.4 fusion.pick
  88.9 7.4 %collective-permute-done.14.refs_7_ = bf16[128,1024]{1,0:T(8,128)(2,1)} collective-permute-done((bf16[128,1024]{1,0:T(8,128)(2,1)}, bf16[128,1024]{1,0:T(8,128)(2,1)}, u32[]{:S(2)}, u32[]{:S(2)}) %collective-permute-start.14) | collective-permute-done | bytes 262176 | tf_op jit(solution)/shard_map/ppermute | solution.py:390
  96.3 8.2 %project_near.2.refs_5_ = f32[512,1536]{1,0:T(8,128)} custom-call(s32[4]{0:T(128)S(1)} %and_select_fusion.1.place, bf16[128,1024]{1,0:T(8,128)(2,1)} %copy-done.2, bf16[128,1024]{1,0:T(8,128)(2,1)} %copy-done.10, bf16[128,1024]{1,0:T(8,128)(2,1)} %copy-done.11, bf16[128,1024]{1,0:T(8,128)(2,1)} %copy-done.13, bf16[128,1024]{1,0:T(8,128)(2,1)} %copy-done.12, ...), custom_call_target="tpu_custom_call" | custom-call | tf_op jit(solution)/shard_map/project_near/pallas_call | solution.py:188
  104.5 0.0 copy-start
  104.6 1.9 %copy-done = f32[512,1536]{1,0:T(8,128)S(1)} copy-done((f32[512,1536]{1,0:T(8,128)S(1)}, f32[512,1536]{1,0:T(8,128)}, u32[]{:S(2)}) %copy-start) | copy-done | bytes 3145752
  106.4 6.2 %project_near.3.refs_5_ = f32[512,1536]{1,0:T(8,128)} custom-call(s32[4]{0:T(128)S(1)} %and_select_fusion.1.place, bf16[128,1024]{1,0:T(8,128)(2,1)} %copy-done.9, bf16[128,1024]{1,0:T(8,128)(2,1)} %collective-permute-done.7.refs_1_, bf16[128,1024]{1,0:T(8,128)(2,1)} %collective-permute-done.8.refs_2_, bf16[128,1024]{1,0:T(8,128)(2,1)} %collective-permute-done.9.refs_3_, ...), custom_call_target="tpu_custom_call" | custom-call | tf_op jit(solution)/shard_map/project_near/pallas_call | solution.py:188
  112.6 0.0 copy-start.1
  112.6 1.9 %copy-done.1 = f32[512,1536]{1,0:T(8,128)S(1)} copy-done((f32[512,1536]{1,0:T(8,128)S(1)}, f32[512,1536]{1,0:T(8,128)}, u32[]{:S(2)}) %copy-start.1) | copy-done | bytes 3145752
  114.5 7.4 %project_far.1 = bf16[1024,1536]{1,0:T(8,128)(2,1)} custom-call(s32[4]{0:T(128)S(1)} %and_select_fusion.1.place, bf16[1024,512]{1,0:T(8,128)(2,1)S(1)} %fusion.pick, bf16[128,1024]{1,0:T(8,128)(2,1)} %copy-done.8, bf16[128,1024]{1,0:T(8,128)(2,1)} %collective-permute-done.4.refs_1_, bf16[128,1024]{1,0:T(8,128)(2,1)} %copy-done.14, ...), custom_call_target="tpu_custom_call" | custom-call | tf_op jit(solution)/shard_map/project_far/pallas_call | solution.py:217
  121.9 11.2 %all-to-all-start.2 = ((bf16[128,8,1536]{2,1,0:T(8,128)(2,1)}), bf16[128,8,1536]{2,1,0:T(8,128)(2,1)S(1)}, u32[]{:S(2)}, u32[]{:S(2)}) async-start(bf16[128,8,1536]{2,1,0:T(8,128)(2,1)} %bitcast.45), calls=%async_computation.2 | async-start | bytes 6291456 | tf_op jit(solution)/shard_map/all_to_all | solution.py:407
  133.2 1.0 fusion.35
  134.2 0.1 copy.48
  134.2 0.1 copy.49
  134.3 0.1 copy.42
  134.4 0.1 sub.71
  134.5 0.1 sub.76.column_ref
  134.6 0.2 copy.43
  134.8 0.1 reshape.207.row_ref
  134.9 40.3 %all-to-all-done.2 = bf16[128,8,1536]{2,1,0:T(8,128)(2,1)S(1)} async-done(((bf16[128,8,1536]{2,1,0:T(8,128)(2,1)}), bf16[128,8,1536]{2,1,0:T(8,128)(2,1)S(1)}, u32[]{:S(2)}, u32[]{:S(2)}) %all-to-all-start.2) | async-done | bytes 3145760 | tf_op jit(solution)/shard_map/all_to_all | solution.py:407
  175.2 2.5 %merge.1 = bf16[1,128,2,6144]{3,2,1,0:T(2,128)(2,1)} custom-call(s32[256,1]{1,0:T(8,128)S(1)} %sub.76.column_ref, s32[1,256]{1,0:T(1,128)S(1)} %reshape.207.row_ref, bf16[4,32,8,1536]{3,2,1,0:T(8,128)(2,1)S(1)} %bitcast.38), custom_call_target="tpu_custom_call" | custom-call | tf_op jit(solution)/shard_map/merge/pallas_call | solution.py:254
  (62 shorter events, 0.3 us)
Async XLA Ops:
  6.5 15.9 %copy-start.4 = (f32[8]{0:T(128)S(1)}, f32[8]{0:T(128)}, u32[]{:S(2)}) copy-start(f32[8]{0:T(128)} %rate_ref.5) | copy-start | bytes 100
  6.5 17.2 %copy-start.6 = (s32[4]{0:T(128)S(1)}, s32[4]{0:T(128)}, u32[]{:S(2)}) copy-start(s32[4]{0:T(128)} %lengths_ref.5) | copy-start | bytes 52
  6.5 14.7 %copy-start.16 = (s32[512,1]{0,1:T(1,128)S(1)}, s32[512,1]{0,1:T(1,128)}, u32[]{:S(2)}) copy-start(s32[512,1]{0,1:T(1,128)} %param.16) | copy-start | bytes 6148
  6.5 15.0 %copy-start.17 = (s32[512]{0:T(512)S(1)}, s32[512]{0:T(512)}, u32[]{:S(2)}) copy-start(s32[512]{0:T(512)} %param.17) | copy-start | bytes 6148
  6.5 89.7 %all-gather.2.cloned.1.call-start = ((), (), s32[]{:S(2)}) async-start(), calls=%async_computation.3 | async-start | bytes 12976128 | tf_op jit(solution)/shard_map/all_gather | solution.py:308
  7.3 0.7 copy-start.3
  7.9 0.7 copy-start.5
  11.6 18.7 %all-to-all-start = ((bf16[32,32,128]{2,1,0:T(8,128)(2,1)}), bf16[32,32,128]{2,1,0:T(8,128)(2,1)S(1)}, u32[]{:S(2)}, u32[]{:S(2)}) async-start(bf16[32,32,128]{2,1,0:T(8,128)(2,1)} %bitcast.4), calls=%async_computation | async-start | bytes 524288 | tf_op jit(solution)/shard_map/all_to_all | solution.py:333
  30.2 26.9 %copy-start.19 = (s32[4]{0:T(128)S(1)}, s32[4]{0:T(128)}, u32[]{:S(2)}) copy-start(s32[4]{0:T(128)} %constant.125) | copy-start | bytes 52
  30.2 26.9 %copy-start.18 = (s32[4]{0:T(128)S(1)}, s32[4]{0:T(128)}, u32[]{:S(2)}) copy-start(s32[4]{0:T(128)} %constant.126) | copy-start | bytes 52
  45.9 58.6 %copy-start.7 = (bf16[32,40,128]{2,1,0:T(8,128)(2,1)}, bf16[32,40,128]{2,1,0:T(8,128)(2,1)S(1)}, u32[]{:S(2)}) copy-start(bf16[32,40,128]{2,1,0:T(8,128)(2,1)S(1)} %all_to_all.15) | copy-start | bytes 983044
  48.2 48.1 %copy-start.2 = (bf16[128,1024]{1,0:T(8,128)(2,1)}, bf16[128,1024]{1,0:T(8,128)(2,1)S(1)}, u32[]{:S(2)}) copy-start(bf16[128,1024]{1,0:T(8,128)(2,1)S(1)} %get-tuple-element.18.refs_0_) | copy-start | bytes 786436
  48.2 8.8 %collective-permute-start.2 = (bf16[128,1024]{1,0:T(8,128)(2,1)S(1)}, bf16[128,1024]{1,0:T(8,128)(2,1)S(1)}, u32[]{:S(2)}, u32[]{:S(2)}) collective-permute-start(bf16[128,1024]{1,0:T(8,128)(2,1)S(1)} %get-tuple-element.18.refs_0_), channel_id=1, source_target_pairs={{0,32},{32,64},{64,96},{96,0},{1,33},{33,65},{65,97},{97,1},{2,34}... | collective-permute-start | bytes 786440 | tf_op jit(solution)/shard_map/ppermute | solution.py:388
  48.9 8.3 %collective-permute-start.10 = (bf16[128,1024]{1,0:T(8,128)(2,1)S(1)}, bf16[128,1024]{1,0:T(8,128)(2,1)S(1)}, u32[]{:S(2)}, u32[]{:S(2)}) collective-permute-start(bf16[128,1024]{1,0:T(8,128)(2,1)S(1)} %get-tuple-element.18.refs_0_), channel_id=1, source_target_pairs={{0,96},{32,0},{64,32},{96,64},{1,97},{33,1},{65,33},{97,65},{2,98}... | collective-permute-start | bytes 786440 | tf_op jit(solution)/shard_map/ppermute | solution.py:389
  51.0 13.7 %collective-permute-start.11 = (bf16[128,1024]{1,0:T(8,128)(2,1)S(1)}, bf16[128,1024]{1,0:T(8,128)(2,1)S(1)}, u32[]{:S(2)}, u32[]{:S(2)}) collective-permute-start(bf16[128,1024]{1,0:T(8,128)(2,1)S(1)} %get-tuple-element.21), channel_id=1, source_target_pairs={{0,3},{1,0},{2,1},{3,2},{4,7},{5,4},{6,5},{7,6},{8,11},{9,8},{10,9... | collective-permute-start | bytes 786440 | tf_op jit(solution)/shard_map/ppermute | solution.py:384
  53.6 15.0 %collective-permute-start = (bf16[128,1024]{1,0:T(8,128)(2,1)S(1)}, bf16[128,1024]{1,0:T(8,128)(2,1)S(1)}, u32[]{:S(2)}, u32[]{:S(2)}) collective-permute-start(bf16[128,1024]{1,0:T(8,128)(2,1)S(1)} %get-tuple-element.16), channel_id=1, source_target_pairs={{0,1},{1,2},{2,3},{3,0},{4,5},{5,6},{6,7},{7,4},{8,9},{9,10},{10,1... | collective-permute-start | bytes 786440 | tf_op jit(solution)/shard_map/ppermute | solution.py:384
  53.6 24.9 %collective-permute-start.1 = (bf16[128,1024]{1,0:T(8,128)(2,1)S(1)}, bf16[128,1024]{1,0:T(8,128)(2,1)S(1)}, u32[]{:S(2)}, u32[]{:S(2)}) collective-permute-start(bf16[128,1024]{1,0:T(8,128)(2,1)S(1)} %get-tuple-element.17), channel_id=1, source_target_pairs={{0,2},{1,3},{2,0},{3,1},{4,6},{5,7},{6,4},{7,5},{8,10},{9,11},{10,... | collective-permute-start | bytes 786440 | tf_op jit(solution)/shard_map/ppermute | solution.py:384
  57.1 39.2 %copy-start.10 = (bf16[128,1024]{1,0:T(8,128)(2,1)}, bf16[128,1024]{1,0:T(8,128)(2,1)S(1)}, u32[]{:S(2)}) copy-start(bf16[128,1024]{1,0:T(8,128)(2,1)S(1)} %collective-permute-done.2.refs_1_) | copy-start | bytes 786436
  57.1 21.5 %collective-permute-start.3 = (bf16[128,1024]{1,0:T(8,128)(2,1)S(1)}, bf16[128,1024]{1,0:T(8,128)(2,1)S(1)}, u32[]{:S(2)}, u32[]{:S(2)}) collective-permute-start(bf16[128,1024]{1,0:T(8,128)(2,1)S(1)} %collective-permute-done.2.refs_1_), channel_id=1, source_target_pairs={{0,32},{32,64},{64,96},{96,0},{1,33},{33,65},{65,97},{97,1},{2,34}... | collective-permute-start | bytes 786440 | tf_op jit(solution)/shard_map/ppermute | solution.py:390
  57.2 39.1 %copy-start.11 = (bf16[128,1024]{1,0:T(8,128)(2,1)}, bf16[128,1024]{1,0:T(8,128)(2,1)S(1)}, u32[]{:S(2)}) copy-start(bf16[128,1024]{1,0:T(8,128)(2,1)S(1)} %collective-permute-done.10.refs_2_) | copy-start | bytes 786436
  64.6 31.6 %copy-start.12 = (bf16[128,1024]{1,0:T(8,128)(2,1)}, bf16[128,1024]{1,0:T(8,128)(2,1)S(1)}, u32[]{:S(2)}) copy-start(bf16[128,1024]{1,0:T(8,128)(2,1)S(1)} %collective-permute-done.11.refs_4_) | copy-start | bytes 786436
  64.6 17.6 %collective-permute-start.13 = (bf16[128,1024]{1,0:T(8,128)(2,1)S(1)}, bf16[128,1024]{1,0:T(8,128)(2,1)}, u32[]{:S(2)}, u32[]{:S(2)}) collective-permute-start(bf16[128,1024]{1,0:T(8,128)(2,1)S(1)} %collective-permute-done.11.refs_4_), channel_id=1, source_target_pairs={{0,96},{32,0},{64,32},{96,64},{1,97},{33,1},{65,33},{97,65},{2,98}... | collective-permute-start | bytes 786440 | tf_op jit(solution)/shard_map/ppermute | solution.py:389
  64.7 18.9 %collective-permute-start.12 = (bf16[128,1024]{1,0:T(8,128)(2,1)S(1)}, bf16[128,1024]{1,0:T(8,128)(2,1)S(1)}, u32[]{:S(2)}, u32[]{:S(2)}) collective-permute-start(bf16[128,1024]{1,0:T(8,128)(2,1)S(1)} %collective-permute-done.11.refs_4_), channel_id=1, source_target_pairs={{0,32},{32,64},{64,96},{96,0},{1,33},{33,65},{65,97},{97,1},{2,34}... | collective-permute-start | bytes 786440 | tf_op jit(solution)/shard_map/ppermute | solution.py:388
  68.6 35.9 %copy-start.9 = (bf16[128,1024]{1,0:T(8,128)(2,1)}, bf16[128,1024]{1,0:T(8,128)(2,1)S(1)}, u32[]{:S(2)}) copy-start(bf16[128,1024]{1,0:T(8,128)(2,1)S(1)} %collective-permute-done.refs_0_) | copy-start | bytes 786436
  78.5 26.0 %copy-start.8 = (bf16[128,1024]{1,0:T(8,128)(2,1)}, bf16[128,1024]{1,0:T(8,128)(2,1)S(1)}, u32[]{:S(2)}) copy-start(bf16[128,1024]{1,0:T(8,128)(2,1)S(1)} %collective-permute-done.1.refs_0_) | copy-start | bytes 786436
  78.5 17.8 %copy-start.13 = (bf16[128,1024]{1,0:T(8,128)(2,1)}, bf16[128,1024]{1,0:T(8,128)(2,1)S(1)}, u32[]{:S(2)}) copy-start(bf16[128,1024]{1,0:T(8,128)(2,1)S(1)} %collective-permute-done.3.refs_3_) | copy-start | bytes 786436
  78.5 7.2 %collective-permute-start.7 = (bf16[128,1024]{1,0:T(8,128)(2,1)S(1)}, bf16[128,1024]{1,0:T(8,128)(2,1)}, u32[]{:S(2)}, u32[]{:S(2)}) collective-permute-start(bf16[128,1024]{1,0:T(8,128)(2,1)S(1)} %collective-permute-done.refs_0_), channel_id=1, source_target_pairs={{0,32},{32,64},{64,96},{96,0},{1,33},{33,65},{65,97},{97,1},{2,34}... | collective-permute-start | bytes 786440 | tf_op jit(solution)/shard_map/ppermute | solution.py:388
  78.6 7.1 %collective-permute-start.5 = (bf16[128,1024]{1,0:T(8,128)(2,1)S(1)}, bf16[128,1024]{1,0:T(8,128)(2,1)S(1)}, u32[]{:S(2)}, u32[]{:S(2)}) collective-permute-start(bf16[128,1024]{1,0:T(8,128)(2,1)S(1)} %collective-permute-done.1.refs_0_), channel_id=1, source_target_pairs={{0,96},{32,0},{64,32},{96,64},{1,97},{33,1},{65,33},{97,65},{2,98}... | collective-permute-start | bytes 786440 | tf_op jit(solution)/shard_map/ppermute | solution.py:389
  82.1 22.4 %collective-permute-start.8 = (bf16[128,1024]{1,0:T(8,128)(2,1)S(1)}, bf16[128,1024]{1,0:T(8,128)(2,1)}, u32[]{:S(2)}, u32[]{:S(2)}) collective-permute-start(bf16[128,1024]{1,0:T(8,128)(2,1)S(1)} %collective-permute-done.refs_0_), channel_id=1, source_target_pairs={{0,96},{32,0},{64,32},{96,64},{1,97},{33,1},{65,33},{97,65},{2,98}... | collective-permute-start | bytes 786440 | tf_op jit(solution)/shard_map/ppermute | solution.py:389
  82.2 30.4 %collective-permute-start.4 = (bf16[128,1024]{1,0:T(8,128)(2,1)S(1)}, bf16[128,1024]{1,0:T(8,128)(2,1)}, u32[]{:S(2)}, u32[]{:S(2)}) collective-permute-start(bf16[128,1024]{1,0:T(8,128)(2,1)S(1)} %collective-permute-done.1.refs_0_), channel_id=1, source_target_pairs={{0,32},{32,64},{64,96},{96,0},{1,33},{33,65},{65,97},{97,1},{2,34}... | collective-permute-start | bytes 786440 | tf_op jit(solution)/shard_map/ppermute | solution.py:388
  83.7 4.7 %copy-start.15 = (bf16[128,1024]{1,0:T(8,128)(2,1)}, bf16[128,1024]{1,0:T(8,128)(2,1)S(1)}, u32[]{:S(2)}) copy-start(bf16[128,1024]{1,0:T(8,128)(2,1)S(1)} %collective-permute-done.12.refs_5_) | copy-start | bytes 786436
  83.7 12.6 %collective-permute-start.14 = (bf16[128,1024]{1,0:T(8,128)(2,1)}, bf16[128,1024]{1,0:T(8,128)(2,1)}, u32[]{:S(2)}, u32[]{:S(2)}) collective-permute-start(bf16[128,1024]{1,0:T(8,128)(2,1)} %collective-permute-done.13.refs_6_), channel_id=1, source_target_pairs={{0,96},{32,0},{64,32},{96,64},{1,97},{33,1},{65,33},{97,65},{2,98}... | collective-permute-start | bytes 786440 | tf_op jit(solution)/shard_map/ppermute | solution.py:390
  85.7 18.8 %collective-permute-start.9 = (bf16[128,1024]{1,0:T(8,128)(2,1)}, bf16[128,1024]{1,0:T(8,128)(2,1)}, u32[]{:S(2)}, u32[]{:S(2)}) collective-permute-start(bf16[128,1024]{1,0:T(8,128)(2,1)} %collective-permute-done.7.refs_1_), channel_id=1, source_target_pairs={{0,32},{32,64},{64,96},{96,0},{1,33},{33,65},{65,97},{97,1},{2,34}... | collective-permute-start | bytes 786440 | tf_op jit(solution)/shard_map/ppermute | solution.py:390
  85.7 18.8 %copy-start.14 = (bf16[128,1024]{1,0:T(8,128)(2,1)}, bf16[128,1024]{1,0:T(8,128)(2,1)S(1)}, u32[]{:S(2)}) copy-start(bf16[128,1024]{1,0:T(8,128)(2,1)S(1)} %collective-permute-done.5.refs_2_) | copy-start | bytes 786436
  85.7 26.9 %collective-permute-start.6 = (bf16[128,1024]{1,0:T(8,128)(2,1)S(1)}, bf16[128,1024]{1,0:T(8,128)(2,1)}, u32[]{:S(2)}, u32[]{:S(2)}) collective-permute-start(bf16[128,1024]{1,0:T(8,128)(2,1)S(1)} %collective-permute-done.5.refs_2_), channel_id=1, source_target_pairs={{0,96},{32,0},{64,32},{96,64},{1,97},{33,1},{65,33},{97,65},{2,98}... | collective-permute-start | bytes 786440 | tf_op jit(solution)/shard_map/ppermute | solution.py:390
  104.5 1.9 %copy-start = (f32[512,1536]{1,0:T(8,128)S(1)}, f32[512,1536]{1,0:T(8,128)}, u32[]{:S(2)}) copy-start(f32[512,1536]{1,0:T(8,128)} %project_near.2.refs_5_) | copy-start | bytes 9437188
  112.6 1.9 %copy-start.1 = (f32[512,1536]{1,0:T(8,128)S(1)}, f32[512,1536]{1,0:T(8,128)}, u32[]{:S(2)}) copy-start(f32[512,1536]{1,0:T(8,128)} %project_near.3.refs_5_) | copy-start | bytes 9437188
  121.9 53.3 %all-to-all-start.2 = ((bf16[128,8,1536]{2,1,0:T(8,128)(2,1)}), bf16[128,8,1536]{2,1,0:T(8,128)(2,1)S(1)}, u32[]{:S(2)}, u32[]{:S(2)}) async-start(bf16[128,8,1536]{2,1,0:T(8,128)(2,1)} %bitcast.45), calls=%async_computation.2 | async-start | bytes 6291456 | tf_op jit(solution)/shard_map/all_to_all | solution.py:407
Sparse Core Ops, SparseCore 0:
  9.6 77.5 all-gather.1

commit v7 on v6

--- a/solution.py
+++ b/solution.py
@@ -159,78 +159,76 @@
     )(rates, lengths, keys, states, intra)
 
 
-def times(rows, weight):
-    rows = jnp.concatenate([part[...] for part in rows], axis=0)
-    return lax.dot_general(
-        rows, weight[0], (((1,), (1,)), ((), ())), preferred_element_type=F32
-    )
-
-
-def near_body(count, place, *refs):
-    out_ref = refs[-1]
-    each = len(TURNS)
+def times(groups, weights):
     total = None
-    for k in range(count):
-        part = times(refs[k * each : (k + 1) * each], refs[count * each + k])
+    for rows, weight in zip(groups, weights):
+        rows = rows[0][...] if len(rows) == 1 else jnp.concatenate([q[...] for q in rows], 0)
+        part = lax.dot_general(
+            rows, weight[0], (((1,), (1,)), ((), ())), preferred_element_type=F32
+        )
         total = part if total is None else total + part
-    for held in refs[count * (each + 1) : -1]:
-        total = total + held[...]
-    out_ref[...] = total
-
-
-def project_near(place, pieces, turns, weight, held, tile):
-    count = len(pieces)
+    return total.astype(BF16)
+
+
+def direct_body(turns, place, *refs):
+    each = (len(refs) - 1 - turns) // turns
+    groups = [refs[k * each : (k + 1) * each] for k in range(turns)]
+    refs[-1][...] = times(groups, refs[turns * each : -1])
+
+
+def project_direct(place, pieces, weight, tile):
+    turns, each = len(pieces), len(pieces[0])
     rows, depth = pieces[0][0].shape
-    toks = rows * len(TURNS)
     width = weight.shape[1]
-    whole = pl.BlockSpec((rows, depth), lambda i, p: (0, 0))
-    part = pl.BlockSpec((toks, tile), lambda i, p: (0, i))
-    return pl.pallas_call(
-        functools.partial(near_body, count),
+    return pl.pallas_call(
+        functools.partial(direct_body, turns),
         grid_spec=pltpu.PrefetchScalarGridSpec(
             num_scalar_prefetch=1,
             grid=(width // tile,),
-            in_specs=[whole] * (count * len(TURNS))
-            + [pl.BlockSpec((1, tile, depth), lambda i, p, k=k: (p[k], i, 0)) for k in turns]
-            + [part] * len(held),
-            out_specs=part,
+            in_specs=[pl.BlockSpec((rows, depth), lambda i, p: (0, 0))] * (turns * each)
+            + [
+                pl.BlockSpec((1, tile, depth), lambda i, p, k=k: (p[k], i, 0))
+                for k in range(turns)
+            ],
+            out_specs=pl.BlockSpec((rows * each, tile), lambda i, p: (0, i)),
         ),
-        out_shape=pltpu.HBM((toks, width), F32),
-        compiler_params=params(),
-        name="project_near",
-    )(place, *[q for piece in pieces for q in piece], *[weight] * count, *held)
-
-
-def far_body(place, pick, *refs):
-    weight, near, out_ref = refs[-3:]
-    total = near[...] + times(refs[:-3], weight)
-    out_ref[...] = jnp.dot(
-        pick[...], total.astype(BF16), preferred_element_type=F32
-    ).astype(BF16)
-
-
-def project_far(place, pick, piece, turn, weight, near, tile):
-    rows, depth = piece[0].shape
+        out_shape=pltpu.HBM((rows * each, width), BF16),
+        compiler_params=params(),
+        name="project_direct",
+    )(place, *[q for piece in pieces for q in piece], *[weight] * turns)
+
+
+def relayed_body(turns, place, pick, direct, *refs):
+    last = times([(q,) for q in refs[:turns]], refs[turns:-1])
+    rows = jnp.concatenate([direct[...], last], axis=0)
+    refs[-1][...] = jnp.dot(pick[...], rows, preferred_element_type=F32).astype(BF16)
+
+
+def project_relayed(place, pick, direct, pieces, weight, tile):
+    turns = len(pieces)
+    rows, depth = pieces[0].shape
     slots, toks = pick.shape
     width = weight.shape[1]
-    whole = pl.BlockSpec((rows, depth), lambda i, p: (0, 0))
-    return pl.pallas_call(
-        far_body,
+    return pl.pallas_call(
+        functools.partial(relayed_body, turns),
         grid_spec=pltpu.PrefetchScalarGridSpec(
             num_scalar_prefetch=1,
             grid=(width // tile,),
-            in_specs=[pl.BlockSpec((slots, toks), lambda i, p: (0, 0))]
-            + [whole] * len(piece)
+            in_specs=[
+                pl.BlockSpec((slots, toks), lambda i, p: (0, 0)),
+                pl.BlockSpec((direct.shape[0], tile), lambda i, p: (0, i)),
+            ]
+            + [pl.BlockSpec((rows, depth), lambda i, p: (0, 0))] * turns
             + [
-                pl.BlockSpec((1, tile, depth), lambda i, p: (p[turn], i, 0)),
-                pl.BlockSpec((toks, tile), lambda i, p: (0, i)),
+                pl.BlockSpec((1, tile, depth), lambda i, p, k=k: (p[k], i, 0))
+                for k in range(turns)
             ],
             out_specs=pl.BlockSpec((slots, tile), lambda i, p: (0, i)),
         ),
         out_shape=pltpu.HBM((slots, width), BF16),
         compiler_params=params(),
-        name="project_far",
-    )(place, pick, *piece, weight, near)
+        name="project_relayed",
+    )(place, pick, direct, *pieces, *[weight] * turns)
 
 
 def merge_body(column_ref, row_ref, rows_ref, out_ref, same_ref):
@@ -400,9 +398,9 @@
         [pltpu.with_memory_space_constraint(q, pltpu.HBM) for q in group] for group in groups
     ]
 
-    near = project_near(place, pieces[:2], (0, 1), weight, (), 512)
-    near = project_near(place, pieces[2:3], (2,), weight, (near,), 512)
-    send = project_far(place, pick, pieces[3], 3, weight, near, 512)
+    direct = project_direct(place, [piece[:3] for piece in pieces], weight, 512)
+    direct = pltpu.with_memory_space_constraint(direct, pltpu.HBM)
+    send = project_relayed(place, pick, direct, [piece[3] for piece in pieces], weight, 512)
     send = send.reshape(devices_all, per, -1)
     got = lax.all_to_all(send, ALL, split_axis=0, concat_axis=0, tiled=True)
     got = got.reshape(n_z, plane * n_head, per, -1)

time: 185 us -> 177 us (0.957)
  waiting for transfers between devices: 72.4 us -> 67.4 us
  local copies, waits for them, and re-layouts: 8.25 us -> 5.22 us
    ppermute x4, waiting for transfers between devices: 7.4 us -> 0.01 us  [spread(): lax.ppermute(above if flip else below, 'z', shift(n_z, -1 if flip else 1))]
    unnamed x44 -> x42, local copies, waits for them, and re-layouts: 5.3 us -> 2.25 us
    pallas_call x3 -> x2, Pallas kernels: 21.7 us -> 22.3 us  [the longest x1 11.6 us: project_relayed(): pl.pallas_call(functools.partial(relayed_body, turns), grid_spec=pltpu.Pr...]
  transfers between devices with their start and end apart: 18 -> 18, of which waited for: 8 -> 9; matrix products, arithmetic and copies ran while one was open for 3% -> 3% of each run, Pallas kernels for 13% -> 12%
where the time goes in v7:
time: 177 us
  waiting for transfers between devices  67.4 us (38%)
  starting transfers between devices  37.4 us (21%)
  Pallas kernels  34.5 us (19%)
  blocking collectives  15 us (8%)
  between operations  14.4 us (8%)
  local copies, waits for them, and re-layouts  5.22 us (3%)
  other arithmetic  2.24 us (1%)
    all_to_all x1, waiting for transfers between devices, per_device(): got = lax.all_to_all(send, ALL, split_axis=0, concat_axis=0, tiled=True)  40.3 us
    ppermute x3, waiting for transfers between devices, per_device(): mine.append(lax.ppermute(own[turn], 'head', shift(n_head, TURNS[turn])))  19.8 us
    all_to_all x1, blocking collectives, per_device(): lax.all_to_all(jnp.concatenate([carried_all, note], axis=1), SEQ, split_a...  15 us
    pallas_call x1, Pallas kernels, project_relayed(): pl.pallas_call(functools.partial(relayed_body, turns), grid_spec=pltpu.Pr...  11.6 us
    all_to_all x1, starting transfers between devices, per_device(): got = lax.all_to_all(send, ALL, split_axis=0, concat_axis=0, tiled=True)  10.8 us
    pallas_call x1, Pallas kernels, project_direct(): pl.pallas_call(functools.partial(direct_body, turns), grid_spec=pltpu.Pre...  10.7 us
    all_to_all x1, starting transfers between devices, per_device(): lax.all_to_all(state.reshape(n_seq, share, head_dim), SEQ, split_axis=0,...  9.62 us
    ppermute x4, starting transfers between devices, spread(): above = lax.ppermute(rows, 'z', shift(n_z, -1))  4.97 us
  transfers between devices with their start and end apart: 18, of which 9 were waited for; matrix products, arithmetic and copies ran while one was open for 3% of the time, Pallas kernels for 12%

profile of v7, /device:TPU:1, one launch (start us, length us, event | category | flops | bytes accessed | tf_op | source)
XLA Modules:
  0.0 176.6 jit_solution(17753593773940431324)
XLA Ops:
  6.5 0.0 all-gather.2.cloned.1.call-start
  6.6 0.7 all-gather.2.cloned.1.call-update
  7.3 0.6 copy-done.1
  7.9 0.7 copy-done.3
  8.6 3.0 %local_states.1 = bf16[8,128,128]{2,1,0:T(8,128)(2,1)} custom-call(f32[8]{0:T(128)S(1)} %copy-done.1, s32[4]{0:T(128)S(1)} %copy-done.3, bf16[512,1024]{1,0:T(8,128)(2,1)} %query_ref.3, bf16[512,1024]{1,0:T(8,128)(2,1)} %grad_ref.3), custom_call_target="tpu_custom_call" | custom-call | tf_op jit(solution)/shard_map/local_states/pallas_call | solution.py:65
  11.6 9.6 %all-to-all-start = ((bf16[32,32,128]{2,1,0:T(8,128)(2,1)}), bf16[32,32,128]{2,1,0:T(8,128)(2,1)S(1)}, u32[]{:S(2)}, u32[]{:S(2)}) async-start(bf16[32,32,128]{2,1,0:T(8,128)(2,1)} %bitcast.4), calls=%async_computation | async-start | bytes 524288 | tf_op jit(solution)/shard_map/all_to_all | solution.py:331
  21.3 0.2 convert_reduce_fusion.1
  21.5 0.1 iota_add_fusion
  21.6 0.7 select_reduce_fusion
  22.3 0.1 maximum_bitcast_fusion
  22.5 0.6 dynamic_slice.9
  23.7 0.2 reduce-window.8
  23.9 4.5 %within.1.intra_ref = f32[512,1024]{1,0:T(8,128)S(1)} custom-call(f32[8]{0:T(128)S(1)} %copy-done.2, s32[4]{0:T(128)S(1)} %copy-done.4, bf16[512,1024]{1,0:T(8,128)(2,1)} %query_ref.3, bf16[512,1024]{1,0:T(8,128)(2,1)} %key_ref.3, bf16[512,1024]{1,0:T(8,128)(2,1)} %grad_ref.3), custom_call_target="tpu_custom_call" | custom-call | tf_op jit(solution)/shard_map/within/pallas_call | solution.py:107
  28.4 0.1 convert_reduce_fusion.3
  28.5 1.8 all-to-all-done
  30.2 0.4 convolution_convert_fusion
  30.7 0.1 copy.39
  30.8 15.0 %all_to_all.15 = bf16[32,40,128]{2,1,0:T(8,128)(2,1)S(1)} all-to-all(bf16[32,40,128]{2,1,0:T(8,128)(2,1)S(1)} %copy.39), channel_id=1, replica_groups=mesh['z'=4,'y'=4,'core'=2,'head'=4] {'z','y','core'}, dimensions={0} | all-to-all | bytes 655360 | tf_op jit(solution)/shard_map/all_to_all | solution.py:356
  45.9 2.3 %across.1 = (bf16[128,1024]{1,0:T(8,128)(2,1)S(1)}, bf16[128,1024]{1,0:T(8,128)(2,1)S(1)}, bf16[128,1024]{1,0:T(8,128)(2,1)S(1)}, bf16[128,1024]{1,0:T(8,128)(2,1)S(1)}) custom-call(f32[8]{0:T(128)S(1)} %copy-done.2, s32[4]{0:T(128)S(1)} %copy-done.4, bf16[512,1024]{1,0:T(8,128)(2,1)} %key_ref.3, bf16[8,128,128]{2,1,0:T(8,128)(2,1)S(1)} %bitcast.39, ...), custom_call_target="tpu_custom_call" | custom-call | tf_op jit(solution)/shard_map/across/pallas_call | solution.py:145
  48.2 0.0 copy-start
  48.3 0.6 collective-permute-start
  48.9 2.1 %collective-permute-start.1 = (bf16[128,1024]{1,0:T(8,128)(2,1)S(1)}, bf16[128,1024]{1,0:T(8,128)(2,1)S(1)}, u32[]{:S(2)}, u32[]{:S(2)}) collective-permute-start(bf16[128,1024]{1,0:T(8,128)(2,1)S(1)} %get-tuple-element.16.refs_0_), channel_id=1, source_target_pairs={{0,96},{32,0},{64,32},{96,64},{1,97},{33,1},{65,33},{97,65},{2,98}... | collective-permute-start | bytes 786440 | tf_op jit(solution)/shard_map/ppermute | solution.py:387
  51.0 2.6 %collective-permute-start.2 = (bf16[128,1024]{1,0:T(8,128)(2,1)S(1)}, bf16[128,1024]{1,0:T(8,128)(2,1)S(1)}, u32[]{:S(2)}, u32[]{:S(2)}) collective-permute-start(bf16[128,1024]{1,0:T(8,128)(2,1)S(1)} %get-tuple-element.17), channel_id=1, source_target_pairs={{0,3},{1,0},{2,1},{3,2},{4,7},{5,4},{6,5},{7,6},{8,11},{9,8},{10,9... | collective-permute-start | bytes 786440 | tf_op jit(solution)/shard_map/ppermute | solution.py:382
  53.6 0.0 collective-permute-start.5
  53.6 1.7 collective-permute-start.6
  55.4 1.7 collective-permute-done.refs_1_
  57.1 0.1 collective-permute-start.7
  57.2 7.4 %collective-permute-done.2.refs_3_ = bf16[128,1024]{1,0:T(8,128)(2,1)S(1)} collective-permute-done((bf16[128,1024]{1,0:T(8,128)(2,1)S(1)}, bf16[128,1024]{1,0:T(8,128)(2,1)S(1)}, u32[]{:S(2)}, u32[]{:S(2)}) %collective-permute-start.2) | collective-permute-done | bytes 262176 | tf_op jit(solution)/shard_map/ppermute | solution.py:382
  64.6 0.0 collective-permute-done.1.refs_2_
  64.6 0.1 collective-permute-start.4
  64.8 1.4 collective-permute-start.3
  66.1 2.5 %collective-permute-done.5.refs_6_ = bf16[128,1024]{1,0:T(8,128)(2,1)S(1)} collective-permute-done((bf16[128,1024]{1,0:T(8,128)(2,1)S(1)}, bf16[128,1024]{1,0:T(8,128)(2,1)S(1)}, u32[]{:S(2)}, u32[]{:S(2)}) %collective-permute-start.5) | collective-permute-done | bytes 262176 | tf_op jit(solution)/shard_map/ppermute | solution.py:382
  68.6 9.9 %collective-permute-done.6.refs_9_ = bf16[128,1024]{1,0:T(8,128)(2,1)S(1)} collective-permute-done((bf16[128,1024]{1,0:T(8,128)(2,1)S(1)}, bf16[128,1024]{1,0:T(8,128)(2,1)S(1)}, u32[]{:S(2)}, u32[]{:S(2)}) %collective-permute-start.6) | collective-permute-done | bytes 262176 | tf_op jit(solution)/shard_map/ppermute | solution.py:382
  78.5 0.0 collective-permute-done.7.refs_0_
  78.5 0.1 collective-permute-start.8
  78.6 2.7 %collective-permute-start.11 = (bf16[128,1024]{1,0:T(8,128)(2,1)S(1)}, bf16[128,1024]{1,0:T(8,128)(2,1)}, u32[]{:S(2)}, u32[]{:S(2)}) collective-permute-start(bf16[128,1024]{1,0:T(8,128)(2,1)S(1)} %collective-permute-done.6.refs_9_), channel_id=1, source_target_pairs={{0,96},{32,0},{64,32},{96,64},{1,97},{33,1},{65,33},{97,65},{2,98}... | collective-permute-start | bytes 786440 | tf_op jit(solution)/shard_map/ppermute | solution.py:387
  81.3 0.6 gather_fusion
  81.9 0.2 convert_reduce_fusion
  82.1 0.1 collective-permute-start.9
  82.3 1.4 collective-permute-start.10
  83.7 0.0 collective-permute-done.3.refs_4_
  83.7 1.3 collective-permute-start.12
  85.0 0.7 collective-permute-done.8.refs_7_
  85.7 0.0 collective-permute-start.13
  85.7 0.0 collective-permute-done.11.refs_11_
  85.7 2.7 %collective-permute-start.14 = (bf16[128,1024]{1,0:T(8,128)(2,1)}, bf16[128,1024]{1,0:T(8,128)(2,1)}, u32[]{:S(2)}, u32[]{:S(2)}) collective-permute-start(bf16[128,1024]{1,0:T(8,128)(2,1)} %collective-permute-done.11.refs_11_), channel_id=1, source_target_pairs={{0,96},{32,0},{64,32},{96,64},{1,97},{33,1},{65,33},{97,65},{2,98}... | collective-permute-start | bytes 786440 | tf_op jit(solution)/shard_map/ppermute | solution.py:388
  88.4 0.1 add_bitcast_fusion
  88.4 0.4 fusion.pick
  88.9 1.8 %collective-permute-done.9.refs_8_ = bf16[128,1024]{1,0:T(8,128)(2,1)S(1)} collective-permute-done((bf16[128,1024]{1,0:T(8,128)(2,1)S(1)}, bf16[128,1024]{1,0:T(8,128)(2,1)S(1)}, u32[]{:S(2)}, u32[]{:S(2)}) %collective-permute-start.9) | collective-permute-done | bytes 262176 | tf_op jit(solution)/shard_map/ppermute | solution.py:387
  90.7 0.7 copy-done.14
  91.4 0.6 collective-permute-done.10.refs_10_
  92.1 10.7 %project_direct.1.direct = bf16[384,1536]{1,0:T(8,128)(2,1)} custom-call(s32[4]{0:T(128)S(1)} %and_select_fusion.1.place, bf16[128,1024]{1,0:T(8,128)(2,1)} %copy-done, bf16[128,1024]{1,0:T(8,128)(2,1)} %copy-done.6, bf16[128,1024]{1,0:T(8,128)(2,1)} %copy-done.8, bf16[128,1024]{1,0:T(8,128)(2,1)} %copy-done.9, bf16[128,1024]{1,0:T(8,128)(2,1)} %copy-done.13, ...), custom_call_target="tpu_custom_call" | custom-call | tf_op jit(solution)/shard_map/project_direct/pallas_call | solution.py:183
  102.8 11.6 %project_relayed.1 = bf16[1024,1536]{1,0:T(8,128)(2,1)} custom-call(s32[4]{0:T(128)S(1)} %and_select_fusion.1.place, bf16[1024,512]{1,0:T(8,128)(2,1)S(1)} %fusion.pick, bf16[384,1536]{1,0:T(8,128)(2,1)} %project_direct.1.direct, bf16[128,1024]{1,0:T(8,128)(2,1)} %copy-done.7, bf16[128,1024]{1,0:T(8,128)(2,1)} %collective-permute-done.12.refs_1_, ...), custom_call_target="tpu_custom_call" | custom-call | tf_op jit(solution)/shard_map/project_relayed/pallas_call | solution.py:212
  114.4 10.8 %all-to-all-start.2 = ((bf16[128,8,1536]{2,1,0:T(8,128)(2,1)}), bf16[128,8,1536]{2,1,0:T(8,128)(2,1)S(1)}, u32[]{:S(2)}, u32[]{:S(2)}) async-start(bf16[128,8,1536]{2,1,0:T(8,128)(2,1)} %bitcast.49), calls=%async_computation.2 | async-start | bytes 6291456 | tf_op jit(solution)/shard_map/all_to_all | solution.py:405
  125.2 1.0 fusion.35
  126.2 0.1 copy.48
  126.3 0.1 copy.49
  126.4 0.1 sub.71
  126.4 0.1 copy.42
  126.5 0.2 copy.43
  126.7 0.2 reshape.207.row_ref
  126.9 0.1 sub.76.column_ref
  127.0 40.3 %all-to-all-done.2 = bf16[128,8,1536]{2,1,0:T(8,128)(2,1)S(1)} async-done(((bf16[128,8,1536]{2,1,0:T(8,128)(2,1)}), bf16[128,8,1536]{2,1,0:T(8,128)(2,1)S(1)}, u32[]{:S(2)}, u32[]{:S(2)}) %all-to-all-start.2) | async-done | bytes 3145760 | tf_op jit(solution)/shard_map/all_to_all | solution.py:405
  167.2 2.5 %merge.1 = bf16[1,128,2,6144]{3,2,1,0:T(2,128)(2,1)} custom-call(s32[256,1]{1,0:T(8,128)S(1)} %sub.76.column_ref, s32[1,256]{1,0:T(1,128)S(1)} %reshape.207.row_ref, bf16[4,32,8,1536]{3,2,1,0:T(8,128)(2,1)S(1)} %bitcast.38), custom_call_target="tpu_custom_call" | custom-call | tf_op jit(solution)/shard_map/merge/pallas_call | solution.py:252
  (59 shorter events, 0.3 us)
Async XLA Ops:
  6.5 17.2 %copy-start.4 = (s32[4]{0:T(128)S(1)}, s32[4]{0:T(128)}, u32[]{:S(2)}) copy-start(s32[4]{0:T(128)} %lengths_ref.5) | copy-start | bytes 52
  6.5 15.9 %copy-start.2 = (f32[8]{0:T(128)S(1)}, f32[8]{0:T(128)}, u32[]{:S(2)}) copy-start(f32[8]{0:T(128)} %rate_ref.5) | copy-start | bytes 100
  6.5 14.7 %copy-start.15 = (s32[512,1]{0,1:T(1,128)S(1)}, s32[512,1]{0,1:T(1,128)}, u32[]{:S(2)}) copy-start(s32[512,1]{0,1:T(1,128)} %param.16) | copy-start | bytes 6148
  6.5 15.0 %copy-start.16 = (s32[512]{0:T(512)S(1)}, s32[512]{0:T(512)}, u32[]{:S(2)}) copy-start(s32[512]{0:T(512)} %param.17) | copy-start | bytes 6148
  6.5 85.5 %all-gather.2.cloned.1.call-start = ((), (), s32[]{:S(2)}) async-start(), calls=%async_computation.3 | async-start | bytes 12976128 | tf_op jit(solution)/shard_map/all_gather | solution.py:306
  7.3 0.7 copy-start.1
  7.9 0.7 copy-start.3
  11.6 18.7 %all-to-all-start = ((bf16[32,32,128]{2,1,0:T(8,128)(2,1)}), bf16[32,32,128]{2,1,0:T(8,128)(2,1)S(1)}, u32[]{:S(2)}, u32[]{:S(2)}) async-start(bf16[32,32,128]{2,1,0:T(8,128)(2,1)} %bitcast.4), calls=%async_computation | async-start | bytes 524288 | tf_op jit(solution)/shard_map/all_to_all | solution.py:331
  30.2 26.9 %copy-start.18 = (s32[4]{0:T(128)S(1)}, s32[4]{0:T(128)}, u32[]{:S(2)}) copy-start(s32[4]{0:T(128)} %constant.125) | copy-start | bytes 52
  30.2 26.9 %copy-start.17 = (s32[4]{0:T(128)S(1)}, s32[4]{0:T(128)}, u32[]{:S(2)}) copy-start(s32[4]{0:T(128)} %constant.126) | copy-start | bytes 52
  45.9 56.9 %copy-start.5 = (bf16[32,40,128]{2,1,0:T(8,128)(2,1)}, bf16[32,40,128]{2,1,0:T(8,128)(2,1)S(1)}, u32[]{:S(2)}) copy-start(bf16[32,40,128]{2,1,0:T(8,128)(2,1)S(1)} %all_to_all.15) | copy-start | bytes 983044
  48.2 43.8 %copy-start = (bf16[128,1024]{1,0:T(8,128)(2,1)}, bf16[128,1024]{1,0:T(8,128)(2,1)S(1)}, u32[]{:S(2)}) copy-start(bf16[128,1024]{1,0:T(8,128)(2,1)S(1)} %get-tuple-element.16.refs_0_) | copy-start | bytes 786436
  48.3 8.8 %collective-permute-start = (bf16[128,1024]{1,0:T(8,128)(2,1)S(1)}, bf16[128,1024]{1,0:T(8,128)(2,1)S(1)}, u32[]{:S(2)}, u32[]{:S(2)}) collective-permute-start(bf16[128,1024]{1,0:T(8,128)(2,1)S(1)} %get-tuple-element.16.refs_0_), channel_id=1, source_target_pairs={{0,32},{32,64},{64,96},{96,0},{1,33},{33,65},{65,97},{97,1},{2,34}... | collective-permute-start | bytes 786440 | tf_op jit(solution)/shard_map/ppermute | solution.py:386
  48.9 15.7 %collective-permute-start.1 = (bf16[128,1024]{1,0:T(8,128)(2,1)S(1)}, bf16[128,1024]{1,0:T(8,128)(2,1)S(1)}, u32[]{:S(2)}, u32[]{:S(2)}) collective-permute-start(bf16[128,1024]{1,0:T(8,128)(2,1)S(1)} %get-tuple-element.16.refs_0_), channel_id=1, source_target_pairs={{0,96},{32,0},{64,32},{96,64},{1,97},{33,1},{65,33},{97,65},{2,98}... | collective-permute-start | bytes 786440 | tf_op jit(solution)/shard_map/ppermute | solution.py:387
  51.0 13.6 %collective-permute-start.2 = (bf16[128,1024]{1,0:T(8,128)(2,1)S(1)}, bf16[128,1024]{1,0:T(8,128)(2,1)S(1)}, u32[]{:S(2)}, u32[]{:S(2)}) collective-permute-start(bf16[128,1024]{1,0:T(8,128)(2,1)S(1)} %get-tuple-element.17), channel_id=1, source_target_pairs={{0,3},{1,0},{2,1},{3,2},{4,7},{5,4},{6,5},{7,6},{8,11},{9,8},{10,9... | collective-permute-start | bytes 786440 | tf_op jit(solution)/shard_map/ppermute | solution.py:382
  53.6 15.0 %collective-permute-start.5 = (bf16[128,1024]{1,0:T(8,128)(2,1)S(1)}, bf16[128,1024]{1,0:T(8,128)(2,1)S(1)}, u32[]{:S(2)}, u32[]{:S(2)}) collective-permute-start(bf16[128,1024]{1,0:T(8,128)(2,1)S(1)} %get-tuple-element.19), channel_id=1, source_target_pairs={{0,1},{1,2},{2,3},{3,0},{4,5},{5,6},{6,7},{7,4},{8,9},{9,10},{10,1... | collective-permute-start | bytes 786440 | tf_op jit(solution)/shard_map/ppermute | solution.py:382
  53.6 24.9 %collective-permute-start.6 = (bf16[128,1024]{1,0:T(8,128)(2,1)S(1)}, bf16[128,1024]{1,0:T(8,128)(2,1)S(1)}, u32[]{:S(2)}, u32[]{:S(2)}) collective-permute-start(bf16[128,1024]{1,0:T(8,128)(2,1)S(1)} %get-tuple-element.20), channel_id=1, source_target_pairs={{0,2},{1,3},{2,0},{3,1},{4,6},{5,7},{6,4},{7,5},{8,10},{9,11},{10,... | collective-permute-start | bytes 786440 | tf_op jit(solution)/shard_map/ppermute | solution.py:382
  57.1 34.9 %copy-start.6 = (bf16[128,1024]{1,0:T(8,128)(2,1)}, bf16[128,1024]{1,0:T(8,128)(2,1)S(1)}, u32[]{:S(2)}) copy-start(bf16[128,1024]{1,0:T(8,128)(2,1)S(1)} %collective-permute-done.refs_1_) | copy-start | bytes 786436
  57.1 21.4 %collective-permute-start.7 = (bf16[128,1024]{1,0:T(8,128)(2,1)S(1)}, bf16[128,1024]{1,0:T(8,128)(2,1)S(1)}, u32[]{:S(2)}, u32[]{:S(2)}) collective-permute-start(bf16[128,1024]{1,0:T(8,128)(2,1)S(1)} %collective-permute-done.refs_1_), channel_id=1, source_target_pairs={{0,32},{32,64},{64,96},{96,0},{1,33},{33,65},{65,97},{97,1},{2,34}... | collective-permute-start | bytes 786440 | tf_op jit(solution)/shard_map/ppermute | solution.py:388
  64.6 27.4 %copy-start.9 = (bf16[128,1024]{1,0:T(8,128)(2,1)}, bf16[128,1024]{1,0:T(8,128)(2,1)S(1)}, u32[]{:S(2)}) copy-start(bf16[128,1024]{1,0:T(8,128)(2,1)S(1)} %collective-permute-done.2.refs_3_) | copy-start | bytes 786436
  64.6 27.4 %copy-start.8 = (bf16[128,1024]{1,0:T(8,128)(2,1)}, bf16[128,1024]{1,0:T(8,128)(2,1)S(1)}, u32[]{:S(2)}) copy-start(bf16[128,1024]{1,0:T(8,128)(2,1)S(1)} %collective-permute-done.1.refs_2_) | copy-start | bytes 786436
  64.6 17.6 %collective-permute-start.4 = (bf16[128,1024]{1,0:T(8,128)(2,1)S(1)}, bf16[128,1024]{1,0:T(8,128)(2,1)S(1)}, u32[]{:S(2)}, u32[]{:S(2)}) collective-permute-start(bf16[128,1024]{1,0:T(8,128)(2,1)S(1)} %collective-permute-done.2.refs_3_), channel_id=1, source_target_pairs={{0,96},{32,0},{64,32},{96,64},{1,97},{33,1},{65,33},{97,65},{2,98}... | collective-permute-start | bytes 786440 | tf_op jit(solution)/shard_map/ppermute | solution.py:387
  64.8 18.9 %collective-permute-start.3 = (bf16[128,1024]{1,0:T(8,128)(2,1)S(1)}, bf16[128,1024]{1,0:T(8,128)(2,1)S(1)}, u32[]{:S(2)}, u32[]{:S(2)}) collective-permute-start(bf16[128,1024]{1,0:T(8,128)(2,1)S(1)} %collective-permute-done.2.refs_3_), channel_id=1, source_target_pairs={{0,32},{32,64},{64,96},{96,0},{1,33},{33,65},{65,97},{97,1},{2,34}... | collective-permute-start | bytes 786440 | tf_op jit(solution)/shard_map/ppermute | solution.py:386
  68.6 23.4 %copy-start.10 = (bf16[128,1024]{1,0:T(8,128)(2,1)}, bf16[128,1024]{1,0:T(8,128)(2,1)S(1)}, u32[]{:S(2)}) copy-start(bf16[128,1024]{1,0:T(8,128)(2,1)S(1)} %collective-permute-done.5.refs_6_) | copy-start | bytes 786436
  78.5 13.5 %copy-start.11 = (bf16[128,1024]{1,0:T(8,128)(2,1)}, bf16[128,1024]{1,0:T(8,128)(2,1)S(1)}, u32[]{:S(2)}) copy-start(bf16[128,1024]{1,0:T(8,128)(2,1)S(1)} %collective-permute-done.6.refs_9_) | copy-start | bytes 786436
  78.5 24.3 %copy-start.7 = (bf16[128,1024]{1,0:T(8,128)(2,1)}, bf16[128,1024]{1,0:T(8,128)(2,1)S(1)}, u32[]{:S(2)}) copy-start(bf16[128,1024]{1,0:T(8,128)(2,1)S(1)} %collective-permute-done.7.refs_0_) | copy-start | bytes 786436
  78.5 7.2 %collective-permute-start.8 = (bf16[128,1024]{1,0:T(8,128)(2,1)S(1)}, bf16[128,1024]{1,0:T(8,128)(2,1)}, u32[]{:S(2)}, u32[]{:S(2)}) collective-permute-start(bf16[128,1024]{1,0:T(8,128)(2,1)S(1)} %collective-permute-done.5.refs_6_), channel_id=1, source_target_pairs={{0,32},{32,64},{64,96},{96,0},{1,33},{33,65},{65,97},{97,1},{2,34}... | collective-permute-start | bytes 786440 | tf_op jit(solution)/shard_map/ppermute | solution.py:386
  78.6 7.1 %collective-permute-start.11 = (bf16[128,1024]{1,0:T(8,128)(2,1)S(1)}, bf16[128,1024]{1,0:T(8,128)(2,1)}, u32[]{:S(2)}, u32[]{:S(2)}) collective-permute-start(bf16[128,1024]{1,0:T(8,128)(2,1)S(1)} %collective-permute-done.6.refs_9_), channel_id=1, source_target_pairs={{0,96},{32,0},{64,32},{96,64},{1,97},{33,1},{65,33},{97,65},{2,98}... | collective-permute-start | bytes 786440 | tf_op jit(solution)/shard_map/ppermute | solution.py:387
  82.1 8.5 %collective-permute-start.9 = (bf16[128,1024]{1,0:T(8,128)(2,1)S(1)}, bf16[128,1024]{1,0:T(8,128)(2,1)S(1)}, u32[]{:S(2)}, u32[]{:S(2)}) collective-permute-start(bf16[128,1024]{1,0:T(8,128)(2,1)S(1)} %collective-permute-done.5.refs_6_), channel_id=1, source_target_pairs={{0,96},{32,0},{64,32},{96,64},{1,97},{33,1},{65,33},{97,65},{2,98}... | collective-permute-start | bytes 786440 | tf_op jit(solution)/shard_map/ppermute | solution.py:387
  82.2 9.8 %copy-start.12 = (bf16[128,1024]{1,0:T(8,128)(2,1)}, bf16[128,1024]{1,0:T(8,128)(2,1)S(1)}, u32[]{:S(2)}) copy-start(bf16[128,1024]{1,0:T(8,128)(2,1)S(1)} %collective-permute-done.4.refs_5_) | copy-start | bytes 786436
  82.3 9.7 %collective-permute-start.10 = (bf16[128,1024]{1,0:T(8,128)(2,1)S(1)}, bf16[128,1024]{1,0:T(8,128)(2,1)}, u32[]{:S(2)}, u32[]{:S(2)}) collective-permute-start(bf16[128,1024]{1,0:T(8,128)(2,1)S(1)} %collective-permute-done.6.refs_9_), channel_id=1, source_target_pairs={{0,32},{32,64},{64,96},{96,0},{1,33},{33,65},{65,97},{97,1},{2,34}... | collective-permute-start | bytes 786440 | tf_op jit(solution)/shard_map/ppermute | solution.py:386
  83.7 4.7 %copy-start.13 = (bf16[128,1024]{1,0:T(8,128)(2,1)}, bf16[128,1024]{1,0:T(8,128)(2,1)S(1)}, u32[]{:S(2)}) copy-start(bf16[128,1024]{1,0:T(8,128)(2,1)S(1)} %collective-permute-done.3.refs_4_) | copy-start | bytes 786436
  83.7 19.1 %collective-permute-start.12 = (bf16[128,1024]{1,0:T(8,128)(2,1)S(1)}, bf16[128,1024]{1,0:T(8,128)(2,1)}, u32[]{:S(2)}, u32[]{:S(2)}) collective-permute-start(bf16[128,1024]{1,0:T(8,128)(2,1)S(1)} %collective-permute-done.4.refs_5_), channel_id=1, source_target_pairs={{0,96},{32,0},{64,32},{96,64},{1,97},{33,1},{65,33},{97,65},{2,98}... | collective-permute-start | bytes 786440 | tf_op jit(solution)/shard_map/ppermute | solution.py:388
  85.7 17.1 %collective-permute-start.13 = (bf16[128,1024]{1,0:T(8,128)(2,1)}, bf16[128,1024]{1,0:T(8,128)(2,1)}, u32[]{:S(2)}, u32[]{:S(2)}) collective-permute-start(bf16[128,1024]{1,0:T(8,128)(2,1)} %collective-permute-done.8.refs_7_), channel_id=1, source_target_pairs={{0,32},{32,64},{64,96},{96,0},{1,33},{33,65},{65,97},{97,1},{2,34}... | collective-permute-start | bytes 786440 | tf_op jit(solution)/shard_map/ppermute | solution.py:388
  85.7 17.1 %collective-permute-start.14 = (bf16[128,1024]{1,0:T(8,128)(2,1)}, bf16[128,1024]{1,0:T(8,128)(2,1)}, u32[]{:S(2)}, u32[]{:S(2)}) collective-permute-start(bf16[128,1024]{1,0:T(8,128)(2,1)} %collective-permute-done.11.refs_11_), channel_id=1, source_target_pairs={{0,96},{32,0},{64,32},{96,64},{1,97},{33,1},{65,33},{97,65},{2,98}... | collective-permute-start | bytes 786440 | tf_op jit(solution)/shard_map/ppermute | solution.py:388
  90.7 0.7 copy-start.14
  114.4 52.9 %all-to-all-start.2 = ((bf16[128,8,1536]{2,1,0:T(8,128)(2,1)}), bf16[128,8,1536]{2,1,0:T(8,128)(2,1)S(1)}, u32[]{:S(2)}, u32[]{:S(2)}) async-start(bf16[128,8,1536]{2,1,0:T(8,128)(2,1)} %bitcast.49), calls=%async_computation.2 | async-start | bytes 6291456 | tf_op jit(solution)/shard_map/all_to_all | solution.py:405
Sparse Core Ops, SparseCore 0:
  9.6 77.5 all-gather.1

commit v8 on v5

--- a/solution.py
+++ b/solution.py
@@ -15,6 +15,7 @@
 SEQ = ("z", "y", "core")
 ALL = ("z", "y", "core", "head")
 TURNS = (0, 3, 1, 2)
+ZTURNS = (1, 3, 2)
 
 
 def doc_of(positions, doc_ends):
@@ -284,67 +285,54 @@
     blocks = tok_rows // ROWS_BLK
     per = blocks * CAPACITY
     owners = owner_block[:, 0].reshape(blocks, ROWS_BLK)
-    slot_index = slots_of(owners, jnp.arange(blocks, dtype=jnp.int32))
-    my_slots = (
-        (jnp.arange(n_seq, dtype=jnp.int32)[:, None] * n_head + head_rank) * per
-        + jnp.arange(per, dtype=jnp.int32)[None, :]
-    )
-    hit = my_slots[:, :, None] == slot_index[None, None, :]
-    named = jnp.sum(jnp.where(hit, row_offset[None, None, :] + 1, 0), axis=2)
-    note = jnp.concatenate([(named // 32).astype(BF16), (named % 32).astype(BF16)], axis=1)
-    note = jnp.pad(note[:, None, :], ((0, 0), (0, 0), (0, head_dim - 2 * per)))
     names = lax.dynamic_slice_in_dim(owners, head_rank, 1, 0).astype(BF16)
-    names = jnp.broadcast_to(names[None], (n_seq, 1, ROWS_BLK))
-    note = jnp.pad(jnp.concatenate([note, names], axis=1), ((0, 0), (0, 6), (0, 0)))
-
-    share = head_local * head_dim // n_seq
-    state_in = lax.all_to_all(
-        state.reshape(n_seq, share, head_dim), SEQ, split_axis=0, concat_axis=0, tiled=True
-    )
+
+    heads_in = ("y", "core")
+    state_in = lax.all_to_all(state, heads_in, split_axis=0, concat_axis=0, tiled=True)
     intra = within(
         decay_rate, doc_lengths, queries, key_vectors, output_grad, head_local // 2
     )
 
-    state_in, intra = lax.optimization_barrier((state_in, intra))
     doc_ends = jnp.cumsum(doc_lengths)
-    ranks = jnp.arange(n_seq, dtype=jnp.int32)
+    ranks = z_rank * plane + jnp.arange(plane, dtype=jnp.int32)
     doc_last = doc_of((ranks + 1) * tok_rows - 1, doc_ends)
     doc_prior = doc_of(jnp.maximum(ranks * tok_rows - 1, 0), doc_ends)
-    my_rate = decay_rate[seq_rank // (n_seq // head_local)]
-    ahead = ranks[None, :] - ranks[:, None] - 1
-    reach = (ahead >= 0) & (doc_last[:, None] == doc_prior[None, :])
-    chain = jnp.where(
-        reach, jnp.exp(-my_rate * (jnp.maximum(ahead, 0) * tok_rows).astype(F32)), 0.0
-    )
-    carried_all = jnp.einsum(
+    my_rate = decay_rate[seq_rank % plane] * tok_rows
+
+    def links(ahead, same):
+        return jnp.where(
+            same & (ahead >= 0), jnp.exp(-my_rate * jnp.maximum(ahead, 0).astype(F32)), 0.0
+        )
+
+    chain = links(ranks[None, :] - ranks[:, None] - 1, doc_last[:, None] == doc_prior[None, :])
+    entry = links(ranks - ranks[0], doc_prior == doc_prior[0])
+    mixed = jnp.einsum(
         "bc,cxy->bxy",
-        chain,
+        jnp.concatenate([chain, entry[None]], axis=0),
         state_in.astype(F32),
         precision=lax.Precision.HIGHEST,
         preferred_element_type=F32,
-    ).astype(BF16)
+    )
+    total = jnp.concatenate([mixed[plane].astype(BF16), jnp.pad(names, ((0, 7), (0, 0)))], axis=0)
+    later = [lax.ppermute(total, "z", shift(n_z, -step)) for step in range(1, n_z)]
+    *later, intra = lax.optimization_barrier((*later, intra))
+    carried_all = mixed[:plane]
+    for step in range(1, n_z):
+        first = (z_rank + step) * plane
+        prior = doc_of(first[None] * tok_rows - 1, doc_ends)
+        weigh = links(first - ranks - 1, (doc_last == prior) & (first < n_seq))
+        carried_all += weigh[:, None, None] * later[step - 1][:head_dim].astype(F32)
     carried = lax.all_to_all(
-        jnp.concatenate([carried_all, note], axis=1),
-        SEQ,
-        split_axis=0,
-        concat_axis=0,
-        tiled=True,
-    )
-    offsets = (
-        carried[:, share, :per].astype(jnp.int32) * 32
-        + carried[:, share, per : 2 * per].astype(jnp.int32)
-        - 1
-    )
-    column = offsets.reshape(-1, 1)
-    row = offsets.reshape(n_z, plane, blocks, CAPACITY).transpose(1, 2, 0, 3).reshape(1, -1)
-    near_z = (z_rank + turns) % n_z
-    theirs = carried[:, share + 1].reshape(n_z, plane, ROWS_BLK)
-    theirs = lax.dynamic_slice_in_dim(theirs, seq_rank % plane, 1, 1)[:, 0]
-    theirs = theirs[near_z].astype(jnp.int32)
-    their_slots = slots_of(theirs, near_z)
+        carried_all.astype(BF16), heads_in, split_axis=0, concat_axis=0, tiled=True
+    )
+
+    near_z = (z_rank - jnp.array((0,) + ZTURNS, jnp.int32)) % n_z
+    theirs = jnp.concatenate(
+        [names] + [later[n_z - 1 - step][head_dim : head_dim + 1] for step in ZTURNS], axis=0
+    )
+    their_slots = slots_of(theirs.astype(jnp.int32), near_z)
     all_slots = jnp.arange(devices_all * per, dtype=jnp.int32)
     pick = (all_slots[:, None] == their_slots[None, :]).astype(BF16)
-    carried = carried[:, :share].reshape(head_local, head_dim, head_dim)
 
     own = across(decay_rate, doc_lengths, key_vectors, carried, intra)
     mine = [own[0]]
@@ -352,18 +340,33 @@
         mine.append(lax.ppermute(own[turn], "head", shift(n_head, TURNS[turn])))
     place = (head_rank - turns) % n_head
 
-    pieces = []
-    for turn, rows in enumerate(mine):
+    def spread(rows, flip):
         below = lax.ppermute(rows, "z", shift(n_z, 1))
         above = lax.ppermute(rows, "z", shift(n_z, -1))
-        if turn % 2 == 0:
-            across_z = lax.ppermute(below, "z", shift(n_z, 1))
-        else:
-            across_z = lax.ppermute(above, "z", shift(n_z, -1))
-        group = (rows, below, above, across_z)
-        pieces.append([pltpu.with_memory_space_constraint(q, pltpu.HBM) for q in group])
+        relay = lax.ppermute(above if flip else below, "z", shift(n_z, -1 if flip else 1))
+        return rows, below, above, relay
+
+    groups = [spread(mine[0], False)]
+    mine[1], *_ = lax.optimization_barrier((mine[1],) + groups[0][1:3])
+    groups.append(spread(mine[1], True))
+    mine[2], mine[3], _ = lax.optimization_barrier((mine[2], mine[3], groups[0][3]))
+    groups.append(spread(mine[2], False))
+    groups.append(spread(mine[3], True))
+    pieces = [
+        [pltpu.with_memory_space_constraint(q, pltpu.HBM) for q in group] for group in groups
+    ]
 
     send = project(place, pick, pieces, weight, 512)
+    ids = owners * 1024 + row_offset.reshape(blocks, ROWS_BLK)
+    ids, _ = lax.optimization_barrier((ids, weight))
+    ids = lax.all_gather(ids, SEQ, axis=0, tiled=True)
+    at = jnp.arange(ROWS_BLK, dtype=jnp.int32)[None, :]
+    hit = ids // 1024 == seq_rank * n_head + head_rank
+    lead = at == jnp.min(jnp.where(hit, at, ROWS_BLK), axis=1, keepdims=True)
+    slot_hits = jnp.stack([hit & lead, hit & ~lead], axis=1)
+    offsets = jnp.sum(jnp.where(slot_hits, (ids % 1024)[:, None, :] + 1, 0), axis=2) - 1
+    column = offsets.reshape(-1, 1)
+    row = offsets.reshape(n_z, plane, blocks, CAPACITY).transpose(1, 2, 0, 3).reshape(1, -1)
     send = send.reshape(devices_all, per, -1)
     got = lax.all_to_all(send, ALL, split_axis=0, concat_axis=0, tiled=True)
     got = got.reshape(n_z, plane * n_head, per, -1)

time: 177 us -> 195 us (1.10); the launches traced: 176 us -> 192 us
  blocking collectives: 15 us -> 61.9 us
  waiting for transfers between devices: 76.4 us -> 41.7 us
  starting transfers between devices: 36 us -> 38.5 us
  other arithmetic: 2.24 us -> 4.49 us
    all_gather x0 -> x1, blocking collectives: none -> 51.1 us  [per_device(): ids = lax.all_gather(ids, SEQ, axis=0, tiled=True)]
    all_to_all x1, waiting for transfers between devices: 40.3 us -> 0.01 us  [per_device(): got = lax.all_to_all(send, ALL, split_axis=0, concat_axis=0, tiled=True)]
    all_to_all x1, starting transfers between devices: 5.88 us -> 10.1 us  [per_device(): got = lax.all_to_all(send, ALL, split_axis=0, concat_axis=0, tiled=True)]
    all_to_all x1, blocking collectives: 15 us -> 10.8 us  [per_device(): lax.all_to_all(carried_all.astype(BF16), heads_in, split_axis=0, concat_a...]
    ppermute x12 -> x15, waiting for transfers between devices: 13.1 us -> 17.1 us  [the longest x4 9.01 us: spread(): lax.ppermute(above if flip else below, 'z', shift(n_z, -1 if flip else 1))]
    all_to_all x1, starting transfers between devices: 9.62 us -> 5.98 us  [per_device(): lax.all_to_all(state, heads_in, split_axis=0, concat_axis=0, tiled=True)]
    all_to_all x1, waiting for transfers between devices: 1.8 us -> 3.86 us  [per_device(): lax.all_to_all(state, heads_in, split_axis=0, concat_axis=0, tiled=True)]
    ppermute x12 -> x15, starting transfers between devices: 16.1 us -> 17.5 us  [the longest x4 4.65 us: spread(): lax.ppermute(above if flip else below, 'z', shift(n_z, -1 if flip else 1))]
  transfers between devices with their start and end apart: 18 -> 21, of which waited for: 9 -> 11; matrix products, arithmetic and copies ran while one was open for 3% -> 4% of each run, Pallas kernels for 6% -> 5%
where the time goes in v8:
time: 195 us; the launch traced here: 192 us
  blocking collectives  61.9 us (32%)
  waiting for transfers between devices  41.7 us (21%)
  starting transfers between devices  38.5 us (20%)
  Pallas kernels  26.5 us (14%)
  between operations  14.6 us (7%)
  other arithmetic  4.49 us (2%)
  local copies, waits for them, and re-layouts  3.67 us (2%)
    all_gather x1, blocking collectives, per_device(): ids = lax.all_gather(ids, SEQ, axis=0, tiled=True)  51.1 us
    ppermute x3, waiting for transfers between devices, per_device(): mine.append(lax.ppermute(own[turn], 'head', shift(n_head, TURNS[turn])))  20 us
    pallas_call x1, Pallas kernels, project(): pl.pallas_call(functools.partial(project_body, turns), grid_spec=pltpu.Pr...  14.4 us
    all_to_all x1, blocking collectives, per_device(): lax.all_to_all(carried_all.astype(BF16), heads_in, split_axis=0, concat_a...  10.8 us
    all_to_all x1, starting transfers between devices, per_device(): got = lax.all_to_all(send, ALL, split_axis=0, concat_axis=0, tiled=True)  10.1 us
    ppermute x4, waiting for transfers between devices, spread(): lax.ppermute(above if flip else below, 'z', shift(n_z, -1 if flip else 1))  9.01 us
    ppermute x4, waiting for transfers between devices, spread(): below = lax.ppermute(rows, 'z', shift(n_z, 1))  6.68 us
    all_to_all x1, starting transfers between devices, per_device(): lax.all_to_all(state, heads_in, split_axis=0, concat_axis=0, tiled=True)  5.98 us
  transfers between devices with their start and end apart: 21, of which 11 were waited for; matrix products, arithmetic and copies ran while one was open for 4% of the time, Pallas kernels for 5%

profile of v8, /device:TPU:1, one launch (start us, length us, event | category | flops | bytes accessed | tf_op | source)
XLA Modules:
  0.0 192.0 jit_solution(9894833401947830485)
XLA Ops:
  6.5 0.7 all-gather.3.cloned.1.call-update
  7.3 0.6 copy-done.1
  7.9 0.7 copy-done.3
  8.6 3.0 %local_states.1 = bf16[8,128,128]{2,1,0:T(8,128)(2,1)} custom-call(f32[8]{0:T(128)S(1)} %copy-done.1, s32[4]{0:T(128)S(1)} %copy-done.3, bf16[512,1024]{1,0:T(8,128)(2,1)} %query_ref.3, bf16[512,1024]{1,0:T(8,128)(2,1)} %grad_ref.3), custom_call_target="tpu_custom_call" | custom-call | tf_op jit(solution)/shard_map/local_states/pallas_call | solution.py:65
  11.6 6.0 %all-to-all-start = ((bf16[8,128,128]{2,1,0:T(8,128)(2,1)}), bf16[8,128,128]{2,1,0:T(8,128)(2,1)S(1)}, u32[]{:S(2)}, u32[]{:S(2)}) async-start(bf16[8,128,128]{2,1,0:T(8,128)(2,1)} %local_states.1), calls=%async_computation | async-start | bytes 524288 | tf_op jit(solution)/shard_map/all_to_all | solution.py:291
  17.5 0.7 dynamic_slice.7
  18.9 0.2 reduce-window.4
  19.1 0.1 convert_reduce_fusion.2
  19.2 0.1 copy.28
  19.3 0.7 fusion.25
  20.1 0.1 exponential_select_fusion.1
  20.2 3.9 %all-to-all-done = bf16[8,128,128]{2,1,0:T(8,128)(2,1)S(1)} async-done(((bf16[8,128,128]{2,1,0:T(8,128)(2,1)}), bf16[8,128,128]{2,1,0:T(8,128)(2,1)S(1)}, u32[]{:S(2)}, u32[]{:S(2)}) %all-to-all-start) | async-done | bytes 262176 | tf_op jit(solution)/shard_map/all_to_all | solution.py:291
  24.0 0.7 fusion.4
  24.8 3.8 %collective-permute-start = (bf16[136,128]{1,0:T(8,128)(2,1)S(1)}, bf16[136,128]{1,0:T(8,128)(2,1)S(1)}, u32[]{:S(2)}, u32[]{:S(2)}) collective-permute-start(bf16[136,128]{1,0:T(8,128)(2,1)S(1)} %fusion.16), channel_id=1, source_target_pairs={{0,96},{32,0},{64,32},{96,64},{1,97},{33,1},{65,33},{97,65},{2,98}... | collective-permute-start | bytes 104456 | tf_op jit(solution)/shard_map/ppermute | solution.py:317
  28.6 0.0 collective-permute-start.1
  28.7 0.7 collective-permute-start.2
  29.3 1.8 and_select_fusion.2
  31.1 4.5 %within.1.intra_ref = f32[512,1024]{1,0:T(8,128)S(1)} custom-call(f32[8]{0:T(128)S(1)} %copy-done.2, s32[4]{0:T(128)S(1)} %copy-done.4, bf16[512,1024]{1,0:T(8,128)(2,1)} %query_ref.3, bf16[512,1024]{1,0:T(8,128)(2,1)} %key_ref.3, bf16[512,1024]{1,0:T(8,128)(2,1)} %grad_ref.3), custom_call_target="tpu_custom_call" | custom-call | tf_op jit(solution)/shard_map/within/pallas_call | solution.py:107
  35.6 0.0 copy-start.22
  35.6 0.0 copy-start.21
  35.8 0.3 fusion.3
  36.1 10.8 %all_to_all.15.state_ref = bf16[8,128,128]{2,1,0:T(8,128)(2,1)S(1)} all-to-all(bf16[8,128,128]{2,1,0:T(8,128)(2,1)S(1)} %fusion.3), channel_id=1, replica_groups=mesh['z'=4,'y'=4,'core'=2,'head'=4] {'y','core'}, dimensions={0} | all-to-all | bytes 524288 | tf_op jit(solution)/shard_map/all_to_all | solution.py:325
  46.9 2.2 %across.1 = (bf16[128,1024]{1,0:T(8,128)(2,1)S(1)}, bf16[128,1024]{1,0:T(8,128)(2,1)S(1)}, bf16[128,1024]{1,0:T(8,128)(2,1)S(1)}, bf16[128,1024]{1,0:T(8,128)(2,1)S(1)}) custom-call(f32[8]{0:T(128)S(1)} %copy-done.2, s32[4]{0:T(128)S(1)} %copy-done.4, bf16[512,1024]{1,0:T(8,128)(2,1)} %key_ref.3, bf16[8,128,128]{2,1,0:T(8,128)(2,1)S(1)} %all_to_all.15.state_ref, ...), custom_call_target="tpu_custom_call" | custom-call | tf_op jit(solution)/shard_map/across/pallas_call | solution.py:145
  49.1 2.1 %collective-permute-start.3 = (bf16[128,1024]{1,0:T(8,128)(2,1)S(1)}, bf16[128,1024]{1,0:T(8,128)(2,1)S(1)}, u32[]{:S(2)}, u32[]{:S(2)}) collective-permute-start(bf16[128,1024]{1,0:T(8,128)(2,1)S(1)} %get-tuple-element.22.refs_0_), channel_id=1, source_target_pairs={{0,32},{32,64},{64,96},{96,0},{1,33},{33,65},{65,97},{97,1},{2,34}... | collective-permute-start | bytes 786440 | tf_op jit(solution)/shard_map/ppermute | solution.py:344
  51.2 0.7 collective-permute-start.4
  51.9 1.3 collective-permute-start.10
  53.1 2.5 %collective-permute-start.11 = (bf16[128,1024]{1,0:T(8,128)(2,1)S(1)}, bf16[128,1024]{1,0:T(8,128)(2,1)S(1)}, u32[]{:S(2)}, u32[]{:S(2)}) collective-permute-start(bf16[128,1024]{1,0:T(8,128)(2,1)S(1)} %get-tuple-element.26), channel_id=1, source_target_pairs={{0,2},{1,3},{2,0},{3,1},{4,6},{5,7},{6,4},{7,5},{8,10},{9,11},{10,... | collective-permute-start | bytes 786440 | tf_op jit(solution)/shard_map/ppermute | solution.py:340
  55.6 1.1 collective-permute-start.6
  56.7 0.5 collective-permute-done.3.refs_1_
  57.3 0.8 collective-permute-start.5
  58.1 20.0 %collective-permute-done.6.refs_4_ = bf16[128,1024]{1,0:T(8,128)(2,1)S(1)} collective-permute-done((bf16[128,1024]{1,0:T(8,128)(2,1)S(1)}, bf16[128,1024]{1,0:T(8,128)(2,1)S(1)}, u32[]{:S(2)}, u32[]{:S(2)}) %collective-permute-start.6) | collective-permute-done | bytes 262176 | tf_op jit(solution)/shard_map/ppermute | solution.py:340
  78.1 0.5 collective-permute-start.8
  78.7 0.9 collective-permute-start.7
  79.6 0.9 collective-permute-start.12
  80.5 1.9 collective-permute-start.16
  82.5 0.2 convert_reduce_fusion
  82.7 0.6 collective-permute-start.13
  83.3 0.5 collective-permute-done.8.refs_6_
  83.8 0.8 collective-permute-start.15
  84.5 0.7 collective-permute-done.7.refs_5_
  85.2 1.2 collective-permute-start.9
  86.4 4.0 %collective-permute-done.12.refs_9_ = bf16[128,1024]{1,0:T(8,128)(2,1)S(1)} collective-permute-done((bf16[128,1024]{1,0:T(8,128)(2,1)S(1)}, bf16[128,1024]{1,0:T(8,128)(2,1)S(1)}, u32[]{:S(2)}, u32[]{:S(2)}) %collective-permute-start.12) | collective-permute-done | bytes 262176 | tf_op jit(solution)/shard_map/ppermute | solution.py:344
  90.4 2.7 %collective-permute-start.17 = (bf16[128,1024]{1,0:T(8,128)(2,1)S(1)}, bf16[128,1024]{1,0:T(8,128)(2,1)}, u32[]{:S(2)}, u32[]{:S(2)}) collective-permute-start(bf16[128,1024]{1,0:T(8,128)(2,1)S(1)} %collective-permute-done.16.refs_14_), channel_id=1, source_target_pairs={{0,96},{32,0},{64,32},{96,64},{1,97},{33,1},{65,33},{97,65},{2,98}... | collective-permute-start | bytes 786440 | tf_op jit(solution)/shard_map/ppermute | solution.py:346
  93.1 0.1 add_bitcast_fusion
  93.2 0.4 fusion.pick
  93.6 0.9 collective-permute-done.13.refs_10_
  94.5 1.5 collective-permute-done.15.refs_13_
  96.0 4.1 %collective-permute-done.9.refs_7_ = bf16[128,1024]{1,0:T(8,128)(2,1)S(1)} collective-permute-done((bf16[128,1024]{1,0:T(8,128)(2,1)S(1)}, bf16[128,1024]{1,0:T(8,128)(2,1)S(1)}, u32[]{:S(2)}, u32[]{:S(2)}) %collective-permute-start.9) | collective-permute-done | bytes 262176 | tf_op jit(solution)/shard_map/ppermute | solution.py:346
  100.2 1.5 collective-permute-done.14.refs_11_
  101.7 0.7 copy-done.18
  102.4 3.4 %collective-permute-done.17.refs_15_ = bf16[128,1024]{1,0:T(8,128)(2,1)} collective-permute-done((bf16[128,1024]{1,0:T(8,128)(2,1)S(1)}, bf16[128,1024]{1,0:T(8,128)(2,1)}, u32[]{:S(2)}, u32[]{:S(2)}) %collective-permute-start.17) | collective-permute-done | bytes 262176 | tf_op jit(solution)/shard_map/ppermute | solution.py:346
  105.9 14.4 %project.1 = bf16[1024,1536]{1,0:T(8,128)(2,1)} custom-call(s32[4]{0:T(128)S(1)} %and_select_fusion.4.place, bf16[1024,512]{1,0:T(8,128)(2,1)S(1)} %fusion.pick, bf16[128,1024]{1,0:T(8,128)(2,1)} %copy-done, bf16[128,1024]{1,0:T(8,128)(2,1)} %copy-done.5, bf16[128,1024]{1,0:T(8,128)(2,1)} %copy-done.6, bf16[128,1024]{1,0:T(8,128)(2,1)} %copy-done.10, ...), custom_call_target="tpu_custom_call" | custom-call | tf_op jit(solution)/shard_map/project/pallas_call | solution.py:186
  120.2 0.0 copy-start.19
  120.2 10.1 %all-to-all-start.2 = ((bf16[128,8,1536]{2,1,0:T(8,128)(2,1)}), bf16[128,8,1536]{2,1,0:T(8,128)(2,1)S(1)}, u32[]{:S(2)}, u32[]{:S(2)}) async-start(bf16[128,8,1536]{2,1,0:T(8,128)(2,1)} %bitcast.38), calls=%async_computation.2 | async-start | bytes 6291456 | tf_op jit(solution)/shard_map/all_to_all | solution.py:371
  130.4 51.1 %all-gather = s32[32,4,128]{2,1,0:T(4,128)S(1)} all-gather(s32[1,4,128]{2,1,0:T(4,128)S(1)} %bitcast.42), channel_id=1, replica_groups=mesh['z'=4,'y'=4,'core'=2,'head'=4] {'z','y','core'}, dimensions={0}, use_global_device_ids=true | all-gather | bytes 67584 | tf_op jit(solution)/shard_map/all_gather | solution.py:362
  181.5 0.2 select_reduce_fusion.1
  181.7 0.1 fusion.12
  181.8 0.1 select_reduce_fusion
  181.9 0.1 copy.26
  182.0 0.1 sub.113
  182.1 0.1 sub.138.column_ref
  182.2 0.3 copy.27
  182.5 0.2 reshape.338.row_ref
  182.7 2.5 %merge.1 = bf16[1,128,2,6144]{3,2,1,0:T(2,128)(2,1)} custom-call(s32[256,1]{1,0:T(8,128)S(1)} %sub.138.column_ref, s32[1,256]{1,0:T(1,128)S(1)} %reshape.338.row_ref, bf16[4,32,8,1536]{3,2,1,0:T(8,128)(2,1)S(1)} %bitcast.32), custom_call_target="tpu_custom_call" | custom-call | tf_op jit(solution)/shard_map/merge/pallas_call | solution.py:223
  (73 shorter events, 0.4 us)
Async XLA Ops:
  6.5 11.0 %copy-start.2 = (f32[8]{0:T(128)S(1)}, f32[8]{0:T(128)}, u32[]{:S(2)}) copy-start(f32[8]{0:T(128)} %rate_ref.5) | copy-start | bytes 100
  6.5 12.3 %copy-start.4 = (s32[4]{0:T(128)S(1)}, s32[4]{0:T(128)}, u32[]{:S(2)}) copy-start(s32[4]{0:T(128)} %lengths_ref.5) | copy-start | bytes 52
  6.5 13.5 %copy-start.20 = (s32[512,1]{0,1:T(1,128)S(1)}, s32[512,1]{0,1:T(1,128)}, u32[]{:S(2)}) copy-start(s32[512,1]{0,1:T(1,128)} %param.16) | copy-start | bytes 6148
  6.5 99.2 %all-gather.3.cloned.1.call-start = ((), (), s32[]{:S(2)}) async-start(), calls=%async_computation.3 | async-start | bytes 12976128 | tf_op jit(solution)/shard_map/all_gather | solution.py:277
  7.3 0.7 copy-start.1
  7.9 0.7 copy-start.3
  11.6 12.5 %all-to-all-start = ((bf16[8,128,128]{2,1,0:T(8,128)(2,1)}), bf16[8,128,128]{2,1,0:T(8,128)(2,1)S(1)}, u32[]{:S(2)}, u32[]{:S(2)}) async-start(bf16[8,128,128]{2,1,0:T(8,128)(2,1)} %local_states.1), calls=%async_computation | async-start | bytes 524288 | tf_op jit(solution)/shard_map/all_to_all | solution.py:291
  24.8 10.9 %collective-permute-start = (bf16[136,128]{1,0:T(8,128)(2,1)S(1)}, bf16[136,128]{1,0:T(8,128)(2,1)S(1)}, u32[]{:S(2)}, u32[]{:S(2)}) collective-permute-start(bf16[136,128]{1,0:T(8,128)(2,1)S(1)} %fusion.16), channel_id=1, source_target_pairs={{0,96},{32,0},{64,32},{96,64},{1,97},{33,1},{65,33},{97,65},{2,98}... | collective-permute-start | bytes 104456 | tf_op jit(solution)/shard_map/ppermute | solution.py:317
  28.6 7.1 %collective-permute-start.1 = (bf16[136,128]{1,0:T(8,128)(2,1)S(1)}, bf16[136,128]{1,0:T(8,128)(2,1)S(1)}, u32[]{:S(2)}, u32[]{:S(2)}) collective-permute-start(bf16[136,128]{1,0:T(8,128)(2,1)S(1)} %fusion.16), channel_id=1, source_target_pairs={{0,64},{32,96},{64,0},{96,32},{1,65},{33,97},{65,1},{97,33},{2,66}... | collective-permute-start | bytes 104456 | tf_op jit(solution)/shard_map/ppermute | solution.py:317
  28.7 7.1 %collective-permute-start.2 = (bf16[136,128]{1,0:T(8,128)(2,1)S(1)}, bf16[136,128]{1,0:T(8,128)(2,1)S(1)}, u32[]{:S(2)}, u32[]{:S(2)}) collective-permute-start(bf16[136,128]{1,0:T(8,128)(2,1)S(1)} %fusion.16), channel_id=1, source_target_pairs={{0,32},{32,64},{64,96},{96,0},{1,33},{33,65},{65,97},{97,1},{2,34}... | collective-permute-start | bytes 104456 | tf_op jit(solution)/shard_map/ppermute | solution.py:317
  35.6 22.4 %copy-start.22 = (s32[4]{0:T(128)S(1)}, s32[4]{0:T(128)}, u32[]{:S(2)}) copy-start(s32[4]{0:T(128)} %constant.138) | copy-start | bytes 52
  35.6 22.4 %copy-start.21 = (s32[4]{0:T(128)S(1)}, s32[4]{0:T(128)}, u32[]{:S(2)}) copy-start(s32[4]{0:T(128)} %constant.137) | copy-start | bytes 52
  49.1 56.7 %copy-start = (bf16[128,1024]{1,0:T(8,128)(2,1)}, bf16[128,1024]{1,0:T(8,128)(2,1)S(1)}, u32[]{:S(2)}) copy-start(bf16[128,1024]{1,0:T(8,128)(2,1)S(1)} %get-tuple-element.22.refs_0_) | copy-start | bytes 786436
  49.1 8.1 %collective-permute-start.3 = (bf16[128,1024]{1,0:T(8,128)(2,1)S(1)}, bf16[128,1024]{1,0:T(8,128)(2,1)S(1)}, u32[]{:S(2)}, u32[]{:S(2)}) collective-permute-start(bf16[128,1024]{1,0:T(8,128)(2,1)S(1)} %get-tuple-element.22.refs_0_), channel_id=1, source_target_pairs={{0,32},{32,64},{64,96},{96,0},{1,33},{33,65},{65,97},{97,1},{2,34}... | collective-permute-start | bytes 786440 | tf_op jit(solution)/shard_map/ppermute | solution.py:344
  51.2 6.9 %collective-permute-start.4 = (bf16[128,1024]{1,0:T(8,128)(2,1)S(1)}, bf16[128,1024]{1,0:T(8,128)(2,1)S(1)}, u32[]{:S(2)}, u32[]{:S(2)}) collective-permute-start(bf16[128,1024]{1,0:T(8,128)(2,1)S(1)} %get-tuple-element.22.refs_0_), channel_id=1, source_target_pairs={{0,96},{32,0},{64,32},{96,64},{1,97},{33,1},{65,33},{97,65},{2,98}... | collective-permute-start | bytes 786440 | tf_op jit(solution)/shard_map/ppermute | solution.py:345
  51.9 27.7 %collective-permute-start.10 = (bf16[128,1024]{1,0:T(8,128)(2,1)S(1)}, bf16[128,1024]{1,0:T(8,128)(2,1)S(1)}, u32[]{:S(2)}, u32[]{:S(2)}) collective-permute-start(bf16[128,1024]{1,0:T(8,128)(2,1)S(1)} %get-tuple-element.25), channel_id=1, source_target_pairs={{0,1},{1,2},{2,3},{3,0},{4,5},{5,6},{6,7},{7,4},{8,9},{9,10},{10,1... | collective-permute-start | bytes 786440 | tf_op jit(solution)/shard_map/ppermute | solution.py:340
  53.1 26.5 %collective-permute-start.11 = (bf16[128,1024]{1,0:T(8,128)(2,1)S(1)}, bf16[128,1024]{1,0:T(8,128)(2,1)S(1)}, u32[]{:S(2)}, u32[]{:S(2)}) collective-permute-start(bf16[128,1024]{1,0:T(8,128)(2,1)S(1)} %get-tuple-element.26), channel_id=1, source_target_pairs={{0,2},{1,3},{2,0},{3,1},{4,6},{5,7},{6,4},{7,5},{8,10},{9,11},{10,... | collective-permute-start | bytes 786440 | tf_op jit(solution)/shard_map/ppermute | solution.py:340
  55.6 22.5 %collective-permute-start.6 = (bf16[128,1024]{1,0:T(8,128)(2,1)S(1)}, bf16[128,1024]{1,0:T(8,128)(2,1)S(1)}, u32[]{:S(2)}, u32[]{:S(2)}) collective-permute-start(bf16[128,1024]{1,0:T(8,128)(2,1)S(1)} %get-tuple-element.23), channel_id=1, source_target_pairs={{0,3},{1,0},{2,1},{3,2},{4,7},{5,4},{6,5},{7,6},{8,11},{9,8},{10,9... | collective-permute-start | bytes 786440 | tf_op jit(solution)/shard_map/ppermute | solution.py:340
  57.3 48.5 %copy-start.5 = (bf16[128,1024]{1,0:T(8,128)(2,1)}, bf16[128,1024]{1,0:T(8,128)(2,1)S(1)}, u32[]{:S(2)}) copy-start(bf16[128,1024]{1,0:T(8,128)(2,1)S(1)} %collective-permute-done.3.refs_1_) | copy-start | bytes 786436
  57.3 22.4 %collective-permute-start.5 = (bf16[128,1024]{1,0:T(8,128)(2,1)S(1)}, bf16[128,1024]{1,0:T(8,128)(2,1)S(1)}, u32[]{:S(2)}, u32[]{:S(2)}) collective-permute-start(bf16[128,1024]{1,0:T(8,128)(2,1)S(1)} %collective-permute-done.3.refs_1_), channel_id=1, source_target_pairs={{0,32},{32,64},{64,96},{96,0},{1,33},{33,65},{65,97},{97,1},{2,34}... | collective-permute-start | bytes 786440 | tf_op jit(solution)/shard_map/ppermute | solution.py:346
  58.1 47.7 %copy-start.6 = (bf16[128,1024]{1,0:T(8,128)(2,1)}, bf16[128,1024]{1,0:T(8,128)(2,1)S(1)}, u32[]{:S(2)}) copy-start(bf16[128,1024]{1,0:T(8,128)(2,1)S(1)} %collective-permute-done.4.refs_2_) | copy-start | bytes 786436
  78.1 27.7 %copy-start.9 = (bf16[128,1024]{1,0:T(8,128)(2,1)}, bf16[128,1024]{1,0:T(8,128)(2,1)S(1)}, u32[]{:S(2)}) copy-start(bf16[128,1024]{1,0:T(8,128)(2,1)S(1)} %collective-permute-done.6.refs_4_) | copy-start | bytes 786436
  78.1 5.6 %collective-permute-start.8 = (bf16[128,1024]{1,0:T(8,128)(2,1)S(1)}, bf16[128,1024]{1,0:T(8,128)(2,1)S(1)}, u32[]{:S(2)}, u32[]{:S(2)}) collective-permute-start(bf16[128,1024]{1,0:T(8,128)(2,1)S(1)} %collective-permute-done.6.refs_4_), channel_id=1, source_target_pairs={{0,96},{32,0},{64,32},{96,64},{1,97},{33,1},{65,33},{97,65},{2,98}... | collective-permute-start | bytes 786440 | tf_op jit(solution)/shard_map/ppermute | solution.py:345
  78.7 6.6 %collective-permute-start.7 = (bf16[128,1024]{1,0:T(8,128)(2,1)S(1)}, bf16[128,1024]{1,0:T(8,128)(2,1)S(1)}, u32[]{:S(2)}, u32[]{:S(2)}) collective-permute-start(bf16[128,1024]{1,0:T(8,128)(2,1)S(1)} %collective-permute-done.6.refs_4_), channel_id=1, source_target_pairs={{0,32},{32,64},{64,96},{96,0},{1,33},{33,65},{65,97},{97,1},{2,34}... | collective-permute-start | bytes 786440 | tf_op jit(solution)/shard_map/ppermute | solution.py:344
  79.6 26.2 %copy-start.7 = (bf16[128,1024]{1,0:T(8,128)(2,1)}, bf16[128,1024]{1,0:T(8,128)(2,1)S(1)}, u32[]{:S(2)}) copy-start(bf16[128,1024]{1,0:T(8,128)(2,1)S(1)} %collective-permute-done.10.refs_8_) | copy-start | bytes 786436
  79.6 26.2 %copy-start.8 = (bf16[128,1024]{1,0:T(8,128)(2,1)}, bf16[128,1024]{1,0:T(8,128)(2,1)S(1)}, u32[]{:S(2)}) copy-start(bf16[128,1024]{1,0:T(8,128)(2,1)S(1)} %collective-permute-done.11.refs_12_) | copy-start | bytes 786436
  79.6 26.2 %copy-start.10 = (bf16[128,1024]{1,0:T(8,128)(2,1)}, bf16[128,1024]{1,0:T(8,128)(2,1)S(1)}, u32[]{:S(2)}) copy-start(bf16[128,1024]{1,0:T(8,128)(2,1)S(1)} %collective-permute-done.5.refs_3_) | copy-start | bytes 786436
  79.6 10.8 %collective-permute-start.12 = (bf16[128,1024]{1,0:T(8,128)(2,1)S(1)}, bf16[128,1024]{1,0:T(8,128)(2,1)S(1)}, u32[]{:S(2)}, u32[]{:S(2)}) collective-permute-start(bf16[128,1024]{1,0:T(8,128)(2,1)S(1)} %collective-permute-done.10.refs_8_), channel_id=1, source_target_pairs={{0,32},{32,64},{64,96},{96,0},{1,33},{33,65},{65,97},{97,1},{2,34}... | collective-permute-start | bytes 786440 | tf_op jit(solution)/shard_map/ppermute | solution.py:344
  80.5 9.9 %collective-permute-start.16 = (bf16[128,1024]{1,0:T(8,128)(2,1)S(1)}, bf16[128,1024]{1,0:T(8,128)(2,1)S(1)}, u32[]{:S(2)}, u32[]{:S(2)}) collective-permute-start(bf16[128,1024]{1,0:T(8,128)(2,1)S(1)} %collective-permute-done.11.refs_12_), channel_id=1, source_target_pairs={{0,96},{32,0},{64,32},{96,64},{1,97},{33,1},{65,33},{97,65},{2,98}... | collective-permute-start | bytes 786440 | tf_op jit(solution)/shard_map/ppermute | solution.py:345
  82.7 11.8 %collective-permute-start.13 = (bf16[128,1024]{1,0:T(8,128)(2,1)S(1)}, bf16[128,1024]{1,0:T(8,128)(2,1)S(1)}, u32[]{:S(2)}, u32[]{:S(2)}) collective-permute-start(bf16[128,1024]{1,0:T(8,128)(2,1)S(1)} %collective-permute-done.10.refs_8_), channel_id=1, source_target_pairs={{0,96},{32,0},{64,32},{96,64},{1,97},{33,1},{65,33},{97,65},{2,98}... | collective-permute-start | bytes 786440 | tf_op jit(solution)/shard_map/ppermute | solution.py:345
  83.8 22.1 %copy-start.11 = (bf16[128,1024]{1,0:T(8,128)(2,1)}, bf16[128,1024]{1,0:T(8,128)(2,1)S(1)}, u32[]{:S(2)}) copy-start(bf16[128,1024]{1,0:T(8,128)(2,1)S(1)} %collective-permute-done.8.refs_6_) | copy-start | bytes 786436
  83.8 12.3 %collective-permute-start.15 = (bf16[128,1024]{1,0:T(8,128)(2,1)S(1)}, bf16[128,1024]{1,0:T(8,128)(2,1)S(1)}, u32[]{:S(2)}, u32[]{:S(2)}) collective-permute-start(bf16[128,1024]{1,0:T(8,128)(2,1)S(1)} %collective-permute-done.11.refs_12_), channel_id=1, source_target_pairs={{0,32},{32,64},{64,96},{96,0},{1,33},{33,65},{65,97},{97,1},{2,34}... | collective-permute-start | bytes 786440 | tf_op jit(solution)/shard_map/ppermute | solution.py:344
  85.2 20.6 %copy-start.12 = (bf16[128,1024]{1,0:T(8,128)(2,1)}, bf16[128,1024]{1,0:T(8,128)(2,1)S(1)}, u32[]{:S(2)}) copy-start(bf16[128,1024]{1,0:T(8,128)(2,1)S(1)} %collective-permute-done.7.refs_5_) | copy-start | bytes 786436
  85.2 14.9 %collective-permute-start.9 = (bf16[128,1024]{1,0:T(8,128)(2,1)S(1)}, bf16[128,1024]{1,0:T(8,128)(2,1)S(1)}, u32[]{:S(2)}, u32[]{:S(2)}) collective-permute-start(bf16[128,1024]{1,0:T(8,128)(2,1)S(1)} %collective-permute-done.8.refs_6_), channel_id=1, source_target_pairs={{0,96},{32,0},{64,32},{96,64},{1,97},{33,1},{65,33},{97,65},{2,98}... | collective-permute-start | bytes 786440 | tf_op jit(solution)/shard_map/ppermute | solution.py:346
  90.4 9.8 %copy-start.13 = (bf16[128,1024]{1,0:T(8,128)(2,1)}, bf16[128,1024]{1,0:T(8,128)(2,1)S(1)}, u32[]{:S(2)}) copy-start(bf16[128,1024]{1,0:T(8,128)(2,1)S(1)} %collective-permute-done.12.refs_9_) | copy-start | bytes 786436
  90.4 11.2 %collective-permute-start.14 = (bf16[128,1024]{1,0:T(8,128)(2,1)S(1)}, bf16[128,1024]{1,0:T(8,128)(2,1)S(1)}, u32[]{:S(2)}, u32[]{:S(2)}) collective-permute-start(bf16[128,1024]{1,0:T(8,128)(2,1)S(1)} %collective-permute-done.12.refs_9_), channel_id=1, source_target_pairs={{0,32},{32,64},{64,96},{96,0},{1,33},{33,65},{65,97},{97,1},{2,34}... | collective-permute-start | bytes 786440 | tf_op jit(solution)/shard_map/ppermute | solution.py:346
  90.4 11.2 %copy-start.14 = (bf16[128,1024]{1,0:T(8,128)(2,1)}, bf16[128,1024]{1,0:T(8,128)(2,1)S(1)}, u32[]{:S(2)}) copy-start(bf16[128,1024]{1,0:T(8,128)(2,1)S(1)} %collective-permute-done.16.refs_14_) | copy-start | bytes 786436
  90.4 15.3 %collective-permute-start.17 = (bf16[128,1024]{1,0:T(8,128)(2,1)S(1)}, bf16[128,1024]{1,0:T(8,128)(2,1)}, u32[]{:S(2)}, u32[]{:S(2)}) collective-permute-start(bf16[128,1024]{1,0:T(8,128)(2,1)S(1)} %collective-permute-done.16.refs_14_), channel_id=1, source_target_pairs={{0,96},{32,0},{64,32},{96,64},{1,97},{33,1},{65,33},{97,65},{2,98}... | collective-permute-start | bytes 786440 | tf_op jit(solution)/shard_map/ppermute | solution.py:346
  94.5 7.1 %copy-start.15 = (bf16[128,1024]{1,0:T(8,128)(2,1)}, bf16[128,1024]{1,0:T(8,128)(2,1)S(1)}, u32[]{:S(2)}) copy-start(bf16[128,1024]{1,0:T(8,128)(2,1)S(1)} %collective-permute-done.13.refs_10_) | copy-start | bytes 786436
  96.0 5.6 %copy-start.16 = (bf16[128,1024]{1,0:T(8,128)(2,1)}, bf16[128,1024]{1,0:T(8,128)(2,1)S(1)}, u32[]{:S(2)}) copy-start(bf16[128,1024]{1,0:T(8,128)(2,1)S(1)} %collective-permute-done.15.refs_13_) | copy-start | bytes 786436
  100.2 1.5 copy-start.17
  101.7 0.7 copy-start.18
  120.2 10.2 %copy-start.19 = (s32[512]{0:T(512)S(1)}, s32[512]{0:T(512)}, u32[]{:S(2)}) copy-start(s32[512]{0:T(512)} %param.17) | copy-start | bytes 6148
  120.2 62.4 %all-to-all-start.2 = ((bf16[128,8,1536]{2,1,0:T(8,128)(2,1)}), bf16[128,8,1536]{2,1,0:T(8,128)(2,1)S(1)}, u32[]{:S(2)}, u32[]{:S(2)}) async-start(bf16[128,8,1536]{2,1,0:T(8,128)(2,1)} %bitcast.38), calls=%async_computation.2 | async-start | bytes 6291456 | tf_op jit(solution)/shard_map/all_to_all | solution.py:371
Sparse Core Ops, SparseCore 0:
  9.6 77.3 all-gather.2

commit v9 on v5

--- a/solution.py
+++ b/solution.py
@@ -15,6 +15,7 @@
 SEQ = ("z", "y", "core")
 ALL = ("z", "y", "core", "head")
 TURNS = (0, 3, 1, 2)
+ZTURNS = (1, 3, 2)
 
 
 def doc_of(positions, doc_ends):
@@ -276,11 +277,11 @@
     weight = lax.all_gather(value_weight, ("head", "y", "core"), axis=0, tiled=True)
     weight = weight.reshape(n_head, -1, value_weight.shape[1])
 
-    queries, key_vectors, output_grad = (
+    queries, key_vectors, output_grad, rates, lengths = (
         pltpu.with_memory_space_constraint(array, pltpu.HBM)
-        for array in (queries, key_vectors, output_grad)
-    )
-    state = local_states(decay_rate, doc_lengths, queries, output_grad, head_local // 2)
+        for array in (queries, key_vectors, output_grad, decay_rate, doc_lengths)
+    )
+    state = local_states(rates, lengths, queries, output_grad, head_local // 2)
     blocks = tok_rows // ROWS_BLK
     per = blocks * CAPACITY
     owners = owner_block[:, 0].reshape(blocks, ROWS_BLK)
@@ -302,7 +303,7 @@
         state.reshape(n_seq, share, head_dim), SEQ, split_axis=0, concat_axis=0, tiled=True
     )
     intra = within(
-        decay_rate, doc_lengths, queries, key_vectors, output_grad, head_local // 2
+        rates, lengths, queries, key_vectors, output_grad, head_local // 2
     )
 
     state_in, intra = lax.optimization_barrier((state_in, intra))
@@ -337,7 +338,7 @@
     )
     column = offsets.reshape(-1, 1)
     row = offsets.reshape(n_z, plane, blocks, CAPACITY).transpose(1, 2, 0, 3).reshape(1, -1)
-    near_z = (z_rank + turns) % n_z
+    near_z = (z_rank - jnp.array((0,) + ZTURNS, jnp.int32)) % n_z
     theirs = carried[:, share + 1].reshape(n_z, plane, ROWS_BLK)
     theirs = lax.dynamic_slice_in_dim(theirs, seq_rank % plane, 1, 1)[:, 0]
     theirs = theirs[near_z].astype(jnp.int32)
@@ -346,22 +347,27 @@
     pick = (all_slots[:, None] == their_slots[None, :]).astype(BF16)
     carried = carried[:, :share].reshape(head_local, head_dim, head_dim)
 
-    own = across(decay_rate, doc_lengths, key_vectors, carried, intra)
+    own = across(rates, lengths, key_vectors, carried, intra)
     mine = [own[0]]
     for turn in range(1, len(TURNS)):
         mine.append(lax.ppermute(own[turn], "head", shift(n_head, TURNS[turn])))
     place = (head_rank - turns) % n_head
 
-    pieces = []
-    for turn, rows in enumerate(mine):
+    def spread(rows, flip):
         below = lax.ppermute(rows, "z", shift(n_z, 1))
         above = lax.ppermute(rows, "z", shift(n_z, -1))
-        if turn % 2 == 0:
-            across_z = lax.ppermute(below, "z", shift(n_z, 1))
-        else:
-            across_z = lax.ppermute(above, "z", shift(n_z, -1))
-        group = (rows, below, above, across_z)
-        pieces.append([pltpu.with_memory_space_constraint(q, pltpu.HBM) for q in group])
+        relay = lax.ppermute(above if flip else below, "z", shift(n_z, -1 if flip else 1))
+        return rows, below, above, relay
+
+    groups = [spread(mine[0], False)]
+    mine[1], mine[2], *_ = lax.optimization_barrier((mine[1], mine[2]) + groups[0][1:3])
+    groups.append(spread(mine[1], True))
+    groups.append(spread(mine[2], False))
+    mine[3], *_ = lax.optimization_barrier((mine[3], groups[0][3]))
+    groups.append(spread(mine[3], True))
+    pieces = [
+        [pltpu.with_memory_space_constraint(q, pltpu.HBM) for q in group] for group in groups
+    ]
 
     send = project(place, pick, pieces, weight, 512)
     send = send.reshape(devices_all, per, -1)

time: 177 us -> 174 us (0.983)
  starting transfers between devices: 36 us -> 30.3 us
  waiting for transfers between devices: 76.4 us -> 79.3 us
    ppermute x12, starting transfers between devices: 16.1 us -> 9.06 us  [the longest x4 3.09 us: spread(): above = lax.ppermute(rows, 'z', shift(n_z, -1))]
    ppermute x12, waiting for transfers between devices: 13.1 us -> 17.4 us  [the longest x4 9.86 us: spread(): lax.ppermute(above if flip else below, 'z', shift(n_z, -1 if flip else 1))]
  transfers between devices with their start and end apart: 18 -> 18, of which waited for: 9 -> 10; matrix products, arithmetic and copies ran while one was open for 3% -> 3% of each run, Pallas kernels for 6% -> 6%
where the time goes in v9:
time: 174 us; the launch traced here: 173 us
  waiting for transfers between devices  79.3 us (46%)
  starting transfers between devices  30.3 us (17%)
  Pallas kernels  27 us (16%)
  blocking collectives  15.2 us (9%)
  between operations  14.4 us (8%)
  local copies, waits for them, and re-layouts  4.64 us (3%)
  other arithmetic  2.24 us (1%)
    all_to_all x1, waiting for transfers between devices, per_device(): got = lax.all_to_all(send, ALL, split_axis=0, concat_axis=0, tiled=True)  40.3 us
    ppermute x3, waiting for transfers between devices, per_device(): mine.append(lax.ppermute(own[turn], 'head', shift(n_head, TURNS[turn])))  19.3 us
    all_to_all x1, blocking collectives, per_device(): lax.all_to_all(jnp.concatenate([carried_all, note], axis=1), SEQ, split_a...  15.2 us
    pallas_call x1, Pallas kernels, project(): pl.pallas_call(functools.partial(project_body, turns), grid_spec=pltpu.Pr...  14.4 us
    ppermute x4, waiting for transfers between devices, spread(): lax.ppermute(above if flip else below, 'z', shift(n_z, -1 if flip else 1))  9.86 us
    all_to_all x1, starting transfers between devices, per_device(): lax.all_to_all(state.reshape(n_seq, share, head_dim), SEQ, split_axis=0,...  9.6 us
    all_to_all x1, starting transfers between devices, per_device(): got = lax.all_to_all(send, ALL, split_axis=0, concat_axis=0, tiled=True)  7.51 us
    ppermute x4, waiting for transfers between devices, spread(): above = lax.ppermute(rows, 'z', shift(n_z, -1))  5.36 us
  transfers between devices with their start and end apart: 18, of which 10 were waited for; matrix products, arithmetic and copies ran while one was open for 3% of the time, Pallas kernels for 6%

profile of v9, /device:TPU:1, one launch (start us, length us, event | category | flops | bytes accessed | tf_op | source)
XLA Modules:
  0.0 173.5 jit_solution(10817804843416605704)
XLA Ops:
  6.5 0.0 all-gather.2.cloned.1.call-start
  6.6 0.7 all-gather.2.cloned.1.call-update
  7.3 3.0 %local_states.1 = bf16[8,128,128]{2,1,0:T(8,128)(2,1)} custom-call(f32[8]{0:T(128)} %rate_ref.5, s32[4]{0:T(128)} %lengths_ref.5, bf16[512,1024]{1,0:T(8,128)(2,1)} %query_ref.3, bf16[512,1024]{1,0:T(8,128)(2,1)} %grad_ref.3), custom_call_target="tpu_custom_call" | custom-call | tf_op jit(solution)/shard_map/local_states/pallas_call | solution.py:65
  10.3 9.6 %all-to-all-start = ((bf16[32,32,128]{2,1,0:T(8,128)(2,1)}), bf16[32,32,128]{2,1,0:T(8,128)(2,1)S(1)}, u32[]{:S(2)}, u32[]{:S(2)}) async-start(bf16[32,32,128]{2,1,0:T(8,128)(2,1)} %bitcast.4), calls=%async_computation | async-start | bytes 524288 | tf_op jit(solution)/shard_map/all_to_all | solution.py:302
  20.0 0.2 convert_reduce_fusion.1
  20.2 0.1 iota_add_fusion
  20.3 0.7 select_reduce_fusion
  21.0 0.1 maximum_bitcast_fusion
  21.2 0.6 dynamic_slice.9
  22.4 0.2 reduce-window.8
  22.6 4.5 %within.1.intra_ref = f32[512,1024]{1,0:T(8,128)S(1)} custom-call(f32[8]{0:T(128)} %rate_ref.5, s32[4]{0:T(128)} %lengths_ref.5, bf16[512,1024]{1,0:T(8,128)(2,1)} %query_ref.3, bf16[512,1024]{1,0:T(8,128)(2,1)} %key_ref.3, bf16[512,1024]{1,0:T(8,128)(2,1)} %grad_ref.3), custom_call_target="tpu_custom_call" | custom-call | tf_op jit(solution)/shard_map/within/pallas_call | solution.py:107
  27.1 0.1 convert_reduce_fusion.3
  27.2 1.6 all-to-all-done
  28.8 0.4 convolution_convert_fusion
  29.3 0.1 copy.39
  29.4 15.2 %all_to_all.15 = bf16[32,40,128]{2,1,0:T(8,128)(2,1)S(1)} all-to-all(bf16[32,40,128]{2,1,0:T(8,128)(2,1)S(1)} %copy.39), channel_id=1, replica_groups=mesh['z'=4,'y'=4,'core'=2,'head'=4] {'z','y','core'}, dimensions={0} | all-to-all | bytes 655360 | tf_op jit(solution)/shard_map/all_to_all | solution.py:327
  44.6 2.6 %across.1 = (bf16[128,1024]{1,0:T(8,128)(2,1)S(1)}, bf16[128,1024]{1,0:T(8,128)(2,1)S(1)}, bf16[128,1024]{1,0:T(8,128)(2,1)S(1)}, bf16[128,1024]{1,0:T(8,128)(2,1)S(1)}) custom-call(f32[8]{0:T(128)} %rate_ref.5, s32[4]{0:T(128)} %lengths_ref.5, bf16[512,1024]{1,0:T(8,128)(2,1)} %key_ref.3, bf16[8,128,128]{2,1,0:T(8,128)(2,1)S(1)} %bitcast.39, ...), custom_call_target="tpu_custom_call" | custom-call | tf_op jit(solution)/shard_map/across/pallas_call | solution.py:145
  47.2 0.1 collective-permute-start
  47.4 2.6 %collective-permute-start.1 = (bf16[128,1024]{1,0:T(8,128)(2,1)S(1)}, bf16[128,1024]{1,0:T(8,128)(2,1)S(1)}, u32[]{:S(2)}, u32[]{:S(2)}) collective-permute-start(bf16[128,1024]{1,0:T(8,128)(2,1)S(1)} %get-tuple-element.16.refs_0_), channel_id=1, source_target_pairs={{0,96},{32,0},{64,32},{96,64},{1,97},{33,1},{65,33},{97,65},{2,98}... | collective-permute-start | bytes 786440 | tf_op jit(solution)/shard_map/ppermute | solution.py:358
  50.0 2.4 %collective-permute-start.3 = (bf16[128,1024]{1,0:T(8,128)(2,1)S(1)}, bf16[128,1024]{1,0:T(8,128)(2,1)S(1)}, u32[]{:S(2)}, u32[]{:S(2)}) collective-permute-start(bf16[128,1024]{1,0:T(8,128)(2,1)S(1)} %get-tuple-element.17), channel_id=1, source_target_pairs={{0,3},{1,0},{2,1},{3,2},{4,7},{5,4},{6,5},{7,6},{8,11},{9,8},{10,9... | collective-permute-start | bytes 786440 | tf_op jit(solution)/shard_map/ppermute | solution.py:353
  52.4 0.0 collective-permute-start.4
  52.4 1.7 collective-permute-start.11
  54.1 2.2 %collective-permute-done.refs_1_ = bf16[128,1024]{1,0:T(8,128)(2,1)S(1)} collective-permute-done((bf16[128,1024]{1,0:T(8,128)(2,1)S(1)}, bf16[128,1024]{1,0:T(8,128)(2,1)S(1)}, u32[]{:S(2)}, u32[]{:S(2)}) %collective-permute-start) | collective-permute-done | bytes 262176 | tf_op jit(solution)/shard_map/ppermute | solution.py:357
  56.3 0.0 collective-permute-start.2
  56.3 7.2 %collective-permute-done.3.refs_4_ = bf16[128,1024]{1,0:T(8,128)(2,1)S(1)} collective-permute-done((bf16[128,1024]{1,0:T(8,128)(2,1)S(1)}, bf16[128,1024]{1,0:T(8,128)(2,1)S(1)}, u32[]{:S(2)}, u32[]{:S(2)}) %collective-permute-start.3) | collective-permute-done | bytes 262176 | tf_op jit(solution)/shard_map/ppermute | solution.py:353
  63.6 3.8 %collective-permute-done.4.refs_8_ = bf16[128,1024]{1,0:T(8,128)(2,1)S(1)} collective-permute-done((bf16[128,1024]{1,0:T(8,128)(2,1)S(1)}, bf16[128,1024]{1,0:T(8,128)(2,1)S(1)}, u32[]{:S(2)}, u32[]{:S(2)}) %collective-permute-start.4) | collective-permute-done | bytes 262176 | tf_op jit(solution)/shard_map/ppermute | solution.py:353
  67.4 0.0 collective-permute-done.1.refs_2_
  67.4 0.2 collective-permute-start.6
  67.6 1.4 collective-permute-start.5
  68.9 0.0 collective-permute-start.8
  69.0 8.3 %collective-permute-done.11.refs_12_ = bf16[128,1024]{1,0:T(8,128)(2,1)S(1)} collective-permute-done((bf16[128,1024]{1,0:T(8,128)(2,1)S(1)}, bf16[128,1024]{1,0:T(8,128)(2,1)S(1)}, u32[]{:S(2)}, u32[]{:S(2)}) %collective-permute-start.11) | collective-permute-done | bytes 262176 | tf_op jit(solution)/shard_map/ppermute | solution.py:353
  77.3 0.0 collective-permute-done.2.refs_3_
  77.3 0.2 collective-permute-start.13
  77.5 0.6 gather_fusion
  78.1 0.2 convert_reduce_fusion
  78.3 0.2 collective-permute-start.9
  78.5 0.0 collective-permute-done.6.refs_6_
  78.5 1.4 collective-permute-start.12
  79.8 1.3 collective-permute-start.7
  81.2 0.2 collective-permute-start.10
  81.3 1.9 %collective-permute-done.13.refs_14_ = bf16[128,1024]{1,0:T(8,128)(2,1)} collective-permute-done((bf16[128,1024]{1,0:T(8,128)(2,1)S(1)}, bf16[128,1024]{1,0:T(8,128)(2,1)}, u32[]{:S(2)}, u32[]{:S(2)}) %collective-permute-start.13) | collective-permute-done | bytes 262176 | tf_op jit(solution)/shard_map/ppermute | solution.py:358
  83.3 1.6 collective-permute-start.14
  84.8 0.1 add_bitcast_fusion
  84.9 0.4 fusion.pick
  85.3 3.4 %collective-permute-done.9.refs_10_ = bf16[128,1024]{1,0:T(8,128)(2,1)S(1)} collective-permute-done((bf16[128,1024]{1,0:T(8,128)(2,1)S(1)}, bf16[128,1024]{1,0:T(8,128)(2,1)S(1)}, u32[]{:S(2)}, u32[]{:S(2)}) %collective-permute-start.9) | collective-permute-done | bytes 262176 | tf_op jit(solution)/shard_map/ppermute | solution.py:358
  88.8 5.6 %collective-permute-done.7.refs_7_ = bf16[128,1024]{1,0:T(8,128)(2,1)S(1)} collective-permute-done((bf16[128,1024]{1,0:T(8,128)(2,1)S(1)}, bf16[128,1024]{1,0:T(8,128)(2,1)S(1)}, u32[]{:S(2)}, u32[]{:S(2)}) %collective-permute-start.7) | collective-permute-done | bytes 262176 | tf_op jit(solution)/shard_map/ppermute | solution.py:359
  94.4 0.0 collective-permute-done.10.refs_11_
  94.4 0.0 collective-permute-done.12.refs_13_
  94.4 0.7 copy-done.12
  95.1 0.1 copy-done.13
  95.2 0.7 copy-done.11
  95.9 4.2 %collective-permute-done.14.refs_15_ = bf16[128,1024]{1,0:T(8,128)(2,1)} collective-permute-done((bf16[128,1024]{1,0:T(8,128)(2,1)}, bf16[128,1024]{1,0:T(8,128)(2,1)}, u32[]{:S(2)}, u32[]{:S(2)}) %collective-permute-start.14) | collective-permute-done | bytes 262176 | tf_op jit(solution)/shard_map/ppermute | solution.py:359
  100.2 14.4 %project.1 = bf16[1024,1536]{1,0:T(8,128)(2,1)} custom-call(s32[4]{0:T(128)S(1)} %and_select_fusion.1.place, bf16[1024,512]{1,0:T(8,128)(2,1)S(1)} %fusion.pick, bf16[128,1024]{1,0:T(8,128)(2,1)} %copy-done, bf16[128,1024]{1,0:T(8,128)(2,1)} %copy-done.2, bf16[128,1024]{1,0:T(8,128)(2,1)} %copy-done.3, bf16[128,1024]{1,0:T(8,128)(2,1)} %copy-done.7, ...), custom_call_target="tpu_custom_call" | custom-call | tf_op jit(solution)/shard_map/project/pallas_call | solution.py:186
  114.5 7.5 %all-to-all-start.2 = ((bf16[128,8,1536]{2,1,0:T(8,128)(2,1)}), bf16[128,8,1536]{2,1,0:T(8,128)(2,1)S(1)}, u32[]{:S(2)}, u32[]{:S(2)}) async-start(bf16[128,8,1536]{2,1,0:T(8,128)(2,1)} %bitcast.44), calls=%async_computation.2 | async-start | bytes 6291456 | tf_op jit(solution)/shard_map/all_to_all | solution.py:374
  122.1 1.0 fusion.35
  123.1 0.1 copy.48
  123.2 0.1 copy.49
  123.2 0.1 sub.71
  123.3 0.1 copy.42
  123.4 0.2 copy.43
  123.6 0.2 reshape.207.row_ref
  123.7 0.1 sub.76.column_ref
  123.8 40.3 %all-to-all-done.2 = bf16[128,8,1536]{2,1,0:T(8,128)(2,1)S(1)} async-done(((bf16[128,8,1536]{2,1,0:T(8,128)(2,1)}), bf16[128,8,1536]{2,1,0:T(8,128)(2,1)S(1)}, u32[]{:S(2)}, u32[]{:S(2)}) %all-to-all-start.2) | async-done | bytes 3145760 | tf_op jit(solution)/shard_map/all_to_all | solution.py:374
  164.1 2.5 %merge.1 = bf16[1,128,2,6144]{3,2,1,0:T(2,128)(2,1)} custom-call(s32[256,1]{1,0:T(8,128)S(1)} %sub.76.column_ref, s32[1,256]{1,0:T(1,128)S(1)} %reshape.207.row_ref, bf16[4,32,8,1536]{3,2,1,0:T(8,128)(2,1)S(1)} %bitcast.38), custom_call_target="tpu_custom_call" | custom-call | tf_op jit(solution)/shard_map/merge/pallas_call | solution.py:223
  (60 shorter events, 0.3 us)
Async XLA Ops:
  6.5 15.9 %copy-start.16 = (s32[4]{0:T(128)S(1)}, s32[4]{0:T(128)}, u32[]{:S(2)}) copy-start(s32[4]{0:T(128)} %lengths_ref.5) | copy-start | bytes 52
  6.5 14.6 %copy-start.15 = (f32[8]{0:T(128)S(1)}, f32[8]{0:T(128)}, u32[]{:S(2)}) copy-start(f32[8]{0:T(128)} %rate_ref.5) | copy-start | bytes 100
  6.5 13.4 %copy-start.14 = (s32[512,1]{0,1:T(1,128)S(1)}, s32[512,1]{0,1:T(1,128)}, u32[]{:S(2)}) copy-start(s32[512,1]{0,1:T(1,128)} %param.16) | copy-start | bytes 6148
  6.5 13.7 %copy-start.17 = (s32[512]{0:T(512)S(1)}, s32[512]{0:T(512)}, u32[]{:S(2)}) copy-start(s32[512]{0:T(512)} %param.17) | copy-start | bytes 6148
  6.5 93.6 %all-gather.2.cloned.1.call-start = ((), (), s32[]{:S(2)}) async-start(), calls=%async_computation.3 | async-start | bytes 12976128 | tf_op jit(solution)/shard_map/all_gather | solution.py:277
  10.3 18.5 %all-to-all-start = ((bf16[32,32,128]{2,1,0:T(8,128)(2,1)}), bf16[32,32,128]{2,1,0:T(8,128)(2,1)S(1)}, u32[]{:S(2)}, u32[]{:S(2)}) async-start(bf16[32,32,128]{2,1,0:T(8,128)(2,1)} %bitcast.4), calls=%async_computation | async-start | bytes 524288 | tf_op jit(solution)/shard_map/all_to_all | solution.py:302
  28.8 27.5 %copy-start.19 = (s32[4]{0:T(128)S(1)}, s32[4]{0:T(128)}, u32[]{:S(2)}) copy-start(s32[4]{0:T(128)} %constant.125) | copy-start | bytes 52
  28.8 27.5 %copy-start.18 = (s32[4]{0:T(128)S(1)}, s32[4]{0:T(128)}, u32[]{:S(2)}) copy-start(s32[4]{0:T(128)} %constant.126) | copy-start | bytes 52
  44.6 69.9 %copy-start.1 = (bf16[32,40,128]{2,1,0:T(8,128)(2,1)}, bf16[32,40,128]{2,1,0:T(8,128)(2,1)S(1)}, u32[]{:S(2)}) copy-start(bf16[32,40,128]{2,1,0:T(8,128)(2,1)S(1)} %all_to_all.15) | copy-start | bytes 983044
  47.2 52.9 %copy-start = (bf16[128,1024]{1,0:T(8,128)(2,1)}, bf16[128,1024]{1,0:T(8,128)(2,1)S(1)}, u32[]{:S(2)}) copy-start(bf16[128,1024]{1,0:T(8,128)(2,1)S(1)} %get-tuple-element.16.refs_0_) | copy-start | bytes 786436
  47.2 9.0 %collective-permute-start = (bf16[128,1024]{1,0:T(8,128)(2,1)S(1)}, bf16[128,1024]{1,0:T(8,128)(2,1)S(1)}, u32[]{:S(2)}, u32[]{:S(2)}) collective-permute-start(bf16[128,1024]{1,0:T(8,128)(2,1)S(1)} %get-tuple-element.16.refs_0_), channel_id=1, source_target_pairs={{0,32},{32,64},{64,96},{96,0},{1,33},{33,65},{65,97},{97,1},{2,34}... | collective-permute-start | bytes 786440 | tf_op jit(solution)/shard_map/ppermute | solution.py:357
  47.4 20.1 %collective-permute-start.1 = (bf16[128,1024]{1,0:T(8,128)(2,1)S(1)}, bf16[128,1024]{1,0:T(8,128)(2,1)S(1)}, u32[]{:S(2)}, u32[]{:S(2)}) collective-permute-start(bf16[128,1024]{1,0:T(8,128)(2,1)S(1)} %get-tuple-element.16.refs_0_), channel_id=1, source_target_pairs={{0,96},{32,0},{64,32},{96,64},{1,97},{33,1},{65,33},{97,65},{2,98}... | collective-permute-start | bytes 786440 | tf_op jit(solution)/shard_map/ppermute | solution.py:358
  50.0 13.6 %collective-permute-start.3 = (bf16[128,1024]{1,0:T(8,128)(2,1)S(1)}, bf16[128,1024]{1,0:T(8,128)(2,1)S(1)}, u32[]{:S(2)}, u32[]{:S(2)}) collective-permute-start(bf16[128,1024]{1,0:T(8,128)(2,1)S(1)} %get-tuple-element.17), channel_id=1, source_target_pairs={{0,3},{1,0},{2,1},{3,2},{4,7},{5,4},{6,5},{7,6},{8,11},{9,8},{10,9... | collective-permute-start | bytes 786440 | tf_op jit(solution)/shard_map/ppermute | solution.py:353
  52.4 15.0 %collective-permute-start.4 = (bf16[128,1024]{1,0:T(8,128)(2,1)S(1)}, bf16[128,1024]{1,0:T(8,128)(2,1)S(1)}, u32[]{:S(2)}, u32[]{:S(2)}) collective-permute-start(bf16[128,1024]{1,0:T(8,128)(2,1)S(1)} %get-tuple-element.18), channel_id=1, source_target_pairs={{0,1},{1,2},{2,3},{3,0},{4,5},{5,6},{6,7},{7,4},{8,9},{9,10},{10,1... | collective-permute-start | bytes 786440 | tf_op jit(solution)/shard_map/ppermute | solution.py:353
  52.4 24.9 %collective-permute-start.11 = (bf16[128,1024]{1,0:T(8,128)(2,1)S(1)}, bf16[128,1024]{1,0:T(8,128)(2,1)S(1)}, u32[]{:S(2)}, u32[]{:S(2)}) collective-permute-start(bf16[128,1024]{1,0:T(8,128)(2,1)S(1)} %get-tuple-element.21), channel_id=1, source_target_pairs={{0,2},{1,3},{2,0},{3,1},{4,6},{5,7},{6,4},{7,5},{8,10},{9,11},{10,... | collective-permute-start | bytes 786440 | tf_op jit(solution)/shard_map/ppermute | solution.py:353
  56.3 43.8 %copy-start.2 = (bf16[128,1024]{1,0:T(8,128)(2,1)}, bf16[128,1024]{1,0:T(8,128)(2,1)S(1)}, u32[]{:S(2)}) copy-start(bf16[128,1024]{1,0:T(8,128)(2,1)S(1)} %collective-permute-done.refs_1_) | copy-start | bytes 786436
  56.3 21.0 %collective-permute-start.2 = (bf16[128,1024]{1,0:T(8,128)(2,1)S(1)}, bf16[128,1024]{1,0:T(8,128)(2,1)S(1)}, u32[]{:S(2)}, u32[]{:S(2)}) collective-permute-start(bf16[128,1024]{1,0:T(8,128)(2,1)S(1)} %collective-permute-done.refs_1_), channel_id=1, source_target_pairs={{0,32},{32,64},{64,96},{96,0},{1,33},{33,65},{65,97},{97,1},{2,34}... | collective-permute-start | bytes 786440 | tf_op jit(solution)/shard_map/ppermute | solution.py:359
  63.6 36.5 %copy-start.4 = (bf16[128,1024]{1,0:T(8,128)(2,1)}, bf16[128,1024]{1,0:T(8,128)(2,1)S(1)}, u32[]{:S(2)}) copy-start(bf16[128,1024]{1,0:T(8,128)(2,1)S(1)} %collective-permute-done.3.refs_4_) | copy-start | bytes 786436
  67.4 32.7 %copy-start.5 = (bf16[128,1024]{1,0:T(8,128)(2,1)}, bf16[128,1024]{1,0:T(8,128)(2,1)S(1)}, u32[]{:S(2)}) copy-start(bf16[128,1024]{1,0:T(8,128)(2,1)S(1)} %collective-permute-done.4.refs_8_) | copy-start | bytes 786436
  67.4 32.7 %copy-start.3 = (bf16[128,1024]{1,0:T(8,128)(2,1)}, bf16[128,1024]{1,0:T(8,128)(2,1)S(1)}, u32[]{:S(2)}) copy-start(bf16[128,1024]{1,0:T(8,128)(2,1)S(1)} %collective-permute-done.1.refs_2_) | copy-start | bytes 786436
  67.4 11.1 %collective-permute-start.6 = (bf16[128,1024]{1,0:T(8,128)(2,1)S(1)}, bf16[128,1024]{1,0:T(8,128)(2,1)S(1)}, u32[]{:S(2)}, u32[]{:S(2)}) collective-permute-start(bf16[128,1024]{1,0:T(8,128)(2,1)S(1)} %collective-permute-done.3.refs_4_), channel_id=1, source_target_pairs={{0,96},{32,0},{64,32},{96,64},{1,97},{33,1},{65,33},{97,65},{2,98}... | collective-permute-start | bytes 786440 | tf_op jit(solution)/shard_map/ppermute | solution.py:358
  67.6 12.3 %collective-permute-start.5 = (bf16[128,1024]{1,0:T(8,128)(2,1)S(1)}, bf16[128,1024]{1,0:T(8,128)(2,1)S(1)}, u32[]{:S(2)}, u32[]{:S(2)}) collective-permute-start(bf16[128,1024]{1,0:T(8,128)(2,1)S(1)} %collective-permute-done.3.refs_4_), channel_id=1, source_target_pairs={{0,32},{32,64},{64,96},{96,0},{1,33},{33,65},{65,97},{97,1},{2,34}... | collective-permute-start | bytes 786440 | tf_op jit(solution)/shard_map/ppermute | solution.py:357
  68.9 12.2 %collective-permute-start.8 = (bf16[128,1024]{1,0:T(8,128)(2,1)S(1)}, bf16[128,1024]{1,0:T(8,128)(2,1)}, u32[]{:S(2)}, u32[]{:S(2)}) collective-permute-start(bf16[128,1024]{1,0:T(8,128)(2,1)S(1)} %collective-permute-done.4.refs_8_), channel_id=1, source_target_pairs={{0,32},{32,64},{64,96},{96,0},{1,33},{33,65},{65,97},{97,1},{2,34}... | collective-permute-start | bytes 786440 | tf_op jit(solution)/shard_map/ppermute | solution.py:357
  77.2 22.9 %copy-start.6 = (bf16[128,1024]{1,0:T(8,128)(2,1)}, bf16[128,1024]{1,0:T(8,128)(2,1)S(1)}, u32[]{:S(2)}) copy-start(bf16[128,1024]{1,0:T(8,128)(2,1)S(1)} %collective-permute-done.11.refs_12_) | copy-start | bytes 786436
  77.3 22.9 %copy-start.7 = (bf16[128,1024]{1,0:T(8,128)(2,1)}, bf16[128,1024]{1,0:T(8,128)(2,1)S(1)}, u32[]{:S(2)}) copy-start(bf16[128,1024]{1,0:T(8,128)(2,1)S(1)} %collective-permute-done.2.refs_3_) | copy-start | bytes 786436
  77.3 6.0 %collective-permute-start.13 = (bf16[128,1024]{1,0:T(8,128)(2,1)S(1)}, bf16[128,1024]{1,0:T(8,128)(2,1)}, u32[]{:S(2)}, u32[]{:S(2)}) collective-permute-start(bf16[128,1024]{1,0:T(8,128)(2,1)S(1)} %collective-permute-done.11.refs_12_), channel_id=1, source_target_pairs={{0,96},{32,0},{64,32},{96,64},{1,97},{33,1},{65,33},{97,65},{2,98}... | collective-permute-start | bytes 786440 | tf_op jit(solution)/shard_map/ppermute | solution.py:358
  78.3 10.5 %collective-permute-start.9 = (bf16[128,1024]{1,0:T(8,128)(2,1)S(1)}, bf16[128,1024]{1,0:T(8,128)(2,1)S(1)}, u32[]{:S(2)}, u32[]{:S(2)}) collective-permute-start(bf16[128,1024]{1,0:T(8,128)(2,1)S(1)} %collective-permute-done.4.refs_8_), channel_id=1, source_target_pairs={{0,96},{32,0},{64,32},{96,64},{1,97},{33,1},{65,33},{97,65},{2,98}... | collective-permute-start | bytes 786440 | tf_op jit(solution)/shard_map/ppermute | solution.py:358
  78.5 21.7 %copy-start.8 = (bf16[128,1024]{1,0:T(8,128)(2,1)}, bf16[128,1024]{1,0:T(8,128)(2,1)S(1)}, u32[]{:S(2)}) copy-start(bf16[128,1024]{1,0:T(8,128)(2,1)S(1)} %collective-permute-done.6.refs_6_) | copy-start | bytes 786436
  78.5 15.9 %collective-permute-start.12 = (bf16[128,1024]{1,0:T(8,128)(2,1)S(1)}, bf16[128,1024]{1,0:T(8,128)(2,1)S(1)}, u32[]{:S(2)}, u32[]{:S(2)}) collective-permute-start(bf16[128,1024]{1,0:T(8,128)(2,1)S(1)} %collective-permute-done.11.refs_12_), channel_id=1, source_target_pairs={{0,32},{32,64},{64,96},{96,0},{1,33},{33,65},{65,97},{97,1},{2,34}... | collective-permute-start | bytes 786440 | tf_op jit(solution)/shard_map/ppermute | solution.py:357
  79.8 5.0 %copy-start.9 = (bf16[128,1024]{1,0:T(8,128)(2,1)}, bf16[128,1024]{1,0:T(8,128)(2,1)S(1)}, u32[]{:S(2)}) copy-start(bf16[128,1024]{1,0:T(8,128)(2,1)S(1)} %collective-permute-done.5.refs_5_) | copy-start | bytes 786436
  79.8 14.5 %collective-permute-start.7 = (bf16[128,1024]{1,0:T(8,128)(2,1)S(1)}, bf16[128,1024]{1,0:T(8,128)(2,1)S(1)}, u32[]{:S(2)}, u32[]{:S(2)}) collective-permute-start(bf16[128,1024]{1,0:T(8,128)(2,1)S(1)} %collective-permute-done.6.refs_6_), channel_id=1, source_target_pairs={{0,96},{32,0},{64,32},{96,64},{1,97},{33,1},{65,33},{97,65},{2,98}... | collective-permute-start | bytes 786440 | tf_op jit(solution)/shard_map/ppermute | solution.py:359
  81.2 13.2 %collective-permute-start.10 = (bf16[128,1024]{1,0:T(8,128)(2,1)}, bf16[128,1024]{1,0:T(8,128)(2,1)S(1)}, u32[]{:S(2)}, u32[]{:S(2)}) collective-permute-start(bf16[128,1024]{1,0:T(8,128)(2,1)} %collective-permute-done.8.refs_9_), channel_id=1, source_target_pairs={{0,32},{32,64},{64,96},{96,0},{1,33},{33,65},{65,97},{97,1},{2,34}... | collective-permute-start | bytes 786440 | tf_op jit(solution)/shard_map/ppermute | solution.py:359
  83.3 16.9 %collective-permute-start.14 = (bf16[128,1024]{1,0:T(8,128)(2,1)}, bf16[128,1024]{1,0:T(8,128)(2,1)}, u32[]{:S(2)}, u32[]{:S(2)}) collective-permute-start(bf16[128,1024]{1,0:T(8,128)(2,1)} %collective-permute-done.13.refs_14_), channel_id=1, source_target_pairs={{0,96},{32,0},{64,32},{96,64},{1,97},{33,1},{65,33},{97,65},{2,98}... | collective-permute-start | bytes 786440 | tf_op jit(solution)/shard_map/ppermute | solution.py:359
  88.8 5.6 %copy-start.10 = (bf16[128,1024]{1,0:T(8,128)(2,1)}, bf16[128,1024]{1,0:T(8,128)(2,1)S(1)}, u32[]{:S(2)}) copy-start(bf16[128,1024]{1,0:T(8,128)(2,1)S(1)} %collective-permute-done.9.refs_10_) | copy-start | bytes 786436
  94.4 0.7 copy-start.12
  94.4 0.8 copy-start.13
  95.2 0.7 copy-start.11
  114.5 49.6 %all-to-all-start.2 = ((bf16[128,8,1536]{2,1,0:T(8,128)(2,1)}), bf16[128,8,1536]{2,1,0:T(8,128)(2,1)S(1)}, u32[]{:S(2)}, u32[]{:S(2)}) async-start(bf16[128,8,1536]{2,1,0:T(8,128)(2,1)} %bitcast.44), calls=%async_computation.2 | async-start | bytes 6291456 | tf_op jit(solution)/shard_map/all_to_all | solution.py:374
Sparse Core Ops, SparseCore 0:
  9.6 77.2 all-gather.1

commit v10 on v9

--- a/solution.py
+++ b/solution.py
@@ -361,7 +361,7 @@
 
     groups = [spread(mine[0], False)]
     mine[1], mine[2], *_ = lax.optimization_barrier((mine[1], mine[2]) + groups[0][1:3])
-    groups.append(spread(mine[1], True))
+    groups.append(spread(mine[1], False))
     groups.append(spread(mine[2], False))
     mine[3], *_ = lax.optimization_barrier((mine[3], groups[0][3]))
     groups.append(spread(mine[3], True))

time: 174 us -> 172 us (0.989)
  no operation moved by 1% of the time
where the time goes in v10:
time: 172 us
  waiting for transfers between devices  78 us (45%)
  starting transfers between devices  30.2 us (18%)
  Pallas kernels  27 us (16%)
  blocking collectives  15.2 us (9%)
  between operations  14.4 us (8%)
  local copies, waits for them, and re-layouts  4.58 us (3%)
  other arithmetic  2.24 us (1%)
    all_to_all x1, waiting for transfers between devices, per_device(): got = lax.all_to_all(send, ALL, split_axis=0, concat_axis=0, tiled=True)  40.3 us
    ppermute x3, waiting for transfers between devices, per_device(): mine.append(lax.ppermute(own[turn], 'head', shift(n_head, TURNS[turn])))  19.4 us
    all_to_all x1, blocking collectives, per_device(): lax.all_to_all(jnp.concatenate([carried_all, note], axis=1), SEQ, split_a...  15.2 us
    pallas_call x1, Pallas kernels, project(): pl.pallas_call(functools.partial(project_body, turns), grid_spec=pltpu.Pr...  14.4 us
    all_to_all x1, starting transfers between devices, per_device(): lax.all_to_all(state.reshape(n_seq, share, head_dim), SEQ, split_axis=0,...  9.6 us
    ppermute x4, waiting for transfers between devices, spread(): lax.ppermute(above if flip else below, 'z', shift(n_z, -1 if flip else 1))  8.56 us
    all_to_all x1, starting transfers between devices, per_device(): got = lax.all_to_all(send, ALL, split_axis=0, concat_axis=0, tiled=True)  7.42 us
    ppermute x4, waiting for transfers between devices, spread(): above = lax.ppermute(rows, 'z', shift(n_z, -1))  5.4 us
  transfers between devices with their start and end apart: 18, of which 10 were waited for; matrix products, arithmetic and copies ran while one was open for 3% of the time, Pallas kernels for 6%

profile of v10, /device:TPU:1, one launch (start us, length us, event | category | flops | bytes accessed | tf_op | source)
XLA Modules:
  0.0 172.1 jit_solution(15909301820716789611)
XLA Ops:
  6.5 0.0 all-gather.2.cloned.1.call-start
  6.6 0.7 all-gather.2.cloned.1.call-update
  7.3 3.0 %local_states.1 = bf16[8,128,128]{2,1,0:T(8,128)(2,1)} custom-call(f32[8]{0:T(128)} %rate_ref.5, s32[4]{0:T(128)} %lengths_ref.5, bf16[512,1024]{1,0:T(8,128)(2,1)} %query_ref.3, bf16[512,1024]{1,0:T(8,128)(2,1)} %grad_ref.3), custom_call_target="tpu_custom_call" | custom-call | tf_op jit(solution)/shard_map/local_states/pallas_call | solution.py:65
  10.3 9.6 %all-to-all-start = ((bf16[32,32,128]{2,1,0:T(8,128)(2,1)}), bf16[32,32,128]{2,1,0:T(8,128)(2,1)S(1)}, u32[]{:S(2)}, u32[]{:S(2)}) async-start(bf16[32,32,128]{2,1,0:T(8,128)(2,1)} %bitcast.4), calls=%async_computation | async-start | bytes 524288 | tf_op jit(solution)/shard_map/all_to_all | solution.py:302
  20.0 0.2 convert_reduce_fusion.1
  20.2 0.1 iota_add_fusion
  20.3 0.7 select_reduce_fusion
  21.0 0.1 maximum_bitcast_fusion
  21.2 0.6 dynamic_slice.9
  22.4 0.2 reduce-window.8
  22.6 4.5 %within.1.intra_ref = f32[512,1024]{1,0:T(8,128)S(1)} custom-call(f32[8]{0:T(128)} %rate_ref.5, s32[4]{0:T(128)} %lengths_ref.5, bf16[512,1024]{1,0:T(8,128)(2,1)} %query_ref.3, bf16[512,1024]{1,0:T(8,128)(2,1)} %key_ref.3, bf16[512,1024]{1,0:T(8,128)(2,1)} %grad_ref.3), custom_call_target="tpu_custom_call" | custom-call | tf_op jit(solution)/shard_map/within/pallas_call | solution.py:107
  27.2 0.1 convert_reduce_fusion.3
  27.3 1.5 all-to-all-done
  28.8 0.4 convolution_convert_fusion
  29.3 0.1 copy.39
  29.4 15.2 %all_to_all.15 = bf16[32,40,128]{2,1,0:T(8,128)(2,1)S(1)} all-to-all(bf16[32,40,128]{2,1,0:T(8,128)(2,1)S(1)} %copy.39), channel_id=1, replica_groups=mesh['z'=4,'y'=4,'core'=2,'head'=4] {'z','y','core'}, dimensions={0} | all-to-all | bytes 655360 | tf_op jit(solution)/shard_map/all_to_all | solution.py:327
  44.6 2.6 %across.1 = (bf16[128,1024]{1,0:T(8,128)(2,1)S(1)}, bf16[128,1024]{1,0:T(8,128)(2,1)S(1)}, bf16[128,1024]{1,0:T(8,128)(2,1)S(1)}, bf16[128,1024]{1,0:T(8,128)(2,1)S(1)}) custom-call(f32[8]{0:T(128)} %rate_ref.5, s32[4]{0:T(128)} %lengths_ref.5, bf16[512,1024]{1,0:T(8,128)(2,1)} %key_ref.3, bf16[8,128,128]{2,1,0:T(8,128)(2,1)S(1)} %bitcast.39, ...), custom_call_target="tpu_custom_call" | custom-call | tf_op jit(solution)/shard_map/across/pallas_call | solution.py:145
  47.3 0.1 collective-permute-start
  47.4 2.6 %collective-permute-start.1 = (bf16[128,1024]{1,0:T(8,128)(2,1)S(1)}, bf16[128,1024]{1,0:T(8,128)(2,1)S(1)}, u32[]{:S(2)}, u32[]{:S(2)}) collective-permute-start(bf16[128,1024]{1,0:T(8,128)(2,1)S(1)} %get-tuple-element.16.refs_0_), channel_id=1, source_target_pairs={{0,96},{32,0},{64,32},{96,64},{1,97},{33,1},{65,33},{97,65},{2,98}... | collective-permute-start | bytes 786440 | tf_op jit(solution)/shard_map/ppermute | solution.py:358
  50.0 2.4 %collective-permute-start.3 = (bf16[128,1024]{1,0:T(8,128)(2,1)S(1)}, bf16[128,1024]{1,0:T(8,128)(2,1)S(1)}, u32[]{:S(2)}, u32[]{:S(2)}) collective-permute-start(bf16[128,1024]{1,0:T(8,128)(2,1)S(1)} %get-tuple-element.17), channel_id=1, source_target_pairs={{0,3},{1,0},{2,1},{3,2},{4,7},{5,4},{6,5},{7,6},{8,11},{9,8},{10,9... | collective-permute-start | bytes 786440 | tf_op jit(solution)/shard_map/ppermute | solution.py:353
  52.4 0.0 collective-permute-start.4
  52.4 1.7 collective-permute-start.11
  54.1 2.1 %collective-permute-done.refs_1_ = bf16[128,1024]{1,0:T(8,128)(2,1)S(1)} collective-permute-done((bf16[128,1024]{1,0:T(8,128)(2,1)S(1)}, bf16[128,1024]{1,0:T(8,128)(2,1)S(1)}, u32[]{:S(2)}, u32[]{:S(2)}) %collective-permute-start) | collective-permute-done | bytes 262176 | tf_op jit(solution)/shard_map/ppermute | solution.py:357
  56.3 0.0 collective-permute-start.2
  56.3 7.3 %collective-permute-done.3.refs_4_ = bf16[128,1024]{1,0:T(8,128)(2,1)S(1)} collective-permute-done((bf16[128,1024]{1,0:T(8,128)(2,1)S(1)}, bf16[128,1024]{1,0:T(8,128)(2,1)S(1)}, u32[]{:S(2)}, u32[]{:S(2)}) %collective-permute-start.3) | collective-permute-done | bytes 262176 | tf_op jit(solution)/shard_map/ppermute | solution.py:353
  63.6 3.9 %collective-permute-done.4.refs_8_ = bf16[128,1024]{1,0:T(8,128)(2,1)S(1)} collective-permute-done((bf16[128,1024]{1,0:T(8,128)(2,1)S(1)}, bf16[128,1024]{1,0:T(8,128)(2,1)S(1)}, u32[]{:S(2)}, u32[]{:S(2)}) %collective-permute-start.4) | collective-permute-done | bytes 262176 | tf_op jit(solution)/shard_map/ppermute | solution.py:353
  67.5 0.0 collective-permute-done.1.refs_2_
  67.5 0.2 collective-permute-start.6
  67.6 1.4 collective-permute-start.5
  69.0 0.0 collective-permute-start.8
  69.0 8.3 %collective-permute-done.11.refs_12_ = bf16[128,1024]{1,0:T(8,128)(2,1)S(1)} collective-permute-done((bf16[128,1024]{1,0:T(8,128)(2,1)S(1)}, bf16[128,1024]{1,0:T(8,128)(2,1)S(1)}, u32[]{:S(2)}, u32[]{:S(2)}) %collective-permute-start.11) | collective-permute-done | bytes 262176 | tf_op jit(solution)/shard_map/ppermute | solution.py:353
  77.3 0.0 collective-permute-done.2.refs_3_
  77.3 0.2 collective-permute-start.13
  77.5 0.6 gather_fusion
  78.1 0.2 convert_reduce_fusion
  78.3 0.1 collective-permute-start.9
  78.5 0.0 collective-permute-done.6.refs_6_
  78.5 1.4 collective-permute-start.12
  79.9 0.0 collective-permute-done.5.refs_5_
  79.9 1.4 collective-permute-start.7
  81.3 0.0 collective-permute-done.8.refs_9_
  81.3 0.1 collective-permute-start.10
  81.4 1.9 %collective-permute-done.13.refs_14_ = bf16[128,1024]{1,0:T(8,128)(2,1)} collective-permute-done((bf16[128,1024]{1,0:T(8,128)(2,1)S(1)}, bf16[128,1024]{1,0:T(8,128)(2,1)}, u32[]{:S(2)}, u32[]{:S(2)}) %collective-permute-start.13) | collective-permute-done | bytes 262176 | tf_op jit(solution)/shard_map/ppermute | solution.py:358
  83.3 1.6 collective-permute-start.14
  84.9 0.1 add_bitcast_fusion
  84.9 0.4 fusion.pick
  85.4 3.4 %collective-permute-done.9.refs_10_ = bf16[128,1024]{1,0:T(8,128)(2,1)S(1)} collective-permute-done((bf16[128,1024]{1,0:T(8,128)(2,1)S(1)}, bf16[128,1024]{1,0:T(8,128)(2,1)S(1)}, u32[]{:S(2)}, u32[]{:S(2)}) %collective-permute-start.9) | collective-permute-done | bytes 262176 | tf_op jit(solution)/shard_map/ppermute | solution.py:358
  88.8 2.9 %collective-permute-done.7.refs_7_ = bf16[128,1024]{1,0:T(8,128)(2,1)S(1)} collective-permute-done((bf16[128,1024]{1,0:T(8,128)(2,1)}, bf16[128,1024]{1,0:T(8,128)(2,1)S(1)}, u32[]{:S(2)}, u32[]{:S(2)}) %collective-permute-start.7) | collective-permute-done | bytes 262176 | tf_op jit(solution)/shard_map/ppermute | solution.py:359
  91.8 5.6 %collective-permute-done.10.refs_11_ = bf16[128,1024]{1,0:T(8,128)(2,1)S(1)} collective-permute-done((bf16[128,1024]{1,0:T(8,128)(2,1)}, bf16[128,1024]{1,0:T(8,128)(2,1)S(1)}, u32[]{:S(2)}, u32[]{:S(2)}) %collective-permute-start.10) | collective-permute-done | bytes 262176 | tf_op jit(solution)/shard_map/ppermute | solution.py:359
  97.4 0.0 collective-permute-done.12.refs_13_
  97.4 0.7 copy-done.12
  98.1 0.7 copy-done.10
  98.8 14.4 %project.1 = bf16[1024,1536]{1,0:T(8,128)(2,1)} custom-call(s32[4]{0:T(128)S(1)} %and_select_fusion.1.place, bf16[1024,512]{1,0:T(8,128)(2,1)S(1)} %fusion.pick, bf16[128,1024]{1,0:T(8,128)(2,1)} %copy-done, bf16[128,1024]{1,0:T(8,128)(2,1)} %copy-done.2, bf16[128,1024]{1,0:T(8,128)(2,1)} %copy-done.3, bf16[128,1024]{1,0:T(8,128)(2,1)} %copy-done.7, ...), custom_call_target="tpu_custom_call" | custom-call | tf_op jit(solution)/shard_map/project/pallas_call | solution.py:186
  113.2 7.4 %all-to-all-start.2 = ((bf16[128,8,1536]{2,1,0:T(8,128)(2,1)}), bf16[128,8,1536]{2,1,0:T(8,128)(2,1)S(1)}, u32[]{:S(2)}, u32[]{:S(2)}) async-start(bf16[128,8,1536]{2,1,0:T(8,128)(2,1)} %bitcast.44), calls=%async_computation.2 | async-start | bytes 6291456 | tf_op jit(solution)/shard_map/all_to_all | solution.py:374
  120.7 1.0 fusion.35
  121.7 0.1 copy.48
  121.7 0.1 copy.49
  121.8 0.1 sub.71
  121.9 0.1 copy.42
  122.0 0.2 copy.43
  122.2 0.2 reshape.207.row_ref
  122.3 0.1 sub.76.column_ref
  122.4 40.3 %all-to-all-done.2 = bf16[128,8,1536]{2,1,0:T(8,128)(2,1)S(1)} async-done(((bf16[128,8,1536]{2,1,0:T(8,128)(2,1)}), bf16[128,8,1536]{2,1,0:T(8,128)(2,1)S(1)}, u32[]{:S(2)}, u32[]{:S(2)}) %all-to-all-start.2) | async-done | bytes 3145760 | tf_op jit(solution)/shard_map/all_to_all | solution.py:374
  162.7 2.5 %merge.1 = bf16[1,128,2,6144]{3,2,1,0:T(2,128)(2,1)} custom-call(s32[256,1]{1,0:T(8,128)S(1)} %sub.76.column_ref, s32[1,256]{1,0:T(1,128)S(1)} %reshape.207.row_ref, bf16[4,32,8,1536]{3,2,1,0:T(8,128)(2,1)S(1)} %bitcast.38), custom_call_target="tpu_custom_call" | custom-call | tf_op jit(solution)/shard_map/merge/pallas_call | solution.py:223
  (58 shorter events, 0.3 us)
Async XLA Ops:
  6.5 15.9 %copy-start.15 = (s32[4]{0:T(128)S(1)}, s32[4]{0:T(128)}, u32[]{:S(2)}) copy-start(s32[4]{0:T(128)} %lengths_ref.5) | copy-start | bytes 52
  6.5 14.6 %copy-start.14 = (f32[8]{0:T(128)S(1)}, f32[8]{0:T(128)}, u32[]{:S(2)}) copy-start(f32[8]{0:T(128)} %rate_ref.5) | copy-start | bytes 100
  6.5 13.4 %copy-start.13 = (s32[512,1]{0,1:T(1,128)S(1)}, s32[512,1]{0,1:T(1,128)}, u32[]{:S(2)}) copy-start(s32[512,1]{0,1:T(1,128)} %param.16) | copy-start | bytes 6148
  6.5 13.7 %copy-start.16 = (s32[512]{0:T(512)S(1)}, s32[512]{0:T(512)}, u32[]{:S(2)}) copy-start(s32[512]{0:T(512)} %param.17) | copy-start | bytes 6148
  6.5 92.2 %all-gather.2.cloned.1.call-start = ((), (), s32[]{:S(2)}) async-start(), calls=%async_computation.3 | async-start | bytes 12976128 | tf_op jit(solution)/shard_map/all_gather | solution.py:277
  10.3 18.5 %all-to-all-start = ((bf16[32,32,128]{2,1,0:T(8,128)(2,1)}), bf16[32,32,128]{2,1,0:T(8,128)(2,1)S(1)}, u32[]{:S(2)}, u32[]{:S(2)}) async-start(bf16[32,32,128]{2,1,0:T(8,128)(2,1)} %bitcast.4), calls=%async_computation | async-start | bytes 524288 | tf_op jit(solution)/shard_map/all_to_all | solution.py:302
  28.8 27.5 %copy-start.18 = (s32[4]{0:T(128)S(1)}, s32[4]{0:T(128)}, u32[]{:S(2)}) copy-start(s32[4]{0:T(128)} %constant.125) | copy-start | bytes 52
  28.8 27.5 %copy-start.17 = (s32[4]{0:T(128)S(1)}, s32[4]{0:T(128)}, u32[]{:S(2)}) copy-start(s32[4]{0:T(128)} %constant.126) | copy-start | bytes 52
  44.6 68.6 %copy-start.1 = (bf16[32,40,128]{2,1,0:T(8,128)(2,1)}, bf16[32,40,128]{2,1,0:T(8,128)(2,1)S(1)}, u32[]{:S(2)}) copy-start(bf16[32,40,128]{2,1,0:T(8,128)(2,1)S(1)} %all_to_all.15) | copy-start | bytes 983044
  47.2 51.5 %copy-start = (bf16[128,1024]{1,0:T(8,128)(2,1)}, bf16[128,1024]{1,0:T(8,128)(2,1)S(1)}, u32[]{:S(2)}) copy-start(bf16[128,1024]{1,0:T(8,128)(2,1)S(1)} %get-tuple-element.16.refs_0_) | copy-start | bytes 786436
  47.3 9.0 %collective-permute-start = (bf16[128,1024]{1,0:T(8,128)(2,1)S(1)}, bf16[128,1024]{1,0:T(8,128)(2,1)S(1)}, u32[]{:S(2)}, u32[]{:S(2)}) collective-permute-start(bf16[128,1024]{1,0:T(8,128)(2,1)S(1)} %get-tuple-element.16.refs_0_), channel_id=1, source_target_pairs={{0,32},{32,64},{64,96},{96,0},{1,33},{33,65},{65,97},{97,1},{2,34}... | collective-permute-start | bytes 786440 | tf_op jit(solution)/shard_map/ppermute | solution.py:357
  47.4 20.1 %collective-permute-start.1 = (bf16[128,1024]{1,0:T(8,128)(2,1)S(1)}, bf16[128,1024]{1,0:T(8,128)(2,1)S(1)}, u32[]{:S(2)}, u32[]{:S(2)}) collective-permute-start(bf16[128,1024]{1,0:T(8,128)(2,1)S(1)} %get-tuple-element.16.refs_0_), channel_id=1, source_target_pairs={{0,96},{32,0},{64,32},{96,64},{1,97},{33,1},{65,33},{97,65},{2,98}... | collective-permute-start | bytes 786440 | tf_op jit(solution)/shard_map/ppermute | solution.py:358
  50.0 13.6 %collective-permute-start.3 = (bf16[128,1024]{1,0:T(8,128)(2,1)S(1)}, bf16[128,1024]{1,0:T(8,128)(2,1)S(1)}, u32[]{:S(2)}, u32[]{:S(2)}) collective-permute-start(bf16[128,1024]{1,0:T(8,128)(2,1)S(1)} %get-tuple-element.17), channel_id=1, source_target_pairs={{0,3},{1,0},{2,1},{3,2},{4,7},{5,4},{6,5},{7,6},{8,11},{9,8},{10,9... | collective-permute-start | bytes 786440 | tf_op jit(solution)/shard_map/ppermute | solution.py:353
  52.4 15.0 %collective-permute-start.4 = (bf16[128,1024]{1,0:T(8,128)(2,1)S(1)}, bf16[128,1024]{1,0:T(8,128)(2,1)S(1)}, u32[]{:S(2)}, u32[]{:S(2)}) collective-permute-start(bf16[128,1024]{1,0:T(8,128)(2,1)S(1)} %get-tuple-element.18), channel_id=1, source_target_pairs={{0,1},{1,2},{2,3},{3,0},{4,5},{5,6},{6,7},{7,4},{8,9},{9,10},{10,1... | collective-permute-start | bytes 786440 | tf_op jit(solution)/shard_map/ppermute | solution.py:353
  52.4 24.9 %collective-permute-start.11 = (bf16[128,1024]{1,0:T(8,128)(2,1)S(1)}, bf16[128,1024]{1,0:T(8,128)(2,1)S(1)}, u32[]{:S(2)}, u32[]{:S(2)}) collective-permute-start(bf16[128,1024]{1,0:T(8,128)(2,1)S(1)} %get-tuple-element.21), channel_id=1, source_target_pairs={{0,2},{1,3},{2,0},{3,1},{4,6},{5,7},{6,4},{7,5},{8,10},{9,11},{10,... | collective-permute-start | bytes 786440 | tf_op jit(solution)/shard_map/ppermute | solution.py:353
  56.3 42.5 %copy-start.2 = (bf16[128,1024]{1,0:T(8,128)(2,1)}, bf16[128,1024]{1,0:T(8,128)(2,1)S(1)}, u32[]{:S(2)}) copy-start(bf16[128,1024]{1,0:T(8,128)(2,1)S(1)} %collective-permute-done.refs_1_) | copy-start | bytes 786436
  56.3 21.0 %collective-permute-start.2 = (bf16[128,1024]{1,0:T(8,128)(2,1)S(1)}, bf16[128,1024]{1,0:T(8,128)(2,1)S(1)}, u32[]{:S(2)}, u32[]{:S(2)}) collective-permute-start(bf16[128,1024]{1,0:T(8,128)(2,1)S(1)} %collective-permute-done.refs_1_), channel_id=1, source_target_pairs={{0,32},{32,64},{64,96},{96,0},{1,33},{33,65},{65,97},{97,1},{2,34}... | collective-permute-start | bytes 786440 | tf_op jit(solution)/shard_map/ppermute | solution.py:359
  63.6 35.2 %copy-start.4 = (bf16[128,1024]{1,0:T(8,128)(2,1)}, bf16[128,1024]{1,0:T(8,128)(2,1)S(1)}, u32[]{:S(2)}) copy-start(bf16[128,1024]{1,0:T(8,128)(2,1)S(1)} %collective-permute-done.3.refs_4_) | copy-start | bytes 786436
  67.5 31.3 %copy-start.5 = (bf16[128,1024]{1,0:T(8,128)(2,1)}, bf16[128,1024]{1,0:T(8,128)(2,1)S(1)}, u32[]{:S(2)}) copy-start(bf16[128,1024]{1,0:T(8,128)(2,1)S(1)} %collective-permute-done.4.refs_8_) | copy-start | bytes 786436
  67.5 31.3 %copy-start.3 = (bf16[128,1024]{1,0:T(8,128)(2,1)}, bf16[128,1024]{1,0:T(8,128)(2,1)S(1)}, u32[]{:S(2)}) copy-start(bf16[128,1024]{1,0:T(8,128)(2,1)S(1)} %collective-permute-done.1.refs_2_) | copy-start | bytes 786436
  67.5 11.0 %collective-permute-start.6 = (bf16[128,1024]{1,0:T(8,128)(2,1)S(1)}, bf16[128,1024]{1,0:T(8,128)(2,1)S(1)}, u32[]{:S(2)}, u32[]{:S(2)}) collective-permute-start(bf16[128,1024]{1,0:T(8,128)(2,1)S(1)} %collective-permute-done.3.refs_4_), channel_id=1, source_target_pairs={{0,96},{32,0},{64,32},{96,64},{1,97},{33,1},{65,33},{97,65},{2,98}... | collective-permute-start | bytes 786440 | tf_op jit(solution)/shard_map/ppermute | solution.py:358
  67.6 12.3 %collective-permute-start.5 = (bf16[128,1024]{1,0:T(8,128)(2,1)S(1)}, bf16[128,1024]{1,0:T(8,128)(2,1)}, u32[]{:S(2)}, u32[]{:S(2)}) collective-permute-start(bf16[128,1024]{1,0:T(8,128)(2,1)S(1)} %collective-permute-done.3.refs_4_), channel_id=1, source_target_pairs={{0,32},{32,64},{64,96},{96,0},{1,33},{33,65},{65,97},{97,1},{2,34}... | collective-permute-start | bytes 786440 | tf_op jit(solution)/shard_map/ppermute | solution.py:357
  69.0 12.3 %collective-permute-start.8 = (bf16[128,1024]{1,0:T(8,128)(2,1)S(1)}, bf16[128,1024]{1,0:T(8,128)(2,1)}, u32[]{:S(2)}, u32[]{:S(2)}) collective-permute-start(bf16[128,1024]{1,0:T(8,128)(2,1)S(1)} %collective-permute-done.4.refs_8_), channel_id=1, source_target_pairs={{0,32},{32,64},{64,96},{96,0},{1,33},{33,65},{65,97},{97,1},{2,34}... | collective-permute-start | bytes 786440 | tf_op jit(solution)/shard_map/ppermute | solution.py:357
  77.3 21.5 %copy-start.6 = (bf16[128,1024]{1,0:T(8,128)(2,1)}, bf16[128,1024]{1,0:T(8,128)(2,1)S(1)}, u32[]{:S(2)}) copy-start(bf16[128,1024]{1,0:T(8,128)(2,1)S(1)} %collective-permute-done.11.refs_12_) | copy-start | bytes 786436
  77.3 21.5 %copy-start.7 = (bf16[128,1024]{1,0:T(8,128)(2,1)}, bf16[128,1024]{1,0:T(8,128)(2,1)S(1)}, u32[]{:S(2)}) copy-start(bf16[128,1024]{1,0:T(8,128)(2,1)S(1)} %collective-permute-done.2.refs_3_) | copy-start | bytes 786436
  77.3 6.0 %collective-permute-start.13 = (bf16[128,1024]{1,0:T(8,128)(2,1)S(1)}, bf16[128,1024]{1,0:T(8,128)(2,1)}, u32[]{:S(2)}, u32[]{:S(2)}) collective-permute-start(bf16[128,1024]{1,0:T(8,128)(2,1)S(1)} %collective-permute-done.11.refs_12_), channel_id=1, source_target_pairs={{0,96},{32,0},{64,32},{96,64},{1,97},{33,1},{65,33},{97,65},{2,98}... | collective-permute-start | bytes 786440 | tf_op jit(solution)/shard_map/ppermute | solution.py:358
  78.3 10.5 %collective-permute-start.9 = (bf16[128,1024]{1,0:T(8,128)(2,1)S(1)}, bf16[128,1024]{1,0:T(8,128)(2,1)S(1)}, u32[]{:S(2)}, u32[]{:S(2)}) collective-permute-start(bf16[128,1024]{1,0:T(8,128)(2,1)S(1)} %collective-permute-done.4.refs_8_), channel_id=1, source_target_pairs={{0,96},{32,0},{64,32},{96,64},{1,97},{33,1},{65,33},{97,65},{2,98}... | collective-permute-start | bytes 786440 | tf_op jit(solution)/shard_map/ppermute | solution.py:358
  78.5 20.4 %copy-start.8 = (bf16[128,1024]{1,0:T(8,128)(2,1)}, bf16[128,1024]{1,0:T(8,128)(2,1)S(1)}, u32[]{:S(2)}) copy-start(bf16[128,1024]{1,0:T(8,128)(2,1)S(1)} %collective-permute-done.6.refs_6_) | copy-start | bytes 786436
  78.5 18.9 %collective-permute-start.12 = (bf16[128,1024]{1,0:T(8,128)(2,1)S(1)}, bf16[128,1024]{1,0:T(8,128)(2,1)S(1)}, u32[]{:S(2)}, u32[]{:S(2)}) collective-permute-start(bf16[128,1024]{1,0:T(8,128)(2,1)S(1)} %collective-permute-done.11.refs_12_), channel_id=1, source_target_pairs={{0,32},{32,64},{64,96},{96,0},{1,33},{33,65},{65,97},{97,1},{2,34}... | collective-permute-start | bytes 786440 | tf_op jit(solution)/shard_map/ppermute | solution.py:357
  79.9 11.9 %collective-permute-start.7 = (bf16[128,1024]{1,0:T(8,128)(2,1)}, bf16[128,1024]{1,0:T(8,128)(2,1)S(1)}, u32[]{:S(2)}, u32[]{:S(2)}) collective-permute-start(bf16[128,1024]{1,0:T(8,128)(2,1)} %collective-permute-done.5.refs_5_), channel_id=1, source_target_pairs={{0,32},{32,64},{64,96},{96,0},{1,33},{33,65},{65,97},{97,1},{2,34}... | collective-permute-start | bytes 786440 | tf_op jit(solution)/shard_map/ppermute | solution.py:359
  81.3 16.1 %collective-permute-start.10 = (bf16[128,1024]{1,0:T(8,128)(2,1)}, bf16[128,1024]{1,0:T(8,128)(2,1)S(1)}, u32[]{:S(2)}, u32[]{:S(2)}) collective-permute-start(bf16[128,1024]{1,0:T(8,128)(2,1)} %collective-permute-done.8.refs_9_), channel_id=1, source_target_pairs={{0,32},{32,64},{64,96},{96,0},{1,33},{33,65},{65,97},{97,1},{2,34}... | collective-permute-start | bytes 786440 | tf_op jit(solution)/shard_map/ppermute | solution.py:359
  83.3 15.5 %collective-permute-start.14 = (bf16[128,1024]{1,0:T(8,128)(2,1)}, bf16[128,1024]{1,0:T(8,128)(2,1)}, u32[]{:S(2)}, u32[]{:S(2)}) collective-permute-start(bf16[128,1024]{1,0:T(8,128)(2,1)} %collective-permute-done.13.refs_14_), channel_id=1, source_target_pairs={{0,96},{32,0},{64,32},{96,64},{1,97},{33,1},{65,33},{97,65},{2,98}... | collective-permute-start | bytes 786440 | tf_op jit(solution)/shard_map/ppermute | solution.py:359
  88.8 8.6 %copy-start.9 = (bf16[128,1024]{1,0:T(8,128)(2,1)}, bf16[128,1024]{1,0:T(8,128)(2,1)S(1)}, u32[]{:S(2)}) copy-start(bf16[128,1024]{1,0:T(8,128)(2,1)S(1)} %collective-permute-done.9.refs_10_) | copy-start | bytes 786436
  91.8 5.6 %copy-start.11 = (bf16[128,1024]{1,0:T(8,128)(2,1)}, bf16[128,1024]{1,0:T(8,128)(2,1)S(1)}, u32[]{:S(2)}) copy-start(bf16[128,1024]{1,0:T(8,128)(2,1)S(1)} %collective-permute-done.7.refs_7_) | copy-start | bytes 786436
  97.4 0.7 copy-start.12
  98.1 0.7 copy-start.10
  113.2 49.5 %all-to-all-start.2 = ((bf16[128,8,1536]{2,1,0:T(8,128)(2,1)}), bf16[128,8,1536]{2,1,0:T(8,128)(2,1)S(1)}, u32[]{:S(2)}, u32[]{:S(2)}) async-start(bf16[128,8,1536]{2,1,0:T(8,128)(2,1)} %bitcast.44), calls=%async_computation.2 | async-start | bytes 6291456 | tf_op jit(solution)/shard_map/all_to_all | solution.py:374
Sparse Core Ops, SparseCore 0:
  9.6 77.2 all-gather.1

commit v11 on v10

--- a/solution.py
+++ b/solution.py
@@ -306,7 +306,6 @@
         rates, lengths, queries, key_vectors, output_grad, head_local // 2
     )
 
-    state_in, intra = lax.optimization_barrier((state_in, intra))
     doc_ends = jnp.cumsum(doc_lengths)
     ranks = jnp.arange(n_seq, dtype=jnp.int32)
     doc_last = doc_of((ranks + 1) * tok_rows - 1, doc_ends)

time: 172 us -> 171 us (level)
  blocking collectives: 15.2 us -> 0 us
  waiting for transfers between devices: 78 us -> 88 us
  starting transfers between devices: 30.2 us -> 34 us
    all_to_all x1 -> x0, blocking collectives: 15.2 us -> none  [per_device(): lax.all_to_all(jnp.concatenate([carried_all, note], axis=1), SEQ, split_a...]
    all_to_all x0 -> x1, waiting for transfers between devices: none -> 5.13 us  [per_device(): lax.all_to_all(jnp.concatenate([carried_all, note], axis=1), SEQ, split_a...]
    all_to_all x1, waiting for transfers between devices: 1.53 us -> 6.18 us  [per_device(): lax.all_to_all(state.reshape(n_seq, share, head_dim), SEQ, split_axis=0,...]
    all_to_all x0 -> x1, starting transfers between devices: none -> 3.76 us  [per_device(): lax.all_to_all(jnp.concatenate([carried_all, note], axis=1), SEQ, split_a...]
  transfers between devices with their start and end apart: 18 -> 19, of which waited for: 10 -> 11; matrix products, arithmetic and copies ran while one was open for 3% -> 4% of each run, Pallas kernels for 6% -> 6%
where the time goes in v11:
time: 171 us
  waiting for transfers between devices  88 us (51%)
  starting transfers between devices  34 us (20%)
  Pallas kernels  26.6 us (16%)
  between operations  14.4 us (8%)
  local copies, waits for them, and re-layouts  5.25 us (3%)
  other arithmetic  2.24 us (1%)
    all_to_all x1, waiting for transfers between devices, per_device(): got = lax.all_to_all(send, ALL, split_axis=0, concat_axis=0, tiled=True)  40.3 us
    ppermute x3, waiting for transfers between devices, per_device(): mine.append(lax.ppermute(own[turn], 'head', shift(n_head, TURNS[turn])))  19.5 us
    pallas_call x1, Pallas kernels, project(): pl.pallas_call(functools.partial(project_body, turns), grid_spec=pltpu.Pr...  14.4 us
    all_to_all x1, starting transfers between devices, per_device(): lax.all_to_all(state.reshape(n_seq, share, head_dim), SEQ, split_axis=0,...  9.6 us
    ppermute x4, waiting for transfers between devices, spread(): lax.ppermute(above if flip else below, 'z', shift(n_z, -1 if flip else 1))  8.75 us
    all_to_all x1, starting transfers between devices, per_device(): got = lax.all_to_all(send, ALL, split_axis=0, concat_axis=0, tiled=True)  7.43 us
    all_to_all x1, waiting for transfers between devices, per_device(): lax.all_to_all(state.reshape(n_seq, share, head_dim), SEQ, split_axis=0,...  6.18 us
    ppermute x4, waiting for transfers between devices, spread(): above = lax.ppermute(rows, 'z', shift(n_z, -1))  5.44 us
  transfers between devices with their start and end apart: 19, of which 11 were waited for; matrix products, arithmetic and copies ran while one was open for 4% of the time, Pallas kernels for 6%

profile of v11, /device:TPU:1, one launch (start us, length us, event | category | flops | bytes accessed | tf_op | source)
XLA Modules:
  0.0 170.9 jit_solution(1894435864607084768)
XLA Ops:
  6.5 0.0 all-gather.2.cloned.1.call-start
  6.6 0.7 all-gather.2.cloned.1.call-update
  7.3 3.0 %local_states.1 = bf16[8,128,128]{2,1,0:T(8,128)(2,1)} custom-call(f32[8]{0:T(128)} %rate_ref.5, s32[4]{0:T(128)} %lengths_ref.5, bf16[512,1024]{1,0:T(8,128)(2,1)} %query_ref.3, bf16[512,1024]{1,0:T(8,128)(2,1)} %grad_ref.3), custom_call_target="tpu_custom_call" | custom-call | tf_op jit(solution)/shard_map/local_states/pallas_call | solution.py:65
  10.3 9.6 %all-to-all-start = ((bf16[32,32,128]{2,1,0:T(8,128)(2,1)}), bf16[32,32,128]{2,1,0:T(8,128)(2,1)S(1)}, u32[]{:S(2)}, u32[]{:S(2)}) async-start(bf16[32,32,128]{2,1,0:T(8,128)(2,1)} %bitcast.4), calls=%async_computation | async-start | bytes 524288 | tf_op jit(solution)/shard_map/all_to_all | solution.py:302
  20.0 0.2 convert_reduce_fusion.1
  20.2 0.1 iota_add_fusion
  20.3 0.7 select_reduce_fusion
  21.0 0.1 maximum_bitcast_fusion
  21.2 0.6 dynamic_slice.9
  22.3 0.2 reduce-window.8
  22.5 0.1 convert_reduce_fusion.3
  22.6 6.2 %all-to-all-done = bf16[32,32,128]{2,1,0:T(8,128)(2,1)S(1)} async-done(((bf16[32,32,128]{2,1,0:T(8,128)(2,1)}), bf16[32,32,128]{2,1,0:T(8,128)(2,1)S(1)}, u32[]{:S(2)}, u32[]{:S(2)}) %all-to-all-start) | async-done | bytes 262176 | tf_op jit(solution)/shard_map/all_to_all | solution.py:302
  28.8 0.4 convolution_convert_fusion
  29.2 0.9 copy.39
  30.1 3.8 %all-to-all-start.1 = ((bf16[32,40,128]{2,1,0:T(8,128)(2,1)}), bf16[32,40,128]{2,1,0:T(8,128)(2,1)S(1)}, u32[]{:S(2)}, u32[]{:S(2)}) async-start(bf16[32,40,128]{2,1,0:T(8,128)(2,1)} %copy.39), calls=%async_computation.1 | async-start | bytes 655360 | tf_op jit(solution)/shard_map/all_to_all | solution.py:326
  33.9 4.5 %within.1.intra_ref = f32[512,1024]{1,0:T(8,128)S(1)} custom-call(f32[8]{0:T(128)} %rate_ref.5, s32[4]{0:T(128)} %lengths_ref.5, bf16[512,1024]{1,0:T(8,128)(2,1)} %query_ref.3, bf16[512,1024]{1,0:T(8,128)(2,1)} %key_ref.3, bf16[512,1024]{1,0:T(8,128)(2,1)} %grad_ref.3), custom_call_target="tpu_custom_call" | custom-call | tf_op jit(solution)/shard_map/within/pallas_call | solution.py:107
  38.4 0.0 copy-start.18
  38.4 0.0 copy-start.17
  38.4 5.1 %all-to-all-done.1 = bf16[32,40,128]{2,1,0:T(8,128)(2,1)S(1)} async-done(((bf16[32,40,128]{2,1,0:T(8,128)(2,1)}), bf16[32,40,128]{2,1,0:T(8,128)(2,1)S(1)}, u32[]{:S(2)}, u32[]{:S(2)}) %all-to-all-start.1) | async-done | bytes 327712 | tf_op jit(solution)/shard_map/all_to_all | solution.py:326
  43.5 2.3 %across.1 = (bf16[128,1024]{1,0:T(8,128)(2,1)S(1)}, bf16[128,1024]{1,0:T(8,128)(2,1)S(1)}, bf16[128,1024]{1,0:T(8,128)(2,1)S(1)}, bf16[128,1024]{1,0:T(8,128)(2,1)S(1)}) custom-call(f32[8]{0:T(128)} %rate_ref.5, s32[4]{0:T(128)} %lengths_ref.5, bf16[512,1024]{1,0:T(8,128)(2,1)} %key_ref.3, bf16[8,128,128]{2,1,0:T(8,128)(2,1)S(1)} %bitcast.39, ...), custom_call_target="tpu_custom_call" | custom-call | tf_op jit(solution)/shard_map/across/pallas_call | solution.py:145
  45.9 0.4 collective-permute-start
  46.3 2.3 %collective-permute-start.1 = (bf16[128,1024]{1,0:T(8,128)(2,1)S(1)}, bf16[128,1024]{1,0:T(8,128)(2,1)S(1)}, u32[]{:S(2)}, u32[]{:S(2)}) collective-permute-start(bf16[128,1024]{1,0:T(8,128)(2,1)S(1)} %get-tuple-element.12.refs_0_), channel_id=1, source_target_pairs={{0,96},{32,0},{64,32},{96,64},{1,97},{33,1},{65,33},{97,65},{2,98}... | collective-permute-start | bytes 786440 | tf_op jit(solution)/shard_map/ppermute | solution.py:357
  48.6 2.5 %collective-permute-start.3 = (bf16[128,1024]{1,0:T(8,128)(2,1)S(1)}, bf16[128,1024]{1,0:T(8,128)(2,1)S(1)}, u32[]{:S(2)}, u32[]{:S(2)}) collective-permute-start(bf16[128,1024]{1,0:T(8,128)(2,1)S(1)} %get-tuple-element.13), channel_id=1, source_target_pairs={{0,3},{1,0},{2,1},{3,2},{4,7},{5,4},{6,5},{7,6},{8,11},{9,8},{10,9... | collective-permute-start | bytes 786440 | tf_op jit(solution)/shard_map/ppermute | solution.py:352
  51.1 0.0 collective-permute-start.4
  51.1 1.7 %collective-permute-start.11 = (bf16[128,1024]{1,0:T(8,128)(2,1)S(1)}, bf16[128,1024]{1,0:T(8,128)(2,1)S(1)}, u32[]{:S(2)}, u32[]{:S(2)}) collective-permute-start(bf16[128,1024]{1,0:T(8,128)(2,1)S(1)} %get-tuple-element.17), channel_id=1, source_target_pairs={{0,2},{1,3},{2,0},{3,1},{4,6},{5,7},{6,4},{7,5},{8,10},{9,11},{10,... | collective-permute-start | bytes 786440 | tf_op jit(solution)/shard_map/ppermute | solution.py:352
  52.8 2.0 %collective-permute-done.refs_1_ = bf16[128,1024]{1,0:T(8,128)(2,1)S(1)} collective-permute-done((bf16[128,1024]{1,0:T(8,128)(2,1)S(1)}, bf16[128,1024]{1,0:T(8,128)(2,1)S(1)}, u32[]{:S(2)}, u32[]{:S(2)}) %collective-permute-start) | collective-permute-done | bytes 262176 | tf_op jit(solution)/shard_map/ppermute | solution.py:356
  54.9 0.0 collective-permute-start.2
  54.9 7.3 %collective-permute-done.3.refs_4_ = bf16[128,1024]{1,0:T(8,128)(2,1)S(1)} collective-permute-done((bf16[128,1024]{1,0:T(8,128)(2,1)S(1)}, bf16[128,1024]{1,0:T(8,128)(2,1)S(1)}, u32[]{:S(2)}, u32[]{:S(2)}) %collective-permute-start.3) | collective-permute-done | bytes 262176 | tf_op jit(solution)/shard_map/ppermute | solution.py:352
  62.2 3.9 %collective-permute-done.4.refs_8_ = bf16[128,1024]{1,0:T(8,128)(2,1)S(1)} collective-permute-done((bf16[128,1024]{1,0:T(8,128)(2,1)S(1)}, bf16[128,1024]{1,0:T(8,128)(2,1)S(1)}, u32[]{:S(2)}, u32[]{:S(2)}) %collective-permute-start.4) | collective-permute-done | bytes 262176 | tf_op jit(solution)/shard_map/ppermute | solution.py:352
  66.1 0.0 collective-permute-done.1.refs_2_
  66.1 0.3 collective-permute-start.6
  66.4 1.2 collective-permute-start.5
  67.7 0.0 collective-permute-start.8
  67.7 8.3 %collective-permute-done.11.refs_12_ = bf16[128,1024]{1,0:T(8,128)(2,1)S(1)} collective-permute-done((bf16[128,1024]{1,0:T(8,128)(2,1)S(1)}, bf16[128,1024]{1,0:T(8,128)(2,1)S(1)}, u32[]{:S(2)}, u32[]{:S(2)}) %collective-permute-start.11) | collective-permute-done | bytes 262176 | tf_op jit(solution)/shard_map/ppermute | solution.py:352
  76.0 0.1 collective-permute-start.13
  76.2 0.6 gather_fusion
  76.7 0.2 convert_reduce_fusion
  77.0 0.1 collective-permute-start.9
  77.1 1.5 collective-permute-start.12
  78.6 0.0 collective-permute-done.5.refs_5_
  78.6 1.4 collective-permute-start.7
  80.0 0.1 collective-permute-start.10
  80.0 1.9 %collective-permute-done.13.refs_14_ = bf16[128,1024]{1,0:T(8,128)(2,1)} collective-permute-done((bf16[128,1024]{1,0:T(8,128)(2,1)S(1)}, bf16[128,1024]{1,0:T(8,128)(2,1)}, u32[]{:S(2)}, u32[]{:S(2)}) %collective-permute-start.13) | collective-permute-done | bytes 262176 | tf_op jit(solution)/shard_map/ppermute | solution.py:357
  82.0 1.5 collective-permute-start.14
  83.5 0.1 add_bitcast_fusion
  83.5 0.4 fusion.pick
  84.0 3.5 %collective-permute-done.9.refs_10_ = bf16[128,1024]{1,0:T(8,128)(2,1)S(1)} collective-permute-done((bf16[128,1024]{1,0:T(8,128)(2,1)S(1)}, bf16[128,1024]{1,0:T(8,128)(2,1)S(1)}, u32[]{:S(2)}, u32[]{:S(2)}) %collective-permute-start.9) | collective-permute-done | bytes 262176 | tf_op jit(solution)/shard_map/ppermute | solution.py:357
  87.5 3.1 %collective-permute-done.7.refs_7_ = bf16[128,1024]{1,0:T(8,128)(2,1)S(1)} collective-permute-done((bf16[128,1024]{1,0:T(8,128)(2,1)}, bf16[128,1024]{1,0:T(8,128)(2,1)S(1)}, u32[]{:S(2)}, u32[]{:S(2)}) %collective-permute-start.7) | collective-permute-done | bytes 262176 | tf_op jit(solution)/shard_map/ppermute | solution.py:358
  90.6 5.6 %collective-permute-done.10.refs_11_ = bf16[128,1024]{1,0:T(8,128)(2,1)S(1)} collective-permute-done((bf16[128,1024]{1,0:T(8,128)(2,1)}, bf16[128,1024]{1,0:T(8,128)(2,1)S(1)}, u32[]{:S(2)}, u32[]{:S(2)}) %collective-permute-start.10) | collective-permute-done | bytes 262176 | tf_op jit(solution)/shard_map/ppermute | solution.py:358
  96.2 0.7 copy-done.12
  96.9 0.7 copy-done.10
  97.6 0.0 collective-permute-done.14.refs_15_
  97.7 14.4 %project.1 = bf16[1024,1536]{1,0:T(8,128)(2,1)} custom-call(s32[4]{0:T(128)S(1)} %and_select_fusion.1.place, bf16[1024,512]{1,0:T(8,128)(2,1)S(1)} %fusion.pick, bf16[128,1024]{1,0:T(8,128)(2,1)} %copy-done, bf16[128,1024]{1,0:T(8,128)(2,1)} %copy-done.2, bf16[128,1024]{1,0:T(8,128)(2,1)} %copy-done.3, bf16[128,1024]{1,0:T(8,128)(2,1)} %copy-done.7, ...), custom_call_target="tpu_custom_call" | custom-call | tf_op jit(solution)/shard_map/project/pallas_call | solution.py:186
  112.1 7.4 %all-to-all-start.2 = ((bf16[128,8,1536]{2,1,0:T(8,128)(2,1)}), bf16[128,8,1536]{2,1,0:T(8,128)(2,1)S(1)}, u32[]{:S(2)}, u32[]{:S(2)}) async-start(bf16[128,8,1536]{2,1,0:T(8,128)(2,1)} %bitcast.44), calls=%async_computation.2 | async-start | bytes 6291456 | tf_op jit(solution)/shard_map/all_to_all | solution.py:373
  119.5 1.0 fusion.35
  120.5 0.1 copy.48
  120.6 0.1 copy.49
  120.7 0.1 sub.71
  120.8 0.1 copy.42
  120.8 0.2 copy.43
  121.0 0.2 reshape.207.row_ref
  121.2 0.1 sub.76.column_ref
  121.3 40.3 %all-to-all-done.2 = bf16[128,8,1536]{2,1,0:T(8,128)(2,1)S(1)} async-done(((bf16[128,8,1536]{2,1,0:T(8,128)(2,1)}), bf16[128,8,1536]{2,1,0:T(8,128)(2,1)S(1)}, u32[]{:S(2)}, u32[]{:S(2)}) %all-to-all-start.2) | async-done | bytes 3145760 | tf_op jit(solution)/shard_map/all_to_all | solution.py:373
  161.6 2.5 %merge.1 = bf16[1,128,2,6144]{3,2,1,0:T(2,128)(2,1)} custom-call(s32[256,1]{1,0:T(8,128)S(1)} %sub.76.column_ref, s32[1,256]{1,0:T(1,128)S(1)} %reshape.207.row_ref, bf16[4,32,8,1536]{3,2,1,0:T(8,128)(2,1)S(1)} %bitcast.38), custom_call_target="tpu_custom_call" | custom-call | tf_op jit(solution)/shard_map/merge/pallas_call | solution.py:223
  (59 shorter events, 0.3 us)
Async XLA Ops:
  6.5 15.8 %copy-start.15 = (s32[4]{0:T(128)S(1)}, s32[4]{0:T(128)}, u32[]{:S(2)}) copy-start(s32[4]{0:T(128)} %lengths_ref.5) | copy-start | bytes 52
  6.5 14.6 %copy-start.14 = (f32[8]{0:T(128)S(1)}, f32[8]{0:T(128)}, u32[]{:S(2)}) copy-start(f32[8]{0:T(128)} %rate_ref.5) | copy-start | bytes 100
  6.5 13.4 %copy-start.13 = (s32[512,1]{0,1:T(1,128)S(1)}, s32[512,1]{0,1:T(1,128)}, u32[]{:S(2)}) copy-start(s32[512,1]{0,1:T(1,128)} %param.16) | copy-start | bytes 6148
  6.5 13.7 %copy-start.16 = (s32[512]{0:T(512)S(1)}, s32[512]{0:T(512)}, u32[]{:S(2)}) copy-start(s32[512]{0:T(512)} %param.17) | copy-start | bytes 6148
  6.5 91.1 %all-gather.2.cloned.1.call-start = ((), (), s32[]{:S(2)}) async-start(), calls=%async_computation.3 | async-start | bytes 12976128 | tf_op jit(solution)/shard_map/all_gather | solution.py:277
  10.3 18.5 %all-to-all-start = ((bf16[32,32,128]{2,1,0:T(8,128)(2,1)}), bf16[32,32,128]{2,1,0:T(8,128)(2,1)S(1)}, u32[]{:S(2)}, u32[]{:S(2)}) async-start(bf16[32,32,128]{2,1,0:T(8,128)(2,1)} %bitcast.4), calls=%async_computation | async-start | bytes 524288 | tf_op jit(solution)/shard_map/all_to_all | solution.py:302
  30.1 13.4 %all-to-all-start.1 = ((bf16[32,40,128]{2,1,0:T(8,128)(2,1)}), bf16[32,40,128]{2,1,0:T(8,128)(2,1)S(1)}, u32[]{:S(2)}, u32[]{:S(2)}) async-start(bf16[32,40,128]{2,1,0:T(8,128)(2,1)} %copy.39), calls=%async_computation.1 | async-start | bytes 655360 | tf_op jit(solution)/shard_map/all_to_all | solution.py:326
  38.4 16.5 %copy-start.18 = (s32[4]{0:T(128)S(1)}, s32[4]{0:T(128)}, u32[]{:S(2)}) copy-start(s32[4]{0:T(128)} %constant.125) | copy-start | bytes 52
  38.4 16.5 %copy-start.17 = (s32[4]{0:T(128)S(1)}, s32[4]{0:T(128)}, u32[]{:S(2)}) copy-start(s32[4]{0:T(128)} %constant.126) | copy-start | bytes 52
  43.5 68.5 %copy-start.1 = (bf16[32,40,128]{2,1,0:T(8,128)(2,1)}, bf16[32,40,128]{2,1,0:T(8,128)(2,1)S(1)}, u32[]{:S(2)}) copy-start(bf16[32,40,128]{2,1,0:T(8,128)(2,1)S(1)} %all-to-all-done.1) | copy-start | bytes 983044
  45.9 51.7 %copy-start = (bf16[128,1024]{1,0:T(8,128)(2,1)}, bf16[128,1024]{1,0:T(8,128)(2,1)S(1)}, u32[]{:S(2)}) copy-start(bf16[128,1024]{1,0:T(8,128)(2,1)S(1)} %get-tuple-element.12.refs_0_) | copy-start | bytes 786436
  45.9 9.0 %collective-permute-start = (bf16[128,1024]{1,0:T(8,128)(2,1)S(1)}, bf16[128,1024]{1,0:T(8,128)(2,1)S(1)}, u32[]{:S(2)}, u32[]{:S(2)}) collective-permute-start(bf16[128,1024]{1,0:T(8,128)(2,1)S(1)} %get-tuple-element.12.refs_0_), channel_id=1, source_target_pairs={{0,32},{32,64},{64,96},{96,0},{1,33},{33,65},{65,97},{97,1},{2,34}... | collective-permute-start | bytes 786440 | tf_op jit(solution)/shard_map/ppermute | solution.py:356
  46.3 19.8 %collective-permute-start.1 = (bf16[128,1024]{1,0:T(8,128)(2,1)S(1)}, bf16[128,1024]{1,0:T(8,128)(2,1)S(1)}, u32[]{:S(2)}, u32[]{:S(2)}) collective-permute-start(bf16[128,1024]{1,0:T(8,128)(2,1)S(1)} %get-tuple-element.12.refs_0_), channel_id=1, source_target_pairs={{0,96},{32,0},{64,32},{96,64},{1,97},{33,1},{65,33},{97,65},{2,98}... | collective-permute-start | bytes 786440 | tf_op jit(solution)/shard_map/ppermute | solution.py:357
  48.6 13.6 %collective-permute-start.3 = (bf16[128,1024]{1,0:T(8,128)(2,1)S(1)}, bf16[128,1024]{1,0:T(8,128)(2,1)S(1)}, u32[]{:S(2)}, u32[]{:S(2)}) collective-permute-start(bf16[128,1024]{1,0:T(8,128)(2,1)S(1)} %get-tuple-element.13), channel_id=1, source_target_pairs={{0,3},{1,0},{2,1},{3,2},{4,7},{5,4},{6,5},{7,6},{8,11},{9,8},{10,9... | collective-permute-start | bytes 786440 | tf_op jit(solution)/shard_map/ppermute | solution.py:352
  51.1 15.0 %collective-permute-start.4 = (bf16[128,1024]{1,0:T(8,128)(2,1)S(1)}, bf16[128,1024]{1,0:T(8,128)(2,1)S(1)}, u32[]{:S(2)}, u32[]{:S(2)}) collective-permute-start(bf16[128,1024]{1,0:T(8,128)(2,1)S(1)} %get-tuple-element.14), channel_id=1, source_target_pairs={{0,1},{1,2},{2,3},{3,0},{4,5},{5,6},{6,7},{7,4},{8,9},{9,10},{10,1... | collective-permute-start | bytes 786440 | tf_op jit(solution)/shard_map/ppermute | solution.py:352
  51.1 24.9 %collective-permute-start.11 = (bf16[128,1024]{1,0:T(8,128)(2,1)S(1)}, bf16[128,1024]{1,0:T(8,128)(2,1)S(1)}, u32[]{:S(2)}, u32[]{:S(2)}) collective-permute-start(bf16[128,1024]{1,0:T(8,128)(2,1)S(1)} %get-tuple-element.17), channel_id=1, source_target_pairs={{0,2},{1,3},{2,0},{3,1},{4,6},{5,7},{6,4},{7,5},{8,10},{9,11},{10,... | collective-permute-start | bytes 786440 | tf_op jit(solution)/shard_map/ppermute | solution.py:352
  54.9 42.8 %copy-start.2 = (bf16[128,1024]{1,0:T(8,128)(2,1)}, bf16[128,1024]{1,0:T(8,128)(2,1)S(1)}, u32[]{:S(2)}) copy-start(bf16[128,1024]{1,0:T(8,128)(2,1)S(1)} %collective-permute-done.refs_1_) | copy-start | bytes 786436
  54.9 21.1 %collective-permute-start.2 = (bf16[128,1024]{1,0:T(8,128)(2,1)S(1)}, bf16[128,1024]{1,0:T(8,128)(2,1)S(1)}, u32[]{:S(2)}, u32[]{:S(2)}) collective-permute-start(bf16[128,1024]{1,0:T(8,128)(2,1)S(1)} %collective-permute-done.refs_1_), channel_id=1, source_target_pairs={{0,32},{32,64},{64,96},{96,0},{1,33},{33,65},{65,97},{97,1},{2,34}... | collective-permute-start | bytes 786440 | tf_op jit(solution)/shard_map/ppermute | solution.py:358
  62.2 35.4 %copy-start.4 = (bf16[128,1024]{1,0:T(8,128)(2,1)}, bf16[128,1024]{1,0:T(8,128)(2,1)S(1)}, u32[]{:S(2)}) copy-start(bf16[128,1024]{1,0:T(8,128)(2,1)S(1)} %collective-permute-done.3.refs_4_) | copy-start | bytes 786436
  66.1 31.5 %copy-start.5 = (bf16[128,1024]{1,0:T(8,128)(2,1)}, bf16[128,1024]{1,0:T(8,128)(2,1)S(1)}, u32[]{:S(2)}) copy-start(bf16[128,1024]{1,0:T(8,128)(2,1)S(1)} %collective-permute-done.4.refs_8_) | copy-start | bytes 786436
  66.1 31.5 %copy-start.3 = (bf16[128,1024]{1,0:T(8,128)(2,1)}, bf16[128,1024]{1,0:T(8,128)(2,1)S(1)}, u32[]{:S(2)}) copy-start(bf16[128,1024]{1,0:T(8,128)(2,1)S(1)} %collective-permute-done.1.refs_2_) | copy-start | bytes 786436
  66.1 11.0 %collective-permute-start.6 = (bf16[128,1024]{1,0:T(8,128)(2,1)S(1)}, bf16[128,1024]{1,0:T(8,128)(2,1)S(1)}, u32[]{:S(2)}, u32[]{:S(2)}) collective-permute-start(bf16[128,1024]{1,0:T(8,128)(2,1)S(1)} %collective-permute-done.3.refs_4_), channel_id=1, source_target_pairs={{0,96},{32,0},{64,32},{96,64},{1,97},{33,1},{65,33},{97,65},{2,98}... | collective-permute-start | bytes 786440 | tf_op jit(solution)/shard_map/ppermute | solution.py:357
  66.4 12.2 %collective-permute-start.5 = (bf16[128,1024]{1,0:T(8,128)(2,1)S(1)}, bf16[128,1024]{1,0:T(8,128)(2,1)}, u32[]{:S(2)}, u32[]{:S(2)}) collective-permute-start(bf16[128,1024]{1,0:T(8,128)(2,1)S(1)} %collective-permute-done.3.refs_4_), channel_id=1, source_target_pairs={{0,32},{32,64},{64,96},{96,0},{1,33},{33,65},{65,97},{97,1},{2,34}... | collective-permute-start | bytes 786440 | tf_op jit(solution)/shard_map/ppermute | solution.py:356
  67.7 12.3 %collective-permute-start.8 = (bf16[128,1024]{1,0:T(8,128)(2,1)S(1)}, bf16[128,1024]{1,0:T(8,128)(2,1)}, u32[]{:S(2)}, u32[]{:S(2)}) collective-permute-start(bf16[128,1024]{1,0:T(8,128)(2,1)S(1)} %collective-permute-done.4.refs_8_), channel_id=1, source_target_pairs={{0,32},{32,64},{64,96},{96,0},{1,33},{33,65},{65,97},{97,1},{2,34}... | collective-permute-start | bytes 786440 | tf_op jit(solution)/shard_map/ppermute | solution.py:356
  76.0 21.7 %copy-start.6 = (bf16[128,1024]{1,0:T(8,128)(2,1)}, bf16[128,1024]{1,0:T(8,128)(2,1)S(1)}, u32[]{:S(2)}) copy-start(bf16[128,1024]{1,0:T(8,128)(2,1)S(1)} %collective-permute-done.11.refs_12_) | copy-start | bytes 786436
  76.0 21.7 %copy-start.7 = (bf16[128,1024]{1,0:T(8,128)(2,1)}, bf16[128,1024]{1,0:T(8,128)(2,1)S(1)}, u32[]{:S(2)}) copy-start(bf16[128,1024]{1,0:T(8,128)(2,1)S(1)} %collective-permute-done.2.refs_3_) | copy-start | bytes 786436
  76.0 6.0 %collective-permute-start.13 = (bf16[128,1024]{1,0:T(8,128)(2,1)S(1)}, bf16[128,1024]{1,0:T(8,128)(2,1)}, u32[]{:S(2)}, u32[]{:S(2)}) collective-permute-start(bf16[128,1024]{1,0:T(8,128)(2,1)S(1)} %collective-permute-done.11.refs_12_), channel_id=1, source_target_pairs={{0,96},{32,0},{64,32},{96,64},{1,97},{33,1},{65,33},{97,65},{2,98}... | collective-permute-start | bytes 786440 | tf_op jit(solution)/shard_map/ppermute | solution.py:357
  77.0 10.5 %collective-permute-start.9 = (bf16[128,1024]{1,0:T(8,128)(2,1)S(1)}, bf16[128,1024]{1,0:T(8,128)(2,1)S(1)}, u32[]{:S(2)}, u32[]{:S(2)}) collective-permute-start(bf16[128,1024]{1,0:T(8,128)(2,1)S(1)} %collective-permute-done.4.refs_8_), channel_id=1, source_target_pairs={{0,96},{32,0},{64,32},{96,64},{1,97},{33,1},{65,33},{97,65},{2,98}... | collective-permute-start | bytes 786440 | tf_op jit(solution)/shard_map/ppermute | solution.py:357
  77.1 20.6 %copy-start.8 = (bf16[128,1024]{1,0:T(8,128)(2,1)}, bf16[128,1024]{1,0:T(8,128)(2,1)S(1)}, u32[]{:S(2)}) copy-start(bf16[128,1024]{1,0:T(8,128)(2,1)S(1)} %collective-permute-done.6.refs_6_) | copy-start | bytes 786436
  77.1 19.1 %collective-permute-start.12 = (bf16[128,1024]{1,0:T(8,128)(2,1)S(1)}, bf16[128,1024]{1,0:T(8,128)(2,1)S(1)}, u32[]{:S(2)}, u32[]{:S(2)}) collective-permute-start(bf16[128,1024]{1,0:T(8,128)(2,1)S(1)} %collective-permute-done.11.refs_12_), channel_id=1, source_target_pairs={{0,32},{32,64},{64,96},{96,0},{1,33},{33,65},{65,97},{97,1},{2,34}... | collective-permute-start | bytes 786440 | tf_op jit(solution)/shard_map/ppermute | solution.py:356
  78.6 12.0 %collective-permute-start.7 = (bf16[128,1024]{1,0:T(8,128)(2,1)}, bf16[128,1024]{1,0:T(8,128)(2,1)S(1)}, u32[]{:S(2)}, u32[]{:S(2)}) collective-permute-start(bf16[128,1024]{1,0:T(8,128)(2,1)} %collective-permute-done.5.refs_5_), channel_id=1, source_target_pairs={{0,32},{32,64},{64,96},{96,0},{1,33},{33,65},{65,97},{97,1},{2,34}... | collective-permute-start | bytes 786440 | tf_op jit(solution)/shard_map/ppermute | solution.py:358
  80.0 16.3 %collective-permute-start.10 = (bf16[128,1024]{1,0:T(8,128)(2,1)}, bf16[128,1024]{1,0:T(8,128)(2,1)S(1)}, u32[]{:S(2)}, u32[]{:S(2)}) collective-permute-start(bf16[128,1024]{1,0:T(8,128)(2,1)} %collective-permute-done.8.refs_9_), channel_id=1, source_target_pairs={{0,32},{32,64},{64,96},{96,0},{1,33},{33,65},{65,97},{97,1},{2,34}... | collective-permute-start | bytes 786440 | tf_op jit(solution)/shard_map/ppermute | solution.py:358
  82.0 15.7 %collective-permute-start.14 = (bf16[128,1024]{1,0:T(8,128)(2,1)}, bf16[128,1024]{1,0:T(8,128)(2,1)}, u32[]{:S(2)}, u32[]{:S(2)}) collective-permute-start(bf16[128,1024]{1,0:T(8,128)(2,1)} %collective-permute-done.13.refs_14_), channel_id=1, source_target_pairs={{0,96},{32,0},{64,32},{96,64},{1,97},{33,1},{65,33},{97,65},{2,98}... | collective-permute-start | bytes 786440 | tf_op jit(solution)/shard_map/ppermute | solution.py:358
  87.5 8.8 %copy-start.9 = (bf16[128,1024]{1,0:T(8,128)(2,1)}, bf16[128,1024]{1,0:T(8,128)(2,1)S(1)}, u32[]{:S(2)}) copy-start(bf16[128,1024]{1,0:T(8,128)(2,1)S(1)} %collective-permute-done.9.refs_10_) | copy-start | bytes 786436
  90.6 5.6 %copy-start.11 = (bf16[128,1024]{1,0:T(8,128)(2,1)}, bf16[128,1024]{1,0:T(8,128)(2,1)S(1)}, u32[]{:S(2)}) copy-start(bf16[128,1024]{1,0:T(8,128)(2,1)S(1)} %collective-permute-done.7.refs_7_) | copy-start | bytes 786436
  96.2 0.7 copy-start.12
  96.9 0.7 copy-start.10
  112.1 49.5 %all-to-all-start.2 = ((bf16[128,8,1536]{2,1,0:T(8,128)(2,1)}), bf16[128,8,1536]{2,1,0:T(8,128)(2,1)S(1)}, u32[]{:S(2)}, u32[]{:S(2)}) async-start(bf16[128,8,1536]{2,1,0:T(8,128)(2,1)} %bitcast.44), calls=%async_computation.2 | async-start | bytes 6291456 | tf_op jit(solution)/shard_map/all_to_all | solution.py:373
Sparse Core Ops, SparseCore 0:
  9.6 79.1 all-gather.1

commit v12 on v11

--- a/solution.py
+++ b/solution.py
@@ -365,7 +365,11 @@
     mine[3], *_ = lax.optimization_barrier((mine[3], groups[0][3]))
     groups.append(spread(mine[3], True))
     pieces = [
-        [pltpu.with_memory_space_constraint(q, pltpu.HBM) for q in group] for group in groups
+        [
+            pltpu.with_memory_space_constraint(q, pltpu.VMEM if turn < 2 else pltpu.HBM)
+            for q in group
+        ]
+        for turn, group in enumerate(groups)
     ]
 
     send = project(place, pick, pieces, weight, 512)

time: 171 us -> 170 us (level)
  transfers between devices with their start and end apart: 19 -> 19, of which waited for: 11 -> 11; matrix products, arithmetic and copies ran while one was open for 4% -> 3% of each run, Pallas kernels for 6% -> 6%
where the time goes in v12:
time: 170 us; the launch traced here: 169 us
  waiting for transfers between devices  88.5 us (52%)
  starting transfers between devices  34.5 us (20%)
  Pallas kernels  25.8 us (15%)
  between operations  14.3 us (8%)
  local copies, waits for them, and re-layouts  3.63 us (2%)
  other arithmetic  2.24 us (1%)
    all_to_all x1, waiting for transfers between devices, per_device(): got = lax.all_to_all(send, ALL, split_axis=0, concat_axis=0, tiled=True)  41.2 us
    ppermute x3, waiting for transfers between devices, per_device(): mine.append(lax.ppermute(own[turn], 'head', shift(n_head, TURNS[turn])))  19.7 us
    pallas_call x1, Pallas kernels, project(): pl.pallas_call(functools.partial(project_body, turns), grid_spec=pltpu.Pr...  13.7 us
    all_to_all x1, starting transfers between devices, per_device(): lax.all_to_all(state.reshape(n_seq, share, head_dim), SEQ, split_axis=0,...  9.6 us
    all_to_all x1, starting transfers between devices, per_device(): got = lax.all_to_all(send, ALL, split_axis=0, concat_axis=0, tiled=True)  8.05 us
    ppermute x4, waiting for transfers between devices, spread(): lax.ppermute(above if flip else below, 'z', shift(n_z, -1 if flip else 1))  7.83 us
    all_to_all x1, waiting for transfers between devices, per_device(): lax.all_to_all(state.reshape(n_seq, share, head_dim), SEQ, split_axis=0,...  6.13 us
    ppermute x4, waiting for transfers between devices, spread(): above = lax.ppermute(rows, 'z', shift(n_z, -1))  5.77 us
  transfers between devices with their start and end apart: 19, of which 11 were waited for; matrix products, arithmetic and copies ran while one was open for 3% of the time, Pallas kernels for 6%

profile of v12, /device:TPU:1, one launch (start us, length us, event | category | flops | bytes accessed | tf_op | source)
XLA Modules:
  0.0 169.3 jit_solution(7881885835996792974)
XLA Ops:
  6.5 0.0 all-gather.2.cloned.1.call-start
  6.6 0.7 all-gather.2.cloned.1.call-update
  7.3 3.0 %local_states.1 = bf16[8,128,128]{2,1,0:T(8,128)(2,1)} custom-call(f32[8]{0:T(128)} %rate_ref.5, s32[4]{0:T(128)} %lengths_ref.5, bf16[512,1024]{1,0:T(8,128)(2,1)} %query_ref.3, bf16[512,1024]{1,0:T(8,128)(2,1)} %grad_ref.3), custom_call_target="tpu_custom_call" | custom-call | tf_op jit(solution)/shard_map/local_states/pallas_call | solution.py:65
  10.3 9.6 %all-to-all-start = ((bf16[32,32,128]{2,1,0:T(8,128)(2,1)}), bf16[32,32,128]{2,1,0:T(8,128)(2,1)S(1)}, u32[]{:S(2)}, u32[]{:S(2)}) async-start(bf16[32,32,128]{2,1,0:T(8,128)(2,1)} %bitcast.4), calls=%async_computation | async-start | bytes 524288 | tf_op jit(solution)/shard_map/all_to_all | solution.py:302
  20.0 0.2 convert_reduce_fusion.1
  20.2 0.1 iota_add_fusion
  20.3 0.7 select_reduce_fusion
  21.0 0.1 maximum_bitcast_fusion
  21.2 0.6 dynamic_slice.9
  22.4 0.2 reduce-window.8
  22.6 0.1 convert_reduce_fusion.3
  22.7 6.1 %all-to-all-done = bf16[32,32,128]{2,1,0:T(8,128)(2,1)S(1)} async-done(((bf16[32,32,128]{2,1,0:T(8,128)(2,1)}), bf16[32,32,128]{2,1,0:T(8,128)(2,1)S(1)}, u32[]{:S(2)}, u32[]{:S(2)}) %all-to-all-start) | async-done | bytes 262176 | tf_op jit(solution)/shard_map/all_to_all | solution.py:302
  28.8 0.4 convolution_convert_fusion
  29.3 0.9 copy.39
  30.1 3.8 %all-to-all-start.1 = ((bf16[32,40,128]{2,1,0:T(8,128)(2,1)}), bf16[32,40,128]{2,1,0:T(8,128)(2,1)S(1)}, u32[]{:S(2)}, u32[]{:S(2)}) async-start(bf16[32,40,128]{2,1,0:T(8,128)(2,1)} %copy.39), calls=%async_computation.1 | async-start | bytes 655360 | tf_op jit(solution)/shard_map/all_to_all | solution.py:326
  33.9 4.5 %within.1.intra_ref = f32[512,1024]{1,0:T(8,128)S(1)} custom-call(f32[8]{0:T(128)} %rate_ref.5, s32[4]{0:T(128)} %lengths_ref.5, bf16[512,1024]{1,0:T(8,128)(2,1)} %query_ref.3, bf16[512,1024]{1,0:T(8,128)(2,1)} %key_ref.3, bf16[512,1024]{1,0:T(8,128)(2,1)} %grad_ref.3), custom_call_target="tpu_custom_call" | custom-call | tf_op jit(solution)/shard_map/within/pallas_call | solution.py:107
  38.4 0.0 copy-start.7
  38.4 0.0 copy-start.6
  38.4 5.1 %all-to-all-done.1 = bf16[32,40,128]{2,1,0:T(8,128)(2,1)S(1)} async-done(((bf16[32,40,128]{2,1,0:T(8,128)(2,1)}), bf16[32,40,128]{2,1,0:T(8,128)(2,1)S(1)}, u32[]{:S(2)}, u32[]{:S(2)}) %all-to-all-start.1) | async-done | bytes 327712 | tf_op jit(solution)/shard_map/all_to_all | solution.py:326
  43.5 2.1 %across.1 = (bf16[128,1024]{1,0:T(8,128)(2,1)S(1)}, bf16[128,1024]{1,0:T(8,128)(2,1)S(1)}, bf16[128,1024]{1,0:T(8,128)(2,1)S(1)}, bf16[128,1024]{1,0:T(8,128)(2,1)S(1)}) custom-call(f32[8]{0:T(128)} %rate_ref.5, s32[4]{0:T(128)} %lengths_ref.5, bf16[512,1024]{1,0:T(8,128)(2,1)} %key_ref.3, bf16[8,128,128]{2,1,0:T(8,128)(2,1)S(1)} %bitcast.39, ...), custom_call_target="tpu_custom_call" | custom-call | tf_op jit(solution)/shard_map/across/pallas_call | solution.py:145
  45.7 0.4 collective-permute-start
  46.1 2.3 %collective-permute-start.1 = (bf16[128,1024]{1,0:T(8,128)(2,1)S(1)}, bf16[128,1024]{1,0:T(8,128)(2,1)S(1)}, u32[]{:S(2)}, u32[]{:S(2)}) collective-permute-start(bf16[128,1024]{1,0:T(8,128)(2,1)S(1)} %get-tuple-element.12.refs_0_), channel_id=1, source_target_pairs={{0,96},{32,0},{64,32},{96,64},{1,97},{33,1},{65,33},{97,65},{2,98}... | collective-permute-start | bytes 786440 | tf_op jit(solution)/shard_map/ppermute | solution.py:357
  48.4 2.5 %collective-permute-start.3 = (bf16[128,1024]{1,0:T(8,128)(2,1)S(1)}, bf16[128,1024]{1,0:T(8,128)(2,1)S(1)}, u32[]{:S(2)}, u32[]{:S(2)}) collective-permute-start(bf16[128,1024]{1,0:T(8,128)(2,1)S(1)} %get-tuple-element.13), channel_id=1, source_target_pairs={{0,3},{1,0},{2,1},{3,2},{4,7},{5,4},{6,5},{7,6},{8,11},{9,8},{10,9... | collective-permute-start | bytes 786440 | tf_op jit(solution)/shard_map/ppermute | solution.py:352
  50.9 0.0 collective-permute-start.4
  50.9 1.7 %collective-permute-start.11 = (bf16[128,1024]{1,0:T(8,128)(2,1)S(1)}, bf16[128,1024]{1,0:T(8,128)(2,1)}, u32[]{:S(2)}, u32[]{:S(2)}) collective-permute-start(bf16[128,1024]{1,0:T(8,128)(2,1)S(1)} %get-tuple-element.17), channel_id=1, source_target_pairs={{0,2},{1,3},{2,0},{3,1},{4,6},{5,7},{6,4},{7,5},{8,10},{9,11},{10,... | collective-permute-start | bytes 786440 | tf_op jit(solution)/shard_map/ppermute | solution.py:352
  52.7 2.0 %collective-permute-done.refs_1_ = bf16[128,1024]{1,0:T(8,128)(2,1)S(1)} collective-permute-done((bf16[128,1024]{1,0:T(8,128)(2,1)S(1)}, bf16[128,1024]{1,0:T(8,128)(2,1)S(1)}, u32[]{:S(2)}, u32[]{:S(2)}) %collective-permute-start) | collective-permute-done | bytes 262176 | tf_op jit(solution)/shard_map/ppermute | solution.py:356
  54.7 0.0 collective-permute-start.2
  54.7 7.3 %collective-permute-done.3.refs_4_ = bf16[128,1024]{1,0:T(8,128)(2,1)S(1)} collective-permute-done((bf16[128,1024]{1,0:T(8,128)(2,1)S(1)}, bf16[128,1024]{1,0:T(8,128)(2,1)S(1)}, u32[]{:S(2)}, u32[]{:S(2)}) %collective-permute-start.3) | collective-permute-done | bytes 262176 | tf_op jit(solution)/shard_map/ppermute | solution.py:352
  62.0 3.9 %collective-permute-done.4.refs_8_ = bf16[128,1024]{1,0:T(8,128)(2,1)} collective-permute-done((bf16[128,1024]{1,0:T(8,128)(2,1)S(1)}, bf16[128,1024]{1,0:T(8,128)(2,1)}, u32[]{:S(2)}, u32[]{:S(2)}) %collective-permute-start.4) | collective-permute-done | bytes 262176 | tf_op jit(solution)/shard_map/ppermute | solution.py:352
  65.9 0.1 collective-permute-start.6
  66.0 1.4 collective-permute-start.5
  67.4 0.0 collective-permute-start.8
  67.4 8.5 %collective-permute-done.11.refs_12_ = bf16[128,1024]{1,0:T(8,128)(2,1)} collective-permute-done((bf16[128,1024]{1,0:T(8,128)(2,1)S(1)}, bf16[128,1024]{1,0:T(8,128)(2,1)}, u32[]{:S(2)}, u32[]{:S(2)}) %collective-permute-start.11) | collective-permute-done | bytes 262176 | tf_op jit(solution)/shard_map/ppermute | solution.py:352
  75.9 0.0 collective-permute-done.2.refs_3_
  75.9 0.0 collective-permute-start.13
  76.0 0.6 gather_fusion
  76.6 0.2 convert_reduce_fusion
  76.8 0.3 collective-permute-start.9
  77.1 1.3 collective-permute-start.12
  78.4 0.0 collective-permute-done.5.refs_5_
  78.4 1.4 collective-permute-start.7
  79.8 0.1 collective-permute-start.10
  79.9 2.1 %collective-permute-done.13.refs_14_ = bf16[128,1024]{1,0:T(8,128)(2,1)} collective-permute-done((bf16[128,1024]{1,0:T(8,128)(2,1)}, bf16[128,1024]{1,0:T(8,128)(2,1)}, u32[]{:S(2)}, u32[]{:S(2)}) %collective-permute-start.13) | collective-permute-done | bytes 262176 | tf_op jit(solution)/shard_map/ppermute | solution.py:357
  82.0 1.5 collective-permute-start.14
  83.5 0.1 add_bitcast_fusion
  83.6 0.4 fusion.pick
  84.0 3.6 %collective-permute-done.9.refs_10_ = bf16[128,1024]{1,0:T(8,128)(2,1)S(1)} collective-permute-done((bf16[128,1024]{1,0:T(8,128)(2,1)}, bf16[128,1024]{1,0:T(8,128)(2,1)S(1)}, u32[]{:S(2)}, u32[]{:S(2)}) %collective-permute-start.9) | collective-permute-done | bytes 262176 | tf_op jit(solution)/shard_map/ppermute | solution.py:357
  87.6 2.2 %collective-permute-done.7.refs_7_ = bf16[128,1024]{1,0:T(8,128)(2,1)S(1)} collective-permute-done((bf16[128,1024]{1,0:T(8,128)(2,1)S(1)}, bf16[128,1024]{1,0:T(8,128)(2,1)S(1)}, u32[]{:S(2)}, u32[]{:S(2)}) %collective-permute-start.7) | collective-permute-done | bytes 262176 | tf_op jit(solution)/shard_map/ppermute | solution.py:358
  89.9 5.6 %collective-permute-done.10.refs_11_ = bf16[128,1024]{1,0:T(8,128)(2,1)S(1)} collective-permute-done((bf16[128,1024]{1,0:T(8,128)(2,1)}, bf16[128,1024]{1,0:T(8,128)(2,1)S(1)}, u32[]{:S(2)}, u32[]{:S(2)}) %collective-permute-start.10) | collective-permute-done | bytes 262176 | tf_op jit(solution)/shard_map/ppermute | solution.py:358
  95.5 0.7 copy-done.1
  96.2 0.0 collective-permute-done.12.refs_13_
  96.2 0.0 collective-permute-done.14.refs_15_
  96.2 13.7 %project.1 = bf16[1024,1536]{1,0:T(8,128)(2,1)} custom-call(s32[4]{0:T(128)S(1)} %and_select_fusion.1.place, bf16[1024,512]{1,0:T(8,128)(2,1)S(1)} %fusion.pick, bf16[128,1024]{1,0:T(8,128)(2,1)S(1)} %get-tuple-element.12.refs_0_, bf16[128,1024]{1,0:T(8,128)(2,1)S(1)} %collective-permute-done.refs_1_, bf16[128,1024]{1,0:T(8,128)(2,1)S(1)} %collective-permute-done.1.refs_2_, ...), custom_call_target="tpu_custom_call" | custom-call | tf_op jit(solution)/shard_map/project/pallas_call | solution.py:186
  109.9 8.1 %all-to-all-start.2 = ((bf16[128,8,1536]{2,1,0:T(8,128)(2,1)}), bf16[128,8,1536]{2,1,0:T(8,128)(2,1)S(1)}, u32[]{:S(2)}, u32[]{:S(2)}) async-start(bf16[128,8,1536]{2,1,0:T(8,128)(2,1)} %bitcast.44), calls=%async_computation.2 | async-start | bytes 6291456 | tf_op jit(solution)/shard_map/all_to_all | solution.py:377
  118.0 0.1 fusion.35
  118.1 0.1 copy.48
  118.1 0.1 copy.49
  118.2 0.1 sub.71
  118.3 0.1 copy.42
  118.4 0.2 copy.43
  118.6 0.2 reshape.207.row_ref
  118.7 0.1 sub.76.column_ref
  118.8 41.2 %all-to-all-done.2 = bf16[128,8,1536]{2,1,0:T(8,128)(2,1)S(1)} async-done(((bf16[128,8,1536]{2,1,0:T(8,128)(2,1)}), bf16[128,8,1536]{2,1,0:T(8,128)(2,1)S(1)}, u32[]{:S(2)}, u32[]{:S(2)}) %all-to-all-start.2) | async-done | bytes 3145760 | tf_op jit(solution)/shard_map/all_to_all | solution.py:377
  160.0 2.5 %merge.1 = bf16[1,128,2,6144]{3,2,1,0:T(2,128)(2,1)} custom-call(s32[256,1]{1,0:T(8,128)S(1)} %sub.76.column_ref, s32[1,256]{1,0:T(1,128)S(1)} %reshape.207.row_ref, bf16[4,32,8,1536]{3,2,1,0:T(8,128)(2,1)S(1)} %bitcast.38), custom_call_target="tpu_custom_call" | custom-call | tf_op jit(solution)/shard_map/merge/pallas_call | solution.py:223
  (37 shorter events, 0.3 us)
Async XLA Ops:
  6.5 15.8 %copy-start.4 = (s32[4]{0:T(128)S(1)}, s32[4]{0:T(128)}, u32[]{:S(2)}) copy-start(s32[4]{0:T(128)} %lengths_ref.5) | copy-start | bytes 52
  6.5 14.6 %copy-start.3 = (f32[8]{0:T(128)S(1)}, f32[8]{0:T(128)}, u32[]{:S(2)}) copy-start(f32[8]{0:T(128)} %rate_ref.5) | copy-start | bytes 100
  6.5 13.4 %copy-start.2 = (s32[512,1]{0,1:T(1,128)S(1)}, s32[512,1]{0,1:T(1,128)}, u32[]{:S(2)}) copy-start(s32[512,1]{0,1:T(1,128)} %param.16) | copy-start | bytes 6148
  6.5 13.7 %copy-start.5 = (s32[512]{0:T(512)S(1)}, s32[512]{0:T(512)}, u32[]{:S(2)}) copy-start(s32[512]{0:T(512)} %param.17) | copy-start | bytes 6148
  6.5 89.6 %all-gather.2.cloned.1.call-start = ((), (), s32[]{:S(2)}) async-start(), calls=%async_computation.3 | async-start | bytes 12976128 | tf_op jit(solution)/shard_map/all_gather | solution.py:277
  10.3 18.5 %all-to-all-start = ((bf16[32,32,128]{2,1,0:T(8,128)(2,1)}), bf16[32,32,128]{2,1,0:T(8,128)(2,1)S(1)}, u32[]{:S(2)}, u32[]{:S(2)}) async-start(bf16[32,32,128]{2,1,0:T(8,128)(2,1)} %bitcast.4), calls=%async_computation | async-start | bytes 524288 | tf_op jit(solution)/shard_map/all_to_all | solution.py:302
  30.1 13.4 %all-to-all-start.1 = ((bf16[32,40,128]{2,1,0:T(8,128)(2,1)}), bf16[32,40,128]{2,1,0:T(8,128)(2,1)S(1)}, u32[]{:S(2)}, u32[]{:S(2)}) async-start(bf16[32,40,128]{2,1,0:T(8,128)(2,1)} %copy.39), calls=%async_computation.1 | async-start | bytes 655360 | tf_op jit(solution)/shard_map/all_to_all | solution.py:326
  38.4 16.3 %copy-start.7 = (s32[4]{0:T(128)S(1)}, s32[4]{0:T(128)}, u32[]{:S(2)}) copy-start(s32[4]{0:T(128)} %constant.125) | copy-start | bytes 52
  38.4 16.3 %copy-start.6 = (s32[4]{0:T(128)S(1)}, s32[4]{0:T(128)}, u32[]{:S(2)}) copy-start(s32[4]{0:T(128)} %constant.126) | copy-start | bytes 52
  45.7 9.0 %collective-permute-start = (bf16[128,1024]{1,0:T(8,128)(2,1)S(1)}, bf16[128,1024]{1,0:T(8,128)(2,1)S(1)}, u32[]{:S(2)}, u32[]{:S(2)}) collective-permute-start(bf16[128,1024]{1,0:T(8,128)(2,1)S(1)} %get-tuple-element.12.refs_0_), channel_id=1, source_target_pairs={{0,32},{32,64},{64,96},{96,0},{1,33},{33,65},{65,97},{97,1},{2,34}... | collective-permute-start | bytes 786440 | tf_op jit(solution)/shard_map/ppermute | solution.py:356
  46.1 19.8 %collective-permute-start.1 = (bf16[128,1024]{1,0:T(8,128)(2,1)S(1)}, bf16[128,1024]{1,0:T(8,128)(2,1)S(1)}, u32[]{:S(2)}, u32[]{:S(2)}) collective-permute-start(bf16[128,1024]{1,0:T(8,128)(2,1)S(1)} %get-tuple-element.12.refs_0_), channel_id=1, source_target_pairs={{0,96},{32,0},{64,32},{96,64},{1,97},{33,1},{65,33},{97,65},{2,98}... | collective-permute-start | bytes 786440 | tf_op jit(solution)/shard_map/ppermute | solution.py:357
  48.4 13.6 %collective-permute-start.3 = (bf16[128,1024]{1,0:T(8,128)(2,1)S(1)}, bf16[128,1024]{1,0:T(8,128)(2,1)S(1)}, u32[]{:S(2)}, u32[]{:S(2)}) collective-permute-start(bf16[128,1024]{1,0:T(8,128)(2,1)S(1)} %get-tuple-element.13), channel_id=1, source_target_pairs={{0,3},{1,0},{2,1},{3,2},{4,7},{5,4},{6,5},{7,6},{8,11},{9,8},{10,9... | collective-permute-start | bytes 786440 | tf_op jit(solution)/shard_map/ppermute | solution.py:352
  50.9 15.0 %collective-permute-start.4 = (bf16[128,1024]{1,0:T(8,128)(2,1)S(1)}, bf16[128,1024]{1,0:T(8,128)(2,1)}, u32[]{:S(2)}, u32[]{:S(2)}) collective-permute-start(bf16[128,1024]{1,0:T(8,128)(2,1)S(1)} %get-tuple-element.14), channel_id=1, source_target_pairs={{0,1},{1,2},{2,3},{3,0},{4,5},{5,6},{6,7},{7,4},{8,9},{9,10},{10,1... | collective-permute-start | bytes 786440 | tf_op jit(solution)/shard_map/ppermute | solution.py:352
  50.9 25.0 %collective-permute-start.11 = (bf16[128,1024]{1,0:T(8,128)(2,1)S(1)}, bf16[128,1024]{1,0:T(8,128)(2,1)}, u32[]{:S(2)}, u32[]{:S(2)}) collective-permute-start(bf16[128,1024]{1,0:T(8,128)(2,1)S(1)} %get-tuple-element.17), channel_id=1, source_target_pairs={{0,2},{1,3},{2,0},{3,1},{4,6},{5,7},{6,4},{7,5},{8,10},{9,11},{10,... | collective-permute-start | bytes 786440 | tf_op jit(solution)/shard_map/ppermute | solution.py:352
  54.7 21.2 %collective-permute-start.2 = (bf16[128,1024]{1,0:T(8,128)(2,1)S(1)}, bf16[128,1024]{1,0:T(8,128)(2,1)S(1)}, u32[]{:S(2)}, u32[]{:S(2)}) collective-permute-start(bf16[128,1024]{1,0:T(8,128)(2,1)S(1)} %collective-permute-done.refs_1_), channel_id=1, source_target_pairs={{0,32},{32,64},{64,96},{96,0},{1,33},{33,65},{65,97},{97,1},{2,34}... | collective-permute-start | bytes 786440 | tf_op jit(solution)/shard_map/ppermute | solution.py:358
  65.9 11.2 %collective-permute-start.6 = (bf16[128,1024]{1,0:T(8,128)(2,1)S(1)}, bf16[128,1024]{1,0:T(8,128)(2,1)S(1)}, u32[]{:S(2)}, u32[]{:S(2)}) collective-permute-start(bf16[128,1024]{1,0:T(8,128)(2,1)S(1)} %collective-permute-done.3.refs_4_), channel_id=1, source_target_pairs={{0,96},{32,0},{64,32},{96,64},{1,97},{33,1},{65,33},{97,65},{2,98}... | collective-permute-start | bytes 786440 | tf_op jit(solution)/shard_map/ppermute | solution.py:357
  66.0 12.4 %collective-permute-start.5 = (bf16[128,1024]{1,0:T(8,128)(2,1)S(1)}, bf16[128,1024]{1,0:T(8,128)(2,1)S(1)}, u32[]{:S(2)}, u32[]{:S(2)}) collective-permute-start(bf16[128,1024]{1,0:T(8,128)(2,1)S(1)} %collective-permute-done.3.refs_4_), channel_id=1, source_target_pairs={{0,32},{32,64},{64,96},{96,0},{1,33},{33,65},{65,97},{97,1},{2,34}... | collective-permute-start | bytes 786440 | tf_op jit(solution)/shard_map/ppermute | solution.py:356
  67.4 12.4 %collective-permute-start.8 = (bf16[128,1024]{1,0:T(8,128)(2,1)}, bf16[128,1024]{1,0:T(8,128)(2,1)}, u32[]{:S(2)}, u32[]{:S(2)}) collective-permute-start(bf16[128,1024]{1,0:T(8,128)(2,1)} %collective-permute-done.4.refs_8_), channel_id=1, source_target_pairs={{0,32},{32,64},{64,96},{96,0},{1,33},{33,65},{65,97},{97,1},{2,34}... | collective-permute-start | bytes 786440 | tf_op jit(solution)/shard_map/ppermute | solution.py:356
  75.9 6.1 %collective-permute-start.13 = (bf16[128,1024]{1,0:T(8,128)(2,1)}, bf16[128,1024]{1,0:T(8,128)(2,1)}, u32[]{:S(2)}, u32[]{:S(2)}) collective-permute-start(bf16[128,1024]{1,0:T(8,128)(2,1)} %collective-permute-done.11.refs_12_), channel_id=1, source_target_pairs={{0,96},{32,0},{64,32},{96,64},{1,97},{33,1},{65,33},{97,65},{2,98}... | collective-permute-start | bytes 786440 | tf_op jit(solution)/shard_map/ppermute | solution.py:357
  76.8 10.8 %collective-permute-start.9 = (bf16[128,1024]{1,0:T(8,128)(2,1)}, bf16[128,1024]{1,0:T(8,128)(2,1)S(1)}, u32[]{:S(2)}, u32[]{:S(2)}) collective-permute-start(bf16[128,1024]{1,0:T(8,128)(2,1)} %collective-permute-done.4.refs_8_), channel_id=1, source_target_pairs={{0,96},{32,0},{64,32},{96,64},{1,97},{33,1},{65,33},{97,65},{2,98}... | collective-permute-start | bytes 786440 | tf_op jit(solution)/shard_map/ppermute | solution.py:357
  77.1 19.1 %collective-permute-start.12 = (bf16[128,1024]{1,0:T(8,128)(2,1)}, bf16[128,1024]{1,0:T(8,128)(2,1)}, u32[]{:S(2)}, u32[]{:S(2)}) collective-permute-start(bf16[128,1024]{1,0:T(8,128)(2,1)} %collective-permute-done.11.refs_12_), channel_id=1, source_target_pairs={{0,32},{32,64},{64,96},{96,0},{1,33},{33,65},{65,97},{97,1},{2,34}... | collective-permute-start | bytes 786440 | tf_op jit(solution)/shard_map/ppermute | solution.py:356
  78.4 11.4 %collective-permute-start.7 = (bf16[128,1024]{1,0:T(8,128)(2,1)S(1)}, bf16[128,1024]{1,0:T(8,128)(2,1)S(1)}, u32[]{:S(2)}, u32[]{:S(2)}) collective-permute-start(bf16[128,1024]{1,0:T(8,128)(2,1)S(1)} %collective-permute-done.5.refs_5_), channel_id=1, source_target_pairs={{0,32},{32,64},{64,96},{96,0},{1,33},{33,65},{65,97},{97,1},{2,34}... | collective-permute-start | bytes 786440 | tf_op jit(solution)/shard_map/ppermute | solution.py:358
  79.8 15.7 %collective-permute-start.10 = (bf16[128,1024]{1,0:T(8,128)(2,1)}, bf16[128,1024]{1,0:T(8,128)(2,1)S(1)}, u32[]{:S(2)}, u32[]{:S(2)}) collective-permute-start(bf16[128,1024]{1,0:T(8,128)(2,1)} %collective-permute-done.8.refs_9_), channel_id=1, source_target_pairs={{0,32},{32,64},{64,96},{96,0},{1,33},{33,65},{65,97},{97,1},{2,34}... | collective-permute-start | bytes 786440 | tf_op jit(solution)/shard_map/ppermute | solution.py:358
  82.0 14.2 %collective-permute-start.14 = (bf16[128,1024]{1,0:T(8,128)(2,1)}, bf16[128,1024]{1,0:T(8,128)(2,1)}, u32[]{:S(2)}, u32[]{:S(2)}) collective-permute-start(bf16[128,1024]{1,0:T(8,128)(2,1)} %collective-permute-done.13.refs_14_), channel_id=1, source_target_pairs={{0,96},{32,0},{64,32},{96,64},{1,97},{33,1},{65,33},{97,65},{2,98}... | collective-permute-start | bytes 786440 | tf_op jit(solution)/shard_map/ppermute | solution.py:358
  87.6 2.2 %copy-start = (bf16[128,1024]{1,0:T(8,128)(2,1)}, bf16[128,1024]{1,0:T(8,128)(2,1)S(1)}, u32[]{:S(2)}) copy-start(bf16[128,1024]{1,0:T(8,128)(2,1)S(1)} %collective-permute-done.9.refs_10_) | copy-start | bytes 786436
  95.5 0.7 copy-start.1
  109.9 50.1 %all-to-all-start.2 = ((bf16[128,8,1536]{2,1,0:T(8,128)(2,1)}), bf16[128,8,1536]{2,1,0:T(8,128)(2,1)S(1)}, u32[]{:S(2)}, u32[]{:S(2)}) async-start(bf16[128,8,1536]{2,1,0:T(8,128)(2,1)} %bitcast.44), calls=%async_computation.2 | async-start | bytes 6291456 | tf_op jit(solution)/shard_map/all_to_all | solution.py:377
Sparse Core Ops, SparseCore 0:
  9.6 79.1 all-gather.1

commit v13 on v12

--- a/solution.py
+++ b/solution.py
@@ -281,7 +281,7 @@
         pltpu.with_memory_space_constraint(array, pltpu.HBM)
         for array in (queries, key_vectors, output_grad, decay_rate, doc_lengths)
     )
-    state = local_states(rates, lengths, queries, output_grad, head_local // 2)
+    state = local_states(rates, lengths, queries, output_grad, head_local // 4)
     blocks = tok_rows // ROWS_BLK
     per = blocks * CAPACITY
     owners = owner_block[:, 0].reshape(blocks, ROWS_BLK)

time: 170 us -> 171 us (level)
  no operation moved by 1% of the time
where the time goes in v13:
time: 171 us
  waiting for transfers between devices  88.3 us (52%)
  starting transfers between devices  34.8 us (20%)
  Pallas kernels  27.3 us (16%)
  between operations  14.3 us (8%)
  local copies, waits for them, and re-layouts  3.63 us (2%)
  other arithmetic  2.24 us (1%)
    all_to_all x1, waiting for transfers between devices, per_device(): got = lax.all_to_all(send, ALL, split_axis=0, concat_axis=0, tiled=True)  41.2 us
    ppermute x3, waiting for transfers between devices, per_device(): mine.append(lax.ppermute(own[turn], 'head', shift(n_head, TURNS[turn])))  19.7 us
    pallas_call x1, Pallas kernels, project(): pl.pallas_call(functools.partial(project_body, turns), grid_spec=pltpu.Pr...  13.7 us
    all_to_all x1, starting transfers between devices, per_device(): lax.all_to_all(state.reshape(n_seq, share, head_dim), SEQ, split_axis=0,...  9.6 us
    all_to_all x1, starting transfers between devices, per_device(): got = lax.all_to_all(send, ALL, split_axis=0, concat_axis=0, tiled=True)  7.86 us
    ppermute x4, waiting for transfers between devices, spread(): lax.ppermute(above if flip else below, 'z', shift(n_z, -1 if flip else 1))  7.84 us
    all_to_all x1, waiting for transfers between devices, per_device(): lax.all_to_all(state.reshape(n_seq, share, head_dim), SEQ, split_axis=0,...  6.14 us
    ppermute x4, waiting for transfers between devices, spread(): above = lax.ppermute(rows, 'z', shift(n_z, -1))  5.71 us
  transfers between devices with their start and end apart: 19, of which 11 were waited for; matrix products, arithmetic and copies ran while one was open for 3% of the time, Pallas kernels for 6%

profile of v13, /device:TPU:1, one launch (start us, length us, event | category | flops | bytes accessed | tf_op | source)
XLA Modules:
  0.0 171.0 jit_solution(14928596256833210193)
XLA Ops:
  6.5 0.0 all-gather.2.cloned.1.call-start
  6.6 0.7 all-gather.2.cloned.1.call-update
  7.3 4.2 %local_states.1 = bf16[8,128,128]{2,1,0:T(8,128)(2,1)} custom-call(f32[8]{0:T(128)} %rate_ref.5, s32[4]{0:T(128)} %lengths_ref.5, bf16[512,1024]{1,0:T(8,128)(2,1)} %query_ref.3, bf16[512,1024]{1,0:T(8,128)(2,1)} %grad_ref.3), custom_call_target="tpu_custom_call" | custom-call | tf_op jit(solution)/shard_map/local_states/pallas_call | solution.py:65
  11.5 9.6 %all-to-all-start = ((bf16[32,32,128]{2,1,0:T(8,128)(2,1)}), bf16[32,32,128]{2,1,0:T(8,128)(2,1)S(1)}, u32[]{:S(2)}, u32[]{:S(2)}) async-start(bf16[32,32,128]{2,1,0:T(8,128)(2,1)} %bitcast.4), calls=%async_computation | async-start | bytes 524288 | tf_op jit(solution)/shard_map/all_to_all | solution.py:302
  21.1 0.2 convert_reduce_fusion.1
  21.4 0.1 iota_add_fusion
  21.5 0.7 select_reduce_fusion
  22.2 0.1 maximum_bitcast_fusion
  22.3 0.6 dynamic_slice.9
  23.6 0.2 reduce-window.8
  23.7 0.1 convert_reduce_fusion.3
  23.8 6.1 %all-to-all-done = bf16[32,32,128]{2,1,0:T(8,128)(2,1)S(1)} async-done(((bf16[32,32,128]{2,1,0:T(8,128)(2,1)}), bf16[32,32,128]{2,1,0:T(8,128)(2,1)S(1)}, u32[]{:S(2)}, u32[]{:S(2)}) %all-to-all-start) | async-done | bytes 262176 | tf_op jit(solution)/shard_map/all_to_all | solution.py:302
  30.0 0.4 convolution_convert_fusion
  30.4 0.9 copy.39
  31.3 4.1 %all-to-all-start.1 = ((bf16[32,40,128]{2,1,0:T(8,128)(2,1)}), bf16[32,40,128]{2,1,0:T(8,128)(2,1)S(1)}, u32[]{:S(2)}, u32[]{:S(2)}) async-start(bf16[32,40,128]{2,1,0:T(8,128)(2,1)} %copy.39), calls=%async_computation.1 | async-start | bytes 655360 | tf_op jit(solution)/shard_map/all_to_all | solution.py:326
  35.4 4.5 %within.1.intra_ref = f32[512,1024]{1,0:T(8,128)S(1)} custom-call(f32[8]{0:T(128)} %rate_ref.5, s32[4]{0:T(128)} %lengths_ref.5, bf16[512,1024]{1,0:T(8,128)(2,1)} %query_ref.3, bf16[512,1024]{1,0:T(8,128)(2,1)} %key_ref.3, bf16[512,1024]{1,0:T(8,128)(2,1)} %grad_ref.3), custom_call_target="tpu_custom_call" | custom-call | tf_op jit(solution)/shard_map/within/pallas_call | solution.py:107
  39.8 0.0 copy-start.7
  39.9 0.0 copy-start.6
  39.9 5.0 %all-to-all-done.1 = bf16[32,40,128]{2,1,0:T(8,128)(2,1)S(1)} async-done(((bf16[32,40,128]{2,1,0:T(8,128)(2,1)}), bf16[32,40,128]{2,1,0:T(8,128)(2,1)S(1)}, u32[]{:S(2)}, u32[]{:S(2)}) %all-to-all-start.1) | async-done | bytes 327712 | tf_op jit(solution)/shard_map/all_to_all | solution.py:326
  44.9 2.4 %across.1 = (bf16[128,1024]{1,0:T(8,128)(2,1)S(1)}, bf16[128,1024]{1,0:T(8,128)(2,1)S(1)}, bf16[128,1024]{1,0:T(8,128)(2,1)S(1)}, bf16[128,1024]{1,0:T(8,128)(2,1)S(1)}) custom-call(f32[8]{0:T(128)} %rate_ref.5, s32[4]{0:T(128)} %lengths_ref.5, bf16[512,1024]{1,0:T(8,128)(2,1)} %key_ref.3, bf16[8,128,128]{2,1,0:T(8,128)(2,1)S(1)} %bitcast.39, ...), custom_call_target="tpu_custom_call" | custom-call | tf_op jit(solution)/shard_map/across/pallas_call | solution.py:145
  47.4 0.1 collective-permute-start
  47.5 2.6 %collective-permute-start.1 = (bf16[128,1024]{1,0:T(8,128)(2,1)S(1)}, bf16[128,1024]{1,0:T(8,128)(2,1)S(1)}, u32[]{:S(2)}, u32[]{:S(2)}) collective-permute-start(bf16[128,1024]{1,0:T(8,128)(2,1)S(1)} %get-tuple-element.12.refs_0_), channel_id=1, source_target_pairs={{0,96},{32,0},{64,32},{96,64},{1,97},{33,1},{65,33},{97,65},{2,98}... | collective-permute-start | bytes 786440 | tf_op jit(solution)/shard_map/ppermute | solution.py:357
  50.1 2.6 %collective-permute-start.3 = (bf16[128,1024]{1,0:T(8,128)(2,1)S(1)}, bf16[128,1024]{1,0:T(8,128)(2,1)S(1)}, u32[]{:S(2)}, u32[]{:S(2)}) collective-permute-start(bf16[128,1024]{1,0:T(8,128)(2,1)S(1)} %get-tuple-element.13), channel_id=1, source_target_pairs={{0,3},{1,0},{2,1},{3,2},{4,7},{5,4},{6,5},{7,6},{8,11},{9,8},{10,9... | collective-permute-start | bytes 786440 | tf_op jit(solution)/shard_map/ppermute | solution.py:352
  52.7 0.0 collective-permute-start.4
  52.7 1.7 collective-permute-start.11
  54.5 2.1 %collective-permute-done.refs_1_ = bf16[128,1024]{1,0:T(8,128)(2,1)S(1)} collective-permute-done((bf16[128,1024]{1,0:T(8,128)(2,1)S(1)}, bf16[128,1024]{1,0:T(8,128)(2,1)S(1)}, u32[]{:S(2)}, u32[]{:S(2)}) %collective-permute-start) | collective-permute-done | bytes 262176 | tf_op jit(solution)/shard_map/ppermute | solution.py:356
  56.5 0.0 collective-permute-start.2
  56.6 7.2 %collective-permute-done.3.refs_4_ = bf16[128,1024]{1,0:T(8,128)(2,1)S(1)} collective-permute-done((bf16[128,1024]{1,0:T(8,128)(2,1)S(1)}, bf16[128,1024]{1,0:T(8,128)(2,1)S(1)}, u32[]{:S(2)}, u32[]{:S(2)}) %collective-permute-start.3) | collective-permute-done | bytes 262176 | tf_op jit(solution)/shard_map/ppermute | solution.py:352
  63.8 4.0 %collective-permute-done.4.refs_8_ = bf16[128,1024]{1,0:T(8,128)(2,1)} collective-permute-done((bf16[128,1024]{1,0:T(8,128)(2,1)S(1)}, bf16[128,1024]{1,0:T(8,128)(2,1)}, u32[]{:S(2)}, u32[]{:S(2)}) %collective-permute-start.4) | collective-permute-done | bytes 262176 | tf_op jit(solution)/shard_map/ppermute | solution.py:352
  67.8 0.0 collective-permute-done.1.refs_2_
  67.8 0.1 collective-permute-start.6
  67.9 1.4 collective-permute-start.5
  69.2 0.0 collective-permute-start.8
  69.3 8.4 %collective-permute-done.11.refs_12_ = bf16[128,1024]{1,0:T(8,128)(2,1)} collective-permute-done((bf16[128,1024]{1,0:T(8,128)(2,1)S(1)}, bf16[128,1024]{1,0:T(8,128)(2,1)}, u32[]{:S(2)}, u32[]{:S(2)}) %collective-permute-start.11) | collective-permute-done | bytes 262176 | tf_op jit(solution)/shard_map/ppermute | solution.py:352
  77.7 0.0 collective-permute-done.2.refs_3_
  77.7 0.1 collective-permute-start.13
  77.9 0.6 gather_fusion
  78.5 0.2 convert_reduce_fusion
  78.7 0.1 collective-permute-start.9
  78.8 0.0 collective-permute-done.6.refs_6_
  78.8 1.4 collective-permute-start.12
  80.2 1.4 collective-permute-start.7
  81.6 0.0 collective-permute-done.8.refs_9_
  81.6 0.1 collective-permute-start.10
  81.7 2.2 %collective-permute-done.13.refs_14_ = bf16[128,1024]{1,0:T(8,128)(2,1)} collective-permute-done((bf16[128,1024]{1,0:T(8,128)(2,1)}, bf16[128,1024]{1,0:T(8,128)(2,1)}, u32[]{:S(2)}, u32[]{:S(2)}) %collective-permute-start.13) | collective-permute-done | bytes 262176 | tf_op jit(solution)/shard_map/ppermute | solution.py:357
  83.9 1.6 collective-permute-start.14
  85.4 0.1 add_bitcast_fusion
  85.5 0.4 fusion.pick
  85.9 3.5 %collective-permute-done.9.refs_10_ = bf16[128,1024]{1,0:T(8,128)(2,1)S(1)} collective-permute-done((bf16[128,1024]{1,0:T(8,128)(2,1)}, bf16[128,1024]{1,0:T(8,128)(2,1)S(1)}, u32[]{:S(2)}, u32[]{:S(2)}) %collective-permute-start.9) | collective-permute-done | bytes 262176 | tf_op jit(solution)/shard_map/ppermute | solution.py:357
  89.5 2.2 %collective-permute-done.7.refs_7_ = bf16[128,1024]{1,0:T(8,128)(2,1)S(1)} collective-permute-done((bf16[128,1024]{1,0:T(8,128)(2,1)S(1)}, bf16[128,1024]{1,0:T(8,128)(2,1)S(1)}, u32[]{:S(2)}, u32[]{:S(2)}) %collective-permute-start.7) | collective-permute-done | bytes 262176 | tf_op jit(solution)/shard_map/ppermute | solution.py:358
  91.7 5.6 %collective-permute-done.10.refs_11_ = bf16[128,1024]{1,0:T(8,128)(2,1)S(1)} collective-permute-done((bf16[128,1024]{1,0:T(8,128)(2,1)}, bf16[128,1024]{1,0:T(8,128)(2,1)S(1)}, u32[]{:S(2)}, u32[]{:S(2)}) %collective-permute-start.10) | collective-permute-done | bytes 262176 | tf_op jit(solution)/shard_map/ppermute | solution.py:358
  97.3 0.7 copy-done.1
  98.0 13.7 %project.1 = bf16[1024,1536]{1,0:T(8,128)(2,1)} custom-call(s32[4]{0:T(128)S(1)} %and_select_fusion.1.place, bf16[1024,512]{1,0:T(8,128)(2,1)S(1)} %fusion.pick, bf16[128,1024]{1,0:T(8,128)(2,1)S(1)} %get-tuple-element.12.refs_0_, bf16[128,1024]{1,0:T(8,128)(2,1)S(1)} %collective-permute-done.refs_1_, bf16[128,1024]{1,0:T(8,128)(2,1)S(1)} %collective-permute-done.1.refs_2_, ...), custom_call_target="tpu_custom_call" | custom-call | tf_op jit(solution)/shard_map/project/pallas_call | solution.py:186
  111.7 7.9 %all-to-all-start.2 = ((bf16[128,8,1536]{2,1,0:T(8,128)(2,1)}), bf16[128,8,1536]{2,1,0:T(8,128)(2,1)S(1)}, u32[]{:S(2)}, u32[]{:S(2)}) async-start(bf16[128,8,1536]{2,1,0:T(8,128)(2,1)} %bitcast.44), calls=%async_computation.2 | async-start | bytes 6291456 | tf_op jit(solution)/shard_map/all_to_all | solution.py:377
  119.6 0.1 fusion.35
  119.7 0.1 copy.48
  119.8 0.1 copy.49
  119.9 0.1 sub.71
  119.9 0.1 copy.42
  120.0 0.2 copy.43
  120.2 0.2 reshape.207.row_ref
  120.4 0.1 sub.76.column_ref
  120.5 41.2 %all-to-all-done.2 = bf16[128,8,1536]{2,1,0:T(8,128)(2,1)S(1)} async-done(((bf16[128,8,1536]{2,1,0:T(8,128)(2,1)}), bf16[128,8,1536]{2,1,0:T(8,128)(2,1)S(1)}, u32[]{:S(2)}, u32[]{:S(2)}) %all-to-all-start.2) | async-done | bytes 3145760 | tf_op jit(solution)/shard_map/all_to_all | solution.py:377
  161.7 2.5 %merge.1 = bf16[1,128,2,6144]{3,2,1,0:T(2,128)(2,1)} custom-call(s32[256,1]{1,0:T(8,128)S(1)} %sub.76.column_ref, s32[1,256]{1,0:T(1,128)S(1)} %reshape.207.row_ref, bf16[4,32,8,1536]{3,2,1,0:T(8,128)(2,1)S(1)} %bitcast.38), custom_call_target="tpu_custom_call" | custom-call | tf_op jit(solution)/shard_map/merge/pallas_call | solution.py:223
  (37 shorter events, 0.2 us)
Async XLA Ops:
  6.5 17.0 %copy-start.4 = (s32[4]{0:T(128)S(1)}, s32[4]{0:T(128)}, u32[]{:S(2)}) copy-start(s32[4]{0:T(128)} %lengths_ref.5) | copy-start | bytes 52
  6.5 15.8 %copy-start.3 = (f32[8]{0:T(128)S(1)}, f32[8]{0:T(128)}, u32[]{:S(2)}) copy-start(f32[8]{0:T(128)} %rate_ref.5) | copy-start | bytes 100
  6.5 14.6 %copy-start.2 = (s32[512,1]{0,1:T(1,128)S(1)}, s32[512,1]{0,1:T(1,128)}, u32[]{:S(2)}) copy-start(s32[512,1]{0,1:T(1,128)} %param.16) | copy-start | bytes 6148
  6.5 14.8 %copy-start.5 = (s32[512]{0:T(512)S(1)}, s32[512]{0:T(512)}, u32[]{:S(2)}) copy-start(s32[512]{0:T(512)} %param.17) | copy-start | bytes 6148
  6.5 91.5 %all-gather.2.cloned.1.call-start = ((), (), s32[]{:S(2)}) async-start(), calls=%async_computation.3 | async-start | bytes 12976128 | tf_op jit(solution)/shard_map/all_gather | solution.py:277
  11.5 18.5 %all-to-all-start = ((bf16[32,32,128]{2,1,0:T(8,128)(2,1)}), bf16[32,32,128]{2,1,0:T(8,128)(2,1)S(1)}, u32[]{:S(2)}, u32[]{:S(2)}) async-start(bf16[32,32,128]{2,1,0:T(8,128)(2,1)} %bitcast.4), calls=%async_computation | async-start | bytes 524288 | tf_op jit(solution)/shard_map/all_to_all | solution.py:302
  31.3 13.6 %all-to-all-start.1 = ((bf16[32,40,128]{2,1,0:T(8,128)(2,1)}), bf16[32,40,128]{2,1,0:T(8,128)(2,1)S(1)}, u32[]{:S(2)}, u32[]{:S(2)}) async-start(bf16[32,40,128]{2,1,0:T(8,128)(2,1)} %copy.39), calls=%async_computation.1 | async-start | bytes 655360 | tf_op jit(solution)/shard_map/all_to_all | solution.py:326
  39.8 16.7 %copy-start.7 = (s32[4]{0:T(128)S(1)}, s32[4]{0:T(128)}, u32[]{:S(2)}) copy-start(s32[4]{0:T(128)} %constant.125) | copy-start | bytes 52
  39.9 16.7 %copy-start.6 = (s32[4]{0:T(128)S(1)}, s32[4]{0:T(128)}, u32[]{:S(2)}) copy-start(s32[4]{0:T(128)} %constant.126) | copy-start | bytes 52
  47.4 9.1 %collective-permute-start = (bf16[128,1024]{1,0:T(8,128)(2,1)S(1)}, bf16[128,1024]{1,0:T(8,128)(2,1)S(1)}, u32[]{:S(2)}, u32[]{:S(2)}) collective-permute-start(bf16[128,1024]{1,0:T(8,128)(2,1)S(1)} %get-tuple-element.12.refs_0_), channel_id=1, source_target_pairs={{0,32},{32,64},{64,96},{96,0},{1,33},{33,65},{65,97},{97,1},{2,34}... | collective-permute-start | bytes 786440 | tf_op jit(solution)/shard_map/ppermute | solution.py:356
  47.5 20.3 %collective-permute-start.1 = (bf16[128,1024]{1,0:T(8,128)(2,1)S(1)}, bf16[128,1024]{1,0:T(8,128)(2,1)S(1)}, u32[]{:S(2)}, u32[]{:S(2)}) collective-permute-start(bf16[128,1024]{1,0:T(8,128)(2,1)S(1)} %get-tuple-element.12.refs_0_), channel_id=1, source_target_pairs={{0,96},{32,0},{64,32},{96,64},{1,97},{33,1},{65,33},{97,65},{2,98}... | collective-permute-start | bytes 786440 | tf_op jit(solution)/shard_map/ppermute | solution.py:357
  50.1 13.6 %collective-permute-start.3 = (bf16[128,1024]{1,0:T(8,128)(2,1)S(1)}, bf16[128,1024]{1,0:T(8,128)(2,1)S(1)}, u32[]{:S(2)}, u32[]{:S(2)}) collective-permute-start(bf16[128,1024]{1,0:T(8,128)(2,1)S(1)} %get-tuple-element.13), channel_id=1, source_target_pairs={{0,3},{1,0},{2,1},{3,2},{4,7},{5,4},{6,5},{7,6},{8,11},{9,8},{10,9... | collective-permute-start | bytes 786440 | tf_op jit(solution)/shard_map/ppermute | solution.py:352
  52.7 15.0 %collective-permute-start.4 = (bf16[128,1024]{1,0:T(8,128)(2,1)S(1)}, bf16[128,1024]{1,0:T(8,128)(2,1)}, u32[]{:S(2)}, u32[]{:S(2)}) collective-permute-start(bf16[128,1024]{1,0:T(8,128)(2,1)S(1)} %get-tuple-element.14), channel_id=1, source_target_pairs={{0,1},{1,2},{2,3},{3,0},{4,5},{5,6},{6,7},{7,4},{8,9},{9,10},{10,1... | collective-permute-start | bytes 786440 | tf_op jit(solution)/shard_map/ppermute | solution.py:352
  52.7 25.0 %collective-permute-start.11 = (bf16[128,1024]{1,0:T(8,128)(2,1)S(1)}, bf16[128,1024]{1,0:T(8,128)(2,1)}, u32[]{:S(2)}, u32[]{:S(2)}) collective-permute-start(bf16[128,1024]{1,0:T(8,128)(2,1)S(1)} %get-tuple-element.17), channel_id=1, source_target_pairs={{0,2},{1,3},{2,0},{3,1},{4,6},{5,7},{6,4},{7,5},{8,10},{9,11},{10,... | collective-permute-start | bytes 786440 | tf_op jit(solution)/shard_map/ppermute | solution.py:352
  56.5 21.2 %collective-permute-start.2 = (bf16[128,1024]{1,0:T(8,128)(2,1)S(1)}, bf16[128,1024]{1,0:T(8,128)(2,1)S(1)}, u32[]{:S(2)}, u32[]{:S(2)}) collective-permute-start(bf16[128,1024]{1,0:T(8,128)(2,1)S(1)} %collective-permute-done.refs_1_), channel_id=1, source_target_pairs={{0,32},{32,64},{64,96},{96,0},{1,33},{33,65},{65,97},{97,1},{2,34}... | collective-permute-start | bytes 786440 | tf_op jit(solution)/shard_map/ppermute | solution.py:358
  67.8 11.0 %collective-permute-start.6 = (bf16[128,1024]{1,0:T(8,128)(2,1)S(1)}, bf16[128,1024]{1,0:T(8,128)(2,1)S(1)}, u32[]{:S(2)}, u32[]{:S(2)}) collective-permute-start(bf16[128,1024]{1,0:T(8,128)(2,1)S(1)} %collective-permute-done.3.refs_4_), channel_id=1, source_target_pairs={{0,96},{32,0},{64,32},{96,64},{1,97},{33,1},{65,33},{97,65},{2,98}... | collective-permute-start | bytes 786440 | tf_op jit(solution)/shard_map/ppermute | solution.py:357
  67.9 12.4 %collective-permute-start.5 = (bf16[128,1024]{1,0:T(8,128)(2,1)S(1)}, bf16[128,1024]{1,0:T(8,128)(2,1)S(1)}, u32[]{:S(2)}, u32[]{:S(2)}) collective-permute-start(bf16[128,1024]{1,0:T(8,128)(2,1)S(1)} %collective-permute-done.3.refs_4_), channel_id=1, source_target_pairs={{0,32},{32,64},{64,96},{96,0},{1,33},{33,65},{65,97},{97,1},{2,34}... | collective-permute-start | bytes 786440 | tf_op jit(solution)/shard_map/ppermute | solution.py:356
  69.2 12.4 %collective-permute-start.8 = (bf16[128,1024]{1,0:T(8,128)(2,1)}, bf16[128,1024]{1,0:T(8,128)(2,1)}, u32[]{:S(2)}, u32[]{:S(2)}) collective-permute-start(bf16[128,1024]{1,0:T(8,128)(2,1)} %collective-permute-done.4.refs_8_), channel_id=1, source_target_pairs={{0,32},{32,64},{64,96},{96,0},{1,33},{33,65},{65,97},{97,1},{2,34}... | collective-permute-start | bytes 786440 | tf_op jit(solution)/shard_map/ppermute | solution.py:356
  77.7 6.1 %collective-permute-start.13 = (bf16[128,1024]{1,0:T(8,128)(2,1)}, bf16[128,1024]{1,0:T(8,128)(2,1)}, u32[]{:S(2)}, u32[]{:S(2)}) collective-permute-start(bf16[128,1024]{1,0:T(8,128)(2,1)} %collective-permute-done.11.refs_12_), channel_id=1, source_target_pairs={{0,96},{32,0},{64,32},{96,64},{1,97},{33,1},{65,33},{97,65},{2,98}... | collective-permute-start | bytes 786440 | tf_op jit(solution)/shard_map/ppermute | solution.py:357
  78.7 10.8 %collective-permute-start.9 = (bf16[128,1024]{1,0:T(8,128)(2,1)}, bf16[128,1024]{1,0:T(8,128)(2,1)S(1)}, u32[]{:S(2)}, u32[]{:S(2)}) collective-permute-start(bf16[128,1024]{1,0:T(8,128)(2,1)} %collective-permute-done.4.refs_8_), channel_id=1, source_target_pairs={{0,96},{32,0},{64,32},{96,64},{1,97},{33,1},{65,33},{97,65},{2,98}... | collective-permute-start | bytes 786440 | tf_op jit(solution)/shard_map/ppermute | solution.py:357
  78.8 19.2 %collective-permute-start.12 = (bf16[128,1024]{1,0:T(8,128)(2,1)}, bf16[128,1024]{1,0:T(8,128)(2,1)}, u32[]{:S(2)}, u32[]{:S(2)}) collective-permute-start(bf16[128,1024]{1,0:T(8,128)(2,1)} %collective-permute-done.11.refs_12_), channel_id=1, source_target_pairs={{0,32},{32,64},{64,96},{96,0},{1,33},{33,65},{65,97},{97,1},{2,34}... | collective-permute-start | bytes 786440 | tf_op jit(solution)/shard_map/ppermute | solution.py:356
  80.2 11.5 %collective-permute-start.7 = (bf16[128,1024]{1,0:T(8,128)(2,1)S(1)}, bf16[128,1024]{1,0:T(8,128)(2,1)S(1)}, u32[]{:S(2)}, u32[]{:S(2)}) collective-permute-start(bf16[128,1024]{1,0:T(8,128)(2,1)S(1)} %collective-permute-done.5.refs_5_), channel_id=1, source_target_pairs={{0,32},{32,64},{64,96},{96,0},{1,33},{33,65},{65,97},{97,1},{2,34}... | collective-permute-start | bytes 786440 | tf_op jit(solution)/shard_map/ppermute | solution.py:358
  81.6 15.7 %collective-permute-start.10 = (bf16[128,1024]{1,0:T(8,128)(2,1)}, bf16[128,1024]{1,0:T(8,128)(2,1)S(1)}, u32[]{:S(2)}, u32[]{:S(2)}) collective-permute-start(bf16[128,1024]{1,0:T(8,128)(2,1)} %collective-permute-done.8.refs_9_), channel_id=1, source_target_pairs={{0,32},{32,64},{64,96},{96,0},{1,33},{33,65},{65,97},{97,1},{2,34}... | collective-permute-start | bytes 786440 | tf_op jit(solution)/shard_map/ppermute | solution.py:358
  83.9 14.2 %collective-permute-start.14 = (bf16[128,1024]{1,0:T(8,128)(2,1)}, bf16[128,1024]{1,0:T(8,128)(2,1)}, u32[]{:S(2)}, u32[]{:S(2)}) collective-permute-start(bf16[128,1024]{1,0:T(8,128)(2,1)} %collective-permute-done.13.refs_14_), channel_id=1, source_target_pairs={{0,96},{32,0},{64,32},{96,64},{1,97},{33,1},{65,33},{97,65},{2,98}... | collective-permute-start | bytes 786440 | tf_op jit(solution)/shard_map/ppermute | solution.py:358
  89.5 2.2 %copy-start = (bf16[128,1024]{1,0:T(8,128)(2,1)}, bf16[128,1024]{1,0:T(8,128)(2,1)S(1)}, u32[]{:S(2)}) copy-start(bf16[128,1024]{1,0:T(8,128)(2,1)S(1)} %collective-permute-done.9.refs_10_) | copy-start | bytes 786436
  97.3 0.7 copy-start.1
  111.7 49.9 %all-to-all-start.2 = ((bf16[128,8,1536]{2,1,0:T(8,128)(2,1)}), bf16[128,8,1536]{2,1,0:T(8,128)(2,1)S(1)}, u32[]{:S(2)}, u32[]{:S(2)}) async-start(bf16[128,8,1536]{2,1,0:T(8,128)(2,1)} %bitcast.44), calls=%async_computation.2 | async-start | bytes 6291456 | tf_op jit(solution)/shard_map/all_to_all | solution.py:377
Sparse Core Ops, SparseCore 0:
  9.6 77.5 all-gather.1
